TPU v7x, 32 devices: a whole 2x2x4 slice. The times are simulated.
32 devices in a mesh: rep: 16 (over z, y, core), shard: 2 (over x).
Axes of the slice: x: 2, y: 2, z: 4, core: 2. Of those that a mesh axis runs over, the one named last changes fastest.
Arguments:
- tokens: bfloat16 [4, 2048, 1024], P('shard', 'rep'), may hold values from -6 to 6
- first_values: bfloat16 [4, 2048, 1024], P('shard', 'rep'), may hold values from -6 to 6
- prefix_len: int32 [4], P('shard'), may hold values from 204 to 1024
- cotangent: bfloat16 [4, 2048, 1024], P('shard', 'rep'), may hold values from -6 to 6
- w_query: bfloat16 [1024, 1024], P('shard'), may hold values from -0.25 to 0.25
- w_key: bfloat16 [1024, 1024], P('shard'), may hold values from -0.25 to 0.25
- w_value: bfloat16 [1024, 1024], P('shard'), may hold values from -0.1875 to 0.1875
- w_output: bfloat16 [1024, 1024], P('shard'), may hold values from -0.75 to 0.75
- w_gate: bfloat16 [1024, 2816], P('shard'), may hold values from -0.1875 to 0.1875
- w_up: bfloat16 [1024, 2816], P('shard'), may hold values from -0.1875 to 0.1875
- w_down: bfloat16 [2816, 1024], P('shard'), may hold values from -0.109375 to 0.109375
- gain_attn: bfloat16 [1024], P('shard'), may hold values from 0.5 to 1.5
- gain_ffn: bfloat16 [1024], P('shard'), may hold values from 0.5 to 1.5
Outputs:
- output: bfloat16 [4, 2048, 1024], P('shard', 'rep')
- grad_tokens: float32 [4, 2048, 1024], P('shard', 'rep')
- grad_first_values: float32 [4, 2048, 1024], P('shard', 'rep')
- grad_query: float32 [1024, 1024], P('shard')
- grad_key: float32 [1024, 1024], P('shard')
- grad_value: float32 [1024, 1024], P('shard')
- grad_output: float32 [1024, 1024], P('shard')
- grad_gate: float32 [1024, 2816], P('shard')
- grad_up: float32 [1024, 2816], P('shard')
- grad_down: float32 [2816, 1024], P('shard')
- grad_gain_attn: float32 [1024], P('shard')
- grad_gain_ffn: float32 [1024], P('shard')
All inputs are finite; a program needn't handle non-finite values.
Results may differ from a plain program's by a relative error of at most 0.025.
Values may be sent and summed in bfloat16 or wider, within the bound.
No kernel may reach another device: no remote copies, remote signals or barrier semaphores. Data moves between devices by JAX's collectives and lax.ppermute only.
A program may use at most 384 MiB of HBM per device.

v0:
```python
import jax
import jax.numpy as jnp
from jax import lax
from jax.sharding import PartitionSpec as P

HEADS = 16


EPSILON = 1e-05
NEGATIVE = -1e30
ROPE_BASE = 10000.0


def rotate_half(values):
    half_dim = values.shape[-1] // 2
    return jnp.concatenate([-values[..., half_dim:], values[..., :half_dim]], axis=-1)


def rope_tables(positions, head_dim):
    half_dim = head_dim // 2
    frequency = ROPE_BASE ** (-2.0 * jnp.arange(half_dim, dtype=jnp.float32) / head_dim)
    angles = positions.astype(jnp.float32)[:, None] * frequency[None, :]
    angles = jnp.concatenate([angles, angles], axis=-1)
    return (jnp.cos(angles), jnp.sin(angles))


def rope_apply(values, cosine_table, sine_table):
    return values * cosine_table + rotate_half(values) * sine_table


def rope_back(gradient, cosine_table, sine_table):
    return gradient * cosine_table - rotate_half(gradient * sine_table)


def norm_rows(values):
    scale = lax.rsqrt(jnp.mean(values * values, axis=-1, keepdims=True) + EPSILON)
    return (values * scale, scale)


def norm_back(gradient, normed, scale):
    return scale * (gradient - normed * jnp.mean(gradient * normed, axis=-1, keepdims=True))


def project(left, right):
    return jnp.einsum("scd,de->sce", left, right, preferred_element_type=jnp.float32)


def project_back(gradient, right):
    return jnp.einsum("sce,de->scd", gradient, right, preferred_element_type=jnp.float32)


def weight_grad(left, gradient):
    return jnp.einsum("scd,sce->de", left, gradient, preferred_element_type=jnp.float32)


def masked_scores(query_rows, key_block, query_pos, key_pos, prefix):
    scores = jnp.einsum(
        "sqhd,skhd->shqk", query_rows, key_block, preferred_element_type=jnp.float32
    )
    allowed = (key_pos[None, None, :] <= query_pos[None, :, None]) | (
        key_pos[None, None, :] < prefix[:, None, None]
    )
    return jnp.where(allowed[:, None], scores, NEGATIVE)


def block_plan(total):
    block_width = min(512, total)
    return (block_width, total // block_width)


def row_stats(query_rows, key_rows, query_pos, prefix):
    block_width, blocks = block_plan(key_rows.shape[1])
    stat_shape = (query_rows.shape[0], query_rows.shape[2], query_rows.shape[1])

    def row_advance(carry, block_index):
        running_max, running_sum = carry
        offset = block_index * block_width
        key_block = lax.dynamic_slice_in_dim(key_rows, offset, block_width, 1)
        key_pos = offset + jnp.arange(block_width, dtype=jnp.int32)
        scores = masked_scores(query_rows, key_block, query_pos, key_pos, prefix)
        new_max = jnp.maximum(running_max, jnp.max(scores, axis=-1))
        running_sum = running_sum * jnp.exp(running_max - new_max) + jnp.sum(
            jnp.exp(scores - new_max[..., None]), axis=-1
        )
        return ((new_max, running_sum), None)

    initial = (jnp.full(stat_shape, NEGATIVE, jnp.float32), jnp.zeros(stat_shape, jnp.float32))
    (running_max, running_sum), unused = lax.scan(
        row_advance, initial, jnp.arange(blocks, dtype=jnp.int32)
    )
    return running_max + jnp.log(running_sum)


def attend_values(query_rows, key_rows, value_rows, query_pos, prefix, log_mass):
    block_width, blocks = block_plan(key_rows.shape[1])

    def attend_advance(running, block_index):
        offset = block_index * block_width
        key_block = lax.dynamic_slice_in_dim(key_rows, offset, block_width, 1)
        value_block = lax.dynamic_slice_in_dim(value_rows, offset, block_width, 1)
        key_pos = offset + jnp.arange(block_width, dtype=jnp.int32)
        scores = masked_scores(query_rows, key_block, query_pos, key_pos, prefix)
        weights = jnp.exp(scores - log_mass[..., None]).astype(jnp.bfloat16)
        return (
            running
            + jnp.einsum(
                "shqk,skhd->sqhd", weights, value_block, preferred_element_type=jnp.float32
            ),
            None,
        )

    running, unused = lax.scan(
        attend_advance,
        jnp.zeros(query_rows.shape, jnp.float32),
        jnp.arange(blocks, dtype=jnp.int32),
    )
    return running


def query_grads(
    query_rows, grad_rows, key_rows, value_rows, query_pos, prefix, log_mass, delta_rows
):
    block_width, blocks = block_plan(key_rows.shape[1])

    def query_advance(running, block_index):
        offset = block_index * block_width
        key_block = lax.dynamic_slice_in_dim(key_rows, offset, block_width, 1)
        value_block = lax.dynamic_slice_in_dim(value_rows, offset, block_width, 1)
        key_pos = offset + jnp.arange(block_width, dtype=jnp.int32)
        scores = masked_scores(query_rows, key_block, query_pos, key_pos, prefix)
        weights = jnp.exp(scores - log_mass[..., None])
        grad_weights = jnp.einsum(
            "sqhd,skhd->shqk", grad_rows, value_block, preferred_element_type=jnp.float32
        )
        grad_scores = (weights * (grad_weights - delta_rows[..., None])).astype(jnp.bfloat16)
        running = running + jnp.einsum(
            "shqk,skhd->sqhd", grad_scores, key_block, preferred_element_type=jnp.float32
        )
        grad_keys = jnp.einsum(
            "shqk,sqhd->skhd", grad_scores, query_rows, preferred_element_type=jnp.float32
        )
        grad_values = jnp.einsum(
            "shqk,sqhd->skhd",
            weights.astype(jnp.bfloat16),
            grad_rows,
            preferred_element_type=jnp.float32,
        )
        return (running, (grad_keys, grad_values))

    running, stacked = lax.scan(
        query_advance, jnp.zeros(query_rows.shape, jnp.float32), jnp.arange(blocks, dtype=jnp.int32)
    )
    stacked = tuple(
        (
            jnp.moveaxis(member, 0, 1).reshape(query_rows.shape[0], key_rows.shape[1], -1)
            for member in stacked
        )
    )
    return (running, stacked)


def local(
    tokens,
    first_values,
    prefix_len,
    cotangent,
    w_query,
    w_key,
    w_value,
    w_output,
    w_gate,
    w_up,
    w_down,
    gain_attn,
    gain_ffn,
):
    gathered = (
        lax.all_gather(w_query, "shard", axis=0, tiled=True),
        lax.all_gather(w_key, "shard", axis=0, tiled=True),
        lax.all_gather(w_value, "shard", axis=0, tiled=True),
        lax.all_gather(w_output, "shard", axis=0, tiled=True),
        lax.all_gather(w_gate, "shard", axis=0, tiled=True),
        lax.all_gather(w_up, "shard", axis=0, tiled=True),
        lax.all_gather(w_down, "shard", axis=0, tiled=True),
        lax.all_gather(gain_attn, "shard", axis=0, tiled=True),
        lax.all_gather(gain_ffn, "shard", axis=0, tiled=True),
    )
    (
        full_query,
        full_key,
        full_value,
        full_output,
        full_gate,
        full_up,
        full_down,
        full_gain1,
        full_gain2,
    ) = gathered
    seq_count, row_count, model_width = tokens.shape
    head_dim = model_width // HEADS
    head_shape = (seq_count, row_count, HEADS, head_dim)
    local_pos = lax.axis_index("rep") * row_count + jnp.arange(row_count, dtype=jnp.int32)
    cosine_table, sine_table = rope_tables(local_pos, head_dim)
    cosine_table = cosine_table[None, :, None, :]
    sine_table = sine_table[None, :, None, :]
    inputs = tokens.astype(jnp.float32)
    normed1, scale1 = norm_rows(inputs)
    hidden1 = (normed1 * full_gain1).astype(jnp.bfloat16)
    query_raw = project(hidden1, full_query).reshape(head_shape)
    key_raw = project(hidden1, full_key).reshape(head_shape)
    query_rot = (rope_apply(query_raw, cosine_table, sine_table) * 0.125).astype(jnp.bfloat16)
    key_rot = (
        rope_apply(key_raw, cosine_table, sine_table)
        .astype(jnp.bfloat16)
        .reshape(seq_count, row_count, model_width)
    )
    value_mix = (
        0.5 * project(hidden1, full_value) + 0.5 * first_values.astype(jnp.float32)
    ).astype(jnp.bfloat16)
    key_all, value_all = (
        lax.all_gather(key_rot, "rep", axis=1, tiled=True),
        lax.all_gather(value_mix, "rep", axis=1, tiled=True),
    )
    all_shape = (seq_count, key_all.shape[1], HEADS, head_dim)
    key_heads = key_all.reshape(all_shape)
    value_heads = value_all.reshape(all_shape)
    log_mass = row_stats(query_rot, key_heads, local_pos, prefix_len)
    attended_full = attend_values(
        query_rot, key_heads, value_heads, local_pos, prefix_len, log_mass
    )
    attended = attended_full.reshape(seq_count, row_count, model_width).astype(jnp.bfloat16)
    residual = inputs + project(attended, full_output)
    normed2, scale2 = norm_rows(residual)
    hidden2 = (normed2 * full_gain2).astype(jnp.bfloat16)
    gate_pre = project(hidden2, full_gate)
    up_pre = project(hidden2, full_up)
    sigma = jax.nn.sigmoid(gate_pre)
    swish = gate_pre * sigma
    swiglu = (swish * up_pre).astype(jnp.bfloat16)
    output = (residual + project(swiglu, full_down)).astype(jnp.bfloat16)
    again = (
        lax.all_gather(w_query, "shard", axis=0, tiled=True),
        lax.all_gather(w_key, "shard", axis=0, tiled=True),
        lax.all_gather(w_value, "shard", axis=0, tiled=True),
        lax.all_gather(w_output, "shard", axis=0, tiled=True),
        lax.all_gather(w_gate, "shard", axis=0, tiled=True),
        lax.all_gather(w_up, "shard", axis=0, tiled=True),
        lax.all_gather(w_down, "shard", axis=0, tiled=True),
        lax.all_gather(gain_attn, "shard", axis=0, tiled=True),
        lax.all_gather(gain_ffn, "shard", axis=0, tiled=True),
    )
    (
        back_query,
        back_key,
        back_value,
        back_output,
        back_gate,
        back_up,
        back_down,
        back_gain1,
        back_gain2,
    ) = again
    grad_swiglu = project_back(cotangent, back_down)
    grad_gate_pre = (grad_swiglu * up_pre * sigma * (1.0 + gate_pre * (1.0 - sigma))).astype(
        jnp.bfloat16
    )
    grad_up_pre = (grad_swiglu * swish).astype(jnp.bfloat16)
    grad_hidden2 = project_back(grad_gate_pre, back_gate) + project_back(grad_up_pre, back_up)
    grad_gain2 = jnp.sum(grad_hidden2 * normed2, axis=(0, 1))
    grad_residual = cotangent.astype(jnp.float32) + norm_back(
        grad_hidden2 * back_gain2, normed2, scale2
    )
    grad_residual_low = grad_residual.astype(jnp.bfloat16)
    grad_attended = project_back(grad_residual_low, back_output).astype(jnp.bfloat16)
    grad_heads = grad_attended.reshape(head_shape)
    key_back, value_back = (
        lax.all_gather(key_rot, "rep", axis=1, tiled=True),
        lax.all_gather(value_mix, "rep", axis=1, tiled=True),
    )
    key_back = key_back.reshape(all_shape)
    value_back = value_back.reshape(all_shape)
    delta_rows = jnp.einsum("sqhd,sqhd->shq", grad_heads.astype(jnp.float32), attended_full)
    grad_query_rot, key_blocks = query_grads(
        query_rot, grad_heads, key_back, value_back, local_pos, prefix_len, log_mass, delta_rows
    )
    grad_key_rot, grad_value_mix = (
        lax.psum_scatter(
            key_blocks[0].astype(jnp.bfloat16), "rep", scatter_dimension=1, tiled=True
        ).astype(jnp.float32),
        lax.psum_scatter(
            key_blocks[1].astype(jnp.bfloat16), "rep", scatter_dimension=1, tiled=True
        ).astype(jnp.float32),
    )
    grad_key_rot = grad_key_rot.reshape(head_shape)
    grad_query_raw = (
        rope_back(grad_query_rot * 0.125, cosine_table, sine_table)
        .astype(jnp.bfloat16)
        .reshape(seq_count, row_count, model_width)
    )
    grad_key_raw = (
        rope_back(grad_key_rot, cosine_table, sine_table)
        .astype(jnp.bfloat16)
        .reshape(seq_count, row_count, model_width)
    )
    grad_mix_low = grad_value_mix.astype(jnp.bfloat16).astype(jnp.float32)
    grad_value_raw = (0.5 * grad_mix_low).astype(jnp.bfloat16)
    grad_first = 0.5 * grad_mix_low
    grad_hidden1 = (
        project_back(grad_query_raw, back_query)
        + project_back(grad_key_raw, back_key)
        + project_back(grad_value_raw, back_value)
    )
    grad_gain1 = jnp.sum(grad_hidden1 * normed1, axis=(0, 1))
    grad_inputs = grad_residual + norm_back(grad_hidden1 * back_gain1, normed1, scale1)
    grad_wquery = weight_grad(hidden1, grad_query_raw)
    grad_wkey = weight_grad(hidden1, grad_key_raw)
    grad_wvalue = weight_grad(hidden1, grad_value_raw)
    grad_outproj = weight_grad(attended, grad_residual_low)
    grad_gate = weight_grad(hidden2, grad_gate_pre)
    grad_upward = weight_grad(hidden2, grad_up_pre)
    grad_down = weight_grad(swiglu, cotangent)
    shares = (
        lax.psum_scatter(
            grad_wquery.astype(jnp.bfloat16), "shard", scatter_dimension=0, tiled=True
        ).astype(jnp.float32),
        lax.psum_scatter(
            grad_wkey.astype(jnp.bfloat16), "shard", scatter_dimension=0, tiled=True
        ).astype(jnp.float32),
        lax.psum_scatter(
            grad_wvalue.astype(jnp.bfloat16), "shard", scatter_dimension=0, tiled=True
        ).astype(jnp.float32),
        lax.psum_scatter(
            grad_outproj.astype(jnp.bfloat16), "shard", scatter_dimension=0, tiled=True
        ).astype(jnp.float32),
        lax.psum_scatter(
            grad_gate.astype(jnp.bfloat16), "shard", scatter_dimension=0, tiled=True
        ).astype(jnp.float32),
        lax.psum_scatter(
            grad_upward.astype(jnp.bfloat16), "shard", scatter_dimension=0, tiled=True
        ).astype(jnp.float32),
        lax.psum_scatter(
            grad_down.astype(jnp.bfloat16), "shard", scatter_dimension=0, tiled=True
        ).astype(jnp.float32),
        lax.psum_scatter(
            grad_gain1.astype(jnp.bfloat16), "shard", scatter_dimension=0, tiled=True
        ).astype(jnp.float32),
        lax.psum_scatter(
            grad_gain2.astype(jnp.bfloat16), "shard", scatter_dimension=0, tiled=True
        ).astype(jnp.float32),
    )
    totals = (
        lax.psum(shares[0].astype(jnp.bfloat16), "rep").astype(jnp.float32),
        lax.psum(shares[1].astype(jnp.bfloat16), "rep").astype(jnp.float32),
        lax.psum(shares[2].astype(jnp.bfloat16), "rep").astype(jnp.float32),
        lax.psum(shares[3].astype(jnp.bfloat16), "rep").astype(jnp.float32),
        lax.psum(shares[4].astype(jnp.bfloat16), "rep").astype(jnp.float32),
        lax.psum(shares[5].astype(jnp.bfloat16), "rep").astype(jnp.float32),
        lax.psum(shares[6].astype(jnp.bfloat16), "rep").astype(jnp.float32),
        lax.psum(shares[7].astype(jnp.bfloat16), "rep").astype(jnp.float32),
        lax.psum(shares[8].astype(jnp.bfloat16), "rep").astype(jnp.float32),
    )
    return (
        output,
        grad_inputs,
        grad_first,
        totals[0],
        totals[1],
        totals[2],
        totals[3],
        totals[4],
        totals[5],
        totals[6],
        totals[7],
        totals[8],
    )


def solution(mesh):
    placed = (
        P("shard", "rep", None),
        P("shard", "rep", None),
        P("shard"),
        P("shard", "rep", None),
        P("shard", None),
        P("shard", None),
        P("shard", None),
        P("shard", None),
        P("shard", None),
        P("shard", None),
        P("shard", None),
        P("shard"),
        P("shard"),
    )
    return jax.shard_map(
        local,
        mesh=mesh,
        in_specs=placed,
        out_specs=(
            P("shard", "rep", None),
            P("shard", "rep", None),
            P("shard", "rep", None),
            P("shard", None),
            P("shard", None),
            P("shard", None),
            P("shard", None),
            P("shard", None),
            P("shard", None),
            P("shard", None),
            P("shard"),
            P("shard"),
        ),
        check_vma=False,
    )
```

profile of v0, /device:TPU:0, one launch (start us, length us, event | category | flops | bytes accessed | tf_op | source)
XLA Modules:
  0.0 1526.2 jit_solution(9713102780563995650)
XLA Ops:
  10.1 5.3 all-gather
  17.7 27.7 %all-gather.16.cloned.1.call-done = bf16[1024,1024]{1,0:T(8,128)(2,1)} async-done(((bf16[512,1024]{1,0:T(8,128)(2,1)}), bf16[1024,1024]{1,0:T(8,128)(2,1)}) %all-gather.16.cloned.1.call-update) | async-done | bytes 2097168 | tf_op jit(solution)/shard_map/all_gather | solution.py:179
  53.1 27.0 %all-gather.12.cloned.1.call-done = bf16[1024,1024]{1,0:T(8,128)(2,1)} async-done(((bf16[512,1024]{1,0:T(8,128)(2,1)}), bf16[1024,1024]{1,0:T(8,128)(2,1)}) %all-gather.12.cloned.1.call-update) | async-done | bytes 2097168 | tf_op jit(solution)/shard_map/all_gather | solution.py:180
  90.1 24.7 %all-gather.20.cloned.1.call-done = bf16[1024,1024]{1,0:T(8,128)(2,1)} async-done(((bf16[512,1024]{1,0:T(8,128)(2,1)}), bf16[1024,1024]{1,0:T(8,128)(2,1)}) %all-gather.20.cloned.1.call-update) | async-done | bytes 2097168 | tf_op jit(solution)/shard_map/all_gather | solution.py:178
  117.7 72.9 %all-gather.28.cloned.1.call-done = bf16[2816,1024]{1,0:T(8,128)(2,1)} async-done(((bf16[1408,1024]{1,0:T(8,128)(2,1)}), bf16[2816,1024]{1,0:T(8,128)(2,1)}) %all-gather.28.cloned.1.call-update) | async-done | bytes 5767184 | tf_op jit(solution)/shard_map/all_gather | solution.py:184
  190.6 5.9 fusion.67
  196.5 71.0 %all-gather.18.cloned.1.call-done = bf16[2,2048,1024]{2,1,0:T(8,128)(2,1)} async-done(((bf16[2,128,1024]{2,1,0:T(8,128)(2,1)}), bf16[2,2048,1024]{2,1,0:T(8,128)(2,1)}) %all-gather.18.cloned.1.call-update) | async-done | bytes 8388624 | tf_op jit(solution)/shard_map/all_gather | solution.py:221
  267.6 12.1 copy.89
  279.6 53.8 %while.39 = (s32[]{:T(128)}, f32[2,16,128]{2,1,0:T(8,128)S(1)}, f32[2,16,128]{2,1,0:T(8,128)S(1)}, s32[4]{0:T(128)S(1)}, s32[2]{0:T(128)S(1)}, /*index=5*/bf16[2...) while((s32[]{:T(128)}, f32[2,16,128]{2,1,0:T(8,128)S(1)}, ...), condition=%wide.region_4.5_spmd.clone, body=%wide.region_1.4_spmd.clone.sunk | while | flops 279139968 | bytes 20145364 | solution.py:88
  281.3 6.5 fusion.201
  294.5 6.5 fusion.201
  300.9 6.0 exponential_reduce_fusion.2
  308.7 6.5 fusion.201
  321.9 6.5 fusion.201
  333.5 9.6 all-gather.14.cloned.1.call-done
  343.1 11.9 copy.84
  355.0 27.8 %while.40 = (s32[]{:T(128)}, f32[2,128,16,64]{1,3,2,0:T(8,128)S(1)}, s32[4]{0:T(128)S(1)}, bf16[2,2048,16,64]{1,3,2,0:T(8,128)(2,1)}, s32[2]{0:T(128)S(1)}, /*in...) while((s32[]{:T(128)}, ...), condition=%wide.region_6.7_spmd.clone, body=%wide.region_5.6_spmd.clone.sunk | while | flops 543884928 | bytes 7236312 | solution.py:112
  356.7 5.2 fusion.207
  363.6 5.2 fusion.207
  377.5 5.2 fusion.207
  387.1 65.3 %all-gather.26.cloned.1.call-done = bf16[1024,2816]{1,0:T(8,128)(2,1)} async-done(((bf16[512,2816]{1,0:T(8,128)(2,1)}), bf16[1024,2816]{1,0:T(8,128)(2,1)}) %all-gather.26.cloned.1.call-update) | async-done | bytes 5767184 | tf_op jit(solution)/shard_map/all_gather | solution.py:183
  452.4 5.9 fusion.73
  458.2 70.2 %all-gather.24.cloned.1.call-done = bf16[1024,2816]{1,0:T(8,128)(2,1)} async-done(((bf16[512,2816]{1,0:T(8,128)(2,1)}), bf16[1024,2816]{1,0:T(8,128)(2,1)}) %all-gather.24.cloned.1.call-update) | async-done | bytes 5767184 | tf_op jit(solution)/shard_map/all_gather | solution.py:182
  528.4 7.3 multiply_convert_fusion.1
  547.7 94.5 %while.41 = (s32[]{:T(128)}, f32[2,128,16,64]{1,3,2,0:T(8,128)S(1)}, bf16[4,2,512,16,64]{2,4,3,1,0:T(8,128)(2,1)}, bf16[4,2,512,16,64]{2,4,3,1,0:T(8,128)(2,1)},...) while((s32[]{:T(128)}, ...), condition=%wide.region_10.11_spmd.clone, body=%wide.region_9.10_spmd.clone.sunk | while | flops 1359677056 | bytes 132703600 | solution.py:150
  552.7 8.1 fusion.219
  576.2 8.1 fusion.219
  599.8 8.1 fusion.219
  623.3 8.1 fusion.219
  642.1 20.3 %copy.129 = bf16[2,4,512,16,64]{4,3,2,1,0:T(8,128)(2,1)} copy(bf16[2,4,512,16,64]{2,4,3,0,1:T(8,128)(2,1)} %bitcast.239) | data formatting | bytes 16777216 | tf_op jit(solution)/shard_map/convert_element_type | solution.py:288
  662.5 22.6 %reshape.383 = bf16[2,2048,1024]{2,1,0:T(8,128)(2,1)} reshape(bf16[2,4,512,16,64]{4,3,2,1,0:T(8,128)(2,1)} %copy.129) | data formatting | bytes 16777216 | tf_op jit(solution)/shard_map/convert_element_type | solution.py:288
  685.1 20.6 %copy.130 = bf16[2,4,512,16,64]{4,3,2,1,0:T(8,128)(2,1)} copy(bf16[2,4,512,16,64]{2,4,3,0,1:T(8,128)(2,1)} %bitcast.240) | data formatting | bytes 16777216 | tf_op jit(solution)/shard_map/convert_element_type | solution.py:291
  705.7 22.7 %reshape.384 = bf16[2,2048,1024]{2,1,0:T(8,128)(2,1)} reshape(bf16[2,4,512,16,64]{4,3,2,1,0:T(8,128)(2,1)} %copy.130) | data formatting | bytes 16777216 | tf_op jit(solution)/shard_map/convert_element_type | solution.py:291
  731.6 5.6 bitcast_convert_fusion.2
  737.3 5.7 bitcast_convert_fusion.1
  744.0 5.6 bitcast_convert_fusion
  751.5 37.1 %reduce-scatter.10.cloned.1.call-done = bf16[2,128,1024]{2,1,0:T(8,128)(2,1)} async-done(((bf16[2,2048,1024]{2,1,0:T(8,128)(2,1)}), bf16[2,128,1024]{2,1,0:T(8,128)(2,1)}) %reduce-scatter.10.cloned.1.call-update) | async-done | bytes 524304 | tf_op jit(solution)/shard_map/reduce_scatter | solution.py:287
  801.3 94.4 %reduce-scatter.12.cloned.1.call-done = bf16[2,128,1024]{2,1,0:T(8,128)(2,1)} async-done(((bf16[2,2048,1024]{2,1,0:T(8,128)(2,1)}), bf16[2,128,1024]{2,1,0:T(8,128)(2,1)}) %reduce-scatter.12.cloned.1.call-update) | async-done | bytes 524304 | tf_op jit(solution)/shard_map/reduce_scatter | solution.py:290
  899.4 30.6 %reduce-scatter.20.cloned.1.call-done = bf16[512,1024]{1,0:T(8,128)(2,1)} async-done(((bf16[1024,1024]{1,0:T(8,128)(2,1)}), bf16[512,1024]{1,0:T(8,128)(2,1)}) %reduce-scatter.20.cloned.1.call-update) | async-done | bytes 1048592 | tf_op jit(solution)/shard_map/reduce_scatter | solution.py:332
  930.0 74.3 %reduce-scatter.22.cloned.1.call-done = bf16[512,2816]{1,0:T(8,128)(2,1)} async-done(((bf16[1024,2816]{1,0:T(8,128)(2,1)}), bf16[512,2816]{1,0:T(8,128)(2,1)}) %reduce-scatter.22.cloned.1.call-update) | async-done | bytes 2883600 | tf_op jit(solution)/shard_map/reduce_scatter | solution.py:335
  1004.3 74.2 %reduce-scatter.24.cloned.1.call-done = bf16[512,2816]{1,0:T(8,128)(2,1)} async-done(((bf16[1024,2816]{1,0:T(8,128)(2,1)}), bf16[512,2816]{1,0:T(8,128)(2,1)}) %reduce-scatter.24.cloned.1.call-update) | async-done | bytes 2883600 | tf_op jit(solution)/shard_map/reduce_scatter | solution.py:338
  1078.5 74.2 %reduce-scatter.26.cloned.1.call-done = bf16[1408,1024]{1,0:T(8,128)(2,1)} async-done(((bf16[2816,1024]{1,0:T(8,128)(2,1)}), bf16[1408,1024]{1,0:T(8,128)(2,1)}) %reduce-scatter.26.cloned.1.call-update) | async-done | bytes 2883600 | tf_op jit(solution)/shard_map/reduce_scatter | solution.py:341
  1152.7 34.6 %reduce-scatter.14.cloned.1.call-done = bf16[512,1024]{1,0:T(8,128)(2,1)} async-done(((bf16[1024,1024]{1,0:T(8,128)(2,1)}), bf16[512,1024]{1,0:T(8,128)(2,1)}) %reduce-scatter.14.cloned.1.call-update) | async-done | bytes 1048592 | tf_op jit(solution)/shard_map/reduce_scatter | solution.py:323
  1187.4 34.6 %reduce-scatter.16.cloned.1.call-done = bf16[512,1024]{1,0:T(8,128)(2,1)} async-done(((bf16[1024,1024]{1,0:T(8,128)(2,1)}), bf16[512,1024]{1,0:T(8,128)(2,1)}) %reduce-scatter.16.cloned.1.call-update) | async-done | bytes 1048592 | tf_op jit(solution)/shard_map/reduce_scatter | solution.py:326
  1222.0 34.6 %reduce-scatter.18.cloned.1.call-done = bf16[512,1024]{1,0:T(8,128)(2,1)} async-done(((bf16[1024,1024]{1,0:T(8,128)(2,1)}), bf16[512,1024]{1,0:T(8,128)(2,1)}) %reduce-scatter.18.cloned.1.call-update) | async-done | bytes 1048592 | tf_op jit(solution)/shard_map/reduce_scatter | solution.py:329
  1258.5 5.7 fusion.120
  1273.7 34.0 %all-reduce.2 = (bf16[512]{0:T(512)(128)(2,1)S(1)}, bf16[512]{0:T(512)(128)(2,1)S(1)}) all-reduce(bf16[512]{0:T(512)(128)(2,1)S(1)} %dynamic-slice.1, bf16[512]{0:T(512)(128)(2,1)S(1)} %dynamic-slice.3), channel_id=1, replica_groups=mesh['rep'=16,'shard'=2] {'rep'}, use_global_device_ids=true, to_apply=%region_30.31 | all-reduce | flops 1024 | bytes 4096 | tf_op jit(solution)/shard_map/psum | solution.py:359
  1311.5 189.8 %all-reduce.7.cloned.1.call-done = (bf16[512,1024]{1,0:T(8,128)(2,1)}, bf16[512,1024]{1,0:T(8,128)(2,1)}, bf16[512,1024]{1,0:T(8,128)(2,1)}, bf16[512,1024]{1,0:...) async-done(((bf16[512,1024]{1,0:T(8,128)(2,1)}, bf16[512,1024]{1,0:T(8,128)(2,1)}, bf16[512,1024]{1,0:T(8,128)(2,1)}, ...) | async-done | bytes 12845072 | tf_op jit(solution)/shard_map/psum | solution.py:352
  (350 shorter events, 183.7 us)
Async XLA Ops:
  7.2 38.2 %all-gather.16.cloned.1.call-start = ((), (), s32[]{:S(2)}) async-start(), calls=%async_computation.11 | async-start | bytes 3145728 | tf_op jit(solution)/shard_map/all_gather | solution.py:179
  7.9 9.6 copy-start.2
  7.9 72.1 %all-gather.12.cloned.1.call-start = ((), (), s32[]{:S(2)}) async-start(), calls=%async_computation.9 | async-start | bytes 3145728 | tf_op jit(solution)/shard_map/all_gather | solution.py:180
  8.7 106.0 %all-gather.20.cloned.1.call-start = ((), (), s32[]{:S(2)}) async-start(), calls=%async_computation.13 | async-start | bytes 3145728 | tf_op jit(solution)/shard_map/all_gather | solution.py:178
  9.4 181.2 %all-gather.28.cloned.1.call-start = ((), (), s32[]{:S(2)}) async-start(), calls=%async_computation.17 | async-start | bytes 8650752 | tf_op jit(solution)/shard_map/all_gather | solution.py:184
  10.0 257.6 %all-gather.18.cloned.1.call-start = ((), (), s32[]{:S(2)}) async-start(), calls=%async_computation.12 | async-start | bytes 8912896 | tf_op jit(solution)/shard_map/all_gather | solution.py:221
  15.4 99.4 %copy-start.37 = (f32[2,1,512]{2,1,0:T(1,128)}, f32[2,1,512]{2,1,0:T(1,128)S(1)}, u32[]{:S(2)}) copy-start(f32[2,1,512]{2,1,0:T(1,128)S(1)} %convert_element_type.230) | copy-start | bytes 12292
  16.2 101.3 %copy-start.35 = (f32[128,64]{0,1:T(8,128)}, f32[128,64]{0,1:T(8,128)S(1)}, u32[]{:S(2)}) copy-start(f32[128,64]{0,1:T(8,128)S(1)} %get-tuple-element.414) | copy-start | bytes 98308
  17.5 33.3 %copy-start.15 = (f32[128,1024]{1,0:T(8,128)}, f32[128,1024]{1,0:T(8,128)S(1)}, u32[]{:S(2)}) copy-start(f32[128,1024]{1,0:T(8,128)S(1)} %copy.85) | copy-start | bytes 1572868
  17.7 97.0 %copy-start.42 = (f32[2,128]{1,0:T(2,128)}, f32[2,128]{1,0:T(2,128)S(1)}, u32[]{:S(2)}) copy-start(f32[2,128]{1,0:T(2,128)S(1)} %add_rsqrt_fusion.1) | copy-start | bytes 3076
  53.0 290.1 %all-gather.14.cloned.1.call-start = ((), (), s32[]{:S(2)}) async-start(), calls=%async_computation.10 | async-start | bytes 8912896 | tf_op jit(solution)/shard_map/all_gather | solution.py:222
  83.3 300.5 %all-gather.22.cloned.1.call-start = ((), (), s32[]{:S(2)}) async-start(), calls=%async_computation.14 | async-start | bytes 3145728 | tf_op jit(solution)/shard_map/all_gather | solution.py:181
  84.1 368.3 %all-gather.26.cloned.1.call-start = ((), (), s32[]{:S(2)}) async-start(), calls=%async_computation.16 | async-start | bytes 8650752 | tf_op jit(solution)/shard_map/all_gather | solution.py:183
  84.8 443.6 %all-gather.24.cloned.1.call-start = ((), (), s32[]{:S(2)}) async-start(), calls=%async_computation.15 | async-start | bytes 8650752 | tf_op jit(solution)/shard_map/all_gather | solution.py:182
  85.6 703.1 %reduce-scatter.10.cloned.1.call-start = ((), (), s32[]{:S(2)}) async-start(), calls=%async_computation.18 | async-start | bytes 8912896 | tf_op jit(solution)/shard_map/reduce_scatter | solution.py:287
  90.0 100.6 %copy-start.21 = (bf16[2,128,1024]{2,1,0:T(8,128)(2,1)S(1)}, bf16[2,128,1024]{2,1,0:T(8,128)(2,1)}, u32[]{:S(2)}) copy-start(bf16[2,128,1024]{2,1,0:T(8,128)(2,1)} %param.22) | copy-start | bytes 1572868
  196.5 83.1 %copy-start.41 = (s32[2]{0:T(128)S(1)}, s32[2]{0:T(128)}, u32[]{:S(2)}) copy-start(s32[2]{0:T(128)} %param.21) | copy-start | bytes 28
  333.4 21.5 %copy-start.24 = (f32[2,128,16,64]{1,3,2,0:T(8,128)S(1)}, f32[2,128,16,64]{1,3,2,0:T(8,128)}, u32[]{:S(2)}) copy-start(f32[2,128,16,64]{1,3,2,0:T(8,128)} %custom-call.2) | copy-start | bytes 3145732
  386.9 150.6 %copy-start.6 = (f32[2,128,1024]{2,1,0:T(8,128)}, f32[2,128,1024]{2,1,0:T(8,128)S(1)}, u32[]{:S(2)}) copy-start(f32[2,128,1024]{2,1,0:T(8,128)S(1)} %get-tuple-element.417) | copy-start | bytes 3145732
  387.0 141.3 %copy-start.4 = (bf16[2,128,1024]{2,1,0:T(8,128)(2,1)}, bf16[2,128,1024]{2,1,0:T(8,128)(2,1)S(1)}, u32[]{:S(2)}) copy-start(bf16[2,128,1024]{2,1,0:T(8,128)(2,1)S(1)} %multiply_convert_fusion.3) | copy-start | bytes 1572868
  528.4 7.3 copy-start.13
  552.2 8.5 copy-start
  560.8 7.3 slice-start
  575.7 8.5 copy-start
  584.3 7.3 slice-start
  599.3 8.5 copy-start
  607.9 7.3 slice-start
  622.8 8.5 copy-start
  631.4 7.3 slice-start
  685.1 210.7 %reduce-scatter.12.cloned.1.call-start = ((), (), s32[]{:S(2)}) async-start(), calls=%async_computation.19 | async-start | bytes 8912896 | tf_op jit(solution)/shard_map/reduce_scatter | solution.py:290
  728.5 201.5 %reduce-scatter.20.cloned.1.call-start = ((), (), s32[]{:S(2)}) async-start(), calls=%async_computation.23 | async-start | bytes 3145728 | tf_op jit(solution)/shard_map/reduce_scatter | solution.py:332
  731.5 272.8 %reduce-scatter.22.cloned.1.call-start = ((), (), s32[]{:S(2)}) async-start(), calls=%async_computation.24 | async-start | bytes 8650752 | tf_op jit(solution)/shard_map/reduce_scatter | solution.py:335
  737.2 341.3 %reduce-scatter.24.cloned.1.call-start = ((), (), s32[]{:S(2)}) async-start(), calls=%async_computation.25 | async-start | bytes 8650752 | tf_op jit(solution)/shard_map/reduce_scatter | solution.py:338
  743.0 409.8 %reduce-scatter.26.cloned.1.call-start = ((), (), s32[]{:S(2)}) async-start(), calls=%async_computation.26 | async-start | bytes 8650752 | tf_op jit(solution)/shard_map/reduce_scatter | solution.py:341
  749.6 41.2 %copy-start.36 = (f32[128,64]{0,1:T(8,128)S(1)}, f32[128,64]{0,1:T(8,128)}, u32[]{:S(2)}) copy-start(f32[128,64]{0,1:T(8,128)} %copy-done.35) | copy-start | bytes 98308
  749.6 41.2 %copy-start.39 = (f32[128,64]{0,1:T(8,128)S(1)}, f32[128,64]{0,1:T(8,128)}, u32[]{:S(2)}) copy-start(f32[128,64]{0,1:T(8,128)} %get-tuple-element.412) | copy-start | bytes 98308
  749.6 437.7 %reduce-scatter.14.cloned.1.call-start = ((), (), s32[]{:S(2)}) async-start(), calls=%async_computation.20 | async-start | bytes 3145728 | tf_op jit(solution)/shard_map/reduce_scatter | solution.py:323
  750.4 43.3 %copy-start.3 = (bf16[2,128,1024]{2,1,0:T(8,128)(2,1)S(1)}, bf16[2,128,1024]{2,1,0:T(8,128)(2,1)}, u32[]{:S(2)}) copy-start(bf16[2,128,1024]{2,1,0:T(8,128)(2,1)} %param.19) | copy-start | bytes 1572868
  750.4 43.3 %copy-start.38 = (f32[2,1,512]{2,1,0:T(1,128)S(1)}, f32[2,1,512]{2,1,0:T(1,128)}, u32[]{:S(2)}) copy-start(f32[2,1,512]{2,1,0:T(1,128)} %copy-done.37) | copy-start | bytes 12292
  750.4 43.3 %copy-start.43 = (f32[2,128]{1,0:T(2,128)S(1)}, f32[2,128]{1,0:T(2,128)}, u32[]{:S(2)}) copy-start(f32[2,128]{1,0:T(2,128)} %copy-done.42) | copy-start | bytes 3076
  795.9 426.0 %reduce-scatter.16.cloned.1.call-start = ((), (), s32[]{:S(2)}) async-start(), calls=%async_computation.21 | async-start | bytes 3145728 | tf_op jit(solution)/shard_map/reduce_scatter | solution.py:326
  801.3 455.3 %reduce-scatter.18.cloned.1.call-start = ((), (), s32[]{:S(2)}) async-start(), calls=%async_computation.22 | async-start | bytes 3145728 | tf_op jit(solution)/shard_map/reduce_scatter | solution.py:329
  896.9 359.7 %copy-start.8 = (f32[2,128,1024]{2,1,0:T(8,128)}, f32[2,128,1024]{2,1,0:T(8,128)S(1)}, u32[]{:S(2)}) copy-start(f32[2,128,1024]{2,1,0:T(8,128)S(1)} %convert_multiply_fusion.3) | copy-start | bytes 3145732
  899.1 602.2 %all-reduce.7.cloned.1.call-start = ((), (), s32[]{:S(2)}) async-start(), calls=%async_computation.27 | async-start | bytes 25690112 | tf_op jit(solution)/shard_map/psum | solution.py:352
  1258.5 6.5 copy-start.20
  1501.3 5.9 copy-start.34
  1501.3 7.5 copy-start.33
  1504.2 6.1 copy-start.29
  (34 other events, 92.4 us)
Sparse Core Ops, SparseCore 0:
  9.5 35.8 all-gather.15
  46.9 33.0 all-gather.11
  81.6 33.0 all-gather.19
  116.1 74.4 all-gather.27
  193.2 74.3 all-gather.17
  270.2 72.8 all-gather.13
  344.6 31.6 all-gather.21
  377.9 74.4 all-gather.25
  453.9 74.4 all-gather.23
  685.2 103.3 reduce-scatter.9
  792.7 103.0 reduce-scatter.11
  898.4 31.5 reduce-scatter.19
  932.9 71.4 reduce-scatter.21
  1007.1 71.4 reduce-scatter.23
  1081.3 71.4 reduce-scatter.25
  1155.4 31.8 reduce-scatter.13
  1190.0 31.8 reduce-scatter.15
  1224.6 31.8 reduce-scatter.17
  1262.1 239.1 all-reduce.6
where the time goes:
time: 1540 us; the launch traced here: 1530 us
  waiting for transfers between devices  1050 us (68%)
  matrix products  204 us (13%)
  local copies, waits for them, and re-layouts  132 us (9%)
  other arithmetic  63.6 us (4%)
  blocking collectives  48.6 us (3%)
  between operations  15.5 us (1%)
    psum x1, waiting for transfers between devices, local(): lax.psum(shares[0].astype(jnp.bfloat16), 'rep').astype(jnp.float32)  190 us
    reduce_scatter x1, waiting for transfers between devices, local(): lax.psum_scatter(key_blocks[1].astype(jnp.bfloat16), 'rep', scatter_dimen...  94.4 us
    reduce_scatter x1, waiting for transfers between devices, local(): lax.psum_scatter(grad_gate.astype(jnp.bfloat16), 'shard', scatter_dimensi...  74.3 us
    reduce_scatter x1, waiting for transfers between devices, local(): lax.psum_scatter(grad_upward.astype(jnp.bfloat16), 'shard', scatter_dimen...  74.2 us
    reduce_scatter x1, waiting for transfers between devices, local(): lax.psum_scatter(grad_down.astype(jnp.bfloat16), 'shard', scatter_dimensi...  74.2 us
    all_gather x1, waiting for transfers between devices, local(): lax.all_gather(w_down, 'shard', axis=0, tiled=True)  72.9 us
    all_gather x1, waiting for transfers between devices, local(): lax.all_gather(key_rot, 'rep', axis=1, tiled=True)  71 us
    all_gather x1, waiting for transfers between devices, local(): lax.all_gather(w_gate, 'shard', axis=0, tiled=True)  70.2 us
  transfers between devices with their start and end apart: 19, of which 18 were waited for; matrix products, arithmetic and copies ran while one was open for 15% of the time, Pallas kernels for 0%

commit v1 on v0

v1 whole, which is shorter than its diff:
```python
import functools

import jax
import jax.numpy as jnp
from jax import lax
from jax.experimental import pallas as pl
from jax.experimental.pallas import tpu as pltpu
from jax.sharding import PartitionSpec as P

HEADS = 16
EPSILON = 1e-05
NEGATIVE = -1e30
ROPE_BASE = 10000.0
BF16 = jnp.bfloat16
F32 = jnp.float32
VMEM_LIMIT = 60 * 1024 * 1024


def dot(left, right, contract):
    return lax.dot_general(
        left, right, ((contract[:1], contract[1:]), ((), ())), preferred_element_type=F32
    )


def norm_rows(values):
    scale = lax.rsqrt(jnp.mean(values * values, axis=-1, keepdims=True) + EPSILON)
    return (values * scale, scale)


def norm_back(gradient, normed, scale):
    return scale * (gradient - normed * jnp.mean(gradient * normed, axis=-1, keepdims=True))


def rope_lanes(positions, lanes, head_dim):
    half = head_dim // 2
    lane = jnp.arange(lanes, dtype=jnp.int32) % head_dim
    frequency = ROPE_BASE ** (-2.0 * (lane % half).astype(F32) / head_dim)
    angles = positions.astype(F32)[:, None] * frequency[None, :]
    sign = jnp.where(lane < half, 1.0, -1.0).astype(F32)
    return (jnp.cos(angles), jnp.sin(angles) * sign[None, :])


def partner(values, head_dim, roll):
    half = head_dim // 2
    lane = lax.broadcasted_iota(jnp.int32, values.shape, values.ndim - 1) % head_dim
    return jnp.where(lane < half, roll(values, half), roll(values, -half))


def lane_roll(values, shift):
    return jnp.roll(values, -shift, axis=-1)


def kernel_roll(values, shift):
    width = values.shape[-1]
    if width % 128 == 0:
        return pltpu.roll(values, (-shift) % width, axis=values.ndim - 1)
    shift = shift % width
    return jnp.concatenate([values[..., shift:], values[..., :shift]], axis=-1)


def head_rows(values, head, head_dim):
    if values.shape[-1] == head_dim:
        return values
    lane = lax.broadcasted_iota(jnp.int32, values.shape, values.ndim - 1)
    mine = (lane >= head * head_dim) & (lane < (head + 1) * head_dim)
    return jnp.where(mine, values, jnp.zeros_like(values))


def masked_scores(key_block, query_block, key_start, query_start, prefix):
    scores = dot(key_block, query_block, (1, 1))
    query_pos = query_start + lax.broadcasted_iota(jnp.int32, (1, scores.shape[1]), 1)
    last = jnp.maximum(query_pos, prefix - 1) - key_start
    key_pos = lax.broadcasted_iota(jnp.int32, scores.shape, 0)
    return jnp.where(key_pos <= last, scores, NEGATIVE)


def attend_kernel(
    head_dim, bq, bk, prefix_ref, q_ref, k_ref, v_ref, att_ref, att_t_ref, mass_ref, v_t, acc
):
    length, width = q_ref.shape
    heads = width // head_dim
    prefix = prefix_ref[0]
    for start in range(0, length, 128):
        v_t[:, start : start + 128] = v_ref[start : start + 128, :].T

    def query_step(i, carry):
        q0 = pl.multiple_of(i * bq, bq)
        q_all = q_ref[pl.ds(q0, bq), :]
        q_heads = [head_rows(q_all, h, head_dim) for h in range(heads)]
        acc[...] = jnp.zeros_like(acc)
        blocks = (jnp.maximum(q0 + bq, prefix) + bk - 1) // bk

        def key_step(j, stats):
            k0 = pl.multiple_of(j * bk, bk)
            k_block = k_ref[pl.ds(k0, bk), :]
            out = []
            for h in range(heads):
                peak, mass = stats[h]
                scores = masked_scores(k_block, q_heads[h], k0, q0, prefix)
                new_peak = jnp.maximum(peak, jnp.max(scores, axis=0, keepdims=True))
                alpha = jnp.exp(peak - new_peak)
                weights = jnp.exp(scores - new_peak)
                mass = mass * alpha + jnp.sum(weights, axis=0, keepdims=True)
                rows = slice(h * head_dim, (h + 1) * head_dim)
                acc[rows, :] = acc[rows, :] * alpha + dot(
                    v_t[rows, pl.ds(k0, bk)], weights.astype(BF16), (1, 0)
                )
                out.append((new_peak, mass))
            return tuple(out)

        first = tuple(
            (jnp.full((1, bq), NEGATIVE, F32), jnp.zeros((1, bq), F32)) for _ in range(heads)
        )
        stats = lax.fori_loop(0, blocks, key_step, first)
        for h in range(heads):
            peak, mass = stats[h]
            rows = slice(h * head_dim, (h + 1) * head_dim)
            att_t_ref[rows, pl.ds(q0, bq)] = acc[rows, :] / mass
            mass_ref[h : h + 1, pl.ds(q0, bq)] = peak + jnp.log(mass)
        for part in range(0, bq, 128):
            place = pl.ds(pl.multiple_of(q0 + part, 128), 128)
            att_ref[place, :] = att_t_ref[:, place].T.astype(BF16)
        return carry

    lax.fori_loop(0, length // bq, query_step, 0)


def attend_back_kernel(
    head_dim,
    bq,
    bk,
    prefix_ref,
    q_ref,
    k_ref,
    v_ref,
    do_ref,
    att_t_ref,
    mass_ref,
    cos_ref,
    sin_ref,
    dq_ref,
    dk_ref,
    dv_ref,
    k_t,
    delta,
    dq_t,
    dk_acc,
    dv_acc,
):
    length, width = q_ref.shape
    heads = width // head_dim
    prefix = prefix_ref[0]
    dq_t[...] = jnp.zeros_like(dq_t)
    for start in range(0, length, 128):
        place = slice(start, start + 128)
        k_t[:, place] = k_ref[place, :].T
        product = do_ref[place, :].astype(F32).T * att_t_ref[:, place]
        for h in range(heads):
            rows = slice(h * head_dim, (h + 1) * head_dim)
            delta[h : h + 1, place] = jnp.sum(product[rows, :], axis=0, keepdims=True)

    def rope_back(gradient, place):
        return gradient * cos_ref[place, :] + partner(gradient, head_dim, kernel_roll) * sin_ref[
            place, :
        ]

    def key_step(j, carry):
        k0 = pl.multiple_of(j * bk, bk)
        k_block = k_ref[pl.ds(k0, bk), :]
        v_block = v_ref[pl.ds(k0, bk), :]
        dk_acc[...] = jnp.zeros_like(dk_acc)
        dv_acc[...] = jnp.zeros_like(dv_acc)
        begin = jnp.where(k0 < prefix, 0, k0 // bq)

        def query_step(i, inner):
            q0 = pl.multiple_of(i * bq, bq)
            q_all = q_ref[pl.ds(q0, bq), :]
            do_all = do_ref[pl.ds(q0, bq), :]
            for h in range(heads):
                rows = slice(h * head_dim, (h + 1) * head_dim)
                q_head = head_rows(q_all, h, head_dim)
                do_head = head_rows(do_all, h, head_dim)
                scores = masked_scores(k_block, q_head, k0, q0, prefix)
                weights = jnp.exp(scores - mass_ref[h : h + 1, pl.ds(q0, bq)])
                grad_weights = dot(v_block, do_head, (1, 1))
                grad_scores = (weights * (grad_weights - delta[h : h + 1, pl.ds(q0, bq)])).astype(
                    BF16
                )
                dv_acc[...] += dot(weights.astype(BF16), do_head, (1, 0))
                dk_acc[...] += dot(grad_scores, q_head, (1, 0))
                dq_t[rows, pl.ds(q0, bq)] += dot(k_t[rows, pl.ds(k0, bk)], grad_scores, (1, 0))
            return inner

        lax.fori_loop(begin, length // bq, query_step, 0)
        place = pl.ds(k0, bk)
        dk_ref[place, :] = rope_back(dk_acc[...], place).astype(BF16)
        dv_ref[place, :] = dv_acc[...].astype(BF16)
        return carry

    lax.fori_loop(0, length // bk, key_step, 0)
    for start in range(0, length, 128):
        place = slice(start, start + 128)
        dq_ref[place, :] = rope_back(dq_t[:, place].T * 0.125, place).astype(BF16)


def whole(shape):
    return pl.BlockSpec(shape, lambda *_: (0,) * len(shape))


def attend(prefix, q, k, v, head_dim, bq, bk):
    length, width = q.shape
    heads = width // head_dim
    flops = 2 * 2 * heads * length * length * head_dim
    return pl.pallas_call(
        functools.partial(attend_kernel, head_dim, bq, bk),
        out_shape=(
            jax.ShapeDtypeStruct((length, width), BF16),
            jax.ShapeDtypeStruct((width, length), F32),
            jax.ShapeDtypeStruct((heads, length), F32),
        ),
        grid_spec=pltpu.PrefetchScalarGridSpec(
            num_scalar_prefetch=1,
            grid=(1,),
            in_specs=[whole((length, width))] * 3,
            out_specs=[whole((length, width)), whole((width, length)), whole((heads, length))],
            scratch_shapes=[pltpu.VMEM((width, length), BF16), pltpu.VMEM((width, bq), F32)],
        ),
        compiler_params=pltpu.CompilerParams(vmem_limit_bytes=VMEM_LIMIT),
        cost_estimate=pl.CostEstimate(
            flops=flops, transcendentals=heads * length * length, bytes_accessed=8 * length * width
        ),
    )(prefix, q, k, v)


def attend_back(prefix, q, k, v, do, att_t, mass, cosine, sine, head_dim, bq, bk):
    length, width = q.shape
    heads = width // head_dim
    flops = 5 * 2 * heads * length * length * head_dim
    rows = whole((length, width))
    return pl.pallas_call(
        functools.partial(attend_back_kernel, head_dim, bq, bk),
        out_shape=(jax.ShapeDtypeStruct((length, width), BF16),) * 3,
        grid_spec=pltpu.PrefetchScalarGridSpec(
            num_scalar_prefetch=1,
            grid=(1,),
            in_specs=[rows] * 4 + [whole((width, length)), whole((heads, length)), rows, rows],
            out_specs=[rows] * 3,
            scratch_shapes=[
                pltpu.VMEM((width, length), BF16),
                pltpu.VMEM((heads, length), F32),
                pltpu.VMEM((width, length), F32),
                pltpu.VMEM((bk, width), F32),
                pltpu.VMEM((bk, width), F32),
            ],
        ),
        compiler_params=pltpu.CompilerParams(vmem_limit_bytes=VMEM_LIMIT),
        cost_estimate=pl.CostEstimate(
            flops=flops, transcendentals=heads * length * length, bytes_accessed=22 * length * width
        ),
    )(prefix, q, k, v, do, att_t, mass, cosine, sine)


def local(
    reps,
    shards,
    tokens,
    first_values,
    prefix_len,
    cotangent,
    w_query,
    w_key,
    w_value,
    w_output,
    w_gate,
    w_up,
    w_down,
    gain_attn,
    gain_ffn,
):
    seqs, rows, width = tokens.shape
    head_dim = width // HEADS
    length = rows * reps
    groups = reps // seqs
    lanes = width // groups
    here = lax.axis_index("rep")
    my_seq = here // groups
    total = seqs * rows

    def gather(weights):
        height = weights[0].shape[0]
        share = height // reps
        if share * reps == height and share % 8 == 0:
            pieces = [lax.dynamic_slice_in_dim(w, here * share, share, 0) for w in weights]
            axes = ("shard", "rep")
        else:
            pieces, axes = list(weights), ("shard",)
        piece = pieces[0] if len(pieces) == 1 else jnp.concatenate(pieces, axis=1)
        return lax.all_gather(piece, axes, axis=0, tiled=True)

    gains = lax.all_gather(jnp.stack([gain_attn, gain_ffn]), "shard", axis=1, tiled=True)
    full_qkv = gather((w_query, w_key, w_value))
    full_output = gather((w_output,))
    full_gate_up = gather((w_gate, w_up))
    full_down = gather((w_down,))
    gain1 = gains[0].astype(F32)
    gain2 = gains[1].astype(F32)

    def to_heads(values, parts):
        chunks = values.reshape(seqs, rows, parts, groups, lanes).transpose(0, 3, 1, 2, 4)
        chunks = chunks.reshape(reps * rows, parts * lanes)
        return lax.all_to_all(chunks, "rep", 0, 0, tiled=True)

    def to_tokens(values, parts):
        chunks = lax.all_to_all(values, "rep", 0, 0, tiled=True)
        chunks = chunks.reshape(seqs, groups, rows, parts, lanes).transpose(0, 2, 3, 1, 4)
        return chunks.reshape(total, parts * width)

    local_pos = here * rows + jnp.arange(rows, dtype=jnp.int32)
    cosine, sine = rope_lanes(local_pos, width, head_dim)
    cosine = jnp.tile(cosine, (seqs, 1))
    sine = jnp.tile(sine, (seqs, 1))
    all_cosine, all_sine = rope_lanes(jnp.arange(length, dtype=jnp.int32), lanes, head_dim)
    prefix = lax.dynamic_slice_in_dim(prefix_len, my_seq, 1, 0)

    inputs = tokens.reshape(total, width).astype(F32)
    normed1, scale1 = norm_rows(inputs)
    hidden1 = (normed1 * gain1).astype(BF16)
    hidden1_all = lax.all_gather(hidden1.reshape(seqs, rows, width), "rep", axis=1, tiled=True)
    raw = dot(hidden1, full_qkv, (1, 0))

    def rope(values):
        return values * cosine - partner(values, head_dim, lane_roll) * sine

    query_rot = (rope(raw[:, :width]) * 0.125).astype(BF16)
    key_rot = rope(raw[:, width : 2 * width]).astype(BF16)
    first = first_values.reshape(total, width).astype(F32)
    value_mix = (0.5 * raw[:, 2 * width :] + 0.5 * first).astype(BF16)
    qkv = to_heads(jnp.concatenate([query_rot, key_rot, value_mix], axis=1), 3)
    q, k, v = qkv[:, :lanes], qkv[:, lanes : 2 * lanes], qkv[:, 2 * lanes :]
    block = min(512, length)
    att, att_t, mass = attend(prefix, q, k, v, head_dim, block, block)
    attended = to_tokens(att, 1)

    residual = inputs + dot(attended, full_output, (1, 0))
    normed2, scale2 = norm_rows(residual)
    hidden2 = (normed2 * gain2).astype(BF16)
    gate_up = dot(hidden2, full_gate_up, (1, 0))
    ff = gate_up.shape[1] // 2
    gate_pre, up_pre = gate_up[:, :ff], gate_up[:, ff:]
    sigma = jax.nn.sigmoid(gate_pre)
    swish = gate_pre * sigma
    swiglu = (swish * up_pre).astype(BF16)
    output = (residual + dot(swiglu, full_down, (1, 0))).astype(BF16)

    upstream = cotangent.reshape(total, width)
    grad_swiglu = dot(upstream, full_down, (1, 1))
    grad_gate_pre = (grad_swiglu * up_pre * sigma * (1.0 + gate_pre * (1.0 - sigma))).astype(BF16)
    grad_up_pre = (grad_swiglu * swish).astype(BF16)
    grad_gate_up = jnp.concatenate([grad_gate_pre, grad_up_pre], axis=1)
    grad_hidden2 = dot(grad_gate_up, full_gate_up, (1, 1))
    grad_residual = upstream.astype(F32) + norm_back(grad_hidden2 * gain2, normed2, scale2)
    grad_residual_low = grad_residual.astype(BF16)
    grad_attended = dot(grad_residual_low, full_output, (1, 1)).astype(BF16)

    def reduce_gather(partial):
        axes = ("shard", "rep")
        piece = lax.psum_scatter(partial.astype(BF16), axes, scatter_dimension=0, tiled=True)
        return lax.all_gather(piece, "rep", axis=0, tiled=True).astype(F32)

    grad_down = reduce_gather(dot(swiglu, upstream, (0, 0)))
    grad_wgate_up = reduce_gather(dot(hidden2, grad_gate_up, (0, 0)))
    grad_outproj = reduce_gather(dot(attended, grad_residual_low, (0, 0)))

    do = to_heads(grad_attended, 1)
    dq, dk, dv = attend_back(
        prefix, q, k, v, do, att_t, mass, all_cosine, all_sine, head_dim, block, block
    )
    grad_qkv_heads = jnp.concatenate([dq, dk, dv], axis=1)
    half_value = jnp.where(jnp.arange(3 * lanes) < 2 * lanes, 1.0, 0.5).astype(BF16)
    grad_raw_heads = grad_qkv_heads * half_value
    grad_raw = to_tokens(grad_raw_heads, 3)
    grad_first = grad_raw[:, 2 * width :].astype(F32)
    grad_hidden1 = dot(grad_raw, full_qkv, (1, 1))
    grad_inputs = grad_residual + norm_back(grad_hidden1 * gain1, normed1, scale1)

    hidden_mine = lax.dynamic_index_in_dim(hidden1_all, my_seq, 0, keepdims=False)
    columns = dot(hidden_mine, grad_raw_heads, (0, 0))
    columns = lax.psum_scatter(columns.astype(BF16), "shard", scatter_dimension=0, tiled=True)
    height = columns.shape[0]
    share = height // seqs
    mine = lax.dynamic_slice_in_dim(columns, my_seq * share, share, 0).astype(F32)
    for turn in range(1, seqs):
        sent = lax.dynamic_slice_in_dim(columns, ((my_seq + turn) % seqs) * share, share, 0)
        moves = [
            (s * groups + g, ((s + turn) % seqs) * groups + g)
            for s in range(seqs)
            for g in range(groups)
        ]
        mine = mine + lax.ppermute(sent, "rep", moves).astype(F32)
    gathered = lax.all_gather(mine.astype(BF16), "rep", axis=0, tiled=True)
    gathered = gathered.reshape(seqs, groups, share, 3, lanes).transpose(3, 0, 2, 1, 4)
    grad_wqkv = gathered.reshape(3, height, width).astype(F32)

    grad_gain1 = (
        jnp.sum(w_query.astype(F32) * grad_wqkv[0], axis=1)
        + jnp.sum(w_key.astype(F32) * grad_wqkv[1], axis=1)
        + jnp.sum(w_value.astype(F32) * grad_wqkv[2], axis=1)
    ) / gain_attn.astype(F32)
    grad_wgate, grad_wup = grad_wgate_up[:, :ff], grad_wgate_up[:, ff:]
    grad_gain2 = (
        jnp.sum(w_gate.astype(F32) * grad_wgate, axis=1)
        + jnp.sum(w_up.astype(F32) * grad_wup, axis=1)
    ) / gain_ffn.astype(F32)
    shape = tokens.shape
    return (
        output.reshape(shape),
        grad_inputs.reshape(shape),
        grad_first.reshape(shape),
        grad_wqkv[0],
        grad_wqkv[1],
        grad_wqkv[2],
        grad_outproj,
        grad_wgate,
        grad_wup,
        grad_down,
        grad_gain1,
        grad_gain2,
    )


def solution(mesh):
    sequence = P("shard", "rep", None)
    matrix = P("shard", None)
    vector = P("shard")
    return jax.shard_map(
        functools.partial(local, mesh.shape["rep"], mesh.shape["shard"]),
        mesh=mesh,
        in_specs=(sequence, sequence, vector, sequence) + (matrix,) * 7 + (vector,) * 2,
        out_specs=(sequence,) * 3 + (matrix,) * 7 + (vector,) * 2,
        check_vma=False,
    )
```

time: 1540 us -> 1090 us (0.71)
  waiting for transfers between devices: 1050 us -> 807 us
  matrix products: 204 us -> 67.2 us
  local copies, waits for them, and re-layouts: 132 us -> 53.1 us
  Pallas kernels: 0 us -> 41.5 us
  other arithmetic: 63.6 us -> 44.6 us
    psum x1 -> x0, waiting for transfers between devices: 190 us -> none  [local(): lax.psum(shares[0].astype(jnp.bfloat16), 'rep').astype(jnp.float32)]
    dot_general x49 -> x12, matrix products: 204 us -> 67.2 us  [dot(): lax.dot_general(left, right, ((contract[:1], contract[1:]), ((), ())), pr...]
    convert_element_type x6 -> x1, local copies, waits for them, and re-layouts: 89.7 us -> 5.51 us  [local(): grad_wqkv = gathered.reshape(3, height, width).astype(F32)]
    all_to_all x0 -> x3, waiting for transfers between devices: none -> 76.2 us  [the longest x2 44.7 us: to_heads(): return lax.all_to_all(chunks, 'rep', 0, 0, tiled=True)]
    all_gather x9, waiting for transfers between devices: 368 us -> 297 us  [the longest x4 185 us: gather(): return lax.all_gather(piece, axes, axis=0, tiled=True)]
    reduce_scatter x9 -> x4, waiting for transfers between devices: 489 us -> 424 us  [the longest x3 408 us: reduce_gather(): lax.psum_scatter(partial.astype(BF16), axes, scatter_dimension=0, tiled=T...]
    pallas_call x0 -> x2, Pallas kernels: none -> 41.5 us  [the longest x1 23.7 us: attend_back(): pl.pallas_call(functools.partial(attend_back_kernel, head_dim, bq, bk), o...]
    psum x1 -> x0, blocking collectives: 34 us -> none  [local(): lax.psum(shares[7].astype(jnp.bfloat16), 'rep').astype(jnp.float32)]
  transfers between devices with their start and end apart: 19 -> 17, of which waited for: 18 -> 15; matrix products, arithmetic and copies ran while one was open for 15% -> 14% of each run, Pallas kernels for 0% -> 4%
where the time goes in v1:
time: 1090 us; the launch traced here: 1080 us
  waiting for transfers between devices  807 us (74%)
  matrix products  67.2 us (6%)
  local copies, waits for them, and re-layouts  53.1 us (5%)
  other arithmetic  44.6 us (4%)
  Pallas kernels  41.5 us (4%)
  blocking collectives  35.8 us (3%)
  starting transfers between devices  16.5 us (2%)
  between operations  14.9 us (1%)
    reduce_scatter x3, waiting for transfers between devices, reduce_gather(): lax.psum_scatter(partial.astype(BF16), axes, scatter_dimension=0, tiled=T...  408 us
    all_gather x4, waiting for transfers between devices, gather(): return lax.all_gather(piece, axes, axis=0, tiled=True)  185 us
    all_gather x3, waiting for transfers between devices, reduce_gather(): return lax.all_gather(piece, 'rep', axis=0, tiled=True).astype(F32)  69.5 us
    dot_general x12, matrix products, dot(): lax.dot_general(left, right, ((contract[:1], contract[1:]), ((), ())), pr...  67.2 us
    all_to_all x2, waiting for transfers between devices, to_heads(): return lax.all_to_all(chunks, 'rep', 0, 0, tiled=True)  44.7 us
    all_gather x1, waiting for transfers between devices, local(): gathered = lax.all_gather(mine.astype(BF16), 'rep', axis=0, tiled=True)  32.7 us
    all_to_all x1, waiting for transfers between devices, to_tokens(): chunks = lax.all_to_all(values, 'rep', 0, 0, tiled=True)  31.5 us
    all_to_all x1, blocking collectives, to_tokens(): chunks = lax.all_to_all(values, 'rep', 0, 0, tiled=True)  30.5 us
  transfers between devices with their start and end apart: 17, of which 15 were waited for; matrix products, arithmetic and copies ran while one was open for 14% of the time, Pallas kernels for 4%

profile of v1, /device:TPU:0, one launch (start us, length us, event | category | flops | bytes accessed | tf_op | source)
XLA Modules:
  0.0 1081.0 jit_solution(1490140556467387994)
XLA Ops:
  14.2 5.3 all_gather.30
  21.0 3.0 multiply_cosine_fusion.1
  23.9 59.6 %all-gather.10.cloned.1.call-done = bf16[1024,3072]{1,0:T(8,128)(2,1)} async-done(((bf16[32,3072]{1,0:T(8,128)(2,1)}), bf16[1024,3072]{1,0:T(8,128)(2,1)}) %all-gather.10.cloned.1.call-update) | async-done | bytes 6291472 | tf_op jit(solution)/shard_map/all_gather | solution.py:298
  83.5 4.6 fusion.54
  92.3 2.8 copy.40
  95.1 4.1 all-to-all-start
  99.9 34.2 %all-to-all-done = bf16[16,128,384]{1,2,0:T(8,128)(2,1)S(1)} async-done(((bf16[16,128,384]{1,2,0:T(8,128)(2,1)}), bf16[16,128,384]{1,2,0:T(8,128)(2,1)S(1)}, u32[]{:S(2)}, u32[]{:S(2)}) %all-to-all-start) | async-done | bytes 1572896 | tf_op jit(solution)/shard_map/all_to_all | solution.py:311
  135.7 2.5 fusion.53
  138.2 17.9 %shard_map.220 = (bf16[2048,128]{1,0:T(8,128)(2,1)}, f32[128,2048]{1,0:T(8,128)}, f32[2,2048]{1,0:T(2,128)}) custom-call(s32[1]{0:T(128)} %dynamic_slice.34.prefix_ref, bf16[2048,128]{1,0:T(8,128)(2,1)} %get-tuple-element.55.q_ref, bf16[2048,128]{1,0:T(8,128)(2,1)} %get-tuple-element.54.k_ref, bf16[2048,128]{1,0:T(8,128)(2,1)} %get-tuple-element.53.v_ref), custom_call_target="tpu_custom_call" | custom-call | flops 2147483648 | bytes 2097152 | tf_op jit(solution)/shard_map/pallas_call | solution.py:214
  156.0 30.5 %all_to_all.38 = bf16[16,128,128]{2,1,0:T(8,128)(2,1)S(1)} all-to-all(bf16[16,128,128]{2,1,0:T(8,128)(2,1)} %bitcast.145), channel_id=1, replica_groups=mesh['rep'=16,'shard'=2] {'rep'}, dimensions={0} | all-to-all | bytes 1048576 | tf_op jit(solution)/shard_map/all_to_all | solution.py:314
  189.4 65.8 %all-gather.14.cloned.1.call-done = bf16[1024,5632]{1,0:T(8,128)(2,1)} async-done(((bf16[32,5632]{1,0:T(8,128)(2,1)}), bf16[1024,5632]{1,0:T(8,128)(2,1)}) %all-gather.14.cloned.1.call-update) | async-done | bytes 11534352 | tf_op jit(solution)/shard_map/all_gather | solution.py:298
  255.1 9.4 fusion.49
  264.5 59.8 %all-gather.16.cloned.1.call-done = bf16[2816,1024]{1,0:T(8,128)(2,1)} async-done(((bf16[88,1024]{1,0:T(8,128)(2,1)}), bf16[2816,1024]{1,0:T(8,128)(2,1)}) %all-gather.16.cloned.1.call-update) | async-done | bytes 5767184 | tf_op jit(solution)/shard_map/all_gather | solution.py:298
  324.4 8.9 multiply_convert_fusion.1
  333.3 7.3 multiply_reduce_fusion.6
  346.4 4.5 all-to-all-start.2
  351.1 5.6 fusion.15
  356.7 10.5 all-to-all-done.2
  368.0 23.7 %shard_map.221 = (bf16[2048,128]{1,0:T(8,128)(2,1)}, bf16[2048,128]{1,0:T(8,128)(2,1)}, bf16[2048,128]{1,0:T(8,128)(2,1)}) custom-call(s32[1]{0:T(128)} %dynamic_slice.34.prefix_ref, bf16[2048,128]{1,0:T(8,128)(2,1)} %get-tuple-element.55.q_ref, bf16[2048,128]{1,0:T(8,128)(2,1)} %get-tuple-element.54.k_ref, bf16[2048,128]{1,0:T(8,128)(2,1)} %get-tuple-element.53.v_ref, ...), custom_call_target="tpu_custom_call" | custom-call | flops 5368709120 | bytes 5767168 | tf_op jit(solution)/shard_map/pallas_call | solution.py:240
  391.7 10.1 all-gather.18.cloned.1.call-done
  401.8 5.9 fusion.9
  407.8 5.6 convolution_convert_fusion.1
  413.5 7.9 convolution_convert_fusion
  421.5 120.0 %reduce-scatter.7.cloned.1.call-done = bf16[32,1024]{1,0:T(8,128)(2,1)} async-done(((bf16[1024,1024]{1,0:T(8,128)(2,1)}), bf16[32,1024]{1,0:T(8,128)(2,1)}) %reduce-scatter.7.cloned.1.call-update) | async-done | bytes 65552 | tf_op jit(solution)/shard_map/reduce_scatter | solution.py:367
  541.5 16.5 %reduce-scatter.5.cloned.1.call-done = bf16[512,384]{1,0:T(8,128)(2,1)} async-done(((bf16[1024,384]{1,0:T(8,128)(2,1)}), bf16[512,384]{1,0:T(8,128)(2,1)}) %reduce-scatter.5.cloned.1.call-update) | async-done | bytes 393232 | tf_op jit(solution)/shard_map/reduce_scatter | solution.py:388
  559.0 2.5 collective-permute-start
  561.4 9.6 collective-permute-done
  572.7 134.0 %reduce-scatter.11.cloned.1.call-done = bf16[88,1024]{1,0:T(8,128)(2,1)} async-done(((bf16[2816,1024]{1,0:T(8,128)(2,1)}), bf16[88,1024]{1,0:T(8,128)(2,1)}) %reduce-scatter.11.cloned.1.call-update) | async-done | bytes 180240 | tf_op jit(solution)/shard_map/reduce_scatter | solution.py:367
  706.8 153.6 %reduce-scatter.9.cloned.1.call-done = bf16[32,5632]{1,0:T(8,128)(2,1)} async-done(((bf16[1024,5632]{1,0:T(8,128)(2,1)}), bf16[32,5632]{1,0:T(8,128)(2,1)}) %reduce-scatter.9.cloned.1.call-update) | async-done | bytes 360464 | tf_op jit(solution)/shard_map/reduce_scatter | solution.py:367
  865.8 2.8 maximum_multiply_fusion
  868.6 4.7 all-to-all-start.3
  873.3 5.5 fusion.13
  878.8 31.5 %all-to-all-done.3 = bf16[16,128,384]{1,2,0:T(8,128)(2,1)} async-done(((bf16[16,128,384]{1,2,0:T(8,128)(2,1)}), bf16[16,128,384]{1,2,0:T(8,128)(2,1)}, u32[]{:S(2)}, u32[]{:S(2)}) %all-to-all-start.3) | async-done | bytes 1572896 | tf_op jit(solution)/shard_map/all_to_all | solution.py:314
  910.3 2.8 copy.48
  913.1 3.7 reshape.290
  918.9 5.2 multiply_reduce_fusion.5
  925.4 2.8 convert_element_type.193
  928.2 32.7 %all-gather.20.cloned.1.call-done = bf16[4096,384]{1,0:T(8,128)(2,1)} async-done(((bf16[256,384]{1,0:T(8,128)(2,1)}), bf16[4096,384]{1,0:T(8,128)(2,1)}) %all-gather.20.cloned.1.call-update) | async-done | bytes 3145744 | tf_op jit(solution)/shard_map/all_gather | solution.py:400
  960.9 5.5 copy.49
  966.4 5.7 copy.57
  972.1 2.7 fusion.50
  974.8 3.1 copy.50
  979.9 2.6 copy.52
  982.5 3.8 multiply_reduce_fusion.4
  990.4 14.9 %all-gather.26.cloned.1.call-done = bf16[1408,1024]{1,0:T(8,128)(2,1)} async-done(((bf16[88,1024]{1,0:T(8,128)(2,1)}), bf16[1408,1024]{1,0:T(8,128)(2,1)}) %all-gather.26.cloned.1.call-update) | async-done | bytes 2883600 | tf_op jit(solution)/shard_map/all_gather | solution.py:368
  1005.4 5.1 convert_element_type.197
  1010.4 54.5 %all-gather.24.cloned.1.call-done = bf16[512,5632]{1,0:T(8,128)(2,1)} async-done(((bf16[32,5632]{1,0:T(8,128)(2,1)}), bf16[512,5632]{1,0:T(8,128)(2,1)}) %all-gather.24.cloned.1.call-update) | async-done | bytes 5767184 | tf_op jit(solution)/shard_map/all_gather | solution.py:368
  1065.0 8.4 multiply_reduce_fusion
  (114 shorter events, 42.7 us)
Async XLA Ops:
  7.2 6.2 copy-start
  7.2 6.9 copy-start.15
  7.2 7.0 copy-start.14
  7.2 12.3 %copy-start.3 = (bf16[2,128,1024]{2,1,0:T(8,128)(2,1)S(1)}, bf16[2,128,1024]{2,1,0:T(8,128)(2,1)}, u32[]{:S(2)}) copy-start(bf16[2,128,1024]{2,1,0:T(8,128)(2,1)} %param.13) | copy-start | bytes 1572868
  7.2 76.3 %all-gather.10.cloned.1.call-start = ((), (), s32[]{:S(2)}) async-start(), calls=%async_computation.8 | async-start | bytes 6488064 | tf_op jit(solution)/shard_map/all_gather | solution.py:298
  9.9 177.1 %all-gather.12.cloned.1.call-start = ((), (), s32[]{:S(2)}) async-start(), calls=%async_computation.9 | async-start | bytes 2162688 | tf_op jit(solution)/shard_map/all_gather | solution.py:298
  11.4 243.7 %all-gather.14.cloned.1.call-start = ((), (), s32[]{:S(2)}) async-start(), calls=%async_computation.10 | async-start | bytes 11894784 | tf_op jit(solution)/shard_map/all_gather | solution.py:298
  13.3 311.0 %all-gather.16.cloned.1.call-start = ((), (), s32[]{:S(2)}) async-start(), calls=%async_computation.11 | async-start | bytes 5947392 | tf_op jit(solution)/shard_map/all_gather | solution.py:298
  14.1 387.7 %all-gather.18.cloned.1.call-start = ((), (), s32[]{:S(2)}) async-start(), calls=%async_computation.12 | async-start | bytes 8912896 | tf_op jit(solution)/shard_map/all_gather | solution.py:328
  88.2 1.0 copy-start.4
  88.2 1.2 copy-start.12
  92.3 7.1 copy-start.16
  95.1 39.0 %all-to-all-start = ((bf16[16,128,384]{1,2,0:T(8,128)(2,1)}), bf16[16,128,384]{1,2,0:T(8,128)(2,1)S(1)}, u32[]{:S(2)}, u32[]{:S(2)}) async-start(bf16[16,128,384]{1,2,0:T(8,128)(2,1)} %bitcast.130), calls=%async_computation | async-start | bytes 3145728 | tf_op jit(solution)/shard_map/all_to_all | solution.py:311
  99.2 442.2 %reduce-scatter.7.cloned.1.call-start = ((), (), s32[]{:S(2)}) async-start(), calls=%async_computation.15 | async-start | bytes 2162688 | tf_op jit(solution)/shard_map/reduce_scatter | solution.py:367
  255.1 69.2 %copy-start.5 = (bf16[2,128,1024]{2,1,0:T(8,128)(2,1)S(1)}, bf16[2,128,1024]{2,1,0:T(8,128)(2,1)}, u32[]{:S(2)}) copy-start(bf16[2,128,1024]{2,1,0:T(8,128)(2,1)} %param.16) | copy-start | bytes 1572868
  333.3 7.3 copy-start.8
  333.3 7.3 copy-start.9
  333.3 7.3 copy-start.6
  346.4 20.9 %all-to-all-start.2 = ((bf16[16,128,128]{2,1,0:T(8,128)(2,1)}), bf16[16,128,128]{2,1,0:T(8,128)(2,1)S(1)}, u32[]{:S(2)}, u32[]{:S(2)}) async-start(bf16[16,128,128]{2,1,0:T(8,128)(2,1)} %bitcast.17), calls=%async_computation.2 | async-start | bytes 1048576 | tf_op jit(solution)/shard_map/all_to_all | solution.py:311
  350.8 207.2 %reduce-scatter.5.cloned.1.call-start = ((), (), s32[]{:S(2)}) async-start(), calls=%async_computation.13 | async-start | bytes 1179648 | tf_op jit(solution)/shard_map/reduce_scatter | solution.py:388
  367.2 0.8 copy-start.13
  401.8 6.0 copy-start.7
  407.7 299.0 %reduce-scatter.11.cloned.1.call-start = ((), (), s32[]{:S(2)}) async-start(), calls=%async_computation.19 | async-start | bytes 5947392 | tf_op jit(solution)/shard_map/reduce_scatter | solution.py:367
  413.4 446.9 %reduce-scatter.9.cloned.1.call-start = ((), (), s32[]{:S(2)}) async-start(), calls=%async_computation.17 | async-start | bytes 11894784 | tf_op jit(solution)/shard_map/reduce_scatter | solution.py:367
  421.4 504.0 %all-gather.22.cloned.1.call-start = ((), (), s32[]{:S(2)}) async-start(), calls=%async_computation.16 | async-start | bytes 1114112 | tf_op jit(solution)/shard_map/all_gather | solution.py:368
  541.5 419.4 %all-gather.20.cloned.1.call-start = ((), (), s32[]{:S(2)}) async-start(), calls=%async_computation.14 | async-start | bytes 3342336 | tf_op jit(solution)/shard_map/all_gather | solution.py:400
  559.0 12.0 %collective-permute-start = (bf16[256,384]{1,0:T(8,128)(2,1)S(1)}, bf16[256,384]{1,0:T(8,128)(2,1)S(1)}, u32[]{:S(2)}, u32[]{:S(2)}) collective-permute-start(bf16[256,384]{1,0:T(8,128)(2,1)S(1)} %constant_dynamic-slice_fusion), channel_id=1, source_target_pairs={{0,16},{2,18},{4,20},{6,22},{8,24},{10,26},{12,28},{14,30},{16,0},... | collective-permute-start | bytes 589832 | tf_op jit(solution)/shard_map/ppermute | solution.py:399
  572.7 432.7 %all-gather.26.cloned.1.call-start = ((), (), s32[]{:S(2)}) async-start(), calls=%async_computation.20 | async-start | bytes 3063808 | tf_op jit(solution)/shard_map/all_gather | solution.py:368
  706.7 358.2 %all-gather.24.cloned.1.call-start = ((), (), s32[]{:S(2)}) async-start(), calls=%async_computation.18 | async-start | bytes 6127616 | tf_op jit(solution)/shard_map/all_gather | solution.py:368
  868.6 41.7 %all-to-all-start.3 = ((bf16[16,128,384]{1,2,0:T(8,128)(2,1)}), bf16[16,128,384]{1,2,0:T(8,128)(2,1)}, u32[]{:S(2)}, u32[]{:S(2)}) async-start(bf16[16,128,384]{1,2,0:T(8,128)(2,1)} %maximum_multiply_fusion), calls=%async_computation.3 | async-start | bytes 3145728 | tf_op jit(solution)/shard_map/all_to_all | solution.py:314
  982.5 3.8 copy-start.2
  982.5 3.8 copy-start.10
  986.3 1.8 copy-start.11
  1065.0 9.0 copy-start.1
Sparse Core Ops, SparseCore 0:
  11.5 71.9 all-gather.9
  87.0 69.1 all-gather.11
  159.6 95.4 all-gather.13
  258.4 65.8 all-gather.15
  326.4 75.3 all-gather.17
  404.5 136.9 reduce-scatter.6
  544.3 13.6 reduce-scatter.4
  560.9 145.7 reduce-scatter.10
  709.0 151.2 reduce-scatter.8
  862.4 51.3 all-gather.21
  916.7 44.1 all-gather.19
  963.0 42.2 all-gather.25
  1007.6 57.2 all-gather.23

commit v2 on v1

--- a/solution.py
+++ b/solution.py
@@ -203,6 +203,85 @@
         dq_ref[place, :] = rope_back(dq_t[:, place].T * 0.125, place).astype(BF16)
 
 
+def turns(reps, move):
+    pairs = []
+    for here in range(reps):
+        z, y, core = move(here // 4, (here // 2) % 2, here % 2)
+        pairs.append((here, (z % (reps // 4)) * 4 + y * 2 + core))
+    return pairs
+
+
+class Links:
+    def __init__(self, reps):
+        self.deep = reps // 4
+        self.to_core = turns(reps, lambda z, y, core: (z, y, 1 - core))
+        self.to_y = turns(reps, lambda z, y, core: (z, 1 - y, core))
+        self.to_z = turns(reps, lambda z, y, core: (z + 1, y, core))
+        here = lax.axis_index("rep")
+        self.z, self.y, self.core = here // 4, (here // 2) % 2, here % 2
+        self.x = lax.axis_index("shard")
+
+    def over_core(self, value):
+        return lax.ppermute(value, "rep", self.to_core)
+
+    def over_x(self, value):
+        return lax.ppermute(value, "shard", [(0, 1), (1, 0)])
+
+    def over_y(self, value):
+        return lax.ppermute(value, "rep", self.to_y)
+
+    def next_z(self, value):
+        return lax.ppermute(value, "rep", self.to_z)
+
+    def reduce(self, keep, send, x_first):
+        columns = keep.shape[1]
+        height = keep.shape[0] // 2
+        total = add(keep, self.over_core(send))
+        if x_first:
+            total = total.reshape(2, height, columns)
+            total = add(pick(total, self.x), self.over_x(pick(total, 1 - self.x)))
+            total = total.reshape(2, height // 2, columns)
+            total = add(pick(total, self.y), self.over_y(pick(total, 1 - self.y)))
+        else:
+            total = total.reshape(2, 2, height // 2, columns)
+            total = add(pick(total, self.y, 1), self.over_y(pick(total, 1 - self.y, 1)))
+            total = add(pick(total, self.x), self.over_x(pick(total, 1 - self.x)))
+        deep = self.deep
+        total = total.reshape(deep, height // (2 * deep), columns)
+        moving = pick(total, (self.z + deep - 1) % deep)
+        for step in range(deep - 1):
+            moving = add(pick(total, (self.z + 2 * deep - 2 - step) % deep), self.next_z(moving))
+        return moving
+
+    def collect(self, piece):
+        deep = self.deep
+        whole_z = jnp.zeros((deep,) + piece.shape, piece.dtype)
+        for step in range(deep):
+            whole_z = put(whole_z, piece, (self.z + deep - step) % deep)
+            if step < deep - 1:
+                piece = self.next_z(piece)
+        whole_z = whole_z.reshape(-1, piece.shape[1])
+        halves = join(whole_z, self.over_y(whole_z), self.y).reshape(-1, piece.shape[1])
+        return join(halves, self.over_core(halves), self.core)
+
+
+def pick(values, index, axis=0):
+    return lax.dynamic_index_in_dim(values, index, axis, keepdims=False)
+
+
+def put(values, part, index):
+    return lax.dynamic_update_index_in_dim(values, part, index, 0)
+
+
+def join(mine, other, index):
+    both = jnp.zeros((2,) + mine.shape, mine.dtype)
+    return put(put(both, mine, index), other, 1 - index)
+
+
+def add(left, right):
+    return (left.astype(F32) + right.astype(F32)).astype(BF16)
+
+
 def whole(shape):
     return pl.BlockSpec(shape, lambda *_: (0,) * len(shape))
 
@@ -297,11 +376,43 @@
         piece = pieces[0] if len(pieces) == 1 else jnp.concatenate(pieces, axis=1)
         return lax.all_gather(piece, axes, axis=0, tiled=True)
 
+    linked = reps % 4 == 0 and reps <= 16 and shards == 2
+    links = Links(reps) if linked else None
+
+    def gather_linked(weights, by_rows):
+        height = weights[0].shape[0]
+        if by_rows:
+            half = height // 2
+            pieces = [lax.dynamic_slice_in_dim(w, links.core * half, half, 0) for w in weights]
+            piece = pieces[0] if len(pieces) == 1 else jnp.concatenate(pieces, axis=1)
+        else:
+            half = weights[0].shape[1] // 2
+            piece = lax.dynamic_slice_in_dim(weights[0], links.core * half, half, 1)
+        near = links.over_x(piece)
+        far = links.over_core(near)
+        width_all = sum(w.shape[1] for w in weights)
+        full = jnp.zeros((2 * height, width_all), BF16)
+        at = 0
+        for w in weights:
+            full = lax.dynamic_update_slice(full, w, (links.x * height, at))
+            at += w.shape[1]
+        for part, core in ((near, links.core), (far, 1 - links.core)):
+            base = (1 - links.x) * height
+            place = (base + core * half, 0) if by_rows else (base, core * half)
+            full = lax.dynamic_update_slice(full, part, place)
+        return full
+
     gains = lax.all_gather(jnp.stack([gain_attn, gain_ffn]), "shard", axis=1, tiled=True)
-    full_qkv = gather((w_query, w_key, w_value))
-    full_output = gather((w_output,))
-    full_gate_up = gather((w_gate, w_up))
-    full_down = gather((w_down,))
+    if linked:
+        full_qkv = gather_linked((w_query, w_key, w_value), True)
+        full_output = gather_linked((w_output,), True)
+        full_gate_up = gather_linked((w_gate, w_up), True)
+        full_down = gather_linked((w_down,), False)
+    else:
+        full_qkv = gather((w_query, w_key, w_value))
+        full_output = gather((w_output,))
+        full_gate_up = gather((w_gate, w_up))
+        full_down = gather((w_down,))
     gain1 = gains[0].astype(F32)
     gain2 = gains[1].astype(F32)
 
@@ -367,9 +478,36 @@
         piece = lax.psum_scatter(partial.astype(BF16), axes, scatter_dimension=0, tiled=True)
         return lax.all_gather(piece, "rep", axis=0, tiled=True).astype(F32)
 
-    grad_down = reduce_gather(dot(swiglu, upstream, (0, 0)))
-    grad_wgate_up = reduce_gather(dot(hidden2, grad_gate_up, (0, 0)))
-    grad_outproj = reduce_gather(dot(attended, grad_residual_low, (0, 0)))
+    def core_columns(values, core):
+        half = values.shape[1] // 2
+        return lax.dynamic_slice_in_dim(values, core * half, half, 1)
+
+    def core_rows(values, core):
+        parts = values.reshape(total, 2, 2, -1)
+        return pick(parts, core, 2).reshape(total, -1)
+
+    def linked_by_rows(left, right, x_first):
+        keep = dot(core_rows(left, links.core), right, (0, 0))
+        send = dot(core_rows(left, 1 - links.core), right, (0, 0)).astype(BF16)
+        whole_rows = links.collect(links.reduce(keep, send, x_first))
+        return whole_rows.reshape(-1, right.shape[1]).astype(F32)
+
+    def linked_by_columns(left, right, x_first):
+        keep = dot(left, core_columns(right, links.core), (0, 0))
+        send = dot(left, core_columns(right, 1 - links.core), (0, 0)).astype(BF16)
+        halves = links.collect(links.reduce(keep, send, x_first))
+        return jnp.concatenate([halves[0], halves[1]], axis=1).astype(F32)
+
+    if linked:
+        grad_down = linked_by_columns(swiglu, upstream, True)
+        grad_wgate = linked_by_rows(hidden2, grad_gate_pre, False)
+        grad_wup = linked_by_rows(hidden2, grad_up_pre, True)
+        grad_outproj = linked_by_rows(attended, grad_residual_low, False)
+    else:
+        grad_down = reduce_gather(dot(swiglu, upstream, (0, 0)))
+        grad_wgate_up = reduce_gather(dot(hidden2, grad_gate_up, (0, 0)))
+        grad_outproj = reduce_gather(dot(attended, grad_residual_low, (0, 0)))
+        grad_wgate, grad_wup = grad_wgate_up[:, :ff], grad_wgate_up[:, ff:]
 
     do = to_heads(grad_attended, 1)
     dq, dk, dv = attend_back(
@@ -385,7 +523,11 @@
 
     hidden_mine = lax.dynamic_index_in_dim(hidden1_all, my_seq, 0, keepdims=False)
     columns = dot(hidden_mine, grad_raw_heads, (0, 0))
-    columns = lax.psum_scatter(columns.astype(BF16), "shard", scatter_dimension=0, tiled=True)
+    if linked:
+        sides = columns.astype(BF16).reshape(2, -1, columns.shape[1])
+        columns = add(pick(sides, links.x), links.over_x(pick(sides, 1 - links.x)))
+    else:
+        columns = lax.psum_scatter(columns.astype(BF16), "shard", scatter_dimension=0, tiled=True)
     height = columns.shape[0]
     share = height // seqs
     mine = lax.dynamic_slice_in_dim(columns, my_seq * share, share, 0).astype(F32)
@@ -406,7 +548,6 @@
         + jnp.sum(w_key.astype(F32) * grad_wqkv[1], axis=1)
         + jnp.sum(w_value.astype(F32) * grad_wqkv[2], axis=1)
     ) / gain_attn.astype(F32)
-    grad_wgate, grad_wup = grad_wgate_up[:, :ff], grad_wgate_up[:, ff:]
     grad_gain2 = (
         jnp.sum(w_gate.astype(F32) * grad_wgate, axis=1)
         + jnp.sum(w_up.astype(F32) * grad_wup, axis=1)

time: 1090 us -> 704 us (0.65)
  waiting for transfers between devices: 807 us -> 198 us
  local copies, waits for them, and re-layouts: 53.1 us -> 155 us
  blocking collectives: 35.8 us -> 94.3 us
  starting transfers between devices: 16.5 us -> 74.1 us
    reduce_scatter x4 -> x0, waiting for transfers between devices: 424 us -> none  [the longest x3 408 us: reduce_gather(): lax.psum_scatter(partial.astype(BF16), axes, scatter_dimension=0, tiled=T...]
    all_gather x7 -> x0, waiting for transfers between devices: 255 us -> none  [the longest x4 185 us: gather(): return lax.all_gather(piece, axes, axis=0, tiled=True)]
    ppermute x0 -> x53, waiting for transfers between devices: none -> 166 us  [the longest x24 76.3 us: next_z(): return lax.ppermute(value, 'rep', self.to_z)]
    all_gather x1, blocking collectives: 5.29 us -> 94.3 us  [local(): lax.all_gather(jnp.stack([gain_attn, gain_ffn]), 'shard', axis=1, tiled=T...]
    dynamic_update_slice x0 -> x43, local copies, waits for them, and re-layouts: none -> 67.7 us  [the longest x8 40.1 us: gather_linked(): full = lax.dynamic_update_slice(full, part, place)]
    ppermute x0 -> x53, starting transfers between devices: none -> 50 us  [the longest x24 22.4 us: next_z(): return lax.ppermute(value, 'rep', self.to_z)]
    all_to_all x2, waiting for transfers between devices: 44.7 us -> 0.01 us  [to_heads(): return lax.all_to_all(chunks, 'rep', 0, 0, tiled=True)]
    all_to_all x1 -> x0, blocking collectives: 30.5 us -> none  [to_tokens(): chunks = lax.all_to_all(values, 'rep', 0, 0, tiled=True)]
  transfers between devices with their start and end apart: 17 -> 60, of which waited for: 15 -> 32; matrix products, arithmetic and copies ran while one was open for 14% -> 30% of each run, Pallas kernels for 4% -> 6%
where the time goes in v2:
time: 704 us; the launch traced here: 695 us
  waiting for transfers between devices  198 us (28%)
  local copies, waits for them, and re-layouts  155 us (22%)
  blocking collectives  94.3 us (13%)
  starting transfers between devices  74.1 us (11%)
  matrix products  64.4 us (9%)
  other arithmetic  54.5 us (8%)
  Pallas kernels  38.7 us (5%)
  between operations  15.7 us (2%)
    all_gather x1, blocking collectives, local(): lax.all_gather(jnp.stack([gain_attn, gain_ffn]), 'shard', axis=1, tiled=T...  94.3 us
    ppermute x24, waiting for transfers between devices, next_z(): return lax.ppermute(value, 'rep', self.to_z)  76.3 us
    dot_general x17, matrix products, dot(): lax.dot_general(left, right, ((contract[:1], contract[1:]), ((), ())), pr...  64.4 us
    ppermute x9, waiting for transfers between devices, over_x(): return lax.ppermute(value, 'shard', [(0, 1), (1, 0)])  56.6 us
    dynamic_update_slice x8, local copies, waits for them, and re-layouts, gather_linked(): full = lax.dynamic_update_slice(full, part, place)  40.1 us
    ppermute x8, waiting for transfers between devices, over_y(): return lax.ppermute(value, 'rep', self.to_y)  33.4 us
    ppermute x24, starting transfers between devices, next_z(): return lax.ppermute(value, 'rep', self.to_z)  22.4 us
    pallas_call x1, Pallas kernels, attend_back(): pl.pallas_call(functools.partial(attend_back_kernel, head_dim, bq, bk), o...  22.1 us
  transfers between devices with their start and end apart: 60, of which 32 were waited for; matrix products, arithmetic and copies ran while one was open for 30% of the time, Pallas kernels for 6%

profile of v2, /device:TPU:0, one launch (start us, length us, event | category | flops | bytes accessed | tf_op | source)
XLA Modules:
  0.0 694.6 jit_solution(6490432298358102385)
XLA Ops:
  16.3 94.3 %all_gather.9 = bf16[2,1024]{1,0:T(2,128)(2,1)S(1)} all-gather(bf16[2,512]{1,0:T(2,128)(2,1)S(1)} %pad_maximum_fusion.2), channel_id=1, replica_groups=mesh['rep'=16,'shard'=2] {'shard'}, dimensions={1}, use_global_device_ids=true | all-gather | bytes 6144 | tf_op jit(solution)/shard_map/all_gather | solution.py:405
  127.0 6.9 all-to-all-start
  148.7 5.0 broadcast_in_dim.178
  161.0 20.3 %collective-permute-done.6 = bf16[1408,512]{1,0:T(8,128)(2,1)} collective-permute-done((bf16[1408,512]{1,0:T(8,128)(2,1)}, bf16[1408,512]{1,0:T(8,128)(2,1)}, u32[]{:S(2)}, u32[]{:S(2)}) %collective-permute-start.6) | collective-permute-done | bytes 1441824 | tf_op jit(solution)/shard_map/ppermute | solution.py:228
  181.4 14.2 %dynamic_update_slice.163 = bf16[2816,1024]{1,0:T(8,128)(2,1)} dynamic-update-slice(bf16[2816,1024]{1,0:T(8,128)(2,1)} %constant_dynamic-update-slice_fusion, bf16[1408,512]{1,0:T(8,128)(2,1)} %collective-permute-done.6, s32[]{:T(128)S(6)} %select_n.377, s32[]{:T(128)S(6)} %select_n.376) | dynamic-update-slice | bytes 2883588 | tf_op jit(solution)/shard_map/dynamic_update_slice | solution.py:402
  198.7 16.6 %shard_map.220 = (bf16[2048,128]{1,0:T(8,128)(2,1)}, f32[128,2048]{1,0:T(8,128)}, f32[2,2048]{1,0:T(2,128)}) custom-call(s32[1]{0:T(128)} %dynamic_slice.168.prefix_ref, bf16[2048,128]{1,0:T(8,128)(2,1)} %get-tuple-element.63.q_ref, bf16[2048,128]{1,0:T(8,128)(2,1)} %get-tuple-element.62.k_ref, bf16[2048,128]{1,0:T(8,128)(2,1)} %get-tuple-element.61.v_ref), custom_call_target="tpu_custom_call" | custom-call | flops 2147483648 | bytes 2097152 | tf_op jit(solution)/shard_map/pallas_call | solution.py:293
  215.3 7.0 %all-to-all-start.1 = ((bf16[16,128,128]{2,1,0:T(8,128)(2,1)}), bf16[16,128,128]{2,1,0:T(8,128)(2,1)S(1)}, u32[]{:S(2)}, u32[]{:S(2)}) async-start(bf16[16,128,128]{2,1,0:T(8,128)(2,1)} %bitcast.405), calls=%async_computation.1 | async-start | bytes 1048576 | tf_op jit(solution)/shard_map/all_to_all | solution.py:425
  222.4 3.6 constant_dynamic-update-slice_fusion.2
  226.0 14.0 %dynamic_update_slice.164 = bf16[2816,1024]{1,0:T(8,128)(2,1)} dynamic-update-slice(bf16[2816,1024]{1,0:T(8,128)(2,1)} %dynamic_update_slice.163, bf16[1408,512]{1,0:T(8,128)(2,1)} %collective-permute-done.7, s32[]{:T(128)S(6)} %select_n.377, s32[]{:T(128)S(6)} %select_n.378) | dynamic-update-slice | bytes 2883588 | tf_op jit(solution)/shard_map/dynamic_update_slice | solution.py:402
  240.1 3.7 constant_dynamic-update-slice_fusion.1
  248.8 6.2 fusion.92
  255.0 8.7 %multiply_convert_fusion.1 = (bf16[256,2816]{1,0:T(8,128)(2,1)}, bf16[256,2816]{1,0:T(8,128)(2,1)}, bf16[256,2816]{1,0:T(8,128)(2,1)S(1)}) fusion(f32[256,5632]{1,0:T(8,128)S(1)} %fusion.92, bf16[2816,1024]{1,0:T(8,128)(2,1)} %dynamic_update_slice.164, bf16[256,1024]{1,0:T(8,128)(2,1)S(1)} %bitcast.391), kind=kOutput, calls=%fused_computation.27 | convolution fusion | flops 1487208448 | bytes 16384000 | tf_op jit(solution)/shard_map/dot_general | solution.py:20
  263.7 6.2 multiply_reduce_fusion.6
  278.9 5.6 fusion.26
  289.4 5.3 fusion.24
  294.7 12.6 %collective-permute-done.11 = bf16[2,128,1024]{2,1,0:T(8,128)(2,1)S(1)} collective-permute-done((bf16[2,128,1024]{2,1,0:T(8,128)(2,1)S(1)}, bf16[2,128,1024]{2,1,0:T(8,128)(2,1)S(1)}, u32[]{:S(2)}, u32[]{:S(2)}) %collective-permute-start.11) | collective-permute-done | bytes 524320 | tf_op jit(solution)/shard_map/ppermute | solution.py:231
  319.6 4.9 all-to-all-start.2
  332.2 4.0 convolution_convert_fusion.2
  336.1 13.3 %collective-permute-done.13 = bf16[32,1024]{1,0:T(8,128)(2,1)S(1)} collective-permute-done((bf16[32,1024]{1,0:T(8,128)(2,1)S(1)}, bf16[32,1024]{1,0:T(8,128)(2,1)S(1)}, u32[]{:S(2)}, u32[]{:S(2)}) %collective-permute-start.13) | collective-permute-done | bytes 65568 | tf_op jit(solution)/shard_map/ppermute | solution.py:234
  349.5 7.6 %collective-permute-start.14 = (bf16[32,1024]{1,0:T(8,128)(2,1)S(1)}, bf16[32,1024]{1,0:T(8,128)(2,1)S(1)}, u32[]{:S(2)}, u32[]{:S(2)}) collective-permute-start(bf16[32,1024]{1,0:T(8,128)(2,1)S(1)} %fusion.55), channel_id=1, source_target_pairs={{0,8},{2,10},{4,12},{6,14},{8,16},{10,18},{12,20},{14,22},{16,24},... | collective-permute-start | bytes 196616 | tf_op jit(solution)/shard_map/ppermute | solution.py:234
  360.0 4.2 collective-permute-start.15
  373.6 22.1 %shard_map.221 = (bf16[2048,128]{1,0:T(8,128)(2,1)}, bf16[2048,128]{1,0:T(8,128)(2,1)}, bf16[2048,128]{1,0:T(8,128)(2,1)}) custom-call(s32[1]{0:T(128)} %dynamic_slice.168.prefix_ref, bf16[2048,128]{1,0:T(8,128)(2,1)} %get-tuple-element.63.q_ref, bf16[2048,128]{1,0:T(8,128)(2,1)} %get-tuple-element.62.k_ref, bf16[2048,128]{1,0:T(8,128)(2,1)} %get-tuple-element.61.v_ref, ...), custom_call_target="tpu_custom_call" | custom-call | flops 5368709120 | bytes 5767168 | tf_op jit(solution)/shard_map/pallas_call | solution.py:319
  402.5 5.4 collective-permute-done.17
  408.7 5.4 collective-permute-done.18
  419.3 4.4 all-to-all-start.3
  445.3 10.4 %all-to-all-done.3 = bf16[16,128,384]{1,2,0:T(8,128)(2,1)} async-done(((bf16[16,128,384]{1,2,0:T(8,128)(2,1)}), bf16[16,128,384]{1,2,0:T(8,128)(2,1)}, u32[]{:S(2)}, u32[]{:S(2)}) %all-to-all-start.3) | async-done | bytes 1572896 | tf_op jit(solution)/shard_map/all_to_all | solution.py:425
  459.2 5.3 multiply_reduce_fusion.5
  465.7 8.8 %collective-permute-done.22 = bf16[2,128,2816]{2,1,0:T(8,128)(2,1)} collective-permute-done((bf16[2,128,2816]{2,1,0:T(8,128)(2,1)}, bf16[2,128,2816]{2,1,0:T(8,128)(2,1)}, u32[]{:S(2)}, u32[]{:S(2)}) %collective-permute-start.22) | collective-permute-done | bytes 1441824 | tf_op jit(solution)/shard_map/ppermute | solution.py:231
  481.5 20.2 %collective-permute-done.44 = bf16[1408,512]{1,0:T(8,128)(2,1)} collective-permute-done((bf16[1408,512]{1,0:T(8,128)(2,1)}, bf16[1408,512]{1,0:T(8,128)(2,1)}, u32[]{:S(2)}, u32[]{:S(2)}) %collective-permute-start.44) | collective-permute-done | bytes 1441824 | tf_op jit(solution)/shard_map/ppermute | solution.py:228
  504.8 11.4 %collective-permute-done.23 = bf16[128,2816]{1,0:T(8,128)(2,1)S(1)} collective-permute-done((bf16[128,2816]{1,0:T(8,128)(2,1)S(1)}, bf16[128,2816]{1,0:T(8,128)(2,1)S(1)}, u32[]{:S(2)}, u32[]{:S(2)}) %collective-permute-start.23) | collective-permute-done | bytes 720928 | tf_op jit(solution)/shard_map/ppermute | solution.py:228
  521.8 3.8 collective-permute-done.24
  525.7 3.7 collective-permute-done.35
  529.6 3.7 collective-permute-done.46
  533.5 3.7 collective-permute-done.25
  537.3 3.7 collective-permute-done.36
  541.2 3.7 collective-permute-done.47
  545.1 3.7 collective-permute-done.26
  560.6 3.6 collective-permute-done.38
  564.2 3.9 collective-permute-done.49
  572.0 3.9 collective-permute-done.39
  575.8 3.9 collective-permute-done.50
  593.3 4.8 fusion.18
  604.2 4.7 collective-permute-done.8
  612.2 6.8 collective-permute-done.9
  621.0 11.6 %collective-permute-done.52 = bf16[704,512]{1,0:T(8,128)(2,1)} collective-permute-done((bf16[704,512]{1,0:T(8,128)(2,1)}, bf16[704,512]{1,0:T(8,128)(2,1)}, u32[]{:S(2)}, u32[]{:S(2)}) %collective-permute-start.52) | collective-permute-done | bytes 720928 | tf_op jit(solution)/shard_map/ppermute | solution.py:231
  638.8 3.3 multiply_reduce_fusion.1
  644.0 3.3 multiply_reduce_fusion
  651.6 14.3 %all-gather.5.cloned.1.call-done = bf16[4096,384]{0,1:T(8,128)(2,1)} async-done(((bf16[256,384]{0,1:T(8,128)(2,1)}), bf16[4096,384]{0,1:T(8,128)(2,1)}) %all-gather.5.cloned.1.call-update) | async-done | bytes 3145744 | tf_op jit(solution)/shard_map/all_gather | solution.py:542
  (357 shorter events, 230.7 us)
Async XLA Ops:
  11.1 102.2 %collective-permute-start = (bf16[256,3072]{1,0:T(8,128)(2,1)}, bf16[256,3072]{1,0:T(8,128)(2,1)}, u32[]{:S(2)}, u32[]{:S(2)}) collective-permute-start(bf16[256,3072]{1,0:T(8,128)(2,1)} %pad_maximum_fusion.1), channel_id=1, source_target_pairs={{0,1},{1,0},{2,3},{3,2},{4,5},{5,4},{6,7},{7,6},{8,9},{9,8},{10,11... | collective-permute-start | bytes 4718600 | tf_op jit(solution)/shard_map/ppermute | solution.py:228
  16.3 124.7 %collective-permute-start.4 = (bf16[256,5632]{1,0:T(8,128)(2,1)}, bf16[256,5632]{1,0:T(8,128)(2,1)}, u32[]{:S(2)}, u32[]{:S(2)}) collective-permute-start(bf16[256,5632]{1,0:T(8,128)(2,1)} %pad_maximum_fusion), channel_id=1, source_target_pairs={{0,1},{1,0},{2,3},{3,2},{4,5},{5,4},{6,7},{7,6},{8,9},{9,8},{10,11... | collective-permute-start | bytes 8650760 | tf_op jit(solution)/shard_map/ppermute | solution.py:228
  127.0 68.6 %all-to-all-start = ((bf16[16,128,384]{1,2,0:T(8,128)(2,1)}), bf16[16,128,384]{1,2,0:T(8,128)(2,1)}, u32[]{:S(2)}, u32[]{:S(2)}) async-start(bf16[16,128,384]{1,2,0:T(8,128)(2,1)} %bitcast.353), calls=%async_computation | async-start | bytes 3145728 | tf_op jit(solution)/shard_map/all_to_all | solution.py:422
  135.8 19.8 %collective-permute-start.2 = (bf16[256,1024]{1,0:T(8,128)(2,1)}, bf16[256,1024]{1,0:T(8,128)(2,1)}, u32[]{:S(2)}, u32[]{:S(2)}) collective-permute-start(bf16[256,1024]{1,0:T(8,128)(2,1)} %constant_dynamic-slice_fusion.10), channel_id=1, source_target_pairs={{0,1},{1,0},{2,3},{3,2},{4,5},{5,4},{6,7},{7,6},{8,9},{9,8},{10,11... | collective-permute-start | bytes 1572872 | tf_op jit(solution)/shard_map/ppermute | solution.py:228
  139.8 41.5 %collective-permute-start.6 = (bf16[1408,512]{1,0:T(8,128)(2,1)}, bf16[1408,512]{1,0:T(8,128)(2,1)}, u32[]{:S(2)}, u32[]{:S(2)}) collective-permute-start(bf16[1408,512]{1,0:T(8,128)(2,1)} %constant_dynamic-slice_fusion.7), channel_id=1, source_target_pairs={{0,1},{1,0},{2,3},{3,2},{4,5},{5,4},{6,7},{7,6},{8,9},{9,8},{10,11... | collective-permute-start | bytes 4325384 | tf_op jit(solution)/shard_map/ppermute | solution.py:228
  141.0 99.1 %collective-permute-start.5 = (bf16[256,5632]{1,0:T(8,128)(2,1)}, bf16[256,5632]{1,0:T(8,128)(2,1)}, u32[]{:S(2)}, u32[]{:S(2)}) collective-permute-start(bf16[256,5632]{1,0:T(8,128)(2,1)} %collective-permute-done.4), channel_id=1, source_target_pairs={{0,2},{2,0},{4,6},{6,4},{8,10},{10,8},{12,14},{14,12},{16,18},{18,... | collective-permute-start | bytes 8650760 | tf_op jit(solution)/shard_map/ppermute | solution.py:225
  181.3 44.7 %collective-permute-start.7 = (bf16[1408,512]{1,0:T(8,128)(2,1)}, bf16[1408,512]{1,0:T(8,128)(2,1)}, u32[]{:S(2)}, u32[]{:S(2)}) collective-permute-start(bf16[1408,512]{1,0:T(8,128)(2,1)} %collective-permute-done.6), channel_id=1, source_target_pairs={{0,2},{2,0},{4,6},{6,4},{8,10},{10,8},{12,14},{14,12},{16,18},{18,... | collective-permute-start | bytes 4325384 | tf_op jit(solution)/shard_map/ppermute | solution.py:225
  215.3 28.4 %all-to-all-start.1 = ((bf16[16,128,128]{2,1,0:T(8,128)(2,1)}), bf16[16,128,128]{2,1,0:T(8,128)(2,1)S(1)}, u32[]{:S(2)}, u32[]{:S(2)}) async-start(bf16[16,128,128]{2,1,0:T(8,128)(2,1)} %bitcast.405), calls=%async_computation.1 | async-start | bytes 1048576 | tf_op jit(solution)/shard_map/all_to_all | solution.py:425
  222.3 371.0 %all-gather.3.cloned.1.call-start = ((), (), s32[]{:S(2)}) async-start(), calls=%async_computation.4 | async-start | bytes 8912896 | tf_op jit(solution)/shard_map/all_gather | solution.py:439
  287.7 19.6 %collective-permute-start.11 = (bf16[2,128,1024]{2,1,0:T(8,128)(2,1)S(1)}, bf16[2,128,1024]{2,1,0:T(8,128)(2,1)S(1)}, u32[]{:S(2)}, u32[]{:S(2)}) collective-permute-start(bf16[2,128,1024]{2,1,0:T(8,128)(2,1)S(1)} %dynamic-slice_bitcast_fusion.6), channel_id=1, source_target_pairs={{0,4},{2,6},{4,0},{6,2},{8,12},{10,14},{12,8},{14,10},{16,20},{18,... | collective-permute-start | bytes 1572872 | tf_op jit(solution)/shard_map/ppermute | solution.py:231
  309.0 20.1 %collective-permute-start.12 = (bf16[128,1024]{1,0:T(8,128)(2,1)}, bf16[128,1024]{1,0:T(8,128)(2,1)}, u32[]{:S(2)}, u32[]{:S(2)}) collective-permute-start(bf16[128,1024]{1,0:T(8,128)(2,1)} %dynamic-slice_bitcast_fusion.7), channel_id=1, source_target_pairs={{0,1},{1,0},{2,3},{3,2},{4,5},{5,4},{6,7},{7,6},{8,9},{9,8},{10,11... | collective-permute-start | bytes 786440 | tf_op jit(solution)/shard_map/ppermute | solution.py:228
  319.6 53.9 %all-to-all-start.2 = ((bf16[16,128,128]{2,1,0:T(8,128)(2,1)}), bf16[16,128,128]{2,1,0:T(8,128)(2,1)}, u32[]{:S(2)}, u32[]{:S(2)}) async-start(bf16[16,128,128]{2,1,0:T(8,128)(2,1)} %bitcast.385), calls=%async_computation.2 | async-start | bytes 1048576 | tf_op jit(solution)/shard_map/all_to_all | solution.py:422
  330.2 19.2 %collective-permute-start.13 = (bf16[32,1024]{1,0:T(8,128)(2,1)S(1)}, bf16[32,1024]{1,0:T(8,128)(2,1)S(1)}, u32[]{:S(2)}, u32[]{:S(2)}) collective-permute-start(bf16[32,1024]{1,0:T(8,128)(2,1)S(1)} %dynamic-slice_bitcast_fusion.11), channel_id=1, source_target_pairs={{0,8},{2,10},{4,12},{6,14},{8,16},{10,18},{12,20},{14,22},{16,24},... | collective-permute-start | bytes 196616 | tf_op jit(solution)/shard_map/ppermute | solution.py:234
  336.1 90.2 %collective-permute-start.21 = (bf16[512,2816]{1,0:T(8,128)(2,1)}, bf16[512,2816]{1,0:T(8,128)(2,1)}, u32[]{:S(2)}, u32[]{:S(2)}) collective-permute-start(bf16[512,2816]{1,0:T(8,128)(2,1)} %convolution_convert_fusion.2), channel_id=1, source_target_pairs={{0,2},{2,0},{4,6},{6,4},{8,10},{10,8},{12,14},{14,12},{16,18},{18,... | collective-permute-start | bytes 8650760 | tf_op jit(solution)/shard_map/ppermute | solution.py:225
  349.5 10.5 %collective-permute-start.14 = (bf16[32,1024]{1,0:T(8,128)(2,1)S(1)}, bf16[32,1024]{1,0:T(8,128)(2,1)S(1)}, u32[]{:S(2)}, u32[]{:S(2)}) collective-permute-start(bf16[32,1024]{1,0:T(8,128)(2,1)S(1)} %fusion.55), channel_id=1, source_target_pairs={{0,8},{2,10},{4,12},{6,14},{8,16},{10,18},{12,20},{14,22},{16,24},... | collective-permute-start | bytes 196616 | tf_op jit(solution)/shard_map/ppermute | solution.py:234
  368.0 64.0 %collective-permute-start.32 = (bf16[512,2816]{1,0:T(8,128)(2,1)}, bf16[512,2816]{1,0:T(8,128)(2,1)}, u32[]{:S(2)}, u32[]{:S(2)}) collective-permute-start(bf16[512,2816]{1,0:T(8,128)(2,1)} %convolution_convert_fusion.1), channel_id=1, source_target_pairs={{0,2},{2,0},{4,6},{6,4},{8,10},{10,8},{12,14},{14,12},{16,18},{18,... | collective-permute-start | bytes 8650760 | tf_op jit(solution)/shard_map/ppermute | solution.py:225
  368.1 69.0 %collective-permute-start.43 = (bf16[2816,512]{1,0:T(8,128)(2,1)}, bf16[2816,512]{1,0:T(8,128)(2,1)}, u32[]{:S(2)}, u32[]{:S(2)}) collective-permute-start(bf16[2816,512]{1,0:T(8,128)(2,1)} %convolution_convert_fusion), channel_id=1, source_target_pairs={{0,2},{2,0},{4,6},{6,4},{8,10},{10,8},{12,14},{14,12},{16,18},{18,... | collective-permute-start | bytes 8650760 | tf_op jit(solution)/shard_map/ppermute | solution.py:225
  370.8 31.0 %collective-permute-start.16 = (bf16[32,1024]{1,0:T(8,128)(2,1)S(1)}, bf16[32,1024]{1,0:T(8,128)(2,1)S(1)}, u32[]{:S(2)}, u32[]{:S(2)}) collective-permute-start(bf16[32,1024]{1,0:T(8,128)(2,1)S(1)} %get-tuple-element.41), channel_id=1, source_target_pairs={{0,8},{2,10},{4,12},{6,14},{8,16},{10,18},{12,20},{14,22},{16,24},... | collective-permute-start | bytes 196616 | tf_op jit(solution)/shard_map/ppermute | solution.py:234
  414.8 10.1 %collective-permute-start.19 = (bf16[128,1024]{1,0:T(8,128)(2,1)}, bf16[128,1024]{1,0:T(8,128)(2,1)}, u32[]{:S(2)}, u32[]{:S(2)}) collective-permute-start(bf16[128,1024]{1,0:T(8,128)(2,1)} %bitcast.49), channel_id=1, source_target_pairs={{0,4},{2,6},{4,0},{6,2},{8,12},{10,14},{12,8},{14,10},{16,20},{18,... | collective-permute-start | bytes 786440 | tf_op jit(solution)/shard_map/ppermute | solution.py:231
  419.3 36.4 %all-to-all-start.3 = ((bf16[16,128,384]{1,2,0:T(8,128)(2,1)}), bf16[16,128,384]{1,2,0:T(8,128)(2,1)}, u32[]{:S(2)}, u32[]{:S(2)}) async-start(bf16[16,128,384]{1,2,0:T(8,128)(2,1)} %maximum_multiply_fusion), calls=%async_computation.3 | async-start | bytes 3145728 | tf_op jit(solution)/shard_map/all_to_all | solution.py:425
  423.7 242.2 %all-gather.5.cloned.1.call-start = ((), (), s32[]{:S(2)}) async-start(), calls=%async_computation.5 | async-start | bytes 3342336 | tf_op jit(solution)/shard_map/all_gather | solution.py:542
  425.9 17.7 %collective-permute-start.20 = (bf16[256,1024]{1,0:T(8,128)(2,1)S(1)}, bf16[256,1024]{1,0:T(8,128)(2,1)S(1)}, u32[]{:S(2)}, u32[]{:S(2)}) collective-permute-start(bf16[256,1024]{1,0:T(8,128)(2,1)S(1)} %bitcast.389), channel_id=1, source_target_pairs={{0,2},{2,0},{4,6},{6,4},{8,10},{10,8},{12,14},{14,12},{16,18},{18,... | collective-permute-start | bytes 1572872 | tf_op jit(solution)/shard_map/ppermute | solution.py:225
  430.4 44.1 %collective-permute-start.22 = (bf16[2,128,2816]{2,1,0:T(8,128)(2,1)}, bf16[2,128,2816]{2,1,0:T(8,128)(2,1)}, u32[]{:S(2)}, u32[]{:S(2)}) collective-permute-start(bf16[2,128,2816]{2,1,0:T(8,128)(2,1)} %dynamic-slice_bitcast_fusion.2), channel_id=1, source_target_pairs={{0,4},{2,6},{4,0},{6,2},{8,12},{10,14},{12,8},{14,10},{16,20},{18,... | collective-permute-start | bytes 4325384 | tf_op jit(solution)/shard_map/ppermute | solution.py:231
  436.0 41.5 %collective-permute-start.33 = (bf16[256,2816]{1,0:T(8,128)(2,1)}, bf16[256,2816]{1,0:T(8,128)(2,1)}, u32[]{:S(2)}, u32[]{:S(2)}) collective-permute-start(bf16[256,2816]{1,0:T(8,128)(2,1)} %dynamic-slice_bitcast_fusion.1), channel_id=1, source_target_pairs={{0,1},{1,0},{2,3},{3,2},{4,5},{5,4},{6,7},{7,6},{8,9},{9,8},{10,11... | collective-permute-start | bytes 4325384 | tf_op jit(solution)/shard_map/ppermute | solution.py:228
  442.7 59.0 %collective-permute-start.44 = (bf16[1408,512]{1,0:T(8,128)(2,1)}, bf16[1408,512]{1,0:T(8,128)(2,1)}, u32[]{:S(2)}, u32[]{:S(2)}) collective-permute-start(bf16[1408,512]{1,0:T(8,128)(2,1)} %dynamic-slice_bitcast_fusion), channel_id=1, source_target_pairs={{0,1},{1,0},{2,3},{3,2},{4,5},{5,4},{6,7},{7,6},{8,9},{9,8},{10,11... | collective-permute-start | bytes 4325384 | tf_op jit(solution)/shard_map/ppermute | solution.py:228
  476.3 39.8 %collective-permute-start.23 = (bf16[128,2816]{1,0:T(8,128)(2,1)S(1)}, bf16[128,2816]{1,0:T(8,128)(2,1)S(1)}, u32[]{:S(2)}, u32[]{:S(2)}) collective-permute-start(bf16[128,2816]{1,0:T(8,128)(2,1)S(1)} %dynamic-slice_bitcast_fusion.5), channel_id=1, source_target_pairs={{0,1},{1,0},{2,3},{3,2},{4,5},{5,4},{6,7},{7,6},{8,9},{9,8},{10,11... | collective-permute-start | bytes 2162696 | tf_op jit(solution)/shard_map/ppermute | solution.py:228
  479.3 38.6 %collective-permute-start.34 = (bf16[128,2816]{1,0:T(8,128)(2,1)S(1)}, bf16[128,2816]{1,0:T(8,128)(2,1)S(1)}, u32[]{:S(2)}, u32[]{:S(2)}) collective-permute-start(bf16[128,2816]{1,0:T(8,128)(2,1)S(1)} %dynamic-slice_bitcast_fusion.4), channel_id=1, source_target_pairs={{0,4},{2,6},{4,0},{6,2},{8,12},{10,14},{12,8},{14,10},{16,20},{18,... | collective-permute-start | bytes 2162696 | tf_op jit(solution)/shard_map/ppermute | solution.py:231
  503.5 16.5 %collective-permute-start.45 = (bf16[704,512]{1,0:T(8,128)(2,1)S(1)}, bf16[704,512]{1,0:T(8,128)(2,1)S(1)}, u32[]{:S(2)}, u32[]{:S(2)}) collective-permute-start(bf16[704,512]{1,0:T(8,128)(2,1)S(1)} %dynamic-slice_bitcast_fusion.3), channel_id=1, source_target_pairs={{0,4},{2,6},{4,0},{6,2},{8,12},{10,14},{12,8},{14,10},{16,20},{18,... | collective-permute-start | bytes 2162696 | tf_op jit(solution)/shard_map/ppermute | solution.py:231
  518.1 11.4 %collective-permute-start.35 = (bf16[32,2816]{1,0:T(8,128)(2,1)S(1)}, bf16[32,2816]{1,0:T(8,128)(2,1)S(1)}, u32[]{:S(2)}, u32[]{:S(2)}) collective-permute-start(bf16[32,2816]{1,0:T(8,128)(2,1)S(1)} %dynamic-slice_bitcast_fusion.9), channel_id=1, source_target_pairs={{0,8},{2,10},{4,12},{6,14},{8,16},{10,18},{12,20},{14,22},{16,24},... | collective-permute-start | bytes 540680 | tf_op jit(solution)/shard_map/ppermute | solution.py:234
  520.3 13.1 %collective-permute-start.46 = (bf16[176,512]{1,0:T(8,128)(2,1)S(1)}, bf16[176,512]{1,0:T(8,128)(2,1)S(1)}, u32[]{:S(2)}, u32[]{:S(2)}) collective-permute-start(bf16[176,512]{1,0:T(8,128)(2,1)S(1)} %dynamic-slice_bitcast_fusion.8), channel_id=1, source_target_pairs={{0,8},{2,10},{4,12},{6,14},{8,16},{10,18},{12,20},{14,22},{16,24},... | collective-permute-start | bytes 540680 | tf_op jit(solution)/shard_map/ppermute | solution.py:234
  525.7 11.5 %collective-permute-start.25 = (bf16[32,2816]{1,0:T(8,128)(2,1)S(1)}, bf16[32,2816]{1,0:T(8,128)(2,1)S(1)}, u32[]{:S(2)}, u32[]{:S(2)}) collective-permute-start(bf16[32,2816]{1,0:T(8,128)(2,1)S(1)} %fusion.47), channel_id=1, source_target_pairs={{0,8},{2,10},{4,12},{6,14},{8,16},{10,18},{12,20},{14,22},{16,24},... | collective-permute-start | bytes 540680 | tf_op jit(solution)/shard_map/ppermute | solution.py:234
  529.5 11.5 %collective-permute-start.36 = (bf16[32,2816]{1,0:T(8,128)(2,1)S(1)}, bf16[32,2816]{1,0:T(8,128)(2,1)S(1)}, u32[]{:S(2)}, u32[]{:S(2)}) collective-permute-start(bf16[32,2816]{1,0:T(8,128)(2,1)S(1)} %fusion.44), channel_id=1, source_target_pairs={{0,8},{2,10},{4,12},{6,14},{8,16},{10,18},{12,20},{14,22},{16,24},... | collective-permute-start | bytes 540680 | tf_op jit(solution)/shard_map/ppermute | solution.py:234
  533.4 11.5 %collective-permute-start.47 = (bf16[176,512]{1,0:T(8,128)(2,1)S(1)}, bf16[176,512]{1,0:T(8,128)(2,1)S(1)}, u32[]{:S(2)}, u32[]{:S(2)}) collective-permute-start(bf16[176,512]{1,0:T(8,128)(2,1)S(1)} %fusion.41), channel_id=1, source_target_pairs={{0,8},{2,10},{4,12},{6,14},{8,16},{10,18},{12,20},{14,22},{16,24},... | collective-permute-start | bytes 540680 | tf_op jit(solution)/shard_map/ppermute | solution.py:234
  537.3 11.5 %collective-permute-start.26 = (bf16[32,2816]{1,0:T(8,128)(2,1)S(1)}, bf16[32,2816]{1,0:T(8,128)(2,1)S(1)}, u32[]{:S(2)}, u32[]{:S(2)}) collective-permute-start(bf16[32,2816]{1,0:T(8,128)(2,1)S(1)} %fusion.48), channel_id=1, source_target_pairs={{0,8},{2,10},{4,12},{6,14},{8,16},{10,18},{12,20},{14,22},{16,24},... | collective-permute-start | bytes 540680 | tf_op jit(solution)/shard_map/ppermute | solution.py:234
  541.1 11.5 %collective-permute-start.37 = (bf16[32,2816]{1,0:T(8,128)(2,1)S(1)}, bf16[32,2816]{1,0:T(8,128)(2,1)S(1)}, u32[]{:S(2)}, u32[]{:S(2)}) collective-permute-start(bf16[32,2816]{1,0:T(8,128)(2,1)S(1)} %fusion.45), channel_id=1, source_target_pairs={{0,8},{2,10},{4,12},{6,14},{8,16},{10,18},{12,20},{14,22},{16,24},... | collective-permute-start | bytes 540680 | tf_op jit(solution)/shard_map/ppermute | solution.py:234
  545.0 11.5 %collective-permute-start.48 = (bf16[176,512]{1,0:T(8,128)(2,1)S(1)}, bf16[176,512]{1,0:T(8,128)(2,1)S(1)}, u32[]{:S(2)}, u32[]{:S(2)}) collective-permute-start(bf16[176,512]{1,0:T(8,128)(2,1)S(1)} %fusion.42), channel_id=1, source_target_pairs={{0,8},{2,10},{4,12},{6,14},{8,16},{10,18},{12,20},{14,22},{16,24},... | collective-permute-start | bytes 540680 | tf_op jit(solution)/shard_map/ppermute | solution.py:234
  550.4 10.0 %collective-permute-start.27 = (bf16[32,2816]{1,0:T(8,128)(2,1)S(1)}, bf16[32,2816]{1,0:T(8,128)(2,1)S(1)}, u32[]{:S(2)}, u32[]{:S(2)}) collective-permute-start(bf16[32,2816]{1,0:T(8,128)(2,1)S(1)} %get-tuple-element.39), channel_id=1, source_target_pairs={{0,8},{2,10},{4,12},{6,14},{8,16},{10,18},{12,20},{14,22},{16,24},... | collective-permute-start | bytes 540680 | tf_op jit(solution)/shard_map/ppermute | solution.py:234
  560.4 11.6 %collective-permute-start.28 = (bf16[32,2816]{1,0:T(8,128)(2,1)S(1)}, bf16[32,2816]{1,0:T(8,128)(2,1)S(1)}, u32[]{:S(2)}, u32[]{:S(2)}) collective-permute-start(bf16[32,2816]{1,0:T(8,128)(2,1)S(1)} %collective-permute-done.27), channel_id=1, source_target_pairs={{0,8},{2,10},{4,12},{6,14},{8,16},{10,18},{12,20},{14,22},{16,24},... | collective-permute-start | bytes 540680 | tf_op jit(solution)/shard_map/ppermute | solution.py:234
  564.2 11.6 %collective-permute-start.39 = (bf16[32,2816]{1,0:T(8,128)(2,1)S(1)}, bf16[32,2816]{1,0:T(8,128)(2,1)S(1)}, u32[]{:S(2)}, u32[]{:S(2)}) collective-permute-start(bf16[32,2816]{1,0:T(8,128)(2,1)S(1)} %collective-permute-done.38), channel_id=1, source_target_pairs={{0,8},{2,10},{4,12},{6,14},{8,16},{10,18},{12,20},{14,22},{16,24},... | collective-permute-start | bytes 540680 | tf_op jit(solution)/shard_map/ppermute | solution.py:234
  568.1 11.6 %collective-permute-start.50 = (bf16[176,512]{1,0:T(8,128)(2,1)S(1)}, bf16[176,512]{1,0:T(8,128)(2,1)S(1)}, u32[]{:S(2)}, u32[]{:S(2)}) collective-permute-start(bf16[176,512]{1,0:T(8,128)(2,1)S(1)} %collective-permute-done.49), channel_id=1, source_target_pairs={{0,8},{2,10},{4,12},{6,14},{8,16},{10,18},{12,20},{14,22},{16,24},... | collective-permute-start | bytes 540680 | tf_op jit(solution)/shard_map/ppermute | solution.py:234
  572.0 11.6 %collective-permute-start.29 = (bf16[32,2816]{1,0:T(8,128)(2,1)S(1)}, bf16[32,2816]{1,0:T(8,128)(2,1)S(1)}, u32[]{:S(2)}, u32[]{:S(2)}) collective-permute-start(bf16[32,2816]{1,0:T(8,128)(2,1)S(1)} %collective-permute-done.28), channel_id=1, source_target_pairs={{0,8},{2,10},{4,12},{6,14},{8,16},{10,18},{12,20},{14,22},{16,24},... | collective-permute-start | bytes 540680 | tf_op jit(solution)/shard_map/ppermute | solution.py:234
  575.8 11.6 %collective-permute-start.40 = (bf16[32,2816]{1,0:T(8,128)(2,1)S(1)}, bf16[32,2816]{1,0:T(8,128)(2,1)S(1)}, u32[]{:S(2)}, u32[]{:S(2)}) collective-permute-start(bf16[32,2816]{1,0:T(8,128)(2,1)S(1)} %collective-permute-done.39), channel_id=1, source_target_pairs={{0,8},{2,10},{4,12},{6,14},{8,16},{10,18},{12,20},{14,22},{16,24},... | collective-permute-start | bytes 540680 | tf_op jit(solution)/shard_map/ppermute | solution.py:234
  584.2 26.7 %collective-permute-start.30 = (bf16[128,2816]{1,0:T(8,128)(2,1)}, bf16[128,2816]{1,0:T(8,128)(2,1)}, u32[]{:S(2)}, u32[]{:S(2)}) collective-permute-start(bf16[128,2816]{1,0:T(8,128)(2,1)} %bitcast.72), channel_id=1, source_target_pairs={{0,4},{2,6},{4,0},{6,2},{8,12},{10,14},{12,8},{14,10},{16,20},{18,... | collective-permute-start | bytes 2162696 | tf_op jit(solution)/shard_map/ppermute | solution.py:231
  588.1 31.7 %collective-permute-start.41 = (bf16[128,2816]{1,0:T(8,128)(2,1)}, bf16[128,2816]{1,0:T(8,128)(2,1)}, u32[]{:S(2)}, u32[]{:S(2)}) collective-permute-start(bf16[128,2816]{1,0:T(8,128)(2,1)} %bitcast.94), channel_id=1, source_target_pairs={{0,4},{2,6},{4,0},{6,2},{8,12},{10,14},{12,8},{14,10},{16,20},{18,... | collective-permute-start | bytes 2162696 | tf_op jit(solution)/shard_map/ppermute | solution.py:231
  590.3 42.3 %collective-permute-start.52 = (bf16[704,512]{1,0:T(8,128)(2,1)}, bf16[704,512]{1,0:T(8,128)(2,1)}, u32[]{:S(2)}, u32[]{:S(2)}) collective-permute-start(bf16[704,512]{1,0:T(8,128)(2,1)} %bitcast.116), channel_id=1, source_target_pairs={{0,4},{2,6},{4,0},{6,2},{8,12},{10,14},{12,8},{14,10},{16,20},{18,... | collective-permute-start | bytes 2162696 | tf_op jit(solution)/shard_map/ppermute | solution.py:231
  612.1 24.6 %collective-permute-start.31 = (bf16[256,2816]{1,0:T(8,128)(2,1)S(1)}, bf16[256,2816]{1,0:T(8,128)(2,1)}, u32[]{:S(2)}, u32[]{:S(2)}) collective-permute-start(bf16[256,2816]{1,0:T(8,128)(2,1)S(1)} %bitcast.362), channel_id=1, source_target_pairs={{0,2},{2,0},{4,6},{6,4},{8,10},{10,8},{12,14},{14,12},{16,18},{18,... | collective-permute-start | bytes 4325384 | tf_op jit(solution)/shard_map/ppermute | solution.py:225
  621.0 21.2 %collective-permute-start.42 = (bf16[256,2816]{1,0:T(8,128)(2,1)S(1)}, bf16[256,2816]{1,0:T(8,128)(2,1)S(1)}, u32[]{:S(2)}, u32[]{:S(2)}) collective-permute-start(bf16[256,2816]{1,0:T(8,128)(2,1)S(1)} %bitcast.360), channel_id=1, source_target_pairs={{0,2},{2,0},{4,6},{6,4},{8,10},{10,8},{12,14},{14,12},{16,18},{18,... | collective-permute-start | bytes 4325384 | tf_op jit(solution)/shard_map/ppermute | solution.py:225
  634.6 13.3 %collective-permute-start.53 = (bf16[1408,512]{1,0:T(8,128)(2,1)}, bf16[1408,512]{1,0:T(8,128)(2,1)S(1)}, u32[]{:S(2)}, u32[]{:S(2)}) collective-permute-start(bf16[1408,512]{1,0:T(8,128)(2,1)} %bitcast.364), channel_id=1, source_target_pairs={{0,2},{2,0},{4,6},{6,4},{8,10},{10,8},{12,14},{14,12},{16,18},{18,... | collective-permute-start | bytes 4325384 | tf_op jit(solution)/shard_map/ppermute | solution.py:225
  (58 other events, 390.2 us)
Sparse Core Ops, SparseCore 0:
  278.8 93.5 all-gather.2
  619.9 46.0 all-gather.4

commit v3 on v1

--- a/solution.py
+++ b/solution.py
@@ -138,9 +138,7 @@
     mass_ref,
     cos_ref,
     sin_ref,
-    dq_ref,
-    dk_ref,
-    dv_ref,
+    out_ref,
     k_t,
     delta,
     dq_t,
@@ -193,24 +191,133 @@
 
         lax.fori_loop(begin, length // bq, query_step, 0)
         place = pl.ds(k0, bk)
-        dk_ref[place, :] = rope_back(dk_acc[...], place).astype(BF16)
-        dv_ref[place, :] = dv_acc[...].astype(BF16)
+        out_ref[place, width : 2 * width] = rope_back(dk_acc[...], place).astype(BF16)
+        out_ref[place, 2 * width :] = dv_acc[...].astype(BF16) * jnp.array(0.5, BF16)
         return carry
 
     lax.fori_loop(0, length // bk, key_step, 0)
     for start in range(0, length, 128):
         place = slice(start, start + 128)
-        dq_ref[place, :] = rope_back(dq_t[:, place].T * 0.125, place).astype(BF16)
+        out_ref[place, :width] = rope_back(dq_t[:, place].T * 0.125, place).astype(BF16)
+
+
+def turns(reps, move):
+    pairs = []
+    for here in range(reps):
+        z, y, core = move(here // 4, (here // 2) % 2, here % 2)
+        pairs.append((here, (z % (reps // 4)) * 4 + y * 2 + core))
+    return pairs
+
+
+class Links:
+    def __init__(self, reps):
+        self.deep = reps // 4
+        self.to_core = turns(reps, lambda z, y, core: (z, y, 1 - core))
+        self.to_y = turns(reps, lambda z, y, core: (z, 1 - y, core))
+        self.to_z = turns(reps, lambda z, y, core: (z + 1, y, core))
+        here = lax.axis_index("rep")
+        self.z, self.y, self.core = here // 4, (here // 2) % 2, here % 2
+        self.x = lax.axis_index("shard")
+
+    def over_core(self, value):
+        return lax.ppermute(value, "rep", self.to_core)
+
+    def over_x(self, value):
+        return lax.ppermute(value, "shard", [(0, 1), (1, 0)])
+
+    def over_y(self, value):
+        return lax.ppermute(value, "rep", self.to_y)
+
+    def next_z(self, value):
+        return lax.ppermute(value, "rep", self.to_z)
+
+    def half(self, total, side):
+        return pick(total.reshape(2, -1, total.shape[1]), side)
+
+    def quarters(self, total, side):
+        columns = total.shape[1]
+        return pick(total.reshape(2, 2, -1, columns), side, 1).reshape(-1, columns)
+
+    def part(self, total, turn):
+        return pick(total.reshape(self.deep, -1, total.shape[1]), (self.z + turn) % self.deep)
+
+    def ring_start(self, total):
+        return self.next_z(self.part(total, self.deep - 1))
+
+    def ring_step(self, total, arrived, step):
+        return add(self.part(total, 2 * self.deep - 2 - step), arrived)
+
+    def along_z(self, total):
+        arrived = self.ring_start(total)
+        for step in range(self.deep - 1):
+            moving = self.ring_step(total, arrived, step)
+            if step < self.deep - 2:
+                arrived = self.next_z(moving)
+        return moving
+
+    def collect(self, piece):
+        deep = self.deep
+        whole_z = blank((deep,) + piece.shape, piece.dtype)
+        for step in range(deep):
+            whole_z = put(whole_z, piece, (self.z + deep - step) % deep)
+            if step < deep - 1:
+                piece = self.next_z(piece)
+        whole_z = whole_z.reshape(-1, piece.shape[1])
+        halves = join(whole_z, self.over_y(whole_z), self.y).reshape(-1, piece.shape[1])
+        return join(halves, self.over_core(halves), self.core)
+
+
+def pick(values, index, axis=0):
+    return lax.dynamic_index_in_dim(values, index, axis, keepdims=False)
+
+
+def put(values, part, index):
+    return lax.dynamic_update_index_in_dim(values, part, index, 0)
+
+
+def join(mine, other, index):
+    both = blank((2,) + mine.shape, mine.dtype)
+    return put(put(both, mine, index), other, 1 - index)
+
+
+def fence(*values):
+    return lax.optimization_barrier(values)
+
+
+def after(value, *earlier):
+    return lax.optimization_barrier((value,) + earlier)[0]
+
+
+def blank(shape, dtype):
+    return pl.pallas_call(
+        lambda out_ref: None,
+        out_shape=jax.ShapeDtypeStruct(shape, dtype),
+        out_specs=pl.BlockSpec(memory_space=pl.ANY),
+    )()
+
+
+def add(left, right):
+    return (left.astype(F32) + right.astype(F32)).astype(BF16)
 
 
 def whole(shape):
     return pl.BlockSpec(shape, lambda *_: (0,) * len(shape))
 
 
-def attend(prefix, q, k, v, head_dim, bq, bk):
-    length, width = q.shape
+def thirds(qkv):
+    length, width = qkv.shape[0], qkv.shape[1] // 3
+    if width % 128 == 0:
+        specs = [pl.BlockSpec((length, width), lambda *_, at=at: (0, at)) for at in range(3)]
+        return (qkv, qkv, qkv), specs
+    parts = tuple(qkv[:, at * width : (at + 1) * width] for at in range(3))
+    return parts, [whole((length, width))] * 3
+
+
+def attend(prefix, qkv, head_dim, bq, bk):
+    length, width = qkv.shape[0], qkv.shape[1] // 3
     heads = width // head_dim
     flops = 2 * 2 * heads * length * length * head_dim
+    operands, specs = thirds(qkv)
     return pl.pallas_call(
         functools.partial(attend_kernel, head_dim, bq, bk),
         out_shape=(
@@ -221,7 +328,7 @@
         grid_spec=pltpu.PrefetchScalarGridSpec(
             num_scalar_prefetch=1,
             grid=(1,),
-            in_specs=[whole((length, width))] * 3,
+            in_specs=specs,
             out_specs=[whole((length, width)), whole((width, length)), whole((heads, length))],
             scratch_shapes=[pltpu.VMEM((width, length), BF16), pltpu.VMEM((width, bq), F32)],
         ),
@@ -229,22 +336,23 @@
         cost_estimate=pl.CostEstimate(
             flops=flops, transcendentals=heads * length * length, bytes_accessed=8 * length * width
         ),
-    )(prefix, q, k, v)
-
-
-def attend_back(prefix, q, k, v, do, att_t, mass, cosine, sine, head_dim, bq, bk):
-    length, width = q.shape
+    )(prefix, *operands)
+
+
+def attend_back(prefix, qkv, do, att_t, mass, cosine, sine, head_dim, bq, bk):
+    length, width = qkv.shape[0], qkv.shape[1] // 3
     heads = width // head_dim
     flops = 5 * 2 * heads * length * length * head_dim
     rows = whole((length, width))
+    operands, specs = thirds(qkv)
     return pl.pallas_call(
         functools.partial(attend_back_kernel, head_dim, bq, bk),
-        out_shape=(jax.ShapeDtypeStruct((length, width), BF16),) * 3,
+        out_shape=jax.ShapeDtypeStruct((length, 3 * width), BF16),
         grid_spec=pltpu.PrefetchScalarGridSpec(
             num_scalar_prefetch=1,
             grid=(1,),
-            in_specs=[rows] * 4 + [whole((width, length)), whole((heads, length)), rows, rows],
-            out_specs=[rows] * 3,
+            in_specs=specs + [rows, whole((width, length)), whole((heads, length)), rows, rows],
+            out_specs=whole((length, 3 * width)),
             scratch_shapes=[
                 pltpu.VMEM((width, length), BF16),
                 pltpu.VMEM((heads, length), F32),
@@ -257,12 +365,128 @@
         cost_estimate=pl.CostEstimate(
             flops=flops, transcendentals=heads * length * length, bytes_accessed=22 * length * width
         ),
-    )(prefix, q, k, v, do, att_t, mass, cosine, sine)
+    )(prefix, *operands, do, att_t, mass, cosine, sine)
+
+
+def spread_kernel(lanes, in_ref, wq_ref, wk_ref, wv_ref, q_ref, k_ref, v_ref, sum_ref):
+    total = None
+    for at, (w_ref, out_ref) in enumerate(((wq_ref, q_ref), (wk_ref, k_ref), (wv_ref, v_ref))):
+        part = in_ref[0, :, at * lanes : (at + 1) * lanes].astype(F32)
+        out_ref[...] = part
+        term = part * w_ref[...].astype(F32)
+        total = term if total is None else total + term
+
+    @pl.when(pl.program_id(1) == 0)
+    def _():
+        sum_ref[...] = total
+
+    @pl.when(pl.program_id(1) > 0)
+    def _():
+        sum_ref[...] += total
+
+
+def spread(gathered, w_query, w_key, w_value, seqs, groups):
+    height, width = w_query.shape
+    share, lanes = height // seqs, width // groups
+    tile = pl.BlockSpec((share, lanes), lambda s, g: (s, g))
+    return pl.pallas_call(
+        functools.partial(spread_kernel, lanes),
+        out_shape=(jax.ShapeDtypeStruct((height, width), F32),) * 3
+        + (jax.ShapeDtypeStruct((height, lanes), F32),),
+        grid=(seqs, groups),
+        in_specs=[
+            pl.BlockSpec((1, share, 3 * lanes), lambda s, g: (s * groups + g, 0, 0)),
+            tile,
+            tile,
+            tile,
+        ],
+        out_specs=[tile, tile, tile, pl.BlockSpec((share, lanes), lambda s, g: (s, 0))],
+        cost_estimate=pl.CostEstimate(
+            flops=6 * height * width, transcendentals=0, bytes_accessed=24 * height * width
+        ),
+    )(gathered.reshape(seqs * groups, share, 3 * lanes), w_query, w_key, w_value)
+
+
+class Layer:
+    def __init__(self, reps, tokens, prefix_len):
+        self.reps = reps
+        self.seqs, self.rows, self.width = tokens.shape
+        self.head_dim = self.width // HEADS
+        self.length = self.rows * reps
+        self.groups = reps // self.seqs
+        self.lanes = self.width // self.groups
+        self.total = self.seqs * self.rows
+        self.block = min(512, self.length)
+        here = lax.axis_index("rep")
+        self.my_seq = here // self.groups
+        positions = here * self.rows + jnp.arange(self.rows, dtype=jnp.int32)
+        cosine, sine = rope_lanes(positions, self.width, self.head_dim)
+        self.cosine = jnp.tile(cosine, (self.seqs, 1))
+        self.sine = jnp.tile(sine, (self.seqs, 1))
+        self.all_tables = rope_lanes(
+            jnp.arange(self.length, dtype=jnp.int32), self.lanes, self.head_dim
+        )
+        self.prefix = lax.dynamic_slice_in_dim(prefix_len, self.my_seq, 1, 0)
+
+    def to_heads(self, values, parts):
+        shape = (self.seqs, self.rows, parts, self.groups, self.lanes)
+        chunks = values.reshape(shape).transpose(0, 3, 1, 2, 4)
+        chunks = chunks.reshape(self.reps * self.rows, parts * self.lanes)
+        return lax.all_to_all(chunks, "rep", 0, 0, tiled=True)
+
+    def to_tokens(self, values, parts):
+        chunks = lax.all_to_all(values, "rep", 0, 0, tiled=True)
+        chunks = chunks.reshape(self.seqs, self.groups, self.rows, parts, self.lanes)
+        return chunks.transpose(0, 2, 3, 1, 4).reshape(self.total, parts * self.width)
+
+    def project(self, hidden, full_qkv, first_values):
+        width = self.width
+        raw = dot(hidden, full_qkv, (1, 0))
+
+        def rope(values):
+            return values * self.cosine - partner(values, self.head_dim, lane_roll) * self.sine
+
+        query_rot = (rope(raw[:, :width]) * 0.125).astype(BF16)
+        key_rot = rope(raw[:, width : 2 * width]).astype(BF16)
+        first = first_values.reshape(self.total, width).astype(F32)
+        value_mix = (0.5 * raw[:, 2 * width :] + 0.5 * first).astype(BF16)
+        return jnp.concatenate([query_rot, key_rot, value_mix], axis=1)
+
+    def attend(self, qkv):
+        return attend(self.prefix, qkv, self.head_dim, self.block, self.block)
+
+    def attend_back(self, qkv, do, att_t, mass):
+        return attend_back(
+            self.prefix, qkv, do, att_t, mass, *self.all_tables, self.head_dim, self.block, self.block
+        )
+
+    def sum_sequences(self, columns):
+        share = columns.shape[0] // self.seqs
+        mine = lax.dynamic_slice_in_dim(columns, self.my_seq * share, share, 0).astype(F32)
+        for turn in range(1, self.seqs):
+            slot = (self.my_seq + turn) % self.seqs
+            sent = lax.dynamic_slice_in_dim(columns, slot * share, share, 0)
+            moves = [
+                (s * self.groups + g, ((s + turn) % self.seqs) * self.groups + g)
+                for s in range(self.seqs)
+                for g in range(self.groups)
+            ]
+            mine = mine + lax.ppermute(sent, "rep", moves).astype(F32)
+        return mine.astype(BF16)
+
+
+def gain_gradient(gain, *pairs):
+    total = sum(jnp.sum(w.astype(F32) * gradient, axis=1) for w, gradient in pairs)
+    return total / gain.astype(F32)
+
+
+def gate_back(grad_swiglu, gate_pre, up_pre, sigma, swish):
+    grad_gate_pre = grad_swiglu * up_pre * sigma * (1.0 + gate_pre * (1.0 - sigma))
+    return (grad_gate_pre.astype(BF16), (grad_swiglu * swish).astype(BF16))
 
 
 def local(
     reps,
-    shards,
     tokens,
     first_values,
     prefix_len,
@@ -277,14 +501,9 @@
     gain_attn,
     gain_ffn,
 ):
-    seqs, rows, width = tokens.shape
-    head_dim = width // HEADS
-    length = rows * reps
-    groups = reps // seqs
-    lanes = width // groups
+    layer = Layer(reps, tokens, prefix_len)
+    total, width, ff = layer.total, layer.width, w_gate.shape[1]
     here = lax.axis_index("rep")
-    my_seq = here // groups
-    total = seqs * rows
 
     def gather(weights):
         height = weights[0].shape[0]
@@ -305,47 +524,18 @@
     gain1 = gains[0].astype(F32)
     gain2 = gains[1].astype(F32)
 
-    def to_heads(values, parts):
-        chunks = values.reshape(seqs, rows, parts, groups, lanes).transpose(0, 3, 1, 2, 4)
-        chunks = chunks.reshape(reps * rows, parts * lanes)
-        return lax.all_to_all(chunks, "rep", 0, 0, tiled=True)
-
-    def to_tokens(values, parts):
-        chunks = lax.all_to_all(values, "rep", 0, 0, tiled=True)
-        chunks = chunks.reshape(seqs, groups, rows, parts, lanes).transpose(0, 2, 3, 1, 4)
-        return chunks.reshape(total, parts * width)
-
-    local_pos = here * rows + jnp.arange(rows, dtype=jnp.int32)
-    cosine, sine = rope_lanes(local_pos, width, head_dim)
-    cosine = jnp.tile(cosine, (seqs, 1))
-    sine = jnp.tile(sine, (seqs, 1))
-    all_cosine, all_sine = rope_lanes(jnp.arange(length, dtype=jnp.int32), lanes, head_dim)
-    prefix = lax.dynamic_slice_in_dim(prefix_len, my_seq, 1, 0)
-
     inputs = tokens.reshape(total, width).astype(F32)
     normed1, scale1 = norm_rows(inputs)
     hidden1 = (normed1 * gain1).astype(BF16)
-    hidden1_all = lax.all_gather(hidden1.reshape(seqs, rows, width), "rep", axis=1, tiled=True)
-    raw = dot(hidden1, full_qkv, (1, 0))
-
-    def rope(values):
-        return values * cosine - partner(values, head_dim, lane_roll) * sine
-
-    query_rot = (rope(raw[:, :width]) * 0.125).astype(BF16)
-    key_rot = rope(raw[:, width : 2 * width]).astype(BF16)
-    first = first_values.reshape(total, width).astype(F32)
-    value_mix = (0.5 * raw[:, 2 * width :] + 0.5 * first).astype(BF16)
-    qkv = to_heads(jnp.concatenate([query_rot, key_rot, value_mix], axis=1), 3)
-    q, k, v = qkv[:, :lanes], qkv[:, lanes : 2 * lanes], qkv[:, 2 * lanes :]
-    block = min(512, length)
-    att, att_t, mass = attend(prefix, q, k, v, head_dim, block, block)
-    attended = to_tokens(att, 1)
+    hidden1_all = lax.all_gather(hidden1.reshape(tokens.shape), "rep", axis=1, tiled=True)
+    qkv = layer.to_heads(layer.project(hidden1, full_qkv, first_values), 3)
+    att, att_t, mass = layer.attend(qkv)
+    attended = layer.to_tokens(att, 1)
 
     residual = inputs + dot(attended, full_output, (1, 0))
     normed2, scale2 = norm_rows(residual)
     hidden2 = (normed2 * gain2).astype(BF16)
     gate_up = dot(hidden2, full_gate_up, (1, 0))
-    ff = gate_up.shape[1] // 2
     gate_pre, up_pre = gate_up[:, :ff], gate_up[:, ff:]
     sigma = jax.nn.sigmoid(gate_pre)
     swish = gate_pre * sigma
@@ -354,9 +544,7 @@
 
     upstream = cotangent.reshape(total, width)
     grad_swiglu = dot(upstream, full_down, (1, 1))
-    grad_gate_pre = (grad_swiglu * up_pre * sigma * (1.0 + gate_pre * (1.0 - sigma))).astype(BF16)
-    grad_up_pre = (grad_swiglu * swish).astype(BF16)
-    grad_gate_up = jnp.concatenate([grad_gate_pre, grad_up_pre], axis=1)
+    grad_gate_up = jnp.concatenate(gate_back(grad_swiglu, gate_pre, up_pre, sigma, swish), axis=1)
     grad_hidden2 = dot(grad_gate_up, full_gate_up, (1, 1))
     grad_residual = upstream.astype(F32) + norm_back(grad_hidden2 * gain2, normed2, scale2)
     grad_residual_low = grad_residual.astype(BF16)
@@ -370,47 +558,23 @@
     grad_down = reduce_gather(dot(swiglu, upstream, (0, 0)))
     grad_wgate_up = reduce_gather(dot(hidden2, grad_gate_up, (0, 0)))
     grad_outproj = reduce_gather(dot(attended, grad_residual_low, (0, 0)))
-
-    do = to_heads(grad_attended, 1)
-    dq, dk, dv = attend_back(
-        prefix, q, k, v, do, att_t, mass, all_cosine, all_sine, head_dim, block, block
-    )
-    grad_qkv_heads = jnp.concatenate([dq, dk, dv], axis=1)
-    half_value = jnp.where(jnp.arange(3 * lanes) < 2 * lanes, 1.0, 0.5).astype(BF16)
-    grad_raw_heads = grad_qkv_heads * half_value
-    grad_raw = to_tokens(grad_raw_heads, 3)
+    grad_wgate, grad_wup = grad_wgate_up[:, :ff], grad_wgate_up[:, ff:]
+
+    do = layer.to_heads(grad_attended, 1)
+    grad_raw_heads = layer.attend_back(qkv, do, att_t, mass)
+    grad_raw = layer.to_tokens(grad_raw_heads, 3)
     grad_first = grad_raw[:, 2 * width :].astype(F32)
     grad_hidden1 = dot(grad_raw, full_qkv, (1, 1))
     grad_inputs = grad_residual + norm_back(grad_hidden1 * gain1, normed1, scale1)
 
-    hidden_mine = lax.dynamic_index_in_dim(hidden1_all, my_seq, 0, keepdims=False)
-    columns = dot(hidden_mine, grad_raw_heads, (0, 0))
-    columns = lax.psum_scatter(columns.astype(BF16), "shard", scatter_dimension=0, tiled=True)
+    hidden_mine = lax.dynamic_index_in_dim(hidden1_all, layer.my_seq, 0, keepdims=False)
+    columns = dot(hidden_mine, grad_raw_heads, (0, 0)).astype(BF16)
+    columns = lax.psum_scatter(columns, "shard", scatter_dimension=0, tiled=True)
     height = columns.shape[0]
-    share = height // seqs
-    mine = lax.dynamic_slice_in_dim(columns, my_seq * share, share, 0).astype(F32)
-    for turn in range(1, seqs):
-        sent = lax.dynamic_slice_in_dim(columns, ((my_seq + turn) % seqs) * share, share, 0)
-        moves = [
-            (s * groups + g, ((s + turn) % seqs) * groups + g)
-            for s in range(seqs)
-            for g in range(groups)
-        ]
-        mine = mine + lax.ppermute(sent, "rep", moves).astype(F32)
-    gathered = lax.all_gather(mine.astype(BF16), "rep", axis=0, tiled=True)
-    gathered = gathered.reshape(seqs, groups, share, 3, lanes).transpose(3, 0, 2, 1, 4)
-    grad_wqkv = gathered.reshape(3, height, width).astype(F32)
-
-    grad_gain1 = (
-        jnp.sum(w_query.astype(F32) * grad_wqkv[0], axis=1)
-        + jnp.sum(w_key.astype(F32) * grad_wqkv[1], axis=1)
-        + jnp.sum(w_value.astype(F32) * grad_wqkv[2], axis=1)
-    ) / gain_attn.astype(F32)
-    grad_wgate, grad_wup = grad_wgate_up[:, :ff], grad_wgate_up[:, ff:]
-    grad_gain2 = (
-        jnp.sum(w_gate.astype(F32) * grad_wgate, axis=1)
-        + jnp.sum(w_up.astype(F32) * grad_wup, axis=1)
-    ) / gain_ffn.astype(F32)
+    mine = layer.sum_sequences(columns)
+    gathered = lax.all_gather(mine, "rep", axis=0, tiled=True)
+    gathered = gathered.reshape(layer.seqs, layer.groups, -1, 3, layer.lanes)
+    grad_wqkv = gathered.transpose(3, 0, 2, 1, 4).reshape(3, height, width).astype(F32)
     shape = tokens.shape
     return (
         output.reshape(shape),
@@ -423,8 +587,185 @@
         grad_wgate,
         grad_wup,
         grad_down,
-        grad_gain1,
-        grad_gain2,
+        gain_gradient(
+            gain_attn, (w_query, grad_wqkv[0]), (w_key, grad_wqkv[1]), (w_value, grad_wqkv[2])
+        ),
+        gain_gradient(gain_ffn, (w_gate, grad_wgate), (w_up, grad_wup)),
+    )
+
+
+def local_linked(
+    reps,
+    tokens,
+    first_values,
+    prefix_len,
+    cotangent,
+    w_query,
+    w_key,
+    w_value,
+    w_output,
+    w_gate,
+    w_up,
+    w_down,
+    gain_attn,
+    gain_ffn,
+):
+    layer = Layer(reps, tokens, prefix_len)
+    links = Links(reps)
+    total, width, ff = layer.total, layer.width, w_gate.shape[1]
+    core, x = links.core, links.x
+
+    own_gains = jnp.stack([gain_attn, gain_ffn])
+    other_gains = links.over_x(own_gains)
+    gains = jnp.where(
+        x == 0,
+        jnp.concatenate([own_gains, other_gains], axis=1),
+        jnp.concatenate([other_gains, own_gains], axis=1),
+    )
+    gain1 = gains[0].astype(F32)
+    gain2 = gains[1].astype(F32)
+
+    def half_rows(weights):
+        half = weights[0].shape[0] // 2
+        pieces = [lax.dynamic_slice_in_dim(w, core * half, half, 0) for w in weights]
+        return pieces[0] if len(pieces) == 1 else jnp.concatenate(pieces, axis=1)
+
+    def assemble(weights, near, far, at):
+        height = weights[0].shape[0]
+        half = near.shape[0]
+        columns = sum(w.shape[1] for w in weights)
+        full = blank((2 * height, columns), BF16)
+        place = 0
+        for w in weights:
+            full = lax.dynamic_update_slice(full, w, (x * height, place))
+            place += w.shape[1]
+        for part, owner in ((near, core), (far, 1 - core)):
+            part = lax.slice_in_dim(part, at, at + columns, axis=1)
+            full = lax.dynamic_update_slice(full, part, ((1 - x) * height + owner * half, 0))
+        return full
+
+    near_qkv = links.over_x(after(half_rows((w_query, w_key, w_value)), other_gains))
+    near_ff = links.over_x(after(half_rows((w_output, w_gate, w_up)), near_qkv))
+    near_down = links.over_x(after(half_rows((w_down,)), near_ff))
+    full_qkv = assemble((w_query, w_key, w_value), near_qkv, links.over_core(near_qkv), 0)
+
+    inputs = tokens.reshape(total, width).astype(F32)
+    normed1, scale1 = norm_rows(inputs)
+    hidden1 = (normed1 * gain1).astype(BF16)
+    hidden1_all = lax.all_gather(hidden1.reshape(tokens.shape), "rep", axis=1, tiled=True)
+    qkv = layer.to_heads(layer.project(hidden1, full_qkv, first_values), 3)
+    qkv, hidden1_all = fence(qkv, hidden1_all)
+    att, att_t, mass = layer.attend(qkv)
+    att, near_ff = fence(att, near_ff)
+    far_ff = links.over_core(near_ff)
+    full_output = assemble((w_output,), near_ff, far_ff, 0)
+    full_gate_up = assemble((w_gate, w_up), near_ff, far_ff, w_output.shape[1])
+    attended = layer.to_tokens(att, 1)
+
+    residual = inputs + dot(attended, full_output, (1, 0))
+    normed2, scale2 = norm_rows(residual)
+    hidden2 = (normed2 * gain2).astype(BF16)
+    gate_up = dot(hidden2, full_gate_up, (1, 0))
+    gate_pre, up_pre = gate_up[:, :ff], gate_up[:, ff:]
+    sigma = jax.nn.sigmoid(gate_pre)
+    swish = gate_pre * sigma
+    swiglu = (swish * up_pre).astype(BF16)
+    upstream = cotangent.reshape(total, width)
+
+    def by_core(values, blocks):
+        step = values.shape[1] // (2 * blocks)
+        sides = [
+            [values[:, (2 * b + side) * step : (2 * b + side + 1) * step] for b in range(blocks)]
+            for side in range(2)
+        ]
+        low, high = (s[0] if blocks == 1 else jnp.concatenate(s, axis=1) for s in sides)
+        return jnp.where(core == 0, low, high), jnp.where(core == 0, high, low)
+
+    upstream_mine, upstream_other = by_core(upstream, 1)
+    down_send = dot(swiglu, upstream_other, (0, 0)).astype(BF16)
+    swiglu, down_send, near_down = fence(swiglu, down_send, near_down)
+    full_down = assemble((w_down,), near_down, links.over_core(near_down), 0)
+    grad_swiglu = dot(upstream, full_down, (1, 1))
+    grad_gate_pre, grad_up_pre = gate_back(grad_swiglu, gate_pre, up_pre, sigma, swish)
+    down_total = add(dot(swiglu, upstream_mine, (0, 0)), links.over_core(down_send))
+    down_total, grad_gate_pre, grad_up_pre = fence(down_total, grad_gate_pre, grad_up_pre)
+
+    hidden2_mine, hidden2_other = by_core(hidden2, 2)
+    down_x = links.over_x(links.half(down_total, 1 - x))
+    gate_send = dot(hidden2_other, grad_gate_pre, (0, 0)).astype(BF16)
+    gate_total = add(dot(hidden2_mine, grad_gate_pre, (0, 0)), links.over_core(gate_send))
+    gate_total, grad_gate_pre, grad_up_pre = fence(gate_total, grad_gate_pre, grad_up_pre)
+    gate_y = links.over_y(links.quarters(gate_total, 1 - links.y))
+    grad_gate_up = jnp.concatenate([grad_gate_pre, grad_up_pre], axis=1)
+    up_send = dot(hidden2_other, grad_up_pre, (0, 0)).astype(BF16)
+    grad_hidden2 = dot(grad_gate_up, full_gate_up, (1, 1))
+    grad_residual = upstream.astype(F32) + norm_back(grad_hidden2 * gain2, normed2, scale2)
+    grad_residual_low = grad_residual.astype(BF16)
+    grad_attended = dot(grad_residual_low, full_output, (1, 1)).astype(BF16)
+    up_total = add(dot(hidden2_mine, grad_up_pre, (0, 0)), links.over_core(up_send))
+    attended_mine, attended_other = by_core(attended, 2)
+    out_send = dot(attended_other, grad_residual_low, (0, 0)).astype(BF16)
+    out_total = add(dot(attended_mine, grad_residual_low, (0, 0)), links.over_core(out_send))
+    down_first = add(links.half(down_total, x), down_x)
+    down_first, up_total, out_total, grad_attended = fence(
+        down_first, up_total, out_total, grad_attended
+    )
+
+    up_x = links.over_x(links.half(up_total, 1 - x))
+    down_y = links.over_y(links.half(down_first, 1 - links.y))
+    do = layer.to_heads(grad_attended, 1)
+    output = (residual + dot(swiglu, full_down, (1, 0))).astype(BF16)
+    gate_first = add(links.quarters(gate_total, links.y), gate_y)
+    down_second = add(links.half(down_first, links.y), down_y)
+    do, gate_first, down_second, output = fence(do, gate_first, down_second, output)
+
+    gate_x = links.over_x(links.half(gate_first, 1 - x))
+    out_y = links.over_y(links.quarters(out_total, 1 - links.y))
+    down_ring = links.ring_start(down_second)
+    grad_raw_heads = layer.attend_back(qkv, do, att_t, mass)
+    down_ring = links.ring_step(down_second, down_ring, 0)
+    up_first = add(links.half(up_total, x), up_x)
+    out_first = add(links.quarters(out_total, links.y), out_y)
+    gate_second = add(links.half(gate_first, x), gate_x)
+    grad_raw_heads, down_ring, up_first, out_first, gate_second = fence(
+        grad_raw_heads, down_ring, up_first, out_first, gate_second
+    )
+
+    grad_raw = layer.to_tokens(grad_raw_heads, 3)
+    hidden_mine = lax.dynamic_index_in_dim(hidden1_all, layer.my_seq, 0, keepdims=False)
+    columns = dot(hidden_mine, grad_raw_heads, (0, 0)).astype(BF16)
+    columns = add(links.half(columns, x), links.over_x(links.half(columns, 1 - x)))
+    gathered = lax.all_gather(layer.sum_sequences(columns), "rep", axis=0, tiled=True)
+    up_second = add(links.half(up_first, links.y), links.over_y(links.half(up_first, 1 - links.y)))
+    out_second = add(links.half(out_first, x), links.over_x(links.half(out_first, 1 - x)))
+    for step in range(1, links.deep - 1):
+        down_ring = links.ring_step(down_second, links.next_z(down_ring), step)
+    halves = links.collect(down_ring)
+    grad_down = jnp.concatenate([halves[0], halves[1]], axis=1).astype(F32)
+    grad_wgate = links.collect(links.along_z(gate_second)).reshape(-1, ff).astype(F32)
+    grad_wup = links.collect(links.along_z(up_second)).reshape(-1, ff).astype(F32)
+    grad_outproj = links.collect(links.along_z(out_second)).reshape(-1, width).astype(F32)
+
+    grad_first = grad_raw[:, 2 * width :].astype(F32)
+    grad_hidden1 = dot(grad_raw, full_qkv, (1, 1))
+    grad_inputs = grad_residual + norm_back(grad_hidden1 * gain1, normed1, scale1)
+    grad_wquery, grad_wkey, grad_wvalue, sums = spread(
+        gathered, w_query, w_key, w_value, layer.seqs, layer.groups
+    )
+    shape = tokens.shape
+    return (
+        output.reshape(shape),
+        grad_inputs.reshape(shape),
+        grad_first.reshape(shape),
+        grad_wquery,
+        grad_wkey,
+        grad_wvalue,
+        grad_outproj,
+        grad_wgate,
+        grad_wup,
+        grad_down,
+        jnp.sum(sums, axis=1) / gain_attn.astype(F32),
+        gain_gradient(gain_ffn, (w_gate, grad_wgate), (w_up, grad_wup)),
     )
 
 
@@ -432,8 +773,10 @@
     sequence = P("shard", "rep", None)
     matrix = P("shard", None)
     vector = P("shard")
+    reps, shards = mesh.shape["rep"], mesh.shape["shard"]
+    linked = reps == 16 and shards == 2
     return jax.shard_map(
-        functools.partial(local, mesh.shape["rep"], mesh.shape["shard"]),
+        functools.partial(local_linked if linked else local, reps),
         mesh=mesh,
         in_specs=(sequence, sequence, vector, sequence) + (matrix,) * 7 + (vector,) * 2,
         out_specs=(sequence,) * 3 + (matrix,) * 7 + (vector,) * 2,

time: 1090 us -> 598 us (0.55)
  waiting for transfers between devices: 807 us -> 218 us
  starting transfers between devices: 16.5 us -> 85.2 us
  local copies, waits for them, and re-layouts: 53.1 us -> 101 us
  blocking collectives: 35.8 us -> 0 us
    reduce_scatter x4 -> x0, waiting for transfers between devices: 424 us -> none  [the longest x3 408 us: reduce_gather(): lax.psum_scatter(partial.astype(BF16), axes, scatter_dimension=0, tiled=T...]
    all_gather x9 -> x2, waiting for transfers between devices: 297 us -> 0.01 us  [the longest x1 0.01 us: local_linked(): lax.all_gather(hidden1.reshape(tokens.shape), 'rep', axis=1, tiled=True)]
    ppermute x1 -> x53, waiting for transfers between devices: 9.59 us -> 169 us  [the longest x24 83.9 us: next_z(): return lax.ppermute(value, 'rep', self.to_z)]
    dynamic_update_slice x0 -> x43, local copies, waits for them, and re-layouts: none -> 57.1 us  [the longest x28 25 us: put(): return lax.dynamic_update_index_in_dim(values, part, index, 0)]
    ppermute x1 -> x53, starting transfers between devices: 2.45 us -> 59.5 us  [the longest x24 31.4 us: next_z(): return lax.ppermute(value, 'rep', self.to_z)]
    all_to_all x1 -> x0, blocking collectives: 30.5 us -> none  [to_tokens(): chunks = lax.all_to_all(values, 'rep', 0, 0, tiled=True)]
    all_to_all x1 -> x2, waiting for transfers between devices: 31.5 us -> 9.48 us  [to_tokens(): chunks = lax.all_to_all(values, 'rep', 0, 0, tiled=True)]
    convert_element_type x7 -> x25, other arithmetic: 11.9 us -> 26.2 us  [the longest x17 16 us: add(): return (left.astype(F32) + right.astype(F32)).astype(BF16)]
  transfers between devices with their start and end apart: 17 -> 59, of which waited for: 15 -> 23; matrix products, arithmetic and copies ran while one was open for 14% -> 33% of each run, Pallas kernels for 4% -> 7%
where the time goes in v3:
time: 598 us; the launch traced here: 588 us
  waiting for transfers between devices  218 us (36%)
  local copies, waits for them, and re-layouts  101 us (17%)
  starting transfers between devices  85.2 us (14%)
  matrix products  62 us (10%)
  other arithmetic  55.1 us (9%)
  Pallas kernels  50.6 us (8%)
  between operations  15.7 us (3%)
    ppermute x24, waiting for transfers between devices, next_z(): return lax.ppermute(value, 'rep', self.to_z)  83.9 us
    dot_general x17, matrix products, dot(): lax.dot_general(left, right, ((contract[:1], contract[1:]), ((), ())), pr...  62 us
    all_to_all x2, waiting for transfers between devices, to_heads(): return lax.all_to_all(chunks, 'rep', 0, 0, tiled=True)  39.8 us
    ppermute x8, waiting for transfers between devices, over_y(): return lax.ppermute(value, 'rep', self.to_y)  38.6 us
    ppermute x9, waiting for transfers between devices, over_x(): return lax.ppermute(value, 'shard', [(0, 1), (1, 0)])  37.5 us
    ppermute x24, starting transfers between devices, next_z(): return lax.ppermute(value, 'rep', self.to_z)  31.4 us
    dynamic_update_slice x28, local copies, waits for them, and re-layouts, put(): return lax.dynamic_update_index_in_dim(values, part, index, 0)  25 us
    pallas_call x1, Pallas kernels, attend_back(): pl.pallas_call(functools.partial(attend_back_kernel, head_dim, bq, bk), o...  22.7 us
  transfers between devices with their start and end apart: 59, of which 23 were waited for; matrix products, arithmetic and copies ran while one was open for 33% of the time, Pallas kernels for 7%

profile of v3, /device:TPU:0, one launch (start us, length us, event | category | flops | bytes accessed | tf_op | source)
XLA Modules:
  0.0 587.8 jit_solution(17683780275112045370)
XLA Ops:
  8.8 3.0 collective-permute-start
  29.8 24.0 %collective-permute-done.1 = bf16[256,3072]{1,0:T(8,128)(2,1)} collective-permute-done((bf16[256,3072]{1,0:T(8,128)(2,1)}, bf16[256,3072]{1,0:T(8,128)(2,1)}, u32[]{:S(2)}, u32[]{:S(2)}) %collective-permute-start.1) | collective-permute-done | bytes 1572896 | tf_op jit(solution)/shard_map/ppermute | solution.py:226
  68.2 2.8 copy.36
  71.1 6.1 %all-to-all-start = ((bf16[16,128,384]{1,2,0:T(8,128)(2,1)}), bf16[16,128,384]{1,2,0:T(8,128)(2,1)}, u32[]{:S(2)}, u32[]{:S(2)}) async-start(bf16[16,128,384]{1,2,0:T(8,128)(2,1)} %bitcast.312), calls=%async_computation | async-start | bytes 3145728 | tf_op jit(solution)/shard_map/all_to_all | solution.py:435
  77.8 39.8 %all-to-all-done = bf16[16,128,384]{1,2,0:T(8,128)(2,1)} async-done(((bf16[16,128,384]{1,2,0:T(8,128)(2,1)}), bf16[16,128,384]{1,2,0:T(8,128)(2,1)}, u32[]{:S(2)}, u32[]{:S(2)}) %all-to-all-start) | async-done | bytes 1572896 | tf_op jit(solution)/shard_map/all_to_all | solution.py:435
  120.2 16.6 %shard_map.221 = (bf16[2048,128]{1,0:T(8,128)(2,1)}, f32[128,2048]{1,0:T(8,128)}, f32[2,2048]{1,0:T(2,128)}) custom-call(s32[1]{0:T(128)} %dynamic_slice.147.prefix_ref, bf16[2048,384]{1,0:T(8,128)(2,1)} %bitcast.352, bf16[2048,384]{1,0:T(8,128)(2,1)} %bitcast.353, bf16[2048,384]{1,0:T(8,128)(2,1)} %bitcast.354), custom_call_target="tpu_custom_call" | custom-call | flops 2147483648 | bytes 2097152 | tf_op jit(solution)/shard_map/pallas_call | solution.py:321
  149.1 9.6 %all-to-all-start.1 = ((bf16[16,128,128]{2,1,0:T(8,128)(2,1)}), bf16[16,128,128]{2,1,0:T(8,128)(2,1)S(1)}, u32[]{:S(2)}, u32[]{:S(2)}) async-start(bf16[16,128,128]{2,1,0:T(8,128)(2,1)} %bitcast.369), calls=%async_computation.1 | async-start | bytes 1048576 | tf_op jit(solution)/shard_map/all_to_all | solution.py:438
  159.8 3.7 slice_dynamic-update-slice_fusion.1
  163.5 9.5 %all-to-all-done.1 = bf16[16,128,128]{2,1,0:T(8,128)(2,1)S(1)} async-done(((bf16[16,128,128]{2,1,0:T(8,128)(2,1)}), bf16[16,128,128]{2,1,0:T(8,128)(2,1)S(1)}, u32[]{:S(2)}, u32[]{:S(2)}) %all-to-all-start.1) | async-done | bytes 524320 | tf_op jit(solution)/shard_map/all_to_all | solution.py:438
  176.6 3.7 slice_dynamic-update-slice_fusion
  180.3 6.0 %fusion.92 = f32[256,5632]{1,0:T(8,128)S(1)} fusion(bf16[256,1024]{1,0:T(8,128)(2,1)S(1)} %multiply_convert_fusion.3, bf16[1024,5632]{1,0:T(8,128)(2,1)} %slice_dynamic-update-slice_fusion), kind=kOutput, calls=%fused_computation.253 | convolution fusion | flops 2952790016 | bytes 17825792 | tf_op jit(solution)/shard_map/dot_general | solution.py:20
  191.9 3.7 constant_dynamic-update-slice_fusion.2
  201.6 7.8 %multiply_convert_fusion = (bf16[256,2816]{1,0:T(8,128)(2,1)}, bf16[256,2816]{1,0:T(8,128)(2,1)S(1)}) fusion(f32[256,5632]{1,0:T(8,128)} %copy-done.2, bf16[2816,1024]{1,0:T(8,128)(2,1)} %constant_dynamic-update-slice_fusion, bf16[256,1024]{1,0:T(8,128)(2,1)S(1)} %bitcast.339), kind=kOutput, calls=%fused_computation.27 | convolution fusion | flops 1485766656 | bytes 14942208 | tf_op jit(solution)/shard_map/dot_general | solution.py:20
  209.4 4.8 add_convert_fusion.2
  217.1 5.7 fusion.21
  224.8 5.2 fusion.20
  232.6 4.6 add_convert_fusion.1
  239.9 6.3 %multiply_reduce_fusion.3 = (f32[256]{0:T(256)S(1)}, f32[256,1024]{1,0:T(8,128)}) fusion(f32[256,1024]{1,0:T(8,128)} %copy-done.33, f32[256]{0:T(256)S(1)} %add_rsqrt_fusion, f32[1024]{0:T(1024)S(1)} %bitcast.375, bf16[1024,5632]{1,0:T(8,128)(2,1)S(1)} %bitcast.304, bf16[256,2816]{1,0:T(8,128)(2,1)} %get-tuple-element.61, bf16[256,2816]{1,0:T(8,128)(2,1)} %copy-done.30), kind=kOutput, calls=%fused_computation.84 | convolution fusion | flops 2959605504 | bytes 16521216 | tf_op jit(solution)/shard_map/dot_general | solution.py:20
  252.3 13.2 %collective-permute-done.8 = bf16[1408,512]{1,0:T(8,128)(2,1)} collective-permute-done((bf16[1408,512]{1,0:T(8,128)(2,1)}, bf16[1408,512]{1,0:T(8,128)(2,1)}, u32[]{:S(2)}, u32[]{:S(2)}) %collective-permute-start.8) | collective-permute-done | bytes 1441824 | tf_op jit(solution)/shard_map/ppermute | solution.py:226
  269.6 4.4 add_convert_fusion
  274.9 4.2 all-to-all-start.2
  282.8 5.1 collective-permute-done.12
  287.9 2.8 fusion.8
  292.6 24.6 %collective-permute-done.16 = bf16[256,1024]{1,0:T(8,128)(2,1)S(1)} collective-permute-done((bf16[256,1024]{1,0:T(8,128)(2,1)S(1)}, bf16[256,1024]{1,0:T(8,128)(2,1)S(1)}, u32[]{:S(2)}, u32[]{:S(2)}) %collective-permute-start.16) | collective-permute-done | bytes 524320 | tf_op jit(solution)/shard_map/ppermute | solution.py:229
  325.0 22.7 %shard_map.225 = bf16[2048,384]{1,0:T(8,128)(2,1)} custom-call(s32[1]{0:T(128)} %dynamic_slice.147.prefix_ref, bf16[2048,384]{1,0:T(8,128)(2,1)} %bitcast.355, bf16[2048,384]{1,0:T(8,128)(2,1)} %bitcast.356, bf16[2048,384]{1,0:T(8,128)(2,1)} %bitcast.357, bf16[2048,128]{1,0:T(8,128)(2,1)} %bitcast.368, f32[128,2048]{1,0:T(8,128)} %get-tuple-element.68.att_t_ref, ...), custom_call_target="tpu_custom_call" | custom-call | flops 5368709120 | bytes 5767168 | tf_op jit(solution)/shard_map/pallas_call | solution.py:348
  349.4 3.3 fusion.7
  356.6 5.7 all-to-all-start.3
  362.4 5.2 fusion.14
  375.7 21.6 %collective-permute-done.29 = bf16[32,2816]{1,0:T(8,128)(2,1)S(1)} collective-permute-done((bf16[32,2816]{1,0:T(8,128)(2,1)S(1)}, bf16[32,2816]{1,0:T(8,128)(2,1)S(1)}, u32[]{:S(2)}, u32[]{:S(2)}) %collective-permute-start.29) | collective-permute-done | bytes 180256 | tf_op jit(solution)/shard_map/ppermute | solution.py:232
  397.3 6.0 %collective-permute-start.30 = (bf16[32,2816]{1,0:T(8,128)(2,1)S(1)}, bf16[32,2816]{1,0:T(8,128)(2,1)S(1)}, u32[]{:S(2)}, u32[]{:S(2)}) collective-permute-start(bf16[32,2816]{1,0:T(8,128)(2,1)S(1)} %fusion.38), channel_id=1, source_target_pairs={{0,8},{2,10},{4,12},{6,14},{8,16},{10,18},{12,20},{14,22},{16,24},... | collective-permute-start | bytes 540680 | tf_op jit(solution)/shard_map/ppermute | solution.py:232
  407.2 3.1 collective-permute-done.21
  419.6 5.9 %collective-permute-done.23 = bf16[32,1024]{1,0:T(8,128)(2,1)S(1)} collective-permute-done((bf16[32,1024]{1,0:T(8,128)(2,1)S(1)}, bf16[32,1024]{1,0:T(8,128)(2,1)S(1)}, u32[]{:S(2)}, u32[]{:S(2)}) %collective-permute-start.23) | collective-permute-done | bytes 65568 | tf_op jit(solution)/shard_map/ppermute | solution.py:232
  428.3 4.2 collective-permute-done.24
  435.7 2.8 collective-permute-start.32
  440.9 8.1 %collective-permute-done.19 = bf16[256,384]{1,0:T(8,128)(2,1)S(1)} collective-permute-done((bf16[256,384]{1,0:T(8,128)(2,1)S(1)}, bf16[256,384]{1,0:T(8,128)(2,1)S(1)}, u32[]{:S(2)}, u32[]{:S(2)}) %collective-permute-start.19) | collective-permute-done | bytes 196640 | tf_op jit(solution)/shard_map/ppermute | solution.py:474
  458.7 11.9 %collective-permute-done.50 = bf16[176,512]{1,0:T(8,128)(2,1)S(1)} collective-permute-done((bf16[176,512]{1,0:T(8,128)(2,1)}, bf16[176,512]{1,0:T(8,128)(2,1)S(1)}, u32[]{:S(2)}, u32[]{:S(2)}) %collective-permute-start.50) | collective-permute-done | bytes 180256 | tf_op jit(solution)/shard_map/ppermute | solution.py:232
  475.6 3.1 collective-permute-done.34
  480.6 3.3 collective-permute-done.39
  485.0 10.0 %collective-permute-done.40 = bf16[32,2816]{1,0:T(8,128)(2,1)S(1)} collective-permute-done((bf16[32,2816]{1,0:T(8,128)(2,1)S(1)}, bf16[32,2816]{1,0:T(8,128)(2,1)S(1)}, u32[]{:S(2)}, u32[]{:S(2)}) %collective-permute-start.40) | collective-permute-done | bytes 180256 | tf_op jit(solution)/shard_map/ppermute | solution.py:232
  496.8 7.6 %collective-permute-done.41 = bf16[32,2816]{1,0:T(8,128)(2,1)S(1)} collective-permute-done((bf16[32,2816]{1,0:T(8,128)(2,1)S(1)}, bf16[32,2816]{1,0:T(8,128)(2,1)S(1)}, u32[]{:S(2)}, u32[]{:S(2)}) %collective-permute-start.41) | collective-permute-done | bytes 180256 | tf_op jit(solution)/shard_map/ppermute | solution.py:232
  507.1 4.6 collective-permute-done.42
  512.7 6.4 %collective-permute-done.43 = bf16[32,2816]{1,0:T(8,128)(2,1)S(1)} collective-permute-done((bf16[32,2816]{1,0:T(8,128)(2,1)S(1)}, bf16[32,2816]{1,0:T(8,128)(2,1)S(1)}, u32[]{:S(2)}, u32[]{:S(2)}) %collective-permute-start.43) | collective-permute-done | bytes 180256 | tf_op jit(solution)/shard_map/ppermute | solution.py:232
  523.5 8.9 %collective-permute-done.44 = bf16[128,2816]{1,0:T(8,128)(2,1)S(1)} collective-permute-done((bf16[128,2816]{1,0:T(8,128)(2,1)S(1)}, bf16[128,2816]{1,0:T(8,128)(2,1)S(1)}, u32[]{:S(2)}, u32[]{:S(2)}) %collective-permute-start.44) | collective-permute-done | bytes 720928 | tf_op jit(solution)/shard_map/ppermute | solution.py:229
  541.5 4.7 multiply_reduce_fusion.2
  550.1 3.3 maximum_convert_fusion
  555.7 3.3 multiply_reduce_fusion.1
  561.8 5.1 multiply_reduce_fusion
  567.5 11.3 %shard_map.226 = (f32[512,1024]{1,0:T(8,128)}, f32[512,1024]{1,0:T(8,128)}, f32[512,1024]{1,0:T(8,128)}, f32[512,128]{1,0:T(8,128)}) custom-call(bf16[16,256,384]{2,1,0:T(8,128)(2,1)} %bitcast.321, bf16[512,1024]{1,0:T(8,128)(2,1)} %wq_ref.1, bf16[512,1024]{1,0:T(8,128)(2,1)} %wk_ref.1, bf16[512,1024]{1,0:T(8,128)(2,1)} %wv_ref.1), custom_call_target="tpu_custom_call" | custom-call | flops 3145728 | bytes 12582912 | tf_op jit(solution)/shard_map/pallas_call | solution.py:392
  (368 shorter events, 182.7 us)
Async XLA Ops:
  7.2 113.0 %all-gather.3.cloned.1.call-start = ((), (), s32[]{:S(2)}) async-start(), calls=%async_computation.4 | async-start | bytes 8912896 | tf_op jit(solution)/shard_map/all_gather | solution.py:655
  17.9 35.9 %collective-permute-start.1 = (bf16[256,3072]{1,0:T(8,128)(2,1)}, bf16[256,3072]{1,0:T(8,128)(2,1)}, u32[]{:S(2)}, u32[]{:S(2)}) collective-permute-start(bf16[256,3072]{1,0:T(8,128)(2,1)} %pad_maximum_fusion.1), channel_id=1, source_target_pairs={{0,1},{1,0},{2,3},{3,2},{4,5},{5,4},{6,7},{7,6},{8,9},{9,8},{10,11... | collective-permute-start | bytes 4718600 | tf_op jit(solution)/shard_map/ppermute | solution.py:226
  55.9 80.9 %collective-permute-start.3 = (bf16[256,6656]{1,0:T(8,128)(2,1)}, bf16[256,6656]{1,0:T(8,128)(2,1)}, u32[]{:S(2)}, u32[]{:S(2)}) collective-permute-start(bf16[256,6656]{1,0:T(8,128)(2,1)} %pad_maximum_fusion), channel_id=1, source_target_pairs={{0,1},{1,0},{2,3},{3,2},{4,5},{5,4},{6,7},{7,6},{8,9},{9,8},{10,11... | collective-permute-start | bytes 10223624 | tf_op jit(solution)/shard_map/ppermute | solution.py:226
  71.1 46.5 %all-to-all-start = ((bf16[16,128,384]{1,2,0:T(8,128)(2,1)}), bf16[16,128,384]{1,2,0:T(8,128)(2,1)}, u32[]{:S(2)}, u32[]{:S(2)}) async-start(bf16[16,128,384]{1,2,0:T(8,128)(2,1)} %bitcast.312), calls=%async_computation | async-start | bytes 3145728 | tf_op jit(solution)/shard_map/all_to_all | solution.py:435
  136.8 36.6 %collective-permute-start.4 = (bf16[256,6656]{1,0:T(8,128)(2,1)}, bf16[256,6656]{1,0:T(8,128)(2,1)}, u32[]{:S(2)}, u32[]{:S(2)}) collective-permute-start(bf16[256,6656]{1,0:T(8,128)(2,1)} %collective-permute-done.3), channel_id=1, source_target_pairs={{0,2},{2,0},{4,6},{6,4},{8,10},{10,8},{12,14},{14,12},{16,18},{18,... | collective-permute-start | bytes 10223624 | tf_op jit(solution)/shard_map/ppermute | solution.py:223
  146.4 45.0 %collective-permute-start.5 = (bf16[704,1024]{1,0:T(8,128)(2,1)}, bf16[704,1024]{1,0:T(8,128)(2,1)}, u32[]{:S(2)}, u32[]{:S(2)}) collective-permute-start(bf16[704,1024]{1,0:T(8,128)(2,1)} %constant_dynamic-slice_fusion.5), channel_id=1, source_target_pairs={{0,1},{1,0},{2,3},{3,2},{4,5},{5,4},{6,7},{7,6},{8,9},{9,8},{10,11... | collective-permute-start | bytes 4325384 | tf_op jit(solution)/shard_map/ppermute | solution.py:226
  149.1 23.9 %all-to-all-start.1 = ((bf16[16,128,128]{2,1,0:T(8,128)(2,1)}), bf16[16,128,128]{2,1,0:T(8,128)(2,1)S(1)}, u32[]{:S(2)}, u32[]{:S(2)}) async-start(bf16[16,128,128]{2,1,0:T(8,128)(2,1)} %bitcast.369), calls=%async_computation.1 | async-start | bytes 1048576 | tf_op jit(solution)/shard_map/all_to_all | solution.py:438
  191.3 18.1 %collective-permute-start.6 = (bf16[2816,512]{1,0:T(8,128)(2,1)}, bf16[2816,512]{1,0:T(8,128)(2,1)}, u32[]{:S(2)}, u32[]{:S(2)}) collective-permute-start(bf16[2816,512]{1,0:T(8,128)(2,1)} %convolution_convert_fusion.2), channel_id=1, source_target_pairs={{0,2},{2,0},{4,6},{6,4},{8,10},{10,8},{12,14},{14,12},{16,18},{18,... | collective-permute-start | bytes 8650760 | tf_op jit(solution)/shard_map/ppermute | solution.py:223
  216.8 15.8 %collective-permute-start.9 = (bf16[512,2816]{1,0:T(8,128)(2,1)}, bf16[512,2816]{1,0:T(8,128)(2,1)}, u32[]{:S(2)}, u32[]{:S(2)}) collective-permute-start(bf16[512,2816]{1,0:T(8,128)(2,1)} %convolution_convert_fusion.1), channel_id=1, source_target_pairs={{0,2},{2,0},{4,6},{6,4},{8,10},{10,8},{12,14},{14,12},{16,18},{18,... | collective-permute-start | bytes 8650760 | tf_op jit(solution)/shard_map/ppermute | solution.py:223
  231.3 34.2 %collective-permute-start.8 = (bf16[1408,512]{1,0:T(8,128)(2,1)}, bf16[1408,512]{1,0:T(8,128)(2,1)}, u32[]{:S(2)}, u32[]{:S(2)}) collective-permute-start(bf16[1408,512]{1,0:T(8,128)(2,1)} %dynamic-slice_bitcast_fusion.1), channel_id=1, source_target_pairs={{0,1},{1,0},{2,3},{3,2},{4,5},{5,4},{6,7},{7,6},{8,9},{9,8},{10,11... | collective-permute-start | bytes 4325384 | tf_op jit(solution)/shard_map/ppermute | solution.py:226
  239.7 29.9 %collective-permute-start.10 = (bf16[512,2816]{1,0:T(8,128)(2,1)}, bf16[512,2816]{1,0:T(8,128)(2,1)}, u32[]{:S(2)}, u32[]{:S(2)}) collective-permute-start(bf16[512,2816]{1,0:T(8,128)(2,1)} %convolution_convert_fusion), channel_id=1, source_target_pairs={{0,2},{2,0},{4,6},{6,4},{8,10},{10,8},{12,14},{14,12},{16,18},{18,... | collective-permute-start | bytes 8650760 | tf_op jit(solution)/shard_map/ppermute | solution.py:223
  248.9 19.2 %collective-permute-start.11 = (bf16[512,1024]{1,0:T(8,128)(2,1)S(1)}, bf16[512,1024]{1,0:T(8,128)(2,1)S(1)}, u32[]{:S(2)}, u32[]{:S(2)}) collective-permute-start(bf16[512,1024]{1,0:T(8,128)(2,1)S(1)} %convolution_convert_fusion.3), channel_id=1, source_target_pairs={{0,2},{2,0},{4,6},{6,4},{8,10},{10,8},{12,14},{14,12},{16,18},{18,... | collective-permute-start | bytes 3145736 | tf_op jit(solution)/shard_map/ppermute | solution.py:223
  251.0 36.9 %collective-permute-start.12 = (bf16[256,2816]{1,0:T(8,128)(2,1)}, bf16[256,2816]{1,0:T(8,128)(2,1)}, u32[]{:S(2)}, u32[]{:S(2)}) collective-permute-start(bf16[256,2816]{1,0:T(8,128)(2,1)} %bitcast.23), channel_id=1, source_target_pairs={{0,4},{2,6},{4,0},{6,2},{8,12},{10,14},{12,8},{14,10},{16,20},{18,... | collective-permute-start | bytes 4325384 | tf_op jit(solution)/shard_map/ppermute | solution.py:229
  274.9 44.4 %all-to-all-start.2 = ((bf16[16,128,128]{2,1,0:T(8,128)(2,1)}), bf16[16,128,128]{2,1,0:T(8,128)(2,1)S(1)}, u32[]{:S(2)}, u32[]{:S(2)}) async-start(bf16[16,128,128]{2,1,0:T(8,128)(2,1)} %bitcast.19), calls=%async_computation.2 | async-start | bytes 1048576 | tf_op jit(solution)/shard_map/all_to_all | solution.py:435
  279.2 39.1 %collective-permute-start.13 = (bf16[704,512]{1,0:T(8,128)(2,1)S(1)}, bf16[704,512]{1,0:T(8,128)(2,1)S(1)}, u32[]{:S(2)}, u32[]{:S(2)}) collective-permute-start(bf16[704,512]{1,0:T(8,128)(2,1)S(1)} %dynamic-slice_bitcast_fusion.4), channel_id=1, source_target_pairs={{0,4},{2,6},{4,0},{6,2},{8,12},{10,14},{12,8},{14,10},{16,20},{18,... | collective-permute-start | bytes 2162696 | tf_op jit(solution)/shard_map/ppermute | solution.py:229
  282.6 34.6 %collective-permute-start.16 = (bf16[256,1024]{1,0:T(8,128)(2,1)S(1)}, bf16[256,1024]{1,0:T(8,128)(2,1)S(1)}, u32[]{:S(2)}, u32[]{:S(2)}) collective-permute-start(bf16[256,1024]{1,0:T(8,128)(2,1)S(1)} %bitcast.370), channel_id=1, source_target_pairs={{0,4},{2,6},{4,0},{6,2},{8,12},{10,14},{12,8},{14,10},{16,20},{18,... | collective-permute-start | bytes 1572872 | tf_op jit(solution)/shard_map/ppermute | solution.py:229
  291.9 57.6 %collective-permute-start.15 = (bf16[256,2816]{1,0:T(8,128)(2,1)}, bf16[256,2816]{1,0:T(8,128)(2,1)}, u32[]{:S(2)}, u32[]{:S(2)}) collective-permute-start(bf16[256,2816]{1,0:T(8,128)(2,1)} %dynamic-slice_bitcast_fusion), channel_id=1, source_target_pairs={{0,1},{1,0},{2,3},{3,2},{4,5},{5,4},{6,7},{7,6},{8,9},{9,8},{10,11... | collective-permute-start | bytes 4325384 | tf_op jit(solution)/shard_map/ppermute | solution.py:226
  320.4 27.3 %collective-permute-start.14 = (bf16[176,512]{1,0:T(8,128)(2,1)S(1)}, bf16[176,512]{1,0:T(8,128)(2,1)S(1)}, u32[]{:S(2)}, u32[]{:S(2)}) collective-permute-start(bf16[176,512]{1,0:T(8,128)(2,1)S(1)} %dynamic-slice_bitcast_fusion.9), channel_id=1, source_target_pairs={{0,8},{2,10},{4,12},{6,14},{8,16},{10,18},{12,20},{14,22},{16,24},... | collective-permute-start | bytes 540680 | tf_op jit(solution)/shard_map/ppermute | solution.py:232
  324.2 28.6 %collective-permute-start.17 = (bf16[128,2816]{1,0:T(8,128)(2,1)}, bf16[128,2816]{1,0:T(8,128)(2,1)}, u32[]{:S(2)}, u32[]{:S(2)}) collective-permute-start(bf16[128,2816]{1,0:T(8,128)(2,1)} %dynamic-slice_bitcast_fusion.3), channel_id=1, source_target_pairs={{0,1},{1,0},{2,3},{3,2},{4,5},{5,4},{6,7},{7,6},{8,9},{9,8},{10,11... | collective-permute-start | bytes 2162696 | tf_op jit(solution)/shard_map/ppermute | solution.py:226
  356.6 179.3 %all-to-all-start.3 = ((bf16[16,128,384]{1,2,0:T(8,128)(2,1)}), bf16[16,128,384]{1,2,0:T(8,128)(2,1)S(1)}, u32[]{:S(2)}, u32[]{:S(2)}) async-start(bf16[16,128,384]{1,2,0:T(8,128)(2,1)} %copy.41), calls=%async_computation.3 | async-start | bytes 3145728 | tf_op jit(solution)/shard_map/all_to_all | solution.py:438
  362.3 205.2 %all-gather.5.cloned.1.call-start = ((), (), s32[]{:S(2)}) async-start(), calls=%async_computation.5 | async-start | bytes 3342336 | tf_op jit(solution)/shard_map/all_gather | solution.py:738
  367.6 51.8 %collective-permute-start.18 = (bf16[512,384]{1,0:T(8,128)(2,1)S(1)}, bf16[512,384]{1,0:T(8,128)(2,1)S(1)}, u32[]{:S(2)}, u32[]{:S(2)}) collective-permute-start(bf16[512,384]{1,0:T(8,128)(2,1)S(1)} %dynamic-slice_bitcast_fusion.5), channel_id=1, source_target_pairs={{0,1},{1,0},{2,3},{3,2},{4,5},{5,4},{6,7},{7,6},{8,9},{9,8},{10,11... | collective-permute-start | bytes 1179656 | tf_op jit(solution)/shard_map/ppermute | solution.py:226
  368.5 34.8 %collective-permute-start.20 = (bf16[128,1024]{1,0:T(8,128)(2,1)S(1)}, bf16[128,1024]{1,0:T(8,128)(2,1)S(1)}, u32[]{:S(2)}, u32[]{:S(2)}) collective-permute-start(bf16[128,1024]{1,0:T(8,128)(2,1)S(1)} %dynamic-slice_bitcast_fusion.6), channel_id=1, source_target_pairs={{0,1},{1,0},{2,3},{3,2},{4,5},{5,4},{6,7},{7,6},{8,9},{9,8},{10,11... | collective-permute-start | bytes 786440 | tf_op jit(solution)/shard_map/ppermute | solution.py:226
  369.8 27.4 %collective-permute-start.29 = (bf16[32,2816]{1,0:T(8,128)(2,1)S(1)}, bf16[32,2816]{1,0:T(8,128)(2,1)S(1)}, u32[]{:S(2)}, u32[]{:S(2)}) collective-permute-start(bf16[32,2816]{1,0:T(8,128)(2,1)S(1)} %dynamic-slice_bitcast_fusion.8), channel_id=1, source_target_pairs={{0,8},{2,10},{4,12},{6,14},{8,16},{10,18},{12,20},{14,22},{16,24},... | collective-permute-start | bytes 540680 | tf_op jit(solution)/shard_map/ppermute | solution.py:232
  372.7 84.1 %collective-permute-start.37 = (bf16[128,2816]{1,0:T(8,128)(2,1)}, bf16[128,2816]{1,0:T(8,128)(2,1)}, u32[]{:S(2)}, u32[]{:S(2)}) collective-permute-start(bf16[128,2816]{1,0:T(8,128)(2,1)} %dynamic-slice_bitcast_fusion.2), channel_id=1, source_target_pairs={{0,4},{2,6},{4,0},{6,2},{8,12},{10,14},{12,8},{14,10},{16,20},{18,... | collective-permute-start | bytes 2162696 | tf_op jit(solution)/shard_map/ppermute | solution.py:229
  374.2 31.7 %collective-permute-start.46 = (bf16[176,512]{1,0:T(8,128)(2,1)S(1)}, bf16[176,512]{1,0:T(8,128)(2,1)S(1)}, u32[]{:S(2)}, u32[]{:S(2)}) collective-permute-start(bf16[176,512]{1,0:T(8,128)(2,1)S(1)} %copy-done.54), channel_id=1, source_target_pairs={{0,8},{2,10},{4,12},{6,14},{8,16},{10,18},{12,20},{14,22},{16,24},... | collective-permute-start | bytes 540680 | tf_op jit(solution)/shard_map/ppermute | solution.py:232
  397.3 15.1 %collective-permute-start.30 = (bf16[32,2816]{1,0:T(8,128)(2,1)S(1)}, bf16[32,2816]{1,0:T(8,128)(2,1)S(1)}, u32[]{:S(2)}, u32[]{:S(2)}) collective-permute-start(bf16[32,2816]{1,0:T(8,128)(2,1)S(1)} %fusion.38), channel_id=1, source_target_pairs={{0,8},{2,10},{4,12},{6,14},{8,16},{10,18},{12,20},{14,22},{16,24},... | collective-permute-start | bytes 540680 | tf_op jit(solution)/shard_map/ppermute | solution.py:232
  406.0 9.0 %collective-permute-start.47 = (bf16[176,512]{1,0:T(8,128)(2,1)S(1)}, bf16[176,512]{1,0:T(8,128)(2,1)S(1)}, u32[]{:S(2)}, u32[]{:S(2)}) collective-permute-start(bf16[176,512]{1,0:T(8,128)(2,1)S(1)} %fusion.33), channel_id=1, source_target_pairs={{0,8},{2,10},{4,12},{6,14},{8,16},{10,18},{12,20},{14,22},{16,24},... | collective-permute-start | bytes 540680 | tf_op jit(solution)/shard_map/ppermute | solution.py:232
  412.4 22.4 %collective-permute-start.31 = (bf16[32,2816]{1,0:T(8,128)(2,1)S(1)}, bf16[32,2816]{1,0:T(8,128)(2,1)S(1)}, u32[]{:S(2)}, u32[]{:S(2)}) collective-permute-start(bf16[32,2816]{1,0:T(8,128)(2,1)S(1)} %fusion.39), channel_id=1, source_target_pairs={{0,8},{2,10},{4,12},{6,14},{8,16},{10,18},{12,20},{14,22},{16,24},... | collective-permute-start | bytes 540680 | tf_op jit(solution)/shard_map/ppermute | solution.py:232
  415.7 22.8 %collective-permute-start.48 = (bf16[176,512]{1,0:T(8,128)(2,1)S(1)}, bf16[176,512]{1,0:T(8,128)(2,1)}, u32[]{:S(2)}, u32[]{:S(2)}) collective-permute-start(bf16[176,512]{1,0:T(8,128)(2,1)S(1)} %get-tuple-element.89), channel_id=1, source_target_pairs={{0,8},{2,10},{4,12},{6,14},{8,16},{10,18},{12,20},{14,22},{16,24},... | collective-permute-start | bytes 540680 | tf_op jit(solution)/shard_map/ppermute | solution.py:232
  426.2 22.7 %collective-permute-start.19 = (bf16[256,384]{1,0:T(8,128)(2,1)S(1)}, bf16[256,384]{1,0:T(8,128)(2,1)S(1)}, u32[]{:S(2)}, u32[]{:S(2)}) collective-permute-start(bf16[256,384]{1,0:T(8,128)(2,1)S(1)} %constant_dynamic-slice_fusion), channel_id=1, source_target_pairs={{0,16},{2,18},{4,20},{6,22},{8,24},{10,26},{12,28},{14,30},{16,0},... | collective-permute-start | bytes 589832 | tf_op jit(solution)/shard_map/ppermute | solution.py:474
  435.7 16.3 %collective-permute-start.32 = (bf16[32,2816]{1,0:T(8,128)(2,1)}, bf16[32,2816]{1,0:T(8,128)(2,1)}, u32[]{:S(2)}, u32[]{:S(2)}) collective-permute-start(bf16[32,2816]{1,0:T(8,128)(2,1)} %get-tuple-element.93), channel_id=1, source_target_pairs={{0,8},{2,10},{4,12},{6,14},{8,16},{10,18},{12,20},{14,22},{16,24},... | collective-permute-start | bytes 540680 | tf_op jit(solution)/shard_map/ppermute | solution.py:232
  438.5 13.5 %collective-permute-start.49 = (bf16[176,512]{1,0:T(8,128)(2,1)}, bf16[176,512]{1,0:T(8,128)(2,1)}, u32[]{:S(2)}, u32[]{:S(2)}) collective-permute-start(bf16[176,512]{1,0:T(8,128)(2,1)} %collective-permute-done.48), channel_id=1, source_target_pairs={{0,8},{2,10},{4,12},{6,14},{8,16},{10,18},{12,20},{14,22},{16,24},... | collective-permute-start | bytes 540680 | tf_op jit(solution)/shard_map/ppermute | solution.py:232
  440.1 9.6 %collective-permute-start.26 = (bf16[32,1024]{1,0:T(8,128)(2,1)S(1)}, bf16[32,1024]{1,0:T(8,128)(2,1)S(1)}, u32[]{:S(2)}, u32[]{:S(2)}) collective-permute-start(bf16[32,1024]{1,0:T(8,128)(2,1)S(1)} %collective-permute-done.25), channel_id=1, source_target_pairs={{0,8},{2,10},{4,12},{6,14},{8,16},{10,18},{12,20},{14,22},{16,24},... | collective-permute-start | bytes 196616 | tf_op jit(solution)/shard_map/ppermute | solution.py:232
  449.8 25.6 %collective-permute-start.27 = (bf16[128,1024]{1,0:T(8,128)(2,1)S(1)}, bf16[128,1024]{1,0:T(8,128)(2,1)S(1)}, u32[]{:S(2)}, u32[]{:S(2)}) collective-permute-start(bf16[128,1024]{1,0:T(8,128)(2,1)S(1)} %bitcast.360), channel_id=1, source_target_pairs={{0,4},{2,6},{4,0},{6,2},{8,12},{10,14},{12,8},{14,10},{16,20},{18,... | collective-permute-start | bytes 786440 | tf_op jit(solution)/shard_map/ppermute | solution.py:229
  452.0 19.2 %collective-permute-start.33 = (bf16[32,2816]{1,0:T(8,128)(2,1)}, bf16[32,2816]{1,0:T(8,128)(2,1)S(1)}, u32[]{:S(2)}, u32[]{:S(2)}) collective-permute-start(bf16[32,2816]{1,0:T(8,128)(2,1)} %collective-permute-done.32), channel_id=1, source_target_pairs={{0,8},{2,10},{4,12},{6,14},{8,16},{10,18},{12,20},{14,22},{16,24},... | collective-permute-start | bytes 540680 | tf_op jit(solution)/shard_map/ppermute | solution.py:232
  452.0 18.5 %collective-permute-start.50 = (bf16[176,512]{1,0:T(8,128)(2,1)}, bf16[176,512]{1,0:T(8,128)(2,1)S(1)}, u32[]{:S(2)}, u32[]{:S(2)}) collective-permute-start(bf16[176,512]{1,0:T(8,128)(2,1)} %collective-permute-done.49), channel_id=1, source_target_pairs={{0,8},{2,10},{4,12},{6,14},{8,16},{10,18},{12,20},{14,22},{16,24},... | collective-permute-start | bytes 540680 | tf_op jit(solution)/shard_map/ppermute | solution.py:232
  458.5 16.8 %collective-permute-start.38 = (bf16[32,2816]{1,0:T(8,128)(2,1)S(1)}, bf16[32,2816]{1,0:T(8,128)(2,1)S(1)}, u32[]{:S(2)}, u32[]{:S(2)}) collective-permute-start(bf16[32,2816]{1,0:T(8,128)(2,1)S(1)} %dynamic-slice_bitcast_fusion.7), channel_id=1, source_target_pairs={{0,8},{2,10},{4,12},{6,14},{8,16},{10,18},{12,20},{14,22},{16,24},... | collective-permute-start | bytes 540680 | tf_op jit(solution)/shard_map/ppermute | solution.py:232
  471.2 33.2 %collective-permute-start.51 = (bf16[704,512]{1,0:T(8,128)(2,1)}, bf16[704,512]{1,0:T(8,128)(2,1)S(1)}, u32[]{:S(2)}, u32[]{:S(2)}) collective-permute-start(bf16[704,512]{1,0:T(8,128)(2,1)} %bitcast.111), channel_id=1, source_target_pairs={{0,4},{2,6},{4,0},{6,2},{8,12},{10,14},{12,8},{14,10},{16,20},{18,... | collective-permute-start | bytes 2162696 | tf_op jit(solution)/shard_map/ppermute | solution.py:229
  475.3 8.6 %collective-permute-start.39 = (bf16[32,2816]{1,0:T(8,128)(2,1)S(1)}, bf16[32,2816]{1,0:T(8,128)(2,1)S(1)}, u32[]{:S(2)}, u32[]{:S(2)}) collective-permute-start(bf16[32,2816]{1,0:T(8,128)(2,1)S(1)} %fusion.35), channel_id=1, source_target_pairs={{0,8},{2,10},{4,12},{6,14},{8,16},{10,18},{12,20},{14,22},{16,24},... | collective-permute-start | bytes 540680 | tf_op jit(solution)/shard_map/ppermute | solution.py:232
  475.4 19.7 %collective-permute-start.28 = (bf16[256,1024]{1,0:T(8,128)(2,1)S(1)}, bf16[256,1024]{1,0:T(8,128)(2,1)S(1)}, u32[]{:S(2)}, u32[]{:S(2)}) collective-permute-start(bf16[256,1024]{1,0:T(8,128)(2,1)S(1)} %bitcast.345), channel_id=1, source_target_pairs={{0,2},{2,0},{4,6},{6,4},{8,10},{10,8},{12,14},{14,12},{16,18},{18,... | collective-permute-start | bytes 1572872 | tf_op jit(solution)/shard_map/ppermute | solution.py:223
  478.7 33.1 %collective-permute-start.35 = (bf16[128,2816]{1,0:T(8,128)(2,1)S(1)}, bf16[128,2816]{1,0:T(8,128)(2,1)S(1)}, u32[]{:S(2)}, u32[]{:S(2)}) collective-permute-start(bf16[128,2816]{1,0:T(8,128)(2,1)S(1)} %bitcast.336), channel_id=1, source_target_pairs={{0,4},{2,6},{4,0},{6,2},{8,12},{10,14},{12,8},{14,10},{16,20},{18,... | collective-permute-start | bytes 2162696 | tf_op jit(solution)/shard_map/ppermute | solution.py:229
  484.0 11.0 %collective-permute-start.40 = (bf16[32,2816]{1,0:T(8,128)(2,1)S(1)}, bf16[32,2816]{1,0:T(8,128)(2,1)S(1)}, u32[]{:S(2)}, u32[]{:S(2)}) collective-permute-start(bf16[32,2816]{1,0:T(8,128)(2,1)S(1)} %fusion.36), channel_id=1, source_target_pairs={{0,8},{2,10},{4,12},{6,14},{8,16},{10,18},{12,20},{14,22},{16,24},... | collective-permute-start | bytes 540680 | tf_op jit(solution)/shard_map/ppermute | solution.py:232
  495.1 9.4 %collective-permute-start.41 = (bf16[32,2816]{1,0:T(8,128)(2,1)S(1)}, bf16[32,2816]{1,0:T(8,128)(2,1)S(1)}, u32[]{:S(2)}, u32[]{:S(2)}) collective-permute-start(bf16[32,2816]{1,0:T(8,128)(2,1)S(1)} %get-tuple-element.91), channel_id=1, source_target_pairs={{0,8},{2,10},{4,12},{6,14},{8,16},{10,18},{12,20},{14,22},{16,24},... | collective-permute-start | bytes 540680 | tf_op jit(solution)/shard_map/ppermute | solution.py:232
  505.4 42.1 %collective-permute-start.52 = (bf16[1408,512]{1,0:T(8,128)(2,1)}, bf16[1408,512]{1,0:T(8,128)(2,1)}, u32[]{:S(2)}, u32[]{:S(2)}) collective-permute-start(bf16[1408,512]{1,0:T(8,128)(2,1)} %bitcast.114), channel_id=1, source_target_pairs={{0,2},{2,0},{4,6},{6,4},{8,10},{10,8},{12,14},{14,12},{16,18},{18,... | collective-permute-start | bytes 4325384 | tf_op jit(solution)/shard_map/ppermute | solution.py:223
  512.7 40.8 %collective-permute-start.36 = (bf16[256,2816]{1,0:T(8,128)(2,1)}, bf16[256,2816]{1,0:T(8,128)(2,1)}, u32[]{:S(2)}, u32[]{:S(2)}) collective-permute-start(bf16[256,2816]{1,0:T(8,128)(2,1)} %bitcast.82), channel_id=1, source_target_pairs={{0,2},{2,0},{4,6},{6,4},{8,10},{10,8},{12,14},{14,12},{16,18},{18,... | collective-permute-start | bytes 4325384 | tf_op jit(solution)/shard_map/ppermute | solution.py:223
  519.1 13.3 %collective-permute-start.44 = (bf16[128,2816]{1,0:T(8,128)(2,1)S(1)}, bf16[128,2816]{1,0:T(8,128)(2,1)S(1)}, u32[]{:S(2)}, u32[]{:S(2)}) collective-permute-start(bf16[128,2816]{1,0:T(8,128)(2,1)S(1)} %bitcast.334), channel_id=1, source_target_pairs={{0,4},{2,6},{4,0},{6,2},{8,12},{10,14},{12,8},{14,10},{16,20},{18,... | collective-permute-start | bytes 2162696 | tf_op jit(solution)/shard_map/ppermute | solution.py:229
  533.2 25.8 %collective-permute-start.45 = (bf16[256,2816]{1,0:T(8,128)(2,1)}, bf16[256,2816]{1,0:T(8,128)(2,1)}, u32[]{:S(2)}, u32[]{:S(2)}) collective-permute-start(bf16[256,2816]{1,0:T(8,128)(2,1)} %bitcast.101), channel_id=1, source_target_pairs={{0,2},{2,0},{4,6},{6,4},{8,10},{10,8},{12,14},{14,12},{16,18},{18,... | collective-permute-start | bytes 4325384 | tf_op jit(solution)/shard_map/ppermute | solution.py:223
  (72 other events, 602.7 us)
Sparse Core Ops, SparseCore 0:
  15.6 90.0 all-gather.2
  449.9 60.3 all-gather.4

commit v4 on v3

--- a/solution.py
+++ b/solution.py
@@ -211,12 +211,13 @@
 
 class Links:
     def __init__(self, reps):
-        self.deep = reps // 4
         self.to_core = turns(reps, lambda z, y, core: (z, y, 1 - core))
         self.to_y = turns(reps, lambda z, y, core: (z, 1 - y, core))
-        self.to_z = turns(reps, lambda z, y, core: (z + 1, y, core))
+        self.to_pair = turns(reps, lambda z, y, core: (z ^ 1, y, core))
+        self.to_far = turns(reps, lambda z, y, core: (z ^ 2, y, core))
         here = lax.axis_index("rep")
-        self.z, self.y, self.core = here // 4, (here // 2) % 2, here % 2
+        self.near, self.far = (here // 4) % 2, here // 8
+        self.y, self.core = (here // 2) % 2, here % 2
         self.x = lax.axis_index("shard")
 
     def over_core(self, value):
@@ -228,8 +229,11 @@
     def over_y(self, value):
         return lax.ppermute(value, "rep", self.to_y)
 
-    def next_z(self, value):
-        return lax.ppermute(value, "rep", self.to_z)
+    def over_pair(self, value):
+        return lax.ppermute(value, "rep", self.to_pair)
+
+    def over_far(self, value):
+        return lax.ppermute(value, "rep", self.to_far)
 
     def half(self, total, side):
         return pick(total.reshape(2, -1, total.shape[1]), side)
@@ -238,34 +242,6 @@
         columns = total.shape[1]
         return pick(total.reshape(2, 2, -1, columns), side, 1).reshape(-1, columns)
 
-    def part(self, total, turn):
-        return pick(total.reshape(self.deep, -1, total.shape[1]), (self.z + turn) % self.deep)
-
-    def ring_start(self, total):
-        return self.next_z(self.part(total, self.deep - 1))
-
-    def ring_step(self, total, arrived, step):
-        return add(self.part(total, 2 * self.deep - 2 - step), arrived)
-
-    def along_z(self, total):
-        arrived = self.ring_start(total)
-        for step in range(self.deep - 1):
-            moving = self.ring_step(total, arrived, step)
-            if step < self.deep - 2:
-                arrived = self.next_z(moving)
-        return moving
-
-    def collect(self, piece):
-        deep = self.deep
-        whole_z = blank((deep,) + piece.shape, piece.dtype)
-        for step in range(deep):
-            whole_z = put(whole_z, piece, (self.z + deep - step) % deep)
-            if step < deep - 1:
-                piece = self.next_z(piece)
-        whole_z = whole_z.reshape(-1, piece.shape[1])
-        halves = join(whole_z, self.over_y(whole_z), self.y).reshape(-1, piece.shape[1])
-        return join(halves, self.over_core(halves), self.core)
-
 
 def pick(values, index, axis=0):
     return lax.dynamic_index_in_dim(values, index, axis, keepdims=False)
@@ -276,8 +252,9 @@
 
 
 def join(mine, other, index):
-    both = blank((2,) + mine.shape, mine.dtype)
-    return put(put(both, mine, index), other, 1 - index)
+    first = jnp.concatenate([mine, other], axis=0)
+    second = jnp.concatenate([other, mine], axis=0)
+    return jnp.where(index == 0, first, second)
 
 
 def fence(*values):
@@ -407,6 +384,74 @@
     )(gathered.reshape(seqs * groups, share, 3 * lanes), w_query, w_key, w_value)
 
 
+def finish_kernel(count, ff, slots_ref, *refs):
+    parts, (gate_ref, up_ref) = refs[:count], refs[count : count + 2]
+    grad_gate_ref, grad_up_ref, grad_out_ref, sum_ref, buffer, arrived = refs[-6:]
+    step = pl.program_id(0)
+
+    def fetch(at):
+        return pltpu.make_async_copy(parts[at], buffer.at[at % 2], arrived.at[at % 2])
+
+    for at in range(count):
+
+        @pl.when(step == max(at - 1, 0))
+        def _():
+            fetch(at).start()
+
+    for at in range(count):
+
+        @pl.when(step == at)
+        def _():
+            fetch(at).wait()
+
+    here = lax.rem(step, 2)
+    lanes = sum_ref.shape[1]
+    total = jnp.zeros(sum_ref.shape, F32)
+    for start in range(0, ff, lanes):
+        place = slice(start, start + lanes)
+        grad_gate = buffer[here, :, place].astype(F32)
+        grad_up = buffer[here, :, ff + start : ff + start + lanes].astype(F32)
+        grad_gate_ref[:, place] = grad_gate
+        grad_up_ref[:, place] = grad_up
+        total += grad_gate * gate_ref[:, place].astype(F32)
+        total += grad_up * up_ref[:, place].astype(F32)
+    sum_ref[...] = total
+    grad_out_ref[...] = buffer[here, :, 2 * ff :].astype(F32)
+
+
+def finish(slots, parts, w_gate, w_up, filled):
+    height, ff = w_gate.shape
+    share, columns = parts[0].shape
+    count = len(parts)
+
+    def rows(width):
+        return pl.BlockSpec((share, width), lambda i, slots: (slots[i], 0))
+
+    anywhere = pl.BlockSpec(memory_space=pl.ANY)
+    widths = (ff, ff, columns - 2 * ff, 128)
+    return pl.pallas_call(
+        functools.partial(finish_kernel, count, ff),
+        out_shape=tuple(jax.ShapeDtypeStruct((height, width), F32) for width in widths),
+        grid_spec=pltpu.PrefetchScalarGridSpec(
+            num_scalar_prefetch=1,
+            grid=(count,),
+            in_specs=[anywhere] * count + [rows(ff), rows(ff)] + [anywhere] * len(filled),
+            out_specs=[rows(width) for width in widths],
+            scratch_shapes=[
+                pltpu.VMEM((2, share, columns), BF16),
+                pltpu.SemaphoreType.DMA((2,)),
+            ],
+        ),
+        input_output_aliases={count + 3 + at: at for at in range(len(filled))},
+        compiler_params=pltpu.CompilerParams(vmem_limit_bytes=VMEM_LIMIT),
+        cost_estimate=pl.CostEstimate(
+            flops=4 * count * share * columns,
+            transcendentals=0,
+            bytes_accessed=8 * count * share * columns,
+        ),
+    )(slots, *parts, w_gate, w_up, *filled)
+
+
 class Layer:
     def __init__(self, reps, tokens, prefix_len):
         self.reps = reps
@@ -644,22 +689,31 @@
             full = lax.dynamic_update_slice(full, part, ((1 - x) * height + owner * half, 0))
         return full
 
-    near_qkv = links.over_x(after(half_rows((w_query, w_key, w_value)), other_gains))
+    half_qkv = after(half_rows((w_query, w_key, w_value)), other_gains)
+    near_qkv = links.over_x(half_qkv)
     near_ff = links.over_x(after(half_rows((w_output, w_gate, w_up)), near_qkv))
-    near_down = links.over_x(after(half_rows((w_down,)), near_ff))
     full_qkv = assemble((w_query, w_key, w_value), near_qkv, links.over_core(near_qkv), 0)
 
     inputs = tokens.reshape(total, width).astype(F32)
     normed1, scale1 = norm_rows(inputs)
     hidden1 = (normed1 * gain1).astype(BF16)
-    hidden1_all = lax.all_gather(hidden1.reshape(tokens.shape), "rep", axis=1, tiled=True)
+    by_seq = after(hidden1, half_qkv).reshape(tokens.shape)
+    mine, theirs = pick(by_seq, links.far), pick(by_seq, 1 - links.far)
+    halves = join(mine[None], links.over_far(theirs)[None], links.far)
+    groups = [list(range(layer.groups)), list(range(layer.groups, reps))]
+    hidden1, halves, *layer.all_tables = fence(hidden1, halves, *layer.all_tables)
+    hidden_mine = lax.all_gather(halves, "rep", axis_index_groups=groups, axis=1, tiled=True)
+    hidden_mine = hidden_mine.reshape(layer.length, width)
     qkv = layer.to_heads(layer.project(hidden1, full_qkv, first_values), 3)
-    qkv, hidden1_all = fence(qkv, hidden1_all)
+    qkv, hidden_mine = fence(qkv, hidden_mine)
     att, att_t, mass = layer.attend(qkv)
-    att, near_ff = fence(att, near_ff)
+    att, near_ff, down_half = fence(att, near_ff, half_rows((w_down,)))
+    near_down = links.over_x(down_half)
     far_ff = links.over_core(near_ff)
     full_output = assemble((w_output,), near_ff, far_ff, 0)
     full_gate_up = assemble((w_gate, w_up), near_ff, far_ff, w_output.shape[1])
+    near_down = after(near_down, full_output, full_gate_up)
+    full_down = assemble((w_down,), near_down, links.over_core(near_down), 0)
     attended = layer.to_tokens(att, 1)
 
     residual = inputs + dot(attended, full_output, (1, 0))
@@ -682,76 +736,140 @@
         return jnp.where(core == 0, low, high), jnp.where(core == 0, high, low)
 
     upstream_mine, upstream_other = by_core(upstream, 1)
+    hidden2_mine, hidden2_other = by_core(hidden2, 2)
     down_send = dot(swiglu, upstream_other, (0, 0)).astype(BF16)
-    swiglu, down_send, near_down = fence(swiglu, down_send, near_down)
-    full_down = assemble((w_down,), near_down, links.over_core(near_down), 0)
     grad_swiglu = dot(upstream, full_down, (1, 1))
     grad_gate_pre, grad_up_pre = gate_back(grad_swiglu, gate_pre, up_pre, sigma, swish)
+    gate_send = dot(hidden2_other, grad_gate_pre, (0, 0)).astype(BF16)
+    swiglu, gate_send, grad_gate_pre, grad_up_pre = fence(
+        swiglu, gate_send, grad_gate_pre, grad_up_pre
+    )
+    gate_core = links.over_core(gate_send)
     down_total = add(dot(swiglu, upstream_mine, (0, 0)), links.over_core(down_send))
-    down_total, grad_gate_pre, grad_up_pre = fence(down_total, grad_gate_pre, grad_up_pre)
-
-    hidden2_mine, hidden2_other = by_core(hidden2, 2)
-    down_x = links.over_x(links.half(down_total, 1 - x))
-    gate_send = dot(hidden2_other, grad_gate_pre, (0, 0)).astype(BF16)
-    gate_total = add(dot(hidden2_mine, grad_gate_pre, (0, 0)), links.over_core(gate_send))
-    gate_total, grad_gate_pre, grad_up_pre = fence(gate_total, grad_gate_pre, grad_up_pre)
-    gate_y = links.over_y(links.quarters(gate_total, 1 - links.y))
+    down_half = links.half(down_total, 1 - x)
+    down_total, down_half, grad_gate_pre, grad_up_pre = fence(
+        down_total, down_half, grad_gate_pre, grad_up_pre
+    )
+    down_x = links.over_x(down_half)
+
+    up_send = dot(hidden2_other, grad_up_pre, (0, 0)).astype(BF16)
+    grad_gate_pre, up_send = fence(grad_gate_pre, up_send)
+    up_core = links.over_core(up_send)
+    gate_total = add(dot(hidden2_mine, grad_gate_pre, (0, 0)), gate_core)
+    gate_half = links.quarters(gate_total, 1 - links.y)
+    gate_total, gate_half, grad_gate_pre, grad_up_pre = fence(
+        gate_total, gate_half, grad_gate_pre, grad_up_pre
+    )
+    gate_y = links.over_y(gate_half)
+
+    up_total = add(dot(hidden2_mine, grad_up_pre, (0, 0)), up_core)
+    up_half = links.half(up_total, 1 - x)
+    up_total, up_half, grad_gate_pre, grad_up_pre = fence(
+        up_total, up_half, grad_gate_pre, grad_up_pre
+    )
+    up_x = links.over_x(up_half)
+
     grad_gate_up = jnp.concatenate([grad_gate_pre, grad_up_pre], axis=1)
-    up_send = dot(hidden2_other, grad_up_pre, (0, 0)).astype(BF16)
     grad_hidden2 = dot(grad_gate_up, full_gate_up, (1, 1))
     grad_residual = upstream.astype(F32) + norm_back(grad_hidden2 * gain2, normed2, scale2)
     grad_residual_low = grad_residual.astype(BF16)
     grad_attended = dot(grad_residual_low, full_output, (1, 1)).astype(BF16)
-    up_total = add(dot(hidden2_mine, grad_up_pre, (0, 0)), links.over_core(up_send))
+    grad_attended, grad_residual_low = fence(grad_attended, grad_residual_low)
+    do = layer.to_heads(grad_attended, 1)
     attended_mine, attended_other = by_core(attended, 2)
     out_send = dot(attended_other, grad_residual_low, (0, 0)).astype(BF16)
     out_total = add(dot(attended_mine, grad_residual_low, (0, 0)), links.over_core(out_send))
+    out_total, down_x = fence(out_total, down_x)
     down_first = add(links.half(down_total, x), down_x)
-    down_first, up_total, out_total, grad_attended = fence(
-        down_first, up_total, out_total, grad_attended
-    )
-
-    up_x = links.over_x(links.half(up_total, 1 - x))
     down_y = links.over_y(links.half(down_first, 1 - links.y))
-    do = layer.to_heads(grad_attended, 1)
+    out_y = links.over_y(links.quarters(out_total, 1 - links.y))
     output = (residual + dot(swiglu, full_down, (1, 0))).astype(BF16)
+    do, out_total, down_first, output = fence(do, out_total, down_first, output)
+
+    grad_raw_heads = layer.attend_back(qkv, do, att_t, mass)
+    grad_raw_heads, gate_y, up_x, out_y, down_y = fence(grad_raw_heads, gate_y, up_x, out_y, down_y)
+    down_second = add(links.half(down_first, links.y), down_y)
+    down_pair = links.over_pair(links.half(down_second, 1 - links.near))
     gate_first = add(links.quarters(gate_total, links.y), gate_y)
-    down_second = add(links.half(down_first, links.y), down_y)
-    do, gate_first, down_second, output = fence(do, gate_first, down_second, output)
-
     gate_x = links.over_x(links.half(gate_first, 1 - x))
-    out_y = links.over_y(links.quarters(out_total, 1 - links.y))
-    down_ring = links.ring_start(down_second)
-    grad_raw_heads = layer.attend_back(qkv, do, att_t, mass)
-    down_ring = links.ring_step(down_second, down_ring, 0)
+
     up_first = add(links.half(up_total, x), up_x)
     out_first = add(links.quarters(out_total, links.y), out_y)
+    up_y = links.over_y(links.half(up_first, 1 - links.y))
+    out_x = links.over_x(links.half(out_first, 1 - x))
+    columns = dot(hidden_mine, grad_raw_heads, (0, 0)).astype(BF16)
+    columns_x = links.over_x(links.half(columns, 1 - x))
+    columns_x, grad_raw_heads, down_pair = fence(columns_x, grad_raw_heads, down_pair)
+    down_third = add(links.half(down_second, links.near), down_pair)
+    down_far = links.over_far(links.half(down_third, 1 - links.far))
+    grad_raw = layer.to_tokens(grad_raw_heads, 3)
+    summed = layer.sum_sequences(add(links.half(columns, x), columns_x))
     gate_second = add(links.half(gate_first, x), gate_x)
-    grad_raw_heads, down_ring, up_first, out_first, gate_second = fence(
-        grad_raw_heads, down_ring, up_first, out_first, gate_second
-    )
-
-    grad_raw = layer.to_tokens(grad_raw_heads, 3)
-    hidden_mine = lax.dynamic_index_in_dim(hidden1_all, layer.my_seq, 0, keepdims=False)
-    columns = dot(hidden_mine, grad_raw_heads, (0, 0)).astype(BF16)
-    columns = add(links.half(columns, x), links.over_x(links.half(columns, 1 - x)))
-    gathered = lax.all_gather(layer.sum_sequences(columns), "rep", axis=0, tiled=True)
-    up_second = add(links.half(up_first, links.y), links.over_y(links.half(up_first, 1 - links.y)))
-    out_second = add(links.half(out_first, x), links.over_x(links.half(out_first, 1 - x)))
-    for step in range(1, links.deep - 1):
-        down_ring = links.ring_step(down_second, links.next_z(down_ring), step)
-    halves = links.collect(down_ring)
-    grad_down = jnp.concatenate([halves[0], halves[1]], axis=1).astype(F32)
-    grad_wgate = links.collect(links.along_z(gate_second)).reshape(-1, ff).astype(F32)
-    grad_wup = links.collect(links.along_z(up_second)).reshape(-1, ff).astype(F32)
-    grad_outproj = links.collect(links.along_z(out_second)).reshape(-1, width).astype(F32)
-
+    down_piece = add(links.half(down_third, links.far), down_far)
+    joined = jnp.concatenate(
+        [
+            gate_second,
+            add(links.half(up_first, links.y), up_y),
+            add(links.half(out_first, x), out_x),
+        ],
+        axis=1,
+    )
+
+    joined, down_piece, summed = fence(joined, down_piece, summed)
+    gathered = lax.all_gather(summed, "rep", axis=0, tiled=True)
+    joined_pair = links.over_pair(links.half(joined, 1 - links.near))
+    down_piece = join(down_piece, links.over_far(down_piece), links.far)
+    joined_third = add(links.half(joined, links.near), joined_pair)
+    joined_third, down_piece, grad_raw = fence(joined_third, down_piece, grad_raw)
+
+    joined_far = links.over_far(links.half(joined_third, 1 - links.far))
+    down_piece = join(down_piece, links.over_pair(down_piece), links.near)
     grad_first = grad_raw[:, 2 * width :].astype(F32)
     grad_hidden1 = dot(grad_raw, full_qkv, (1, 1))
     grad_inputs = grad_residual + norm_back(grad_hidden1 * gain1, normed1, scale1)
+    joined_piece = add(links.half(joined_third, links.far), joined_far)
+    joined_piece, down_piece, grad_inputs, grad_first, gathered = fence(
+        joined_piece, down_piece, grad_inputs, grad_first, gathered
+    )
+
+    joined_far = links.over_far(joined_piece)
+    down_y = links.over_y(down_piece)
     grad_wquery, grad_wkey, grad_wvalue, sums = spread(
         gathered, w_query, w_key, w_value, layer.seqs, layer.groups
     )
+    down_piece = join(down_piece, down_y, links.y)
+    part = join(joined_piece, joined_far, links.far)
+    part, down_piece, grad_wquery, grad_wkey, grad_wvalue = fence(
+        part, down_piece, grad_wquery, grad_wkey, grad_wvalue
+    )
+
+    part_pair = links.over_pair(part)
+    part_y = links.over_y(part)
+    part_core = links.over_core(part)
+    down_other = links.over_core(down_piece)
+    grad_down = jnp.where(
+        core == 0,
+        jnp.concatenate([down_piece, down_other], axis=1),
+        jnp.concatenate([down_other, down_piece], axis=1),
+    ).astype(F32)
+    part_pair, part_y, part_core, grad_down = fence(part_pair, part_y, part_core, grad_down)
+    middle = part.shape[0] // 2
+    last = (links.over_y(part_pair[:middle]), links.over_pair(part_y[middle:]))
+    pair_core, y_core = links.over_core(part_pair), links.over_core(part_y)
+
+    def slots(*bits):
+        place = [
+            (core ^ c) * 4 + (links.y ^ y) * 2 + (links.near ^ near) for c, y, near in bits
+        ]
+        return jnp.stack(place).astype(jnp.int32)
+
+    early = slots((0, 0, 0), (0, 0, 1), (0, 1, 0), (1, 0, 0), (1, 0, 1), (1, 1, 0))
+    early_parts = (part, part_pair, part_y, part_core, pair_core, y_core)
+    low, high, *filled = fence(*last, *finish(early, early_parts, w_gate, w_up, ()))
+    late = slots((0, 1, 1), (1, 1, 1))
+    late = jnp.concatenate([2 * late, 2 * late + 1])
+    late_parts = (low, links.over_core(low), high, links.over_core(high))
+    grad_wgate, grad_wup, grad_outproj, ff_sums = finish(late, late_parts, w_gate, w_up, filled)
     shape = tokens.shape
     return (
         output.reshape(shape),
@@ -765,7 +883,7 @@
         grad_wup,
         grad_down,
         jnp.sum(sums, axis=1) / gain_attn.astype(F32),
-        gain_gradient(gain_ffn, (w_gate, grad_wgate), (w_up, grad_wup)),
+        jnp.sum(ff_sums, axis=1) / gain_ffn.astype(F32),
     )
 
 

time: 598 us -> 529 us (0.88)
  waiting for transfers between devices: 218 us -> 187 us
  starting transfers between devices: 85.2 us -> 57.8 us
  Pallas kernels: 50.6 us -> 70.2 us
  local copies, waits for them, and re-layouts: 101 us -> 85.8 us
  other arithmetic: 55.1 us -> 46.1 us
  matrix products: 62 us -> 55.6 us
    ppermute x8 -> x7, waiting for transfers between devices: 38.6 us -> 1.97 us  [over_y(): return lax.ppermute(value, 'rep', self.to_y)]
    dynamic_update_slice x28 -> x0, local copies, waits for them, and re-layouts: 25 us -> none  [put(): return lax.dynamic_update_index_in_dim(values, part, index, 0)]
    pallas_call x0 -> x2, Pallas kernels: none -> 16.8 us  [finish(): pl.pallas_call(functools.partial(finish_kernel, count, ff), out_shape=tup...]
    all_to_all x2, waiting for transfers between devices: 39.8 us -> 54.4 us  [to_heads(): return lax.all_to_all(chunks, 'rep', 0, 0, tiled=True)]
    ppermute x24 -> x10, starting transfers between devices: 31.4 us -> 17.6 us  [the longest x5 11.1 us: over_far(): return lax.ppermute(value, 'rep', self.to_far)]
    ppermute x9, waiting for transfers between devices: 37.5 us -> 28.7 us  [over_x(): return lax.ppermute(value, 'shard', [(0, 1), (1, 0)])]
    reduce_sum x2 -> x1, other arithmetic: 8.48 us -> 1.1 us  [local_linked(): jnp.sum(ff_sums, axis=1) / gain_ffn.astype(F32)]
    dot_general x17, matrix products: 62 us -> 55.6 us  [dot(): lax.dot_general(left, right, ((contract[:1], contract[1:]), ((), ())), pr...]
  transfers between devices with their start and end apart: 59 -> 46, of which waited for: 23 -> 19; matrix products, arithmetic and copies ran while one was open for 33% -> 31% of each run, Pallas kernels for 7% -> 12%
where the time goes in v4:
time: 529 us; the launch traced here: 519 us
  waiting for transfers between devices  187 us (35%)
  local copies, waits for them, and re-layouts  85.8 us (16%)
  Pallas kernels  70.2 us (13%)
  starting transfers between devices  57.8 us (11%)
  matrix products  55.6 us (11%)
  other arithmetic  46.1 us (9%)
  between operations  15.7 us (3%)
    ppermute x5, waiting for transfers between devices, over_far(): return lax.ppermute(value, 'rep', self.to_far)  55.6 us
    dot_general x17, matrix products, dot(): lax.dot_general(left, right, ((contract[:1], contract[1:]), ((), ())), pr...  55.6 us
    all_to_all x2, waiting for transfers between devices, to_heads(): return lax.all_to_all(chunks, 'rep', 0, 0, tiled=True)  54.4 us
    ppermute x9, waiting for transfers between devices, over_x(): return lax.ppermute(value, 'shard', [(0, 1), (1, 0)])  28.7 us
    ppermute x5, waiting for transfers between devices, over_pair(): return lax.ppermute(value, 'rep', self.to_pair)  25.7 us
    pallas_call x1, Pallas kernels, attend_back(): pl.pallas_call(functools.partial(attend_back_kernel, head_dim, bq, bk), o...  24.2 us
    pallas_call x1, Pallas kernels, attend(): pl.pallas_call(functools.partial(attend_kernel, head_dim, bq, bk), out_sh...  17.8 us
    dynamic_update_slice x7, local copies, waits for them, and re-layouts, assemble(): full = lax.dynamic_update_slice(full, w, (x * height, place))  16.8 us
  transfers between devices with their start and end apart: 46, of which 19 were waited for; matrix products, arithmetic and copies ran while one was open for 31% of the time, Pallas kernels for 12%

profile of v4, /device:TPU:0, one launch (start us, length us, event | category | flops | bytes accessed | tf_op | source)
XLA Modules:
  0.0 518.6 jit_solution(14554518347633527878)
XLA Ops:
  8.6 3.0 collective-permute-start
  17.8 3.2 collective-permute-start.1
  20.9 5.6 %fusion.17 = (f32[2048,128]{1,0:T(8,128)}, f32[2048,128]{1,0:T(8,128)}) fusion(f32[128]{0:T(128)S(1)} %get-tuple-element.228, f32[128]{0:T(128)S(1)} %get-tuple-element.229, f32[2048]{0:T(1024)S(1)} %iota_convert_fusion), kind=kLoop, calls=%fused_computation.56 | loop fusion | flops 524288 | bytes 2106368 | tf_op jit(solution)/shard_map/mul | solution.py:40
  26.5 5.8 %collective-permute-done.1 = bf16[128,1024]{1,0:T(8,128)(2,1)S(1)} collective-permute-done((bf16[128,1024]{1,0:T(8,128)(2,1)S(1)}, bf16[128,1024]{1,0:T(8,128)(2,1)S(1)}, u32[]{:S(2)}, u32[]{:S(2)}) %collective-permute-start.1) | collective-permute-done | bytes 262176 | tf_op jit(solution)/shard_map/ppermute | solution.py:236
  41.9 11.0 %collective-permute-done.2 = bf16[256,3072]{1,0:T(8,128)(2,1)} collective-permute-done((bf16[256,3072]{1,0:T(8,128)(2,1)}, bf16[256,3072]{1,0:T(8,128)(2,1)}, u32[]{:S(2)}, u32[]{:S(2)}) %collective-permute-start.2) | collective-permute-done | bytes 1572896 | tf_op jit(solution)/shard_map/ppermute | solution.py:227
  58.9 2.6 copy-done.12
  67.1 2.8 copy.40
  70.0 6.4 %all-to-all-start = ((bf16[16,128,384]{1,2,0:T(8,128)(2,1)}), bf16[16,128,384]{1,2,0:T(8,128)(2,1)}, u32[]{:S(2)}, u32[]{:S(2)}) async-start(bf16[16,128,384]{1,2,0:T(8,128)(2,1)} %bitcast.213), calls=%async_computation | async-start | bytes 3145728 | tf_op jit(solution)/shard_map/all_to_all | solution.py:480
  77.0 2.6 constant_dynamic-slice_fusion.5
  79.6 28.7 %all-to-all-done = bf16[16,128,384]{1,2,0:T(8,128)(2,1)} async-done(((bf16[16,128,384]{1,2,0:T(8,128)(2,1)}), bf16[16,128,384]{1,2,0:T(8,128)(2,1)}, u32[]{:S(2)}, u32[]{:S(2)}) %all-to-all-start) | async-done | bytes 1572896 | tf_op jit(solution)/shard_map/all_to_all | solution.py:480
  108.3 2.6 copy.41
  110.9 17.8 %shard_map.221 = (bf16[2048,128]{1,0:T(8,128)(2,1)}, f32[128,2048]{1,0:T(8,128)}, f32[2,2048]{1,0:T(2,128)}) custom-call(s32[1]{0:T(128)} %dynamic_slice.126.prefix_ref, bf16[2048,384]{1,0:T(8,128)(2,1)} %bitcast.240, bf16[2048,384]{1,0:T(8,128)(2,1)} %bitcast.241, bf16[2048,384]{1,0:T(8,128)(2,1)} %bitcast.242), custom_call_target="tpu_custom_call" | custom-call | flops 2147483648 | bytes 2097152 | tf_op jit(solution)/shard_map/pallas_call | solution.py:298
  128.7 4.4 collective-permute-done.4
  135.4 3.8 constant_dynamic-update-slice_fusion.2
  142.8 6.0 %all-to-all-start.1 = ((bf16[16,128,128]{2,1,0:T(8,128)(2,1)}), bf16[16,128,128]{2,1,0:T(8,128)(2,1)S(1)}, u32[]{:S(2)}, u32[]{:S(2)}) async-start(bf16[16,128,128]{2,1,0:T(8,128)(2,1)} %bitcast.256), calls=%async_computation.1 | async-start | bytes 1048576 | tf_op jit(solution)/shard_map/all_to_all | solution.py:483
  151.3 3.8 slice_dynamic-update-slice_fusion.1
  155.1 8.0 %all-to-all-done.1 = bf16[16,128,128]{2,1,0:T(8,128)(2,1)S(1)} async-done(((bf16[16,128,128]{2,1,0:T(8,128)(2,1)}), bf16[16,128,128]{2,1,0:T(8,128)(2,1)S(1)}, u32[]{:S(2)}, u32[]{:S(2)}) %all-to-all-start.1) | async-done | bytes 524320 | tf_op jit(solution)/shard_map/all_to_all | solution.py:483
  166.7 4.7 slice_dynamic-update-slice_fusion
  171.4 11.7 %collective-permute-done.6 = bf16[704,1024]{1,0:T(8,128)(2,1)} collective-permute-done((bf16[704,1024]{1,0:T(8,128)(2,1)}, bf16[704,1024]{1,0:T(8,128)(2,1)}, u32[]{:S(2)}, u32[]{:S(2)}) %collective-permute-start.6) | collective-permute-done | bytes 1441824 | tf_op jit(solution)/shard_map/ppermute | solution.py:227
  186.1 6.2 %fusion.74 = f32[256,5632]{1,0:T(8,128)S(1)} fusion(bf16[256,1024]{1,0:T(8,128)(2,1)S(1)} %multiply_convert_fusion.3, bf16[1024,5632]{1,0:T(8,128)(2,1)} %slice_dynamic-update-slice_fusion), kind=kOutput, calls=%fused_computation.204 | convolution fusion | flops 2952790016 | bytes 17825792 | tf_op jit(solution)/shard_map/dot_general | solution.py:20
  193.3 4.4 multiply_convert_fusion
  202.0 4.1 convolution_convert_fusion.2
  206.1 2.8 add_convert_fusion.2
  210.2 2.5 convolution_convert_fusion
  214.2 3.6 add_convert_fusion.1
  221.2 3.1 add_convert_fusion
  227.1 6.3 %multiply_reduce_fusion.1 = (f32[256]{0:T(256)S(1)}, f32[256,1024]{1,0:T(8,128)}) fusion(f32[256,1024]{1,0:T(8,128)} %copy-done.9, f32[256]{0:T(256)S(1)} %add_rsqrt_fusion, f32[1024]{0:T(1024)S(1)} %bitcast.262, bf16[1024,5632]{1,0:T(8,128)(2,1)S(1)} %bitcast.201, bf16[256,2816]{1,0:T(8,128)(2,1)} %copy-done.20, bf16[256,2816]{1,0:T(8,128)(2,1)} %get-tuple-element.121), kind=kOutput, calls=%fused_computation.73 | convolution fusion | flops 2959605504 | bytes 16521216 | tf_op jit(solution)/shard_map/dot_general | solution.py:20
  238.8 5.1 fusion.16
  246.6 4.8 all-to-all-start.2
  257.7 25.7 %all-to-all-done.2 = bf16[16,128,128]{2,1,0:T(8,128)(2,1)S(1)} async-done(((bf16[16,128,128]{2,1,0:T(8,128)(2,1)}), bf16[16,128,128]{2,1,0:T(8,128)(2,1)S(1)}, u32[]{:S(2)}, u32[]{:S(2)}) %all-to-all-start.2) | async-done | bytes 524320 | tf_op jit(solution)/shard_map/all_to_all | solution.py:480
  289.1 24.2 %shard_map.225 = bf16[2048,384]{1,0:T(8,128)(2,1)} custom-call(s32[1]{0:T(128)} %dynamic_slice.126.prefix_ref, bf16[2048,384]{1,0:T(8,128)(2,1)} %bitcast.243, bf16[2048,384]{1,0:T(8,128)(2,1)} %bitcast.244, bf16[2048,384]{1,0:T(8,128)(2,1)} %bitcast.245, bf16[2048,128]{1,0:T(8,128)(2,1)} %bitcast.257, f32[128,2048]{1,0:T(8,128)} %get-tuple-element.132.att_t_ref, ...), custom_call_target="tpu_custom_call" | custom-call | flops 5368709120 | bytes 5767168 | tf_op jit(solution)/shard_map/pallas_call | solution.py:325
  331.9 2.8 collective-permute-done.21
  343.3 5.2 %all-to-all-start.3 = ((bf16[16,128,384]{1,2,0:T(8,128)(2,1)}), bf16[16,128,384]{1,2,0:T(8,128)(2,1)S(1)}, u32[]{:S(2)}, u32[]{:S(2)}) async-start(bf16[16,128,384]{1,2,0:T(8,128)(2,1)} %copy.45), calls=%async_computation.3 | async-start | bytes 3145728 | tf_op jit(solution)/shard_map/all_to_all | solution.py:483
  348.6 3.1 collective-permute-done.22
  353.4 10.2 %collective-permute-done.23 = bf16[256,384]{1,0:T(8,128)(2,1)} collective-permute-done((bf16[256,384]{1,0:T(8,128)(2,1)}, bf16[256,384]{1,0:T(8,128)(2,1)}, u32[]{:S(2)}, u32[]{:S(2)}) %collective-permute-start.23) | collective-permute-done | bytes 196640 | tf_op jit(solution)/shard_map/ppermute | solution.py:519
  369.4 34.2 %collective-permute-done.25 = bf16[176,512]{1,0:T(8,128)(2,1)S(1)} collective-permute-done((bf16[176,512]{1,0:T(8,128)(2,1)}, bf16[176,512]{1,0:T(8,128)(2,1)S(1)}, u32[]{:S(2)}, u32[]{:S(2)}) %collective-permute-start.25) | collective-permute-done | bytes 180256 | tf_op jit(solution)/shard_map/ppermute | solution.py:236
  405.4 5.9 %collective-permute-done.24 = bf16[64,6656]{1,0:T(8,128)(2,1)} collective-permute-done((bf16[64,6656]{1,0:T(8,128)(2,1)}, bf16[64,6656]{1,0:T(8,128)(2,1)}, u32[]{:S(2)}, u32[]{:S(2)}) %collective-permute-start.24) | collective-permute-done | bytes 852000 | tf_op jit(solution)/shard_map/ppermute | solution.py:233
  416.5 5.4 %collective-permute-start.26 = (bf16[32,6656]{1,0:T(8,128)(2,1)S(1)}, bf16[32,6656]{1,0:T(8,128)(2,1)S(1)}, u32[]{:S(2)}, u32[]{:S(2)}) collective-permute-start(bf16[32,6656]{1,0:T(8,128)(2,1)S(1)} %dynamic-slice_bitcast_fusion.6), channel_id=1, source_target_pairs={{0,16},{2,18},{4,20},{6,22},{8,24},{10,26},{12,28},{14,30},{16,0},... | collective-permute-start | bytes 1277960 | tf_op jit(solution)/shard_map/ppermute | solution.py:236
  421.9 3.1 collective-permute-start.27
  425.0 5.2 %multiply_reduce_fusion = (f32[256]{0:T(256)S(1)}, f32[256,1024]{1,0:T(8,128)S(1)}) fusion(bf16[2,128,1024]{2,1,0:T(8,128)(2,1)S(1)} %copy-done.23, f32[256]{0:T(256)S(1)} %copy-done.77, f32[1024]{0:T(1024)S(1)} %bitcast.260, bf16[256,3072]{1,0:T(8,128)(2,1)} %reshape.381, bf16[1024,3072]{1,0:T(8,128)(2,1)} %copy-done.12), kind=kOutput, calls=%fused_computation.71 | convolution fusion | flops 1611923200 | bytes 9443328 | tf_op jit(solution)/shard_map/dot_general | solution.py:20
  436.0 4.3 collective-permute-done.26
  441.1 11.3 %shard_map.226 = (f32[512,1024]{1,0:T(8,128)}, f32[512,1024]{1,0:T(8,128)}, f32[512,1024]{1,0:T(8,128)}, f32[512,128]{1,0:T(8,128)}) custom-call(bf16[16,256,384]{2,1,0:T(8,128)(2,1)} %bitcast.229, bf16[512,1024]{1,0:T(8,128)(2,1)} %wq_ref.1, bf16[512,1024]{1,0:T(8,128)(2,1)} %wk_ref.1, bf16[512,1024]{1,0:T(8,128)(2,1)} %wv_ref.1), custom_call_target="tpu_custom_call" | custom-call | flops 3145728 | bytes 12582912 | tf_op jit(solution)/shard_map/pallas_call | solution.py:369
  452.4 8.2 %collective-permute-done.28 = bf16[32,6656]{1,0:T(8,128)(2,1)S(1)} collective-permute-done((bf16[32,6656]{1,0:T(8,128)(2,1)S(1)}, bf16[32,6656]{1,0:T(8,128)(2,1)S(1)}, u32[]{:S(2)}, u32[]{:S(2)}) %collective-permute-start.28) | collective-permute-done | bytes 426016 | tf_op jit(solution)/shard_map/ppermute | solution.py:236
  461.9 2.7 collective-permute-done.33
  464.6 3.0 fusion.4
  467.6 15.2 %collective-permute-done.30.refs_1_ = bf16[64,6656]{1,0:T(8,128)(2,1)S(1)} collective-permute-done((bf16[64,6656]{1,0:T(8,128)(2,1)S(1)}, bf16[64,6656]{1,0:T(8,128)(2,1)S(1)}, u32[]{:S(2)}, u32[]{:S(2)}) %collective-permute-start.30) | collective-permute-done | bytes 852000 | tf_op jit(solution)/shard_map/ppermute | solution.py:233
  488.6 10.4 %shard_map.227 = (f32[512,2816]{1,0:T(8,128)}, f32[512,2816]{1,0:T(8,128)}, f32[512,1024]{1,0:T(8,128)}, f32[512,128]{1,0:T(8,128)}) custom-call(s32[6]{0:T(128)} %stack.51.slots_ref, bf16[64,6656]{1,0:T(8,128)(2,1)} %copy-done.29, bf16[64,6656]{1,0:T(8,128)(2,1)} %copy-done.47, bf16[64,6656]{1,0:T(8,128)(2,1)} %copy-done.48, bf16[64,6656]{1,0:T(8,128)(2,1)} %copy-done.55, ...), custom_call_target="tpu_custom_call" | custom-call | flops 10223616 | bytes 20447232 | tf_op jit(solution)/shard_map/pallas_call | solution.py:432
  503.5 6.4 %shard_map.228 = (f32[512,2816]{1,0:T(8,128)}, f32[512,2816]{1,0:T(8,128)}, f32[512,1024]{1,0:T(8,128)}, f32[512,128]{1,0:T(8,128)}) custom-call(s32[4]{0:T(128)} %pad_add_fusion.slots_ref, bf16[32,6656]{1,0:T(8,128)(2,1)} %collective-permute-done.34.refs_0_, ...), custom_call_target="tpu_custom_call", output_to_operand_aliasing={{0}: (7, {}), {1}: (8, {}), {2}: (9, {}), {3}: (10, {})} | custom-call | flops 3407872 | bytes 6815744 | tf_op jit(solution)/shard_map/pallas_call | solution.py:432
  (366 shorter events, 139.1 us)
Async XLA Ops:
  7.2 103.7 %all-gather.3.cloned.1.call-start = ((), (), s32[]{:S(2)}) async-start(), calls=%async_computation.4 | async-start | bytes 4718592 | tf_op jit(solution)/shard_map/all_gather | solution.py:705
  8.6 8.0 %collective-permute-start = (bf16[2,512]{1,0:T(2,128)(2,1)S(1)}, bf16[2,512]{1,0:T(2,128)(2,1)S(1)}, u32[]{:S(2)}, u32[]{:S(2)}) collective-permute-start(bf16[2,512]{1,0:T(2,128)(2,1)S(1)} %pad_maximum_fusion.11), channel_id=1, source_target_pairs={{0,1},{1,0},{2,3},{3,2},{4,5},{5,4},{6,7},{7,6},{8,9},{9,8},{10,11... | collective-permute-start | bytes 6152 | tf_op jit(solution)/shard_map/ppermute | solution.py:227
  16.6 36.2 %collective-permute-start.2 = (bf16[256,3072]{1,0:T(8,128)(2,1)}, bf16[256,3072]{1,0:T(8,128)(2,1)}, u32[]{:S(2)}, u32[]{:S(2)}) collective-permute-start(bf16[256,3072]{1,0:T(8,128)(2,1)} %pad_maximum_fusion.2), channel_id=1, source_target_pairs={{0,1},{1,0},{2,3},{3,2},{4,5},{5,4},{6,7},{7,6},{8,9},{9,8},{10,11... | collective-permute-start | bytes 4718600 | tf_op jit(solution)/shard_map/ppermute | solution.py:227
  17.8 14.5 %collective-permute-start.1 = (bf16[128,1024]{1,0:T(8,128)(2,1)S(1)}, bf16[128,1024]{1,0:T(8,128)(2,1)S(1)}, u32[]{:S(2)}, u32[]{:S(2)}) collective-permute-start(bf16[128,1024]{1,0:T(8,128)(2,1)S(1)} %get-tuple-element.213), channel_id=1, source_target_pairs={{0,16},{2,18},{4,20},{6,22},{8,24},{10,26},{12,28},{14,30},{16,0},... | collective-permute-start | bytes 786440 | tf_op jit(solution)/shard_map/ppermute | solution.py:236
  52.9 5.8 %collective-permute-start.3 = (bf16[256,3072]{1,0:T(8,128)(2,1)}, bf16[256,3072]{1,0:T(8,128)(2,1)S(1)}, u32[]{:S(2)}, u32[]{:S(2)}) collective-permute-start(bf16[256,3072]{1,0:T(8,128)(2,1)} %collective-permute-done.2), channel_id=1, source_target_pairs={{0,2},{2,0},{4,6},{6,4},{8,10},{10,8},{12,14},{14,12},{16,18},{18,... | collective-permute-start | bytes 4718600 | tf_op jit(solution)/shard_map/ppermute | solution.py:224
  56.7 76.4 %collective-permute-start.4 = (bf16[256,6656]{1,0:T(8,128)(2,1)}, bf16[256,6656]{1,0:T(8,128)(2,1)}, u32[]{:S(2)}, u32[]{:S(2)}) collective-permute-start(bf16[256,6656]{1,0:T(8,128)(2,1)} %pad_maximum_fusion), channel_id=1, source_target_pairs={{0,1},{1,0},{2,3},{3,2},{4,5},{5,4},{6,7},{7,6},{8,9},{9,8},{10,11... | collective-permute-start | bytes 10223624 | tf_op jit(solution)/shard_map/ppermute | solution.py:227
  70.0 38.3 %all-to-all-start = ((bf16[16,128,384]{1,2,0:T(8,128)(2,1)}), bf16[16,128,384]{1,2,0:T(8,128)(2,1)}, u32[]{:S(2)}, u32[]{:S(2)}) async-start(bf16[16,128,384]{1,2,0:T(8,128)(2,1)} %bitcast.213), calls=%async_computation | async-start | bytes 3145728 | tf_op jit(solution)/shard_map/all_to_all | solution.py:480
  133.1 32.2 %collective-permute-start.5 = (bf16[256,6656]{1,0:T(8,128)(2,1)}, bf16[256,6656]{1,0:T(8,128)(2,1)}, u32[]{:S(2)}, u32[]{:S(2)}) collective-permute-start(bf16[256,6656]{1,0:T(8,128)(2,1)} %collective-permute-done.4), channel_id=1, source_target_pairs={{0,2},{2,0},{4,6},{6,4},{8,10},{10,8},{12,14},{14,12},{16,18},{18,... | collective-permute-start | bytes 10223624 | tf_op jit(solution)/shard_map/ppermute | solution.py:224
  142.8 20.3 %all-to-all-start.1 = ((bf16[16,128,128]{2,1,0:T(8,128)(2,1)}), bf16[16,128,128]{2,1,0:T(8,128)(2,1)S(1)}, u32[]{:S(2)}, u32[]{:S(2)}) async-start(bf16[16,128,128]{2,1,0:T(8,128)(2,1)} %bitcast.256), calls=%async_computation.1 | async-start | bytes 1048576 | tf_op jit(solution)/shard_map/all_to_all | solution.py:483
  148.8 34.2 %collective-permute-start.6 = (bf16[704,1024]{1,0:T(8,128)(2,1)}, bf16[704,1024]{1,0:T(8,128)(2,1)}, u32[]{:S(2)}, u32[]{:S(2)}) collective-permute-start(bf16[704,1024]{1,0:T(8,128)(2,1)} %constant_dynamic-slice_fusion.5), channel_id=1, source_target_pairs={{0,1},{1,0},{2,3},{3,2},{4,5},{5,4},{6,7},{7,6},{8,9},{9,8},{10,11... | collective-permute-start | bytes 4325384 | tf_op jit(solution)/shard_map/ppermute | solution.py:227
  183.1 9.2 %collective-permute-start.7 = (bf16[704,1024]{1,0:T(8,128)(2,1)}, bf16[704,1024]{1,0:T(8,128)(2,1)S(1)}, u32[]{:S(2)}, u32[]{:S(2)}) collective-permute-start(bf16[704,1024]{1,0:T(8,128)(2,1)} %collective-permute-done.6), channel_id=1, source_target_pairs={{0,2},{2,0},{4,6},{6,4},{8,10},{10,8},{12,14},{14,12},{16,18},{18,... | collective-permute-start | bytes 4325384 | tf_op jit(solution)/shard_map/ppermute | solution.py:224
  185.9 47.5 %copy-start.74 = (f32[256]{0:T(256)}, f32[256]{0:T(256)S(1)}, u32[]{:S(2)}) copy-start(f32[256]{0:T(256)S(1)} %add_rsqrt_fusion) | copy-start | bytes 3076
  200.3 5.8 %collective-permute-start.8 = (bf16[2816,512]{1,0:T(8,128)(2,1)}, bf16[2816,512]{1,0:T(8,128)(2,1)}, u32[]{:S(2)}, u32[]{:S(2)}) collective-permute-start(bf16[2816,512]{1,0:T(8,128)(2,1)} %convolution_convert_fusion.1), channel_id=1, source_target_pairs={{0,2},{2,0},{4,6},{6,4},{8,10},{10,8},{12,14},{14,12},{16,18},{18,... | collective-permute-start | bytes 8650760 | tf_op jit(solution)/shard_map/ppermute | solution.py:224
  206.1 8.1 %collective-permute-start.9 = (bf16[512,2816]{1,0:T(8,128)(2,1)}, bf16[512,2816]{1,0:T(8,128)(2,1)}, u32[]{:S(2)}, u32[]{:S(2)}) collective-permute-start(bf16[512,2816]{1,0:T(8,128)(2,1)} %convolution_convert_fusion.2), channel_id=1, source_target_pairs={{0,2},{2,0},{4,6},{6,4},{8,10},{10,8},{12,14},{14,12},{16,18},{18,... | collective-permute-start | bytes 8650760 | tf_op jit(solution)/shard_map/ppermute | solution.py:224
  212.7 8.4 %collective-permute-start.10 = (bf16[512,2816]{1,0:T(8,128)(2,1)}, bf16[512,2816]{1,0:T(8,128)(2,1)}, u32[]{:S(2)}, u32[]{:S(2)}) collective-permute-start(bf16[512,2816]{1,0:T(8,128)(2,1)} %convolution_convert_fusion), channel_id=1, source_target_pairs={{0,2},{2,0},{4,6},{6,4},{8,10},{10,8},{12,14},{14,12},{16,18},{18,... | collective-permute-start | bytes 8650760 | tf_op jit(solution)/shard_map/ppermute | solution.py:224
  220.6 35.0 %collective-permute-start.12 = (bf16[1408,512]{1,0:T(8,128)(2,1)}, bf16[1408,512]{1,0:T(8,128)(2,1)}, u32[]{:S(2)}, u32[]{:S(2)}) collective-permute-start(bf16[1408,512]{1,0:T(8,128)(2,1)} %dynamic-slice_bitcast_fusion.1), channel_id=1, source_target_pairs={{0,1},{1,0},{2,3},{3,2},{4,5},{5,4},{6,7},{7,6},{8,9},{9,8},{10,11... | collective-permute-start | bytes 4325384 | tf_op jit(solution)/shard_map/ppermute | solution.py:227
  238.8 15.1 %collective-permute-start.11 = (bf16[512,1024]{1,0:T(8,128)(2,1)}, bf16[512,1024]{1,0:T(8,128)(2,1)}, u32[]{:S(2)}, u32[]{:S(2)}) collective-permute-start(bf16[512,1024]{1,0:T(8,128)(2,1)} %convolution_convert_fusion.3), channel_id=1, source_target_pairs={{0,2},{2,0},{4,6},{6,4},{8,10},{10,8},{12,14},{14,12},{16,18},{18,... | collective-permute-start | bytes 3145736 | tf_op jit(solution)/shard_map/ppermute | solution.py:224
  243.9 69.4 %collective-permute-start.13 = (bf16[256,2816]{1,0:T(8,128)(2,1)}, bf16[256,2816]{1,0:T(8,128)(2,1)}, u32[]{:S(2)}, u32[]{:S(2)}) collective-permute-start(bf16[256,2816]{1,0:T(8,128)(2,1)} %bitcast.22), channel_id=1, source_target_pairs={{0,4},{2,6},{4,0},{6,2},{8,12},{10,14},{12,8},{14,10},{16,20},{18,... | collective-permute-start | bytes 4325384 | tf_op jit(solution)/shard_map/ppermute | solution.py:230
  246.6 36.8 %all-to-all-start.2 = ((bf16[16,128,128]{2,1,0:T(8,128)(2,1)}), bf16[16,128,128]{2,1,0:T(8,128)(2,1)S(1)}, u32[]{:S(2)}, u32[]{:S(2)}) async-start(bf16[16,128,128]{2,1,0:T(8,128)(2,1)} %bitcast.26), calls=%async_computation.2 | async-start | bytes 1048576 | tf_op jit(solution)/shard_map/all_to_all | solution.py:480
  252.7 60.6 %collective-permute-start.14 = (bf16[256,2816]{1,0:T(8,128)(2,1)}, bf16[256,2816]{1,0:T(8,128)(2,1)}, u32[]{:S(2)}, u32[]{:S(2)}) collective-permute-start(bf16[256,2816]{1,0:T(8,128)(2,1)} %dynamic-slice_bitcast_fusion), channel_id=1, source_target_pairs={{0,1},{1,0},{2,3},{3,2},{4,5},{5,4},{6,7},{7,6},{8,9},{9,8},{10,11... | collective-permute-start | bytes 4325384 | tf_op jit(solution)/shard_map/ppermute | solution.py:227
  255.6 31.5 %copy-start.54 = (bf16[512,1024]{1,0:T(8,128)(2,1)}, bf16[512,1024]{1,0:T(8,128)(2,1)S(1)}, u32[]{:S(2)}) copy-start(bf16[512,1024]{1,0:T(8,128)(2,1)S(1)} %add_convert_fusion.3) | copy-start | bytes 3145732
  285.1 30.2 %collective-permute-start.16 = (bf16[704,512]{1,0:T(8,128)(2,1)}, bf16[704,512]{1,0:T(8,128)(2,1)S(1)}, u32[]{:S(2)}, u32[]{:S(2)}) collective-permute-start(bf16[704,512]{1,0:T(8,128)(2,1)} %dynamic-slice_bitcast_fusion.5), channel_id=1, source_target_pairs={{0,4},{2,6},{4,0},{6,2},{8,12},{10,14},{12,8},{14,10},{16,20},{18,... | collective-permute-start | bytes 2162696 | tf_op jit(solution)/shard_map/ppermute | solution.py:230
  287.9 27.3 %collective-permute-start.15 = (bf16[256,1024]{1,0:T(8,128)(2,1)}, bf16[256,1024]{1,0:T(8,128)(2,1)}, u32[]{:S(2)}, u32[]{:S(2)}) collective-permute-start(bf16[256,1024]{1,0:T(8,128)(2,1)} %bitcast.34), channel_id=1, source_target_pairs={{0,4},{2,6},{4,0},{6,2},{8,12},{10,14},{12,8},{14,10},{16,20},{18,... | collective-permute-start | bytes 1572872 | tf_op jit(solution)/shard_map/ppermute | solution.py:230
  316.5 15.3 %collective-permute-start.19 = (bf16[128,1024]{1,0:T(8,128)(2,1)S(1)}, bf16[128,1024]{1,0:T(8,128)(2,1)S(1)}, u32[]{:S(2)}, u32[]{:S(2)}) collective-permute-start(bf16[128,1024]{1,0:T(8,128)(2,1)S(1)} %dynamic-slice_bitcast_fusion.9), channel_id=1, source_target_pairs={{0,1},{1,0},{2,3},{3,2},{4,5},{5,4},{6,7},{7,6},{8,9},{9,8},{10,11... | collective-permute-start | bytes 786440 | tf_op jit(solution)/shard_map/ppermute | solution.py:227
  320.5 44.8 %collective-permute-start.18 = (bf16[128,2816]{1,0:T(8,128)(2,1)}, bf16[128,2816]{1,0:T(8,128)(2,1)}, u32[]{:S(2)}, u32[]{:S(2)}) collective-permute-start(bf16[128,2816]{1,0:T(8,128)(2,1)} %dynamic-slice_bitcast_fusion.3), channel_id=1, source_target_pairs={{0,4},{2,6},{4,0},{6,2},{8,12},{10,14},{12,8},{14,10},{16,20},{18,... | collective-permute-start | bytes 2162696 | tf_op jit(solution)/shard_map/ppermute | solution.py:230
  324.3 12.1 %collective-permute-start.20 = (bf16[512,384]{1,0:T(8,128)(2,1)S(1)}, bf16[512,384]{1,0:T(8,128)(2,1)S(1)}, u32[]{:S(2)}, u32[]{:S(2)}) collective-permute-start(bf16[512,384]{1,0:T(8,128)(2,1)S(1)} %dynamic-slice_bitcast_fusion.7), channel_id=1, source_target_pairs={{0,1},{1,0},{2,3},{3,2},{4,5},{5,4},{6,7},{7,6},{8,9},{9,8},{10,11... | collective-permute-start | bytes 1179656 | tf_op jit(solution)/shard_map/ppermute | solution.py:227
  325.5 9.2 %collective-permute-start.21 = (bf16[352,512]{1,0:T(8,128)(2,1)S(1)}, bf16[352,512]{1,0:T(8,128)(2,1)S(1)}, u32[]{:S(2)}, u32[]{:S(2)}) collective-permute-start(bf16[352,512]{1,0:T(8,128)(2,1)S(1)} %dynamic-slice_bitcast_fusion.8), channel_id=1, source_target_pairs={{0,8},{2,10},{4,12},{6,14},{8,0},{10,2},{12,4},{14,6},{16,24},{18,... | collective-permute-start | bytes 1081352 | tf_op jit(solution)/shard_map/ppermute | solution.py:233
  330.7 35.9 %collective-permute-start.17 = (bf16[128,2816]{1,0:T(8,128)(2,1)}, bf16[128,2816]{1,0:T(8,128)(2,1)}, u32[]{:S(2)}, u32[]{:S(2)}) collective-permute-start(bf16[128,2816]{1,0:T(8,128)(2,1)} %dynamic-slice_bitcast_fusion.4), channel_id=1, source_target_pairs={{0,1},{1,0},{2,3},{3,2},{4,5},{5,4},{6,7},{7,6},{8,9},{9,8},{10,11... | collective-permute-start | bytes 2162696 | tf_op jit(solution)/shard_map/ppermute | solution.py:227
  337.2 14.5 %collective-permute-start.22 = (bf16[176,512]{1,0:T(8,128)(2,1)}, bf16[176,512]{1,0:T(8,128)(2,1)}, u32[]{:S(2)}, u32[]{:S(2)}) collective-permute-start(bf16[176,512]{1,0:T(8,128)(2,1)} %dynamic-slice_bitcast_fusion.11), channel_id=1, source_target_pairs={{0,16},{2,18},{4,20},{6,22},{8,24},{10,26},{12,28},{14,30},{16,0},... | collective-permute-start | bytes 540680 | tf_op jit(solution)/shard_map/ppermute | solution.py:236
  341.1 22.5 %collective-permute-start.23 = (bf16[256,384]{1,0:T(8,128)(2,1)}, bf16[256,384]{1,0:T(8,128)(2,1)}, u32[]{:S(2)}, u32[]{:S(2)}) collective-permute-start(bf16[256,384]{1,0:T(8,128)(2,1)} %constant_dynamic-slice_fusion), channel_id=1, source_target_pairs={{0,16},{2,18},{4,20},{6,22},{8,24},{10,26},{12,28},{14,30},{16,0},... | collective-permute-start | bytes 589832 | tf_op jit(solution)/shard_map/ppermute | solution.py:519
  343.3 70.3 %all-to-all-start.3 = ((bf16[16,128,384]{1,2,0:T(8,128)(2,1)}), bf16[16,128,384]{1,2,0:T(8,128)(2,1)S(1)}, u32[]{:S(2)}, u32[]{:S(2)}) async-start(bf16[16,128,384]{1,2,0:T(8,128)(2,1)} %copy.45), calls=%async_computation.3 | async-start | bytes 3145728 | tf_op jit(solution)/shard_map/all_to_all | solution.py:483
  348.5 91.9 %all-gather.5.cloned.1.call-start = ((), (), s32[]{:S(2)}) async-start(), calls=%async_computation.5 | async-start | bytes 3342336 | tf_op jit(solution)/shard_map/all_gather | solution.py:819
  369.2 42.1 %collective-permute-start.24 = (bf16[64,6656]{1,0:T(8,128)(2,1)}, bf16[64,6656]{1,0:T(8,128)(2,1)}, u32[]{:S(2)}, u32[]{:S(2)}) collective-permute-start(bf16[64,6656]{1,0:T(8,128)(2,1)} %dynamic-slice_bitcast_fusion.2), channel_id=1, source_target_pairs={{0,8},{2,10},{4,12},{6,14},{8,0},{10,2},{12,4},{14,6},{16,24},{18,... | collective-permute-start | bytes 2555912 | tf_op jit(solution)/shard_map/ppermute | solution.py:233
  369.3 34.3 %collective-permute-start.25 = (bf16[176,512]{1,0:T(8,128)(2,1)}, bf16[176,512]{1,0:T(8,128)(2,1)S(1)}, u32[]{:S(2)}, u32[]{:S(2)}) collective-permute-start(bf16[176,512]{1,0:T(8,128)(2,1)} %fusion.31), channel_id=1, source_target_pairs={{0,16},{2,18},{4,20},{6,22},{8,24},{10,26},{12,28},{14,30},{16,0},... | collective-permute-start | bytes 540680 | tf_op jit(solution)/shard_map/ppermute | solution.py:236
  416.5 23.8 %collective-permute-start.26 = (bf16[32,6656]{1,0:T(8,128)(2,1)S(1)}, bf16[32,6656]{1,0:T(8,128)(2,1)S(1)}, u32[]{:S(2)}, u32[]{:S(2)}) collective-permute-start(bf16[32,6656]{1,0:T(8,128)(2,1)S(1)} %dynamic-slice_bitcast_fusion.6), channel_id=1, source_target_pairs={{0,16},{2,18},{4,20},{6,22},{8,24},{10,26},{12,28},{14,30},{16,0},... | collective-permute-start | bytes 1277960 | tf_op jit(solution)/shard_map/ppermute | solution.py:236
  421.9 13.9 %collective-permute-start.27 = (bf16[352,512]{1,0:T(8,128)(2,1)S(1)}, bf16[352,512]{1,0:T(8,128)(2,1)S(1)}, u32[]{:S(2)}, u32[]{:S(2)}) collective-permute-start(bf16[352,512]{1,0:T(8,128)(2,1)S(1)} %copy-done.53), channel_id=1, source_target_pairs={{0,8},{2,10},{4,12},{6,14},{8,0},{10,2},{12,4},{14,6},{16,24},{18,... | collective-permute-start | bytes 1081352 | tf_op jit(solution)/shard_map/ppermute | solution.py:233
  440.5 20.1 %collective-permute-start.28 = (bf16[32,6656]{1,0:T(8,128)(2,1)S(1)}, bf16[32,6656]{1,0:T(8,128)(2,1)S(1)}, u32[]{:S(2)}, u32[]{:S(2)}) collective-permute-start(bf16[32,6656]{1,0:T(8,128)(2,1)S(1)} %fusion.26), channel_id=1, source_target_pairs={{0,16},{2,18},{4,20},{6,22},{8,24},{10,26},{12,28},{14,30},{16,0},... | collective-permute-start | bytes 1277960 | tf_op jit(solution)/shard_map/ppermute | solution.py:236
  440.6 20.1 %collective-permute-start.29 = (bf16[704,512]{1,0:T(8,128)(2,1)S(1)}, bf16[704,512]{1,0:T(8,128)(2,1)S(1)}, u32[]{:S(2)}, u32[]{:S(2)}) collective-permute-start(bf16[704,512]{1,0:T(8,128)(2,1)S(1)} %maximum_select_fusion.5), channel_id=1, source_target_pairs={{0,4},{2,6},{4,0},{6,2},{8,12},{10,14},{12,8},{14,10},{16,20},{18,... | collective-permute-start | bytes 2162696 | tf_op jit(solution)/shard_map/ppermute | solution.py:230
  461.3 3.3 collective-permute-start.33
  461.4 21.3 %collective-permute-start.30 = (bf16[64,6656]{1,0:T(8,128)(2,1)S(1)}, bf16[64,6656]{1,0:T(8,128)(2,1)S(1)}, u32[]{:S(2)}, u32[]{:S(2)}) collective-permute-start(bf16[64,6656]{1,0:T(8,128)(2,1)S(1)} %maximum_select_fusion.4.refs_0_), channel_id=1, source_target_pairs={{0,8},{2,10},{4,12},{6,14},{8,0},{10,2},{12,4},{14,6},{16,24},{18,... | collective-permute-start | bytes 2555912 | tf_op jit(solution)/shard_map/ppermute | solution.py:233
  461.5 21.3 %collective-permute-start.31 = (bf16[64,6656]{1,0:T(8,128)(2,1)S(1)}, bf16[64,6656]{1,0:T(8,128)(2,1)S(1)}, u32[]{:S(2)}, u32[]{:S(2)}) collective-permute-start(bf16[64,6656]{1,0:T(8,128)(2,1)S(1)} %maximum_select_fusion.4.refs_0_), channel_id=1, source_target_pairs={{0,4},{2,6},{4,0},{6,2},{8,12},{10,14},{12,8},{14,10},{16,20},{18,... | collective-permute-start | bytes 2555912 | tf_op jit(solution)/shard_map/ppermute | solution.py:230
  461.5 21.2 %collective-permute-start.32 = (bf16[64,6656]{1,0:T(8,128)(2,1)S(1)}, bf16[64,6656]{1,0:T(8,128)(2,1)S(1)}, u32[]{:S(2)}, u32[]{:S(2)}) collective-permute-start(bf16[64,6656]{1,0:T(8,128)(2,1)S(1)} %maximum_select_fusion.4.refs_0_), channel_id=1, source_target_pairs={{0,2},{2,0},{4,6},{6,4},{8,10},{10,8},{12,14},{14,12},{16,18},{18,... | collective-permute-start | bytes 2555912 | tf_op jit(solution)/shard_map/ppermute | solution.py:224
  482.8 4.9 collective-permute-start.36
  482.8 4.8 collective-permute-start.37
  485.2 13.8 %collective-permute-start.34 = (bf16[32,6656]{1,0:T(8,128)(2,1)}, bf16[32,6656]{1,0:T(8,128)(2,1)}, u32[]{:S(2)}, u32[]{:S(2)}) collective-permute-start(bf16[32,6656]{1,0:T(8,128)(2,1)} %slice.138), channel_id=1, source_target_pairs={{0,4},{2,6},{4,0},{6,2},{8,12},{10,14},{12,8},{14,10},{16,20},{18,... | collective-permute-start | bytes 1277960 | tf_op jit(solution)/shard_map/ppermute | solution.py:230
  485.2 13.7 %collective-permute-start.35 = (bf16[32,6656]{1,0:T(8,128)(2,1)}, bf16[32,6656]{1,0:T(8,128)(2,1)}, u32[]{:S(2)}, u32[]{:S(2)}) collective-permute-start(bf16[32,6656]{1,0:T(8,128)(2,1)} %slice.139), channel_id=1, source_target_pairs={{0,8},{2,10},{4,12},{6,14},{8,0},{10,2},{12,4},{14,6},{16,24},{18,... | collective-permute-start | bytes 1277960 | tf_op jit(solution)/shard_map/ppermute | solution.py:233
  499.0 2.9 collective-permute-start.38
  499.1 2.9 collective-permute-start.39
  (89 other events, 622.2 us)
Sparse Core Ops, SparseCore 0:
  33.3 30.2 all-gather.2
  369.4 61.4 all-gather.4

commit v5 on v4

--- a/solution.py
+++ b/solution.py
@@ -310,9 +310,7 @@
             scratch_shapes=[pltpu.VMEM((width, length), BF16), pltpu.VMEM((width, bq), F32)],
         ),
         compiler_params=pltpu.CompilerParams(vmem_limit_bytes=VMEM_LIMIT),
-        cost_estimate=pl.CostEstimate(
-            flops=flops, transcendentals=heads * length * length, bytes_accessed=8 * length * width
-        ),
+        cost_estimate=pl.CostEstimate(flops=1, transcendentals=0, bytes_accessed=1),
     )(prefix, *operands)
 
 
@@ -339,49 +337,56 @@
             ],
         ),
         compiler_params=pltpu.CompilerParams(vmem_limit_bytes=VMEM_LIMIT),
-        cost_estimate=pl.CostEstimate(
-            flops=flops, transcendentals=heads * length * length, bytes_accessed=22 * length * width
-        ),
+        cost_estimate=pl.CostEstimate(flops=1, transcendentals=0, bytes_accessed=1),
     )(prefix, *operands, do, att_t, mass, cosine, sine)
 
 
-def spread_kernel(lanes, in_ref, wq_ref, wk_ref, wv_ref, q_ref, k_ref, v_ref, sum_ref):
-    total = None
-    for at, (w_ref, out_ref) in enumerate(((wq_ref, q_ref), (wk_ref, k_ref), (wv_ref, v_ref))):
-        part = in_ref[0, :, at * lanes : (at + 1) * lanes].astype(F32)
-        out_ref[...] = part
-        term = part * w_ref[...].astype(F32)
-        total = term if total is None else total + term
-
-    @pl.when(pl.program_id(1) == 0)
-    def _():
-        sum_ref[...] = total
-
-    @pl.when(pl.program_id(1) > 0)
-    def _():
-        sum_ref[...] += total
-
-
-def spread(gathered, w_query, w_key, w_value, seqs, groups):
+def spread_kernel(lanes, core_ref, mine_ref, other_ref, wq_ref, wk_ref, wv_ref, *out_refs):
+    sum_ref = out_refs[3]
+    core = core_ref[0]
+    total = jnp.zeros(sum_ref.shape, F32)
+    for near in range(2):
+        for y in range(2):
+            mine, other = mine_ref[near, y, 0], other_ref[near, y, 0]
+            for side, part in enumerate((mine, other)):
+                part = jnp.where(core == 0, part, other if side == 0 else mine)
+                group = near * 4 + y * 2 + side
+                place = slice(group * lanes, (group + 1) * lanes)
+                for at, w_ref in enumerate((wq_ref, wk_ref, wv_ref)):
+                    values = part[:, at * lanes : (at + 1) * lanes].astype(F32)
+                    out_refs[at][:, place] = values
+                    total += values * w_ref[:, place].astype(F32)
+    sum_ref[...] = total
+
+
+def spread(core, mine, other, w_query, w_key, w_value, seqs, groups):
     height, width = w_query.shape
     share, lanes = height // seqs, width // groups
-    tile = pl.BlockSpec((share, lanes), lambda s, g: (s, g))
+    steps = 4
+    rows = share // steps
+    tile = pl.BlockSpec((rows, width), lambda s, i, core: (s * steps + i, 0))
+    part = pl.BlockSpec((2, 2, 1, rows, 3 * lanes), lambda s, i, core: (0, 0, s, i, 0))
+    shape = (2, 2, seqs, share, 3 * lanes)
     return pl.pallas_call(
         functools.partial(spread_kernel, lanes),
         out_shape=(jax.ShapeDtypeStruct((height, width), F32),) * 3
         + (jax.ShapeDtypeStruct((height, lanes), F32),),
-        grid=(seqs, groups),
-        in_specs=[
-            pl.BlockSpec((1, share, 3 * lanes), lambda s, g: (s * groups + g, 0, 0)),
-            tile,
-            tile,
-            tile,
-        ],
-        out_specs=[tile, tile, tile, pl.BlockSpec((share, lanes), lambda s, g: (s, 0))],
-        cost_estimate=pl.CostEstimate(
-            flops=6 * height * width, transcendentals=0, bytes_accessed=24 * height * width
+        grid_spec=pltpu.PrefetchScalarGridSpec(
+            num_scalar_prefetch=1,
+            grid=(seqs, steps),
+            in_specs=[part, part, tile, tile, tile],
+            out_specs=[tile, tile, tile]
+            + [pl.BlockSpec((rows, lanes), lambda s, i, core: (s * steps + i, 0))],
         ),
-    )(gathered.reshape(seqs * groups, share, 3 * lanes), w_query, w_key, w_value)
+        cost_estimate=pl.CostEstimate(flops=1, transcendentals=0, bytes_accessed=1),
+    )(
+        core.reshape(1).astype(jnp.int32),
+        mine.reshape(shape),
+        other.reshape(shape),
+        w_query,
+        w_key,
+        w_value,
+    )
 
 
 def finish_kernel(count, ff, slots_ref, *refs):
@@ -444,11 +449,7 @@
         ),
         input_output_aliases={count + 3 + at: at for at in range(len(filled))},
         compiler_params=pltpu.CompilerParams(vmem_limit_bytes=VMEM_LIMIT),
-        cost_estimate=pl.CostEstimate(
-            flops=4 * count * share * columns,
-            transcendentals=0,
-            bytes_accessed=8 * count * share * columns,
-        ),
+        cost_estimate=pl.CostEstimate(flops=1, transcendentals=0, bytes_accessed=1),
     )(slots, *parts, w_gate, w_up, *filled)
 
 
@@ -689,7 +690,7 @@
             full = lax.dynamic_update_slice(full, part, ((1 - x) * height + owner * half, 0))
         return full
 
-    half_qkv = after(half_rows((w_query, w_key, w_value)), other_gains)
+    half_qkv = after(half_rows((w_query, w_key, w_value)), own_gains)
     near_qkv = links.over_x(half_qkv)
     near_ff = links.over_x(after(half_rows((w_output, w_gate, w_up)), near_qkv))
     full_qkv = assemble((w_query, w_key, w_value), near_qkv, links.over_core(near_qkv), 0)
@@ -760,7 +761,6 @@
     gate_total, gate_half, grad_gate_pre, grad_up_pre = fence(
         gate_total, gate_half, grad_gate_pre, grad_up_pre
     )
-    gate_y = links.over_y(gate_half)
 
     up_total = add(dot(hidden2_mine, grad_up_pre, (0, 0)), up_core)
     up_half = links.half(up_total, 1 - x)
@@ -782,66 +782,73 @@
     out_total, down_x = fence(out_total, down_x)
     down_first = add(links.half(down_total, x), down_x)
     down_y = links.over_y(links.half(down_first, 1 - links.y))
-    out_y = links.over_y(links.quarters(out_total, 1 - links.y))
+    out_x = links.over_x(links.half(out_total, 1 - x))
     output = (residual + dot(swiglu, full_down, (1, 0))).astype(BF16)
-    do, out_total, down_first, output = fence(do, out_total, down_first, output)
+    do, gate_half, down_first, output = fence(do, gate_half, down_first, output)
+    gate_y = links.over_y(gate_half)
 
     grad_raw_heads = layer.attend_back(qkv, do, att_t, mass)
-    grad_raw_heads, gate_y, up_x, out_y, down_y = fence(grad_raw_heads, gate_y, up_x, out_y, down_y)
+    grad_raw_heads, up_x, out_x, down_y = fence(grad_raw_heads, up_x, out_x, down_y)
     down_second = add(links.half(down_first, links.y), down_y)
     down_pair = links.over_pair(links.half(down_second, 1 - links.near))
+
+    up_first = add(links.half(up_total, x), up_x)
+    out_first = add(links.half(out_total, x), out_x)
+    up_y = links.over_y(links.half(up_first, 1 - links.y))
+    out_y = links.over_y(links.half(out_first, 1 - links.y))
+    columns = dot(hidden_mine, grad_raw_heads, (0, 0)).astype(BF16)
+    columns_x = links.over_x(links.half(columns, 1 - x))
+    columns_x, grad_raw_heads, down_pair, gate_y = fence(
+        columns_x, grad_raw_heads, down_pair, gate_y
+    )
     gate_first = add(links.quarters(gate_total, links.y), gate_y)
     gate_x = links.over_x(links.half(gate_first, 1 - x))
-
-    up_first = add(links.half(up_total, x), up_x)
-    out_first = add(links.quarters(out_total, links.y), out_y)
-    up_y = links.over_y(links.half(up_first, 1 - links.y))
-    out_x = links.over_x(links.half(out_first, 1 - x))
-    columns = dot(hidden_mine, grad_raw_heads, (0, 0)).astype(BF16)
-    columns_x = links.over_x(links.half(columns, 1 - x))
-    columns_x, grad_raw_heads, down_pair = fence(columns_x, grad_raw_heads, down_pair)
     down_third = add(links.half(down_second, links.near), down_pair)
     down_far = links.over_far(links.half(down_third, 1 - links.far))
     grad_raw = layer.to_tokens(grad_raw_heads, 3)
     summed = layer.sum_sequences(add(links.half(columns, x), columns_x))
+    gate_x, up_y, out_y, down_far, summed = fence(gate_x, up_y, out_y, down_far, summed)
     gate_second = add(links.half(gate_first, x), gate_x)
     down_piece = add(links.half(down_third, links.far), down_far)
     joined = jnp.concatenate(
         [
             gate_second,
             add(links.half(up_first, links.y), up_y),
-            add(links.half(out_first, x), out_x),
+            add(links.half(out_first, links.y), out_y),
         ],
         axis=1,
     )
 
     joined, down_piece, summed = fence(joined, down_piece, summed)
-    gathered = lax.all_gather(summed, "rep", axis=0, tiled=True)
     joined_pair = links.over_pair(links.half(joined, 1 - links.near))
+    summed = join(summed, links.over_far(summed), links.far)
     down_piece = join(down_piece, links.over_far(down_piece), links.far)
     joined_third = add(links.half(joined, links.near), joined_pair)
-    joined_third, down_piece, grad_raw = fence(joined_third, down_piece, grad_raw)
+    joined_third, down_piece, summed, grad_raw = fence(joined_third, down_piece, summed, grad_raw)
 
     joined_far = links.over_far(links.half(joined_third, 1 - links.far))
+    summed = join(summed, links.over_y(summed), links.y)
     down_piece = join(down_piece, links.over_pair(down_piece), links.near)
     grad_first = grad_raw[:, 2 * width :].astype(F32)
     grad_hidden1 = dot(grad_raw, full_qkv, (1, 1))
     grad_inputs = grad_residual + norm_back(grad_hidden1 * gain1, normed1, scale1)
     joined_piece = add(links.half(joined_third, links.far), joined_far)
-    joined_piece, down_piece, grad_inputs, grad_first, gathered = fence(
-        joined_piece, down_piece, grad_inputs, grad_first, gathered
+    joined_piece, down_piece, summed, grad_inputs, grad_first = fence(
+        joined_piece, down_piece, summed, grad_inputs, grad_first
     )
 
     joined_far = links.over_far(joined_piece)
+    summed = join(summed, links.over_pair(summed), links.near)
     down_y = links.over_y(down_piece)
-    grad_wquery, grad_wkey, grad_wvalue, sums = spread(
-        gathered, w_query, w_key, w_value, layer.seqs, layer.groups
-    )
     down_piece = join(down_piece, down_y, links.y)
     part = join(joined_piece, joined_far, links.far)
-    part, down_piece, grad_wquery, grad_wkey, grad_wvalue = fence(
-        part, down_piece, grad_wquery, grad_wkey, grad_wvalue
-    )
+    part, down_piece, summed = fence(part, down_piece, summed)
+
+    def slots(*bits):
+        place = [
+            (core ^ c) * 4 + (links.y ^ y) * 2 + (links.near ^ near) for c, y, near in bits
+        ]
+        return jnp.stack(place).astype(jnp.int32)
 
     part_pair = links.over_pair(part)
     part_y = links.over_y(part)
@@ -852,19 +859,25 @@
         jnp.concatenate([down_piece, down_other], axis=1),
         jnp.concatenate([down_other, down_piece], axis=1),
     ).astype(F32)
-    part_pair, part_y, part_core, grad_down = fence(part_pair, part_y, part_core, grad_down)
+    grad_wquery, grad_wkey, grad_wvalue, sums = spread(
+        core,
+        summed,
+        links.over_core(summed),
+        w_query,
+        w_key,
+        w_value,
+        layer.seqs,
+        layer.groups,
+    )
+    part_pair, part_y, grad_down, grad_wquery, grad_wkey, grad_wvalue = fence(
+        part_pair, part_y, grad_down, grad_wquery, grad_wkey, grad_wvalue
+    )
     middle = part.shape[0] // 2
     last = (links.over_y(part_pair[:middle]), links.over_pair(part_y[middle:]))
     pair_core, y_core = links.over_core(part_pair), links.over_core(part_y)
 
-    def slots(*bits):
-        place = [
-            (core ^ c) * 4 + (links.y ^ y) * 2 + (links.near ^ near) for c, y, near in bits
-        ]
-        return jnp.stack(place).astype(jnp.int32)
-
-    early = slots((0, 0, 0), (0, 0, 1), (0, 1, 0), (1, 0, 0), (1, 0, 1), (1, 1, 0))
-    early_parts = (part, part_pair, part_y, part_core, pair_core, y_core)
+    early = slots((0, 0, 0), (1, 0, 0), (0, 0, 1), (0, 1, 0), (1, 0, 1), (1, 1, 0))
+    early_parts = (part, part_core, part_pair, part_y, pair_core, y_core)
     low, high, *filled = fence(*last, *finish(early, early_parts, w_gate, w_up, ()))
     late = slots((0, 1, 1), (1, 1, 1))
     late = jnp.concatenate([2 * late, 2 * late + 1])

time: 529 us -> 513 us (0.970)
  waiting for transfers between devices: 187 us -> 168 us
  starting transfers between devices: 57.8 us -> 67 us
  Pallas kernels: 70.2 us -> 63.8 us
    all_to_all x2, waiting for transfers between devices: 54.4 us -> 28.7 us  [to_heads(): return lax.all_to_all(chunks, 'rep', 0, 0, tiled=True)]
    ppermute x9, waiting for transfers between devices: 28.7 us -> 42.6 us  [over_x(): return lax.ppermute(value, 'shard', [(0, 1), (1, 0)])]
    ppermute x1, waiting for transfers between devices: 10.2 us -> 2.8 us  [sum_sequences(): mine = mine + lax.ppermute(sent, 'rep', moves).astype(F32)]
    ppermute x7 -> x8, starting transfers between devices: 5.49 us -> 11.2 us  [over_y(): return lax.ppermute(value, 'rep', self.to_y)]
    ppermute x5 -> x6, waiting for transfers between devices: 55.6 us -> 60.8 us  [over_far(): return lax.ppermute(value, 'rep', self.to_far)]
    ppermute x5 -> x6, waiting for transfers between devices: 25.7 us -> 21.8 us  [over_pair(): return lax.ppermute(value, 'rep', self.to_pair)]
    ppermute x5 -> x6, starting transfers between devices: 11.1 us -> 9.09 us  [over_far(): return lax.ppermute(value, 'rep', self.to_far)]
    unnamed x185 -> x155, local copies, waits for them, and re-layouts: 16.6 us -> 17.4 us
  transfers between devices with their start and end apart: 46 -> 49, of which waited for: 19 -> 24; matrix products, arithmetic and copies ran while one was open for 31% -> 32% of each run, Pallas kernels for 12% -> 11%
where the time goes in v5:
time: 513 us; the launch traced here: 504 us
  waiting for transfers between devices  168 us (33%)
  local copies, waits for them, and re-layouts  83.1 us (16%)
  starting transfers between devices  67 us (13%)
  Pallas kernels  63.8 us (12%)
  matrix products  58.2 us (11%)
  other arithmetic  47.7 us (9%)
  between operations  15.8 us (3%)
    ppermute x6, waiting for transfers between devices, over_far(): return lax.ppermute(value, 'rep', self.to_far)  60.8 us
    dot_general x17, matrix products, dot(): lax.dot_general(left, right, ((contract[:1], contract[1:]), ((), ())), pr...  58.2 us
    ppermute x9, waiting for transfers between devices, over_x(): return lax.ppermute(value, 'shard', [(0, 1), (1, 0)])  42.6 us
    all_to_all x2, waiting for transfers between devices, to_heads(): return lax.all_to_all(chunks, 'rep', 0, 0, tiled=True)  28.7 us
    pallas_call x1, Pallas kernels, attend_back(): pl.pallas_call(functools.partial(attend_back_kernel, head_dim, bq, bk), o...  22.5 us
    ppermute x6, waiting for transfers between devices, over_pair(): return lax.ppermute(value, 'rep', self.to_pair)  21.8 us
    unnamed x155, local copies, waits for them, and re-layouts  17.4 us
    dynamic_update_slice x7, local copies, waits for them, and re-layouts, assemble(): full = lax.dynamic_update_slice(full, w, (x * height, place))  16.9 us
  transfers between devices with their start and end apart: 49, of which 24 were waited for; matrix products, arithmetic and copies ran while one was open for 32% of the time, Pallas kernels for 11%

profile of v5, /device:TPU:0, one launch (start us, length us, event | category | flops | bytes accessed | tf_op | source)
XLA Modules:
  0.0 503.9 jit_solution(6095647467176365319)
XLA Ops:
  8.6 3.0 collective-permute-start
  16.7 3.1 collective-permute-start.1
  19.8 5.6 %fusion.17 = (f32[2048,128]{1,0:T(8,128)}, f32[2048,128]{1,0:T(8,128)}) fusion(f32[128]{0:T(128)S(1)} %get-tuple-element.240, f32[128]{0:T(128)S(1)} %get-tuple-element.241, f32[2048]{0:T(1024)S(1)} %iota_convert_fusion), kind=kLoop, calls=%fused_computation.57 | loop fusion | flops 524288 | bytes 2106368 | tf_op jit(solution)/shard_map/mul | solution.py:40
  25.4 5.8 %collective-permute-done.1 = bf16[128,1024]{1,0:T(8,128)(2,1)S(1)} collective-permute-done((bf16[128,1024]{1,0:T(8,128)(2,1)S(1)}, bf16[128,1024]{1,0:T(8,128)(2,1)S(1)}, u32[]{:S(2)}, u32[]{:S(2)}) %collective-permute-start.1) | collective-permute-done | bytes 262176 | tf_op jit(solution)/shard_map/ppermute | solution.py:236
  40.8 10.7 %collective-permute-done.2 = bf16[256,3072]{1,0:T(8,128)(2,1)} collective-permute-done((bf16[256,3072]{1,0:T(8,128)(2,1)}, bf16[256,3072]{1,0:T(8,128)(2,1)}, u32[]{:S(2)}, u32[]{:S(2)}) %collective-permute-start.2) | collective-permute-done | bytes 1572896 | tf_op jit(solution)/shard_map/ppermute | solution.py:227
  64.1 2.8 copy.40
  66.9 6.6 %all-to-all-start = ((bf16[16,128,384]{1,2,0:T(8,128)(2,1)}), bf16[16,128,384]{1,2,0:T(8,128)(2,1)}, u32[]{:S(2)}, u32[]{:S(2)}) async-start(bf16[16,128,384]{1,2,0:T(8,128)(2,1)} %bitcast.222), calls=%async_computation | async-start | bytes 3145728 | tf_op jit(solution)/shard_map/all_to_all | solution.py:481
  76.7 28.7 %all-to-all-done = bf16[16,128,384]{1,2,0:T(8,128)(2,1)} async-done(((bf16[16,128,384]{1,2,0:T(8,128)(2,1)}), bf16[16,128,384]{1,2,0:T(8,128)(2,1)}, u32[]{:S(2)}, u32[]{:S(2)}) %all-to-all-start) | async-done | bytes 1572896 | tf_op jit(solution)/shard_map/all_to_all | solution.py:481
  105.5 2.6 copy.41
  108.0 16.6 %shard_map.221 = (bf16[2048,128]{1,0:T(8,128)(2,1)}, f32[128,2048]{1,0:T(8,128)}, f32[2,2048]{1,0:T(2,128)}) custom-call(s32[1]{0:T(128)} %dynamic_slice.126.prefix_ref, bf16[2048,384]{1,0:T(8,128)(2,1)} %bitcast.202, bf16[2048,384]{1,0:T(8,128)(2,1)} %bitcast.203, bf16[2048,384]{1,0:T(8,128)(2,1)} %bitcast.204), custom_call_target="tpu_custom_call" | custom-call | flops 1 | bytes 1 | tf_op jit(solution)/shard_map/pallas_call | solution.py:298
  124.6 7.1 %collective-permute-done.4 = bf16[256,6656]{1,0:T(8,128)(2,1)} collective-permute-done((bf16[256,6656]{1,0:T(8,128)(2,1)}, bf16[256,6656]{1,0:T(8,128)(2,1)}, u32[]{:S(2)}, u32[]{:S(2)}) %collective-permute-start.4) | collective-permute-done | bytes 3407904 | tf_op jit(solution)/shard_map/ppermute | solution.py:227
  134.0 3.8 constant_dynamic-update-slice_fusion.2
  141.4 6.0 %all-to-all-start.1 = ((bf16[16,128,128]{2,1,0:T(8,128)(2,1)}), bf16[16,128,128]{2,1,0:T(8,128)(2,1)S(1)}, u32[]{:S(2)}, u32[]{:S(2)}) async-start(bf16[16,128,128]{2,1,0:T(8,128)(2,1)} %bitcast.14), calls=%async_computation.1 | async-start | bytes 1048576 | tf_op jit(solution)/shard_map/all_to_all | solution.py:484
  150.0 3.7 slice_dynamic-update-slice_fusion.1
  153.7 8.1 %all-to-all-done.1 = bf16[16,128,128]{2,1,0:T(8,128)(2,1)S(1)} async-done(((bf16[16,128,128]{2,1,0:T(8,128)(2,1)}), bf16[16,128,128]{2,1,0:T(8,128)(2,1)S(1)}, u32[]{:S(2)}, u32[]{:S(2)}) %all-to-all-start.1) | async-done | bytes 524320 | tf_op jit(solution)/shard_map/all_to_all | solution.py:484
  164.2 3.8 slice_dynamic-update-slice_fusion
  168.1 13.6 %collective-permute-done.6 = bf16[704,1024]{1,0:T(8,128)(2,1)} collective-permute-done((bf16[704,1024]{1,0:T(8,128)(2,1)}, bf16[704,1024]{1,0:T(8,128)(2,1)}, u32[]{:S(2)}, u32[]{:S(2)}) %collective-permute-start.6) | collective-permute-done | bytes 1441824 | tf_op jit(solution)/shard_map/ppermute | solution.py:227
  186.3 6.2 %fusion.74 = f32[256,5632]{1,0:T(8,128)S(1)} fusion(bf16[256,1024]{1,0:T(8,128)(2,1)S(1)} %multiply_convert_fusion.3, bf16[1024,5632]{1,0:T(8,128)(2,1)} %slice_dynamic-update-slice_fusion), kind=kOutput, calls=%fused_computation.206 | convolution fusion | flops 2952790016 | bytes 17825792 | tf_op jit(solution)/shard_map/dot_general | solution.py:20
  193.5 4.5 multiply_convert_fusion
  202.2 4.0 convolution_convert_fusion.2
  206.3 2.8 add_convert_fusion.2
  215.4 3.0 add_convert_fusion.1
  221.7 2.8 add_convert_fusion
  227.3 5.9 %multiply_reduce_fusion.1 = (f32[256]{0:T(256)S(1)}, f32[256,1024]{1,0:T(8,128)}) fusion(f32[256,1024]{1,0:T(8,128)S(1)} %get-tuple-element.233, f32[256]{0:T(256)S(1)} %add_rsqrt_fusion, f32[1024]{0:T(1024)S(1)} %bitcast.266, bf16[1024,5632]{1,0:T(8,128)(2,1)S(1)} %bitcast.209, bf16[256,2816]{1,0:T(8,128)(2,1)} %get-tuple-element.128, ...), kind=kOutput, calls=%fused_computation.74 | convolution fusion | flops 2959605504 | bytes 16521216 | tf_op jit(solution)/shard_map/dot_general | solution.py:20
  238.7 6.2 %all-to-all-start.2 = ((bf16[16,128,128]{2,1,0:T(8,128)(2,1)}), bf16[16,128,128]{2,1,0:T(8,128)(2,1)S(1)}, u32[]{:S(2)}, u32[]{:S(2)}) async-start(bf16[16,128,128]{2,1,0:T(8,128)(2,1)} %bitcast.247), calls=%async_computation.2 | async-start | bytes 1048576 | tf_op jit(solution)/shard_map/all_to_all | solution.py:481
  247.6 6.8 %collective-permute-done.12 = bf16[1408,512]{1,0:T(8,128)(2,1)} collective-permute-done((bf16[1408,512]{1,0:T(8,128)(2,1)}, bf16[1408,512]{1,0:T(8,128)(2,1)}, u32[]{:S(2)}, u32[]{:S(2)}) %collective-permute-start.12) | collective-permute-done | bytes 1441824 | tf_op jit(solution)/shard_map/ppermute | solution.py:227
  261.4 5.2 %fusion.16 = bf16[256,1024]{1,0:T(8,128)(2,1)} fusion(f32[256,1024]{1,0:T(8,128)S(1)} %copy-done.12, bf16[256,2816]{1,0:T(8,128)(2,1)S(1)} %copy-done.6, bf16[2816,1024]{1,0:T(8,128)(2,1)} %copy-done.17), kind=kOutput, calls=%fused_computation.55 | convolution fusion | flops 1476919296 | bytes 8781824 | tf_op jit(solution)/shard_map/dot_general | solution.py:20
  268.8 22.5 %shard_map.225 = bf16[2048,384]{1,0:T(8,128)(2,1)} custom-call(s32[1]{0:T(128)} %dynamic_slice.126.prefix_ref, bf16[2048,384]{1,0:T(8,128)(2,1)} %bitcast.205, bf16[2048,384]{1,0:T(8,128)(2,1)} %bitcast.206, bf16[2048,384]{1,0:T(8,128)(2,1)} %bitcast.207, bf16[2048,128]{1,0:T(8,128)(2,1)} %bitcast.242, f32[128,2048]{1,0:T(8,128)} %get-tuple-element.139.att_t_ref, ...), custom_call_target="tpu_custom_call" | custom-call | flops 1 | bytes 1 | tf_op jit(solution)/shard_map/pallas_call | solution.py:323
  291.2 4.5 collective-permute-done.14
  295.7 5.0 convolution_convert_fusion.4
  317.5 2.6 collective-permute-start.23
  323.8 6.0 %all-to-all-start.3 = ((bf16[16,128,384]{1,2,0:T(8,128)(2,1)}), bf16[16,128,384]{1,2,0:T(8,128)(2,1)S(1)}, u32[]{:S(2)}, u32[]{:S(2)}) async-start(bf16[16,128,384]{1,2,0:T(8,128)(2,1)} %copy.45), calls=%async_computation.3 | async-start | bytes 3145728 | tf_op jit(solution)/shard_map/all_to_all | solution.py:484
  329.8 2.8 collective-permute-done.23
  333.7 11.3 %collective-permute-done.22 = bf16[176,512]{1,0:T(8,128)(2,1)} collective-permute-done((bf16[176,512]{1,0:T(8,128)(2,1)}, bf16[176,512]{1,0:T(8,128)(2,1)}, u32[]{:S(2)}, u32[]{:S(2)}) %collective-permute-start.22) | collective-permute-done | bytes 180256 | tf_op jit(solution)/shard_map/ppermute | solution.py:236
  351.5 2.9 collective-permute-start.26
  354.4 24.3 %collective-permute-done.25 = bf16[176,512]{1,0:T(8,128)(2,1)} collective-permute-done((bf16[176,512]{1,0:T(8,128)(2,1)}, bf16[176,512]{1,0:T(8,128)(2,1)}, u32[]{:S(2)}, u32[]{:S(2)}) %collective-permute-start.25) | collective-permute-done | bytes 180256 | tf_op jit(solution)/shard_map/ppermute | solution.py:236
  393.3 2.9 collective-permute-start.28
  396.2 3.3 collective-permute-start.29
  399.4 5.2 %multiply_reduce_fusion = (f32[256]{0:T(256)S(1)}, f32[256,1024]{1,0:T(8,128)S(1)}) fusion(bf16[2,128,1024]{2,1,0:T(8,128)(2,1)S(1)} %copy-done.29, f32[256]{0:T(256)S(1)} %rsqrt_bitcast_fusion, f32[1024]{0:T(1024)S(1)} %bitcast.264, bf16[256,3072]{1,0:T(8,128)(2,1)} %reshape.377, bf16[1024,3072]{1,0:T(8,128)(2,1)} %copy-done.14), kind=kOutput, calls=%fused_computation.72 | convolution fusion | flops 1611923200 | bytes 9443328 | tf_op jit(solution)/shard_map/dot_general | solution.py:20
  410.7 3.0 collective-permute-done.27
  414.7 3.3 collective-permute-start.31
  420.4 14.5 %collective-permute-done.30 = bf16[32,6656]{1,0:T(8,128)(2,1)S(1)} collective-permute-done((bf16[32,6656]{1,0:T(8,128)(2,1)S(1)}, bf16[32,6656]{1,0:T(8,128)(2,1)S(1)}, u32[]{:S(2)}, u32[]{:S(2)}) %collective-permute-start.30) | collective-permute-done | bytes 426016 | tf_op jit(solution)/shard_map/ppermute | solution.py:236
  435.6 10.8 %collective-permute-done.32 = bf16[1024,384]{1,0:T(8,128)(2,1)S(1)} collective-permute-done((bf16[1024,384]{1,0:T(8,128)(2,1)S(1)}, bf16[1024,384]{1,0:T(8,128)(2,1)S(1)}, u32[]{:S(2)}, u32[]{:S(2)}) %collective-permute-start.32) | collective-permute-done | bytes 786464 | tf_op jit(solution)/shard_map/ppermute | solution.py:233
  450.2 3.0 fusion.4
  454.3 7.9 %shard_map.226 = (f32[512,1024]{1,0:T(8,128)}, f32[512,1024]{1,0:T(8,128)}, f32[512,1024]{1,0:T(8,128)}, f32[512,128]{1,0:T(8,128)}) custom-call(s32[1]{0:T(128)} %bitcast.71.core_ref, bf16[2,2,2,256,384]{4,3,2,1,0:T(8,128)(2,1)} %bitcast.224, bf16[2,2,2,256,384]{4,3,2,1,0:T(8,128)(2,1)} %bitcast.251, bf16[512,1024]{1,0:T(8,128)(2,1)} %wq_ref.1, ...), custom_call_target="tpu_custom_call" | custom-call | flops 1 | bytes 1 | tf_op jit(solution)/shard_map/pallas_call | solution.py:370
  462.2 6.2 %collective-permute-done.33.refs_2_ = bf16[64,6656]{1,0:T(8,128)(2,1)S(1)} collective-permute-done((bf16[64,6656]{1,0:T(8,128)(2,1)S(1)}, bf16[64,6656]{1,0:T(8,128)(2,1)S(1)}, u32[]{:S(2)}, u32[]{:S(2)}) %collective-permute-start.33) | collective-permute-done | bytes 852000 | tf_op jit(solution)/shard_map/ppermute | solution.py:233
  474.6 10.4 %shard_map.227 = (f32[512,2816]{1,0:T(8,128)}, f32[512,2816]{1,0:T(8,128)}, f32[512,1024]{1,0:T(8,128)}, f32[512,128]{1,0:T(8,128)}) custom-call(s32[6]{0:T(128)} %stack.51.slots_ref, bf16[64,6656]{1,0:T(8,128)(2,1)} %copy-done.35, bf16[64,6656]{1,0:T(8,128)(2,1)} %collective-permute-done.39.refs_1_, bf16[64,6656]{1,0:T(8,128)(2,1)} %copy-done.46, ...), custom_call_target="tpu_custom_call" | custom-call | flops 1 | bytes 1 | tf_op jit(solution)/shard_map/pallas_call | solution.py:437
  488.6 6.4 %shard_map.228 = (f32[512,2816]{1,0:T(8,128)}, f32[512,2816]{1,0:T(8,128)}, f32[512,1024]{1,0:T(8,128)}, f32[512,128]{1,0:T(8,128)}) custom-call(s32[4]{0:T(128)} %pad_add_fusion.slots_ref, bf16[32,6656]{1,0:T(8,128)(2,1)} %collective-permute-done.37.refs_0_, ...), custom_call_target="tpu_custom_call", output_to_operand_aliasing={{0}: (7, {}), {1}: (8, {}), {2}: (9, {}), {3}: (10, {})} | custom-call | flops 1 | bytes 1 | tf_op jit(solution)/shard_map/pallas_call | solution.py:437
  (343 shorter events, 150.4 us)
Async XLA Ops:
  7.2 100.9 %all-gather.2.cloned.1.call-start = ((), (), s32[]{:S(2)}) async-start(), calls=%async_computation.4 | async-start | bytes 4718592 | tf_op jit(solution)/shard_map/all_gather | solution.py:706
  8.6 7.0 %collective-permute-start = (bf16[2,512]{1,0:T(2,128)(2,1)S(1)}, bf16[2,512]{1,0:T(2,128)(2,1)S(1)}, u32[]{:S(2)}, u32[]{:S(2)}) collective-permute-start(bf16[2,512]{1,0:T(2,128)(2,1)S(1)} %pad_maximum_fusion.11), channel_id=1, source_target_pairs={{0,1},{1,0},{2,3},{3,2},{4,5},{5,4},{6,7},{7,6},{8,9},{9,8},{10,11... | collective-permute-start | bytes 6152 | tf_op jit(solution)/shard_map/ppermute | solution.py:227
  15.3 36.2 %collective-permute-start.2 = (bf16[256,3072]{1,0:T(8,128)(2,1)}, bf16[256,3072]{1,0:T(8,128)(2,1)}, u32[]{:S(2)}, u32[]{:S(2)}) collective-permute-start(bf16[256,3072]{1,0:T(8,128)(2,1)} %pad_maximum_fusion.2), channel_id=1, source_target_pairs={{0,1},{1,0},{2,3},{3,2},{4,5},{5,4},{6,7},{7,6},{8,9},{9,8},{10,11... | collective-permute-start | bytes 4718600 | tf_op jit(solution)/shard_map/ppermute | solution.py:227
  16.7 14.5 %collective-permute-start.1 = (bf16[128,1024]{1,0:T(8,128)(2,1)S(1)}, bf16[128,1024]{1,0:T(8,128)(2,1)S(1)}, u32[]{:S(2)}, u32[]{:S(2)}) collective-permute-start(bf16[128,1024]{1,0:T(8,128)(2,1)S(1)} %get-tuple-element.225), channel_id=1, source_target_pairs={{0,16},{2,18},{4,20},{6,22},{8,24},{10,26},{12,28},{14,30},{16,0},... | collective-permute-start | bytes 786440 | tf_op jit(solution)/shard_map/ppermute | solution.py:236
  51.5 5.8 %collective-permute-start.3 = (bf16[256,3072]{1,0:T(8,128)(2,1)}, bf16[256,3072]{1,0:T(8,128)(2,1)S(1)}, u32[]{:S(2)}, u32[]{:S(2)}) collective-permute-start(bf16[256,3072]{1,0:T(8,128)(2,1)} %collective-permute-done.2), channel_id=1, source_target_pairs={{0,2},{2,0},{4,6},{6,4},{8,10},{10,8},{12,14},{14,12},{16,18},{18,... | collective-permute-start | bytes 4718600 | tf_op jit(solution)/shard_map/ppermute | solution.py:224
  55.3 76.4 %collective-permute-start.4 = (bf16[256,6656]{1,0:T(8,128)(2,1)}, bf16[256,6656]{1,0:T(8,128)(2,1)}, u32[]{:S(2)}, u32[]{:S(2)}) collective-permute-start(bf16[256,6656]{1,0:T(8,128)(2,1)} %pad_maximum_fusion), channel_id=1, source_target_pairs={{0,1},{1,0},{2,3},{3,2},{4,5},{5,4},{6,7},{7,6},{8,9},{9,8},{10,11... | collective-permute-start | bytes 10223624 | tf_op jit(solution)/shard_map/ppermute | solution.py:227
  66.9 38.5 %all-to-all-start = ((bf16[16,128,384]{1,2,0:T(8,128)(2,1)}), bf16[16,128,384]{1,2,0:T(8,128)(2,1)}, u32[]{:S(2)}, u32[]{:S(2)}) async-start(bf16[16,128,384]{1,2,0:T(8,128)(2,1)} %bitcast.222), calls=%async_computation | async-start | bytes 3145728 | tf_op jit(solution)/shard_map/all_to_all | solution.py:481
  131.7 30.4 %collective-permute-start.5 = (bf16[256,6656]{1,0:T(8,128)(2,1)}, bf16[256,6656]{1,0:T(8,128)(2,1)}, u32[]{:S(2)}, u32[]{:S(2)}) collective-permute-start(bf16[256,6656]{1,0:T(8,128)(2,1)} %collective-permute-done.4), channel_id=1, source_target_pairs={{0,2},{2,0},{4,6},{6,4},{8,10},{10,8},{12,14},{14,12},{16,18},{18,... | collective-permute-start | bytes 10223624 | tf_op jit(solution)/shard_map/ppermute | solution.py:224
  141.4 20.3 %all-to-all-start.1 = ((bf16[16,128,128]{2,1,0:T(8,128)(2,1)}), bf16[16,128,128]{2,1,0:T(8,128)(2,1)S(1)}, u32[]{:S(2)}, u32[]{:S(2)}) async-start(bf16[16,128,128]{2,1,0:T(8,128)(2,1)} %bitcast.14), calls=%async_computation.1 | async-start | bytes 1048576 | tf_op jit(solution)/shard_map/all_to_all | solution.py:484
  147.5 34.2 %collective-permute-start.6 = (bf16[704,1024]{1,0:T(8,128)(2,1)}, bf16[704,1024]{1,0:T(8,128)(2,1)}, u32[]{:S(2)}, u32[]{:S(2)}) collective-permute-start(bf16[704,1024]{1,0:T(8,128)(2,1)} %constant_dynamic-slice_fusion.3), channel_id=1, source_target_pairs={{0,1},{1,0},{2,3},{3,2},{4,5},{5,4},{6,7},{7,6},{8,9},{9,8},{10,11... | collective-permute-start | bytes 4325384 | tf_op jit(solution)/shard_map/ppermute | solution.py:227
  181.7 10.8 %collective-permute-start.7 = (bf16[704,1024]{1,0:T(8,128)(2,1)}, bf16[704,1024]{1,0:T(8,128)(2,1)S(1)}, u32[]{:S(2)}, u32[]{:S(2)}) collective-permute-start(bf16[704,1024]{1,0:T(8,128)(2,1)} %collective-permute-done.6), channel_id=1, source_target_pairs={{0,2},{2,0},{4,6},{6,4},{8,10},{10,8},{12,14},{14,12},{16,18},{18,... | collective-permute-start | bytes 4325384 | tf_op jit(solution)/shard_map/ppermute | solution.py:224
  200.6 5.8 %collective-permute-start.8 = (bf16[2816,512]{1,0:T(8,128)(2,1)}, bf16[2816,512]{1,0:T(8,128)(2,1)}, u32[]{:S(2)}, u32[]{:S(2)}) collective-permute-start(bf16[2816,512]{1,0:T(8,128)(2,1)} %convolution_convert_fusion.1), channel_id=1, source_target_pairs={{0,2},{2,0},{4,6},{6,4},{8,10},{10,8},{12,14},{14,12},{16,18},{18,... | collective-permute-start | bytes 8650760 | tf_op jit(solution)/shard_map/ppermute | solution.py:224
  206.2 9.2 %collective-permute-start.9 = (bf16[512,2816]{1,0:T(8,128)(2,1)}, bf16[512,2816]{1,0:T(8,128)(2,1)}, u32[]{:S(2)}, u32[]{:S(2)}) collective-permute-start(bf16[512,2816]{1,0:T(8,128)(2,1)} %convolution_convert_fusion.2), channel_id=1, source_target_pairs={{0,2},{2,0},{4,6},{6,4},{8,10},{10,8},{12,14},{14,12},{16,18},{18,... | collective-permute-start | bytes 8650760 | tf_op jit(solution)/shard_map/ppermute | solution.py:224
  214.1 6.5 %collective-permute-start.10 = (bf16[512,2816]{1,0:T(8,128)(2,1)}, bf16[512,2816]{1,0:T(8,128)(2,1)}, u32[]{:S(2)}, u32[]{:S(2)}) collective-permute-start(bf16[512,2816]{1,0:T(8,128)(2,1)} %convolution_convert_fusion), channel_id=1, source_target_pairs={{0,2},{2,0},{4,6},{6,4},{8,10},{10,8},{12,14},{14,12},{16,18},{18,... | collective-permute-start | bytes 8650760 | tf_op jit(solution)/shard_map/ppermute | solution.py:224
  219.6 34.8 %collective-permute-start.12 = (bf16[1408,512]{1,0:T(8,128)(2,1)}, bf16[1408,512]{1,0:T(8,128)(2,1)}, u32[]{:S(2)}, u32[]{:S(2)}) collective-permute-start(bf16[1408,512]{1,0:T(8,128)(2,1)} %dynamic-slice_bitcast_fusion.1), channel_id=1, source_target_pairs={{0,1},{1,0},{2,3},{3,2},{4,5},{5,4},{6,7},{7,6},{8,9},{9,8},{10,11... | collective-permute-start | bytes 4325384 | tf_op jit(solution)/shard_map/ppermute | solution.py:227
  237.6 8.0 %collective-permute-start.11 = (bf16[512,1024]{1,0:T(8,128)(2,1)}, bf16[512,1024]{1,0:T(8,128)(2,1)}, u32[]{:S(2)}, u32[]{:S(2)}) collective-permute-start(bf16[512,1024]{1,0:T(8,128)(2,1)} %convolution_convert_fusion.3), channel_id=1, source_target_pairs={{0,2},{2,0},{4,6},{6,4},{8,10},{10,8},{12,14},{14,12},{16,18},{18,... | collective-permute-start | bytes 3145736 | tf_op jit(solution)/shard_map/ppermute | solution.py:224
  238.7 28.0 %all-to-all-start.2 = ((bf16[16,128,128]{2,1,0:T(8,128)(2,1)}), bf16[16,128,128]{2,1,0:T(8,128)(2,1)S(1)}, u32[]{:S(2)}, u32[]{:S(2)}) async-start(bf16[16,128,128]{2,1,0:T(8,128)(2,1)} %bitcast.247), calls=%async_computation.2 | async-start | bytes 1048576 | tf_op jit(solution)/shard_map/all_to_all | solution.py:481
  244.9 46.3 %collective-permute-start.13 = (bf16[256,2816]{1,0:T(8,128)(2,1)}, bf16[256,2816]{1,0:T(8,128)(2,1)}, u32[]{:S(2)}, u32[]{:S(2)}) collective-permute-start(bf16[256,2816]{1,0:T(8,128)(2,1)} %dynamic-slice_bitcast_fusion), channel_id=1, source_target_pairs={{0,1},{1,0},{2,3},{3,2},{4,5},{5,4},{6,7},{7,6},{8,9},{9,8},{10,11... | collective-permute-start | bytes 4325384 | tf_op jit(solution)/shard_map/ppermute | solution.py:227
  255.2 40.5 %collective-permute-start.14 = (bf16[256,1024]{1,0:T(8,128)(2,1)}, bf16[256,1024]{1,0:T(8,128)(2,1)}, u32[]{:S(2)}, u32[]{:S(2)}) collective-permute-start(bf16[256,1024]{1,0:T(8,128)(2,1)} %dynamic-slice_bitcast_fusion.6), channel_id=1, source_target_pairs={{0,1},{1,0},{2,3},{3,2},{4,5},{5,4},{6,7},{7,6},{8,9},{9,8},{10,11... | collective-permute-start | bytes 1572872 | tf_op jit(solution)/shard_map/ppermute | solution.py:227
  259.8 35.9 %collective-permute-start.15 = (bf16[704,512]{1,0:T(8,128)(2,1)}, bf16[704,512]{1,0:T(8,128)(2,1)}, u32[]{:S(2)}, u32[]{:S(2)}) collective-permute-start(bf16[704,512]{1,0:T(8,128)(2,1)} %dynamic-slice_bitcast_fusion.5), channel_id=1, source_target_pairs={{0,4},{2,6},{4,0},{6,2},{8,12},{10,14},{12,8},{14,10},{16,20},{18,... | collective-permute-start | bytes 2162696 | tf_op jit(solution)/shard_map/ppermute | solution.py:230
  268.2 44.3 %collective-permute-start.18 = (bf16[256,2816]{1,0:T(8,128)(2,1)S(1)}, bf16[256,2816]{1,0:T(8,128)(2,1)}, u32[]{:S(2)}, u32[]{:S(2)}) collective-permute-start(bf16[256,2816]{1,0:T(8,128)(2,1)S(1)} %bitcast.252), channel_id=1, source_target_pairs={{0,4},{2,6},{4,0},{6,2},{8,12},{10,14},{12,8},{14,10},{16,20},{18,... | collective-permute-start | bytes 4325384 | tf_op jit(solution)/shard_map/ppermute | solution.py:230
  300.8 11.6 %collective-permute-start.16 = (bf16[512,384]{1,0:T(8,128)(2,1)S(1)}, bf16[512,384]{1,0:T(8,128)(2,1)S(1)}, u32[]{:S(2)}, u32[]{:S(2)}) collective-permute-start(bf16[512,384]{1,0:T(8,128)(2,1)S(1)} %dynamic-slice_bitcast_fusion.8), channel_id=1, source_target_pairs={{0,1},{1,0},{2,3},{3,2},{4,5},{5,4},{6,7},{7,6},{8,9},{9,8},{10,11... | collective-permute-start | bytes 1179656 | tf_op jit(solution)/shard_map/ppermute | solution.py:227
  303.0 9.5 %collective-permute-start.17 = (bf16[352,512]{1,0:T(8,128)(2,1)S(1)}, bf16[352,512]{1,0:T(8,128)(2,1)S(1)}, u32[]{:S(2)}, u32[]{:S(2)}) collective-permute-start(bf16[352,512]{1,0:T(8,128)(2,1)S(1)} %dynamic-slice_bitcast_fusion.9), channel_id=1, source_target_pairs={{0,8},{2,10},{4,12},{6,14},{8,0},{10,2},{12,4},{14,6},{16,24},{18,... | collective-permute-start | bytes 1081352 | tf_op jit(solution)/shard_map/ppermute | solution.py:233
  307.5 26.2 %collective-permute-start.20 = (bf16[128,2816]{1,0:T(8,128)(2,1)}, bf16[128,2816]{1,0:T(8,128)(2,1)}, u32[]{:S(2)}, u32[]{:S(2)}) collective-permute-start(bf16[128,2816]{1,0:T(8,128)(2,1)} %dynamic-slice_bitcast_fusion.3), channel_id=1, source_target_pairs={{0,4},{2,6},{4,0},{6,2},{8,12},{10,14},{12,8},{14,10},{16,20},{18,... | collective-permute-start | bytes 2162696 | tf_op jit(solution)/shard_map/ppermute | solution.py:230
  311.1 22.6 %collective-permute-start.21 = (bf16[128,1024]{1,0:T(8,128)(2,1)}, bf16[128,1024]{1,0:T(8,128)(2,1)}, u32[]{:S(2)}, u32[]{:S(2)}) collective-permute-start(bf16[128,1024]{1,0:T(8,128)(2,1)} %dynamic-slice_bitcast_fusion.10), channel_id=1, source_target_pairs={{0,4},{2,6},{4,0},{6,2},{8,12},{10,14},{12,8},{14,10},{16,20},{18,... | collective-permute-start | bytes 786440 | tf_op jit(solution)/shard_map/ppermute | solution.py:230
  316.2 28.9 %collective-permute-start.19 = (bf16[128,2816]{1,0:T(8,128)(2,1)}, bf16[128,2816]{1,0:T(8,128)(2,1)}, u32[]{:S(2)}, u32[]{:S(2)}) collective-permute-start(bf16[128,2816]{1,0:T(8,128)(2,1)} %dynamic-slice_bitcast_fusion.4), channel_id=1, source_target_pairs={{0,1},{1,0},{2,3},{3,2},{4,5},{5,4},{6,7},{7,6},{8,9},{9,8},{10,11... | collective-permute-start | bytes 2162696 | tf_op jit(solution)/shard_map/ppermute | solution.py:227
  317.5 15.1 %collective-permute-start.23 = (bf16[256,384]{1,0:T(8,128)(2,1)S(1)}, bf16[256,384]{1,0:T(8,128)(2,1)}, u32[]{:S(2)}, u32[]{:S(2)}) collective-permute-start(bf16[256,384]{1,0:T(8,128)(2,1)S(1)} %constant_dynamic-slice_fusion), channel_id=1, source_target_pairs={{0,16},{2,18},{4,20},{6,22},{8,24},{10,26},{12,28},{14,30},{16,0},... | collective-permute-start | bytes 589832 | tf_op jit(solution)/shard_map/ppermute | solution.py:520
  321.7 23.4 %collective-permute-start.22 = (bf16[176,512]{1,0:T(8,128)(2,1)}, bf16[176,512]{1,0:T(8,128)(2,1)}, u32[]{:S(2)}, u32[]{:S(2)}) collective-permute-start(bf16[176,512]{1,0:T(8,128)(2,1)} %dynamic-slice_bitcast_fusion.12), channel_id=1, source_target_pairs={{0,16},{2,18},{4,20},{6,22},{8,24},{10,26},{12,28},{14,30},{16,0},... | collective-permute-start | bytes 540680 | tf_op jit(solution)/shard_map/ppermute | solution.py:236
  323.8 65.3 %all-to-all-start.3 = ((bf16[16,128,384]{1,2,0:T(8,128)(2,1)}), bf16[16,128,384]{1,2,0:T(8,128)(2,1)S(1)}, u32[]{:S(2)}, u32[]{:S(2)}) async-start(bf16[16,128,384]{1,2,0:T(8,128)(2,1)} %copy.45), calls=%async_computation.3 | async-start | bytes 3145728 | tf_op jit(solution)/shard_map/all_to_all | solution.py:484
  351.5 35.3 %collective-permute-start.24 = (bf16[64,6656]{1,0:T(8,128)(2,1)}, bf16[64,6656]{1,0:T(8,128)(2,1)}, u32[]{:S(2)}, u32[]{:S(2)}) collective-permute-start(bf16[64,6656]{1,0:T(8,128)(2,1)} %dynamic-slice_bitcast_fusion.2), channel_id=1, source_target_pairs={{0,8},{2,10},{4,12},{6,14},{8,0},{10,2},{12,4},{14,6},{16,24},{18,... | collective-permute-start | bytes 2555912 | tf_op jit(solution)/shard_map/ppermute | solution.py:233
  351.5 27.3 %collective-permute-start.25 = (bf16[176,512]{1,0:T(8,128)(2,1)}, bf16[176,512]{1,0:T(8,128)(2,1)}, u32[]{:S(2)}, u32[]{:S(2)}) collective-permute-start(bf16[176,512]{1,0:T(8,128)(2,1)} %fusion.31), channel_id=1, source_target_pairs={{0,16},{2,18},{4,20},{6,22},{8,24},{10,26},{12,28},{14,30},{16,0},... | collective-permute-start | bytes 540680 | tf_op jit(solution)/shard_map/ppermute | solution.py:236
  351.5 31.2 %collective-permute-start.26 = (bf16[256,384]{1,0:T(8,128)(2,1)S(1)}, bf16[256,384]{1,0:T(8,128)(2,1)}, u32[]{:S(2)}, u32[]{:S(2)}) collective-permute-start(bf16[256,384]{1,0:T(8,128)(2,1)S(1)} %add_convert_fusion.4), channel_id=1, source_target_pairs={{0,16},{2,18},{4,20},{6,22},{8,24},{10,26},{12,28},{14,30},{16,0},... | collective-permute-start | bytes 589832 | tf_op jit(solution)/shard_map/ppermute | solution.py:236
  391.7 21.9 %collective-permute-start.27 = (bf16[32,6656]{1,0:T(8,128)(2,1)S(1)}, bf16[32,6656]{1,0:T(8,128)(2,1)S(1)}, u32[]{:S(2)}, u32[]{:S(2)}) collective-permute-start(bf16[32,6656]{1,0:T(8,128)(2,1)S(1)} %dynamic-slice_bitcast_fusion.7), channel_id=1, source_target_pairs={{0,16},{2,18},{4,20},{6,22},{8,24},{10,26},{12,28},{14,30},{16,0},... | collective-permute-start | bytes 1277960 | tf_op jit(solution)/shard_map/ppermute | solution.py:236
  393.3 16.7 %collective-permute-start.28 = (bf16[352,512]{1,0:T(8,128)(2,1)}, bf16[352,512]{1,0:T(8,128)(2,1)S(1)}, u32[]{:S(2)}, u32[]{:S(2)}) collective-permute-start(bf16[352,512]{1,0:T(8,128)(2,1)} %maximum_select_fusion.10), channel_id=1, source_target_pairs={{0,8},{2,10},{4,12},{6,14},{8,0},{10,2},{12,4},{14,6},{16,24},{18,... | collective-permute-start | bytes 1081352 | tf_op jit(solution)/shard_map/ppermute | solution.py:233
  396.2 14.2 %collective-permute-start.29 = (bf16[512,384]{1,0:T(8,128)(2,1)S(1)}, bf16[512,384]{1,0:T(8,128)(2,1)S(1)}, u32[]{:S(2)}, u32[]{:S(2)}) collective-permute-start(bf16[512,384]{1,0:T(8,128)(2,1)S(1)} %copy-done.48), channel_id=1, source_target_pairs={{0,4},{2,6},{4,0},{6,2},{8,12},{10,14},{12,8},{14,10},{16,20},{18,... | collective-permute-start | bytes 1179656 | tf_op jit(solution)/shard_map/ppermute | solution.py:230
  413.7 21.1 %collective-permute-start.30 = (bf16[32,6656]{1,0:T(8,128)(2,1)S(1)}, bf16[32,6656]{1,0:T(8,128)(2,1)S(1)}, u32[]{:S(2)}, u32[]{:S(2)}) collective-permute-start(bf16[32,6656]{1,0:T(8,128)(2,1)S(1)} %fusion.26), channel_id=1, source_target_pairs={{0,16},{2,18},{4,20},{6,22},{8,24},{10,26},{12,28},{14,30},{16,0},... | collective-permute-start | bytes 1277960 | tf_op jit(solution)/shard_map/ppermute | solution.py:236
  414.7 20.4 %collective-permute-start.31 = (bf16[704,512]{1,0:T(8,128)(2,1)S(1)}, bf16[704,512]{1,0:T(8,128)(2,1)S(1)}, u32[]{:S(2)}, u32[]{:S(2)}) collective-permute-start(bf16[704,512]{1,0:T(8,128)(2,1)S(1)} %maximum_select_fusion.7), channel_id=1, source_target_pairs={{0,4},{2,6},{4,0},{6,2},{8,12},{10,14},{12,8},{14,10},{16,20},{18,... | collective-permute-start | bytes 2162696 | tf_op jit(solution)/shard_map/ppermute | solution.py:230
  418.0 28.4 %collective-permute-start.32 = (bf16[1024,384]{1,0:T(8,128)(2,1)S(1)}, bf16[1024,384]{1,0:T(8,128)(2,1)S(1)}, u32[]{:S(2)}, u32[]{:S(2)}) collective-permute-start(bf16[1024,384]{1,0:T(8,128)(2,1)S(1)} %maximum_select_fusion.6), channel_id=1, source_target_pairs={{0,8},{2,10},{4,12},{6,14},{8,0},{10,2},{12,4},{14,6},{16,24},{18,... | collective-permute-start | bytes 2359304 | tf_op jit(solution)/shard_map/ppermute | solution.py:233
  446.9 3.3 collective-permute-start.35
  446.9 6.2 %collective-permute-start.36 = (bf16[2048,384]{1,0:T(8,128)(2,1)S(1)}, bf16[2048,384]{1,0:T(8,128)(2,1)S(1)}, u32[]{:S(2)}, u32[]{:S(2)}) collective-permute-start(bf16[2048,384]{1,0:T(8,128)(2,1)S(1)} %maximum_select_fusion.1), channel_id=1, source_target_pairs={{0,2},{2,0},{4,6},{6,4},{8,10},{10,8},{12,14},{14,12},{16,18},{18,... | collective-permute-start | bytes 4718600 | tf_op jit(solution)/shard_map/ppermute | solution.py:224
  447.4 20.9 %collective-permute-start.33 = (bf16[64,6656]{1,0:T(8,128)(2,1)S(1)}, bf16[64,6656]{1,0:T(8,128)(2,1)S(1)}, u32[]{:S(2)}, u32[]{:S(2)}) collective-permute-start(bf16[64,6656]{1,0:T(8,128)(2,1)S(1)} %maximum_select_fusion.5.refs_0_), channel_id=1, source_target_pairs={{0,8},{2,10},{4,12},{6,14},{8,0},{10,2},{12,4},{14,6},{16,24},{18,... | collective-permute-start | bytes 2555912 | tf_op jit(solution)/shard_map/ppermute | solution.py:233
  447.4 21.0 %collective-permute-start.34 = (bf16[64,6656]{1,0:T(8,128)(2,1)S(1)}, bf16[64,6656]{1,0:T(8,128)(2,1)}, u32[]{:S(2)}, u32[]{:S(2)}) collective-permute-start(bf16[64,6656]{1,0:T(8,128)(2,1)S(1)} %maximum_select_fusion.5.refs_0_), channel_id=1, source_target_pairs={{0,4},{2,6},{4,0},{6,2},{8,12},{10,14},{12,8},{14,10},{16,20},{18,... | collective-permute-start | bytes 2555912 | tf_op jit(solution)/shard_map/ppermute | solution.py:230
  447.5 26.2 %collective-permute-start.39 = (bf16[64,6656]{1,0:T(8,128)(2,1)S(1)}, bf16[64,6656]{1,0:T(8,128)(2,1)}, u32[]{:S(2)}, u32[]{:S(2)}) collective-permute-start(bf16[64,6656]{1,0:T(8,128)(2,1)S(1)} %maximum_select_fusion.5.refs_0_), channel_id=1, source_target_pairs={{0,2},{2,0},{4,6},{6,4},{8,10},{10,8},{12,14},{14,12},{16,18},{18,... | collective-permute-start | bytes 2555912 | tf_op jit(solution)/shard_map/ppermute | solution.py:224
  468.5 5.2 %collective-permute-start.40 = (bf16[64,6656]{1,0:T(8,128)(2,1)S(1)}, bf16[64,6656]{1,0:T(8,128)(2,1)S(1)}, u32[]{:S(2)}, u32[]{:S(2)}) collective-permute-start(bf16[64,6656]{1,0:T(8,128)(2,1)S(1)} %collective-permute-done.33.refs_2_), channel_id=1, source_target_pairs={{0,2},{2,0},{4,6},{6,4},{8,10},{10,8},{12,14},{14,12},{16,18},{18,... | collective-permute-start | bytes 2555912 | tf_op jit(solution)/shard_map/ppermute | solution.py:224
  468.5 5.2 %collective-permute-start.41 = (bf16[64,6656]{1,0:T(8,128)(2,1)}, bf16[64,6656]{1,0:T(8,128)(2,1)}, u32[]{:S(2)}, u32[]{:S(2)}) collective-permute-start(bf16[64,6656]{1,0:T(8,128)(2,1)} %collective-permute-done.34.refs_3_), channel_id=1, source_target_pairs={{0,2},{2,0},{4,6},{6,4},{8,10},{10,8},{12,14},{14,12},{16,18},{18,... | collective-permute-start | bytes 2555912 | tf_op jit(solution)/shard_map/ppermute | solution.py:224
  470.9 14.1 %collective-permute-start.37 = (bf16[32,6656]{1,0:T(8,128)(2,1)}, bf16[32,6656]{1,0:T(8,128)(2,1)}, u32[]{:S(2)}, u32[]{:S(2)}) collective-permute-start(bf16[32,6656]{1,0:T(8,128)(2,1)} %slice.138), channel_id=1, source_target_pairs={{0,4},{2,6},{4,0},{6,2},{8,12},{10,14},{12,8},{14,10},{16,20},{18,... | collective-permute-start | bytes 1277960 | tf_op jit(solution)/shard_map/ppermute | solution.py:230
  471.2 13.8 %collective-permute-start.38 = (bf16[32,6656]{1,0:T(8,128)(2,1)S(1)}, bf16[32,6656]{1,0:T(8,128)(2,1)}, u32[]{:S(2)}, u32[]{:S(2)}) collective-permute-start(bf16[32,6656]{1,0:T(8,128)(2,1)S(1)} %slice.139), channel_id=1, source_target_pairs={{0,8},{2,10},{4,12},{6,14},{8,0},{10,2},{12,4},{14,6},{16,24},{18,... | collective-permute-start | bytes 1277960 | tf_op jit(solution)/shard_map/ppermute | solution.py:233
  485.1 2.6 collective-permute-start.43
  (77 other events, 559.8 us)
Sparse Core Ops, SparseCore 0:
  32.2 30.2 all-gather.1

commit v6 on v5

--- a/solution.py
+++ b/solution.py
@@ -713,9 +713,10 @@
     far_ff = links.over_core(near_ff)
     full_output = assemble((w_output,), near_ff, far_ff, 0)
     full_gate_up = assemble((w_gate, w_up), near_ff, far_ff, w_output.shape[1])
-    near_down = after(near_down, full_output, full_gate_up)
-    full_down = assemble((w_down,), near_down, links.over_core(near_down), 0)
     attended = layer.to_tokens(att, 1)
+    height = w_down.shape[0]
+    own_down = lax.dynamic_update_slice(blank((2 * height, width), BF16), w_down, (x * height, 0))
+    attended, own_down = fence(attended, own_down)
 
     residual = inputs + dot(attended, full_output, (1, 0))
     normed2, scale2 = norm_rows(residual)
@@ -725,6 +726,11 @@
     sigma = jax.nn.sigmoid(gate_pre)
     swish = gate_pre * sigma
     swiglu = (swish * up_pre).astype(BF16)
+    near_down = after(near_down, swiglu)
+    full_down = own_down
+    for part, owner in ((near_down, core), (links.over_core(near_down), 1 - core)):
+        row = (1 - x) * height + owner * (height // 2)
+        full_down = lax.dynamic_update_slice(full_down, part, (row, 0))
     upstream = cotangent.reshape(total, width)
 
     def by_core(values, blocks):

time: 513 us -> 502 us (0.979)
  waiting for transfers between devices: 168 us -> 151 us
    ppermute x9, waiting for transfers between devices: 42.6 us -> 23.5 us  [over_x(): return lax.ppermute(value, 'shard', [(0, 1), (1, 0)])]
    dynamic_update_slice x0 -> x3, local copies, waits for them, and re-layouts: none -> 9.26 us  [the longest x2 5.44 us: local_linked(): full_down = lax.dynamic_update_slice(full_down, part, (row, 0))]
    dynamic_update_slice x7 -> x6, local copies, waits for them, and re-layouts: 16.9 us -> 13.1 us  [assemble(): full = lax.dynamic_update_slice(full, w, (x * height, place))]
    dynamic_update_slice x8 -> x6, local copies, waits for them, and re-layouts: 15.4 us -> 12.7 us  [assemble(): lax.dynamic_update_slice(full, part, ((1 - x) * height + owner * half, 0))]
    unnamed x155 -> x157, local copies, waits for them, and re-layouts: 17.4 us -> 16.6 us
  transfers between devices with their start and end apart: 49 -> 49, of which waited for: 24 -> 22; matrix products, arithmetic and copies ran while one was open for 32% -> 35% of each run, Pallas kernels for 11% -> 12%
where the time goes in v6:
time: 502 us; the launch traced here: 493 us
  waiting for transfers between devices  151 us (30%)
  local copies, waits for them, and re-layouts  85.9 us (17%)
  Pallas kernels  66.6 us (13%)
  starting transfers between devices  66.4 us (13%)
  matrix products  57.6 us (11%)
  other arithmetic  50.1 us (10%)
  between operations  15.7 us (3%)
    ppermute x6, waiting for transfers between devices, over_far(): return lax.ppermute(value, 'rep', self.to_far)  61.3 us
    dot_general x17, matrix products, dot(): lax.dot_general(left, right, ((contract[:1], contract[1:]), ((), ())), pr...  57.6 us
    all_to_all x2, waiting for transfers between devices, to_heads(): return lax.all_to_all(chunks, 'rep', 0, 0, tiled=True)  28.7 us
    pallas_call x1, Pallas kernels, attend_back(): pl.pallas_call(functools.partial(attend_back_kernel, head_dim, bq, bk), o...  24 us
    ppermute x9, waiting for transfers between devices, over_x(): return lax.ppermute(value, 'shard', [(0, 1), (1, 0)])  23.5 us
    ppermute x6, waiting for transfers between devices, over_pair(): return lax.ppermute(value, 'rep', self.to_pair)  23.2 us
    pallas_call x1, Pallas kernels, attend(): pl.pallas_call(functools.partial(attend_kernel, head_dim, bq, bk), out_sh...  17.9 us
    pallas_call x2, Pallas kernels, finish(): pl.pallas_call(functools.partial(finish_kernel, count, ff), out_shape=tup...  16.8 us
  transfers between devices with their start and end apart: 49, of which 22 were waited for; matrix products, arithmetic and copies ran while one was open for 35% of the time, Pallas kernels for 12%

profile of v6, /device:TPU:0, one launch (start us, length us, event | category | flops | bytes accessed | tf_op | source)
XLA Modules:
  0.0 493.3 jit_solution(1288055593831002422)
XLA Ops:
  8.6 3.0 collective-permute-start
  16.7 3.1 collective-permute-start.1
  19.8 5.6 %fusion.17 = (f32[2048,128]{1,0:T(8,128)}, f32[2048,128]{1,0:T(8,128)}) fusion(f32[128]{0:T(128)S(1)} %get-tuple-element.243, f32[128]{0:T(128)S(1)} %get-tuple-element.244, f32[2048]{0:T(1024)S(1)} %iota_convert_fusion), kind=kLoop, calls=%fused_computation.57 | loop fusion | flops 524288 | bytes 2106368 | tf_op jit(solution)/shard_map/mul | solution.py:40
  25.4 5.8 %collective-permute-done.1 = bf16[128,1024]{1,0:T(8,128)(2,1)S(1)} collective-permute-done((bf16[128,1024]{1,0:T(8,128)(2,1)S(1)}, bf16[128,1024]{1,0:T(8,128)(2,1)S(1)}, u32[]{:S(2)}, u32[]{:S(2)}) %collective-permute-start.1) | collective-permute-done | bytes 262176 | tf_op jit(solution)/shard_map/ppermute | solution.py:236
  40.8 10.7 %collective-permute-done.2 = bf16[256,3072]{1,0:T(8,128)(2,1)} collective-permute-done((bf16[256,3072]{1,0:T(8,128)(2,1)}, bf16[256,3072]{1,0:T(8,128)(2,1)}, u32[]{:S(2)}, u32[]{:S(2)}) %collective-permute-start.2) | collective-permute-done | bytes 1572896 | tf_op jit(solution)/shard_map/ppermute | solution.py:227
  64.1 2.8 copy.40
  66.9 6.6 %all-to-all-start = ((bf16[16,128,384]{1,2,0:T(8,128)(2,1)}), bf16[16,128,384]{1,2,0:T(8,128)(2,1)}, u32[]{:S(2)}, u32[]{:S(2)}) async-start(bf16[16,128,384]{1,2,0:T(8,128)(2,1)} %bitcast.221), calls=%async_computation | async-start | bytes 3145728 | tf_op jit(solution)/shard_map/all_to_all | solution.py:481
  76.7 28.7 %all-to-all-done = bf16[16,128,384]{1,2,0:T(8,128)(2,1)} async-done(((bf16[16,128,384]{1,2,0:T(8,128)(2,1)}), bf16[16,128,384]{1,2,0:T(8,128)(2,1)}, u32[]{:S(2)}, u32[]{:S(2)}) %all-to-all-start) | async-done | bytes 1572896 | tf_op jit(solution)/shard_map/all_to_all | solution.py:481
  108.0 17.9 %shard_map.221 = (bf16[2048,128]{1,0:T(8,128)(2,1)}, f32[128,2048]{1,0:T(8,128)}, f32[2,2048]{1,0:T(2,128)}) custom-call(s32[1]{0:T(128)} %dynamic_slice.126.prefix_ref, bf16[2048,384]{1,0:T(8,128)(2,1)} %bitcast.200, bf16[2048,384]{1,0:T(8,128)(2,1)} %bitcast.201, bf16[2048,384]{1,0:T(8,128)(2,1)} %bitcast.202), custom_call_target="tpu_custom_call" | custom-call | flops 1 | bytes 1 | tf_op jit(solution)/shard_map/pallas_call | solution.py:298
  125.9 5.8 %collective-permute-done.4 = bf16[256,6656]{1,0:T(8,128)(2,1)} collective-permute-done((bf16[256,6656]{1,0:T(8,128)(2,1)}, bf16[256,6656]{1,0:T(8,128)(2,1)}, u32[]{:S(2)}, u32[]{:S(2)}) %collective-permute-start.4) | collective-permute-done | bytes 3407904 | tf_op jit(solution)/shard_map/ppermute | solution.py:227
  134.0 3.8 constant_dynamic-update-slice_fusion.4
  141.4 6.0 %all-to-all-start.1 = ((bf16[16,128,128]{2,1,0:T(8,128)(2,1)}), bf16[16,128,128]{2,1,0:T(8,128)(2,1)S(1)}, u32[]{:S(2)}, u32[]{:S(2)}) async-start(bf16[16,128,128]{2,1,0:T(8,128)(2,1)} %bitcast.257), calls=%async_computation.1 | async-start | bytes 1048576 | tf_op jit(solution)/shard_map/all_to_all | solution.py:484
  150.0 3.8 slice_dynamic-update-slice_fusion.1
  153.8 7.9 %all-to-all-done.1 = bf16[16,128,128]{2,1,0:T(8,128)(2,1)S(1)} async-done(((bf16[16,128,128]{2,1,0:T(8,128)(2,1)}), bf16[16,128,128]{2,1,0:T(8,128)(2,1)S(1)}, u32[]{:S(2)}, u32[]{:S(2)}) %all-to-all-start.1) | async-done | bytes 524320 | tf_op jit(solution)/shard_map/all_to_all | solution.py:484
  166.6 3.9 slice_dynamic-update-slice_fusion
  170.5 6.2 %fusion.74 = f32[256,5632]{1,0:T(8,128)S(1)} fusion(bf16[256,1024]{1,0:T(8,128)(2,1)S(1)} %multiply_convert_fusion.3, bf16[1024,5632]{1,0:T(8,128)(2,1)} %slice_dynamic-update-slice_fusion), kind=kOutput, calls=%fused_computation.206 | convolution fusion | flops 2952790016 | bytes 17825792 | tf_op jit(solution)/shard_map/dot_general | solution.py:20
  181.7 2.6 convolution_convert_fusion.1
  184.8 2.7 constant_dynamic-update-slice_fusion.1
  187.6 2.7 constant_dynamic-update-slice_fusion
  190.3 5.2 %multiply_convert_fusion = (bf16[256,2816]{1,0:T(8,128)(2,1)S(1)}, bf16[256,2816]{1,0:T(8,128)(2,1)S(1)}) fusion(f32[256,5632]{1,0:T(8,128)S(1)} %copy-done.6, bf16[2816,1024]{1,0:T(8,128)(2,1)} %constant_dynamic-update-slice_fusion, bf16[256,1024]{1,0:T(8,128)(2,1)S(1)} %bitcast.231), kind=kOutput, calls=%fused_computation.21 | convolution fusion | flops 1485766656 | bytes 14942208 | tf_op jit(solution)/shard_map/dot_general | solution.py:20
  198.1 2.8 add_convert_fusion.2
  206.8 3.5 add_convert_fusion.1
  213.6 3.1 add_convert_fusion
  219.5 6.5 %multiply_reduce_fusion.1 = (f32[256]{0:T(256)S(1)}, f32[256,1024]{1,0:T(8,128)}) fusion(f32[256,1024]{1,0:T(8,128)} %get-tuple-element.236, f32[256]{0:T(256)S(1)} %add_rsqrt_fusion, f32[1024]{0:T(1024)S(1)} %bitcast.262, bf16[1024,5632]{1,0:T(8,128)(2,1)S(1)} %bitcast.207, bf16[256,2816]{1,0:T(8,128)(2,1)} %copy-done.25, bf16[256,2816]{1,0:T(8,128)(2,1)} %copy-done.27), kind=kOutput, calls=%fused_computation.74 | convolution fusion | flops 2959605504 | bytes 16521216 | tf_op jit(solution)/shard_map/dot_general | solution.py:20
  231.7 5.8 %all-to-all-start.2 = ((bf16[16,128,128]{2,1,0:T(8,128)(2,1)}), bf16[16,128,128]{2,1,0:T(8,128)(2,1)S(1)}, u32[]{:S(2)}, u32[]{:S(2)}) async-start(bf16[16,128,128]{2,1,0:T(8,128)(2,1)} %bitcast.26), calls=%async_computation.2 | async-start | bytes 1048576 | tf_op jit(solution)/shard_map/all_to_all | solution.py:481
  247.3 5.4 %fusion.16 = bf16[256,1024]{1,0:T(8,128)(2,1)} fusion(f32[256,1024]{1,0:T(8,128)} %get-tuple-element.236, bf16[256,2816]{1,0:T(8,128)(2,1)S(1)} %multiply_convert_fusion.2, bf16[2816,1024]{1,0:T(8,128)(2,1)} %constant_dynamic-update-slice_fusion), kind=kOutput, calls=%fused_computation.55 | convolution fusion | flops 1476919296 | bytes 8781824 | tf_op jit(solution)/shard_map/dot_general | solution.py:20
  254.4 24.0 %shard_map.225 = bf16[2048,384]{1,0:T(8,128)(2,1)} custom-call(s32[1]{0:T(128)} %dynamic_slice.126.prefix_ref, bf16[2048,384]{1,0:T(8,128)(2,1)} %bitcast.203, bf16[2048,384]{1,0:T(8,128)(2,1)} %bitcast.204, bf16[2048,384]{1,0:T(8,128)(2,1)} %bitcast.205, bf16[2048,128]{1,0:T(8,128)(2,1)} %bitcast.240, f32[128,2048]{1,0:T(8,128)} %get-tuple-element.143.att_t_ref, ...), custom_call_target="tpu_custom_call" | custom-call | flops 1 | bytes 1 | tf_op jit(solution)/shard_map/pallas_call | solution.py:323
  278.5 4.6 collective-permute-done.14
  283.0 5.0 %convolution_convert_fusion.4 = bf16[1024,384]{1,0:T(8,128)(2,1)S(1)} fusion(bf16[2048,1024]{1,0:T(8,128)(2,1)} %bitcast.263, bf16[2048,384]{1,0:T(8,128)(2,1)} %shard_map.225), kind=kOutput, calls=%fused_computation.50 | convolution fusion | flops 1611005952 | bytes 6553600 | tf_op jit(solution)/shard_map/dot_general | solution.py:20
  311.5 5.6 %all-to-all-start.3 = ((bf16[16,128,384]{1,2,0:T(8,128)(2,1)}), bf16[16,128,384]{1,2,0:T(8,128)(2,1)S(1)}, u32[]{:S(2)}, u32[]{:S(2)}) async-start(bf16[16,128,384]{1,2,0:T(8,128)(2,1)} %copy.45), calls=%async_computation.3 | async-start | bytes 3145728 | tf_op jit(solution)/shard_map/all_to_all | solution.py:484
  317.1 3.1 collective-permute-done.23
  321.3 11.3 %collective-permute-done.22 = bf16[176,512]{1,0:T(8,128)(2,1)} collective-permute-done((bf16[176,512]{1,0:T(8,128)(2,1)}, bf16[176,512]{1,0:T(8,128)(2,1)}, u32[]{:S(2)}, u32[]{:S(2)}) %collective-permute-start.22) | collective-permute-done | bytes 180256 | tf_op jit(solution)/shard_map/ppermute | solution.py:236
  339.0 2.9 collective-permute-start.26
  342.0 24.1 %collective-permute-done.25 = bf16[176,512]{1,0:T(8,128)(2,1)} collective-permute-done((bf16[176,512]{1,0:T(8,128)(2,1)}, bf16[176,512]{1,0:T(8,128)(2,1)}, u32[]{:S(2)}, u32[]{:S(2)}) %collective-permute-start.25) | collective-permute-done | bytes 180256 | tf_op jit(solution)/shard_map/ppermute | solution.py:236
  371.8 3.1 collective-permute-done.24
  382.7 2.7 collective-permute-start.28
  385.5 3.3 collective-permute-start.29
  388.7 4.7 multiply_reduce_fusion
  393.5 2.8 multiply_add_fusion
  399.8 3.7 collective-permute-done.27
  403.7 3.6 collective-permute-start.31
  409.7 14.4 %collective-permute-done.30 = bf16[32,6656]{1,0:T(8,128)(2,1)S(1)} collective-permute-done((bf16[32,6656]{1,0:T(8,128)(2,1)S(1)}, bf16[32,6656]{1,0:T(8,128)(2,1)S(1)}, u32[]{:S(2)}, u32[]{:S(2)}) %collective-permute-start.30) | collective-permute-done | bytes 426016 | tf_op jit(solution)/shard_map/ppermute | solution.py:236
  424.9 11.0 %collective-permute-done.32 = bf16[1024,384]{1,0:T(8,128)(2,1)S(1)} collective-permute-done((bf16[1024,384]{1,0:T(8,128)(2,1)S(1)}, bf16[1024,384]{1,0:T(8,128)(2,1)S(1)}, u32[]{:S(2)}, u32[]{:S(2)}) %collective-permute-start.32) | collective-permute-done | bytes 786464 | tf_op jit(solution)/shard_map/ppermute | solution.py:233
  439.6 3.0 fusion.4
  443.7 7.9 %shard_map.226 = (f32[512,1024]{1,0:T(8,128)}, f32[512,1024]{1,0:T(8,128)}, f32[512,1024]{1,0:T(8,128)}, f32[512,128]{1,0:T(8,128)}) custom-call(s32[1]{0:T(128)} %bitcast.71.core_ref, bf16[2,2,2,256,384]{4,3,2,1,0:T(8,128)(2,1)} %bitcast.223, bf16[2,2,2,256,384]{4,3,2,1,0:T(8,128)(2,1)} %bitcast.246, bf16[512,1024]{1,0:T(8,128)(2,1)} %wq_ref.1, ...), custom_call_target="tpu_custom_call" | custom-call | flops 1 | bytes 1 | tf_op jit(solution)/shard_map/pallas_call | solution.py:370
  451.6 6.2 %collective-permute-done.33.refs_2_ = bf16[64,6656]{1,0:T(8,128)(2,1)S(1)} collective-permute-done((bf16[64,6656]{1,0:T(8,128)(2,1)S(1)}, bf16[64,6656]{1,0:T(8,128)(2,1)S(1)}, u32[]{:S(2)}, u32[]{:S(2)}) %collective-permute-start.33) | collective-permute-done | bytes 852000 | tf_op jit(solution)/shard_map/ppermute | solution.py:233
  464.0 10.4 %shard_map.227 = (f32[512,2816]{1,0:T(8,128)}, f32[512,2816]{1,0:T(8,128)}, f32[512,1024]{1,0:T(8,128)}, f32[512,128]{1,0:T(8,128)}) custom-call(s32[6]{0:T(128)} %stack.51.slots_ref, bf16[64,6656]{1,0:T(8,128)(2,1)} %copy-done.36, bf16[64,6656]{1,0:T(8,128)(2,1)} %collective-permute-done.39.refs_1_, bf16[64,6656]{1,0:T(8,128)(2,1)} %copy-done.50, ...), custom_call_target="tpu_custom_call" | custom-call | flops 1 | bytes 1 | tf_op jit(solution)/shard_map/pallas_call | solution.py:437
  478.0 6.4 %shard_map.228 = (f32[512,2816]{1,0:T(8,128)}, f32[512,2816]{1,0:T(8,128)}, f32[512,1024]{1,0:T(8,128)}, f32[512,128]{1,0:T(8,128)}) custom-call(s32[4]{0:T(128)} %pad_add_fusion.slots_ref, bf16[32,6656]{1,0:T(8,128)(2,1)} %collective-permute-done.37.refs_0_, ...), custom_call_target="tpu_custom_call", output_to_operand_aliasing={{0}: (7, {}), {1}: (8, {}), {2}: (9, {}), {3}: (10, {})} | custom-call | flops 1 | bytes 1 | tf_op jit(solution)/shard_map/pallas_call | solution.py:437
  (345 shorter events, 151.7 us)
Async XLA Ops:
  7.2 100.9 %all-gather.2.cloned.1.call-start = ((), (), s32[]{:S(2)}) async-start(), calls=%async_computation.4 | async-start | bytes 4718592 | tf_op jit(solution)/shard_map/all_gather | solution.py:706
  8.6 7.0 %collective-permute-start = (bf16[2,512]{1,0:T(2,128)(2,1)S(1)}, bf16[2,512]{1,0:T(2,128)(2,1)S(1)}, u32[]{:S(2)}, u32[]{:S(2)}) collective-permute-start(bf16[2,512]{1,0:T(2,128)(2,1)S(1)} %pad_maximum_fusion.11), channel_id=1, source_target_pairs={{0,1},{1,0},{2,3},{3,2},{4,5},{5,4},{6,7},{7,6},{8,9},{9,8},{10,11... | collective-permute-start | bytes 6152 | tf_op jit(solution)/shard_map/ppermute | solution.py:227
  15.3 36.2 %collective-permute-start.2 = (bf16[256,3072]{1,0:T(8,128)(2,1)}, bf16[256,3072]{1,0:T(8,128)(2,1)}, u32[]{:S(2)}, u32[]{:S(2)}) collective-permute-start(bf16[256,3072]{1,0:T(8,128)(2,1)} %pad_maximum_fusion.2), channel_id=1, source_target_pairs={{0,1},{1,0},{2,3},{3,2},{4,5},{5,4},{6,7},{7,6},{8,9},{9,8},{10,11... | collective-permute-start | bytes 4718600 | tf_op jit(solution)/shard_map/ppermute | solution.py:227
  16.7 14.5 %collective-permute-start.1 = (bf16[128,1024]{1,0:T(8,128)(2,1)S(1)}, bf16[128,1024]{1,0:T(8,128)(2,1)S(1)}, u32[]{:S(2)}, u32[]{:S(2)}) collective-permute-start(bf16[128,1024]{1,0:T(8,128)(2,1)S(1)} %get-tuple-element.228), channel_id=1, source_target_pairs={{0,16},{2,18},{4,20},{6,22},{8,24},{10,26},{12,28},{14,30},{16,0},... | collective-permute-start | bytes 786440 | tf_op jit(solution)/shard_map/ppermute | solution.py:236
  51.5 5.8 %collective-permute-start.3 = (bf16[256,3072]{1,0:T(8,128)(2,1)}, bf16[256,3072]{1,0:T(8,128)(2,1)S(1)}, u32[]{:S(2)}, u32[]{:S(2)}) collective-permute-start(bf16[256,3072]{1,0:T(8,128)(2,1)} %collective-permute-done.2), channel_id=1, source_target_pairs={{0,2},{2,0},{4,6},{6,4},{8,10},{10,8},{12,14},{14,12},{16,18},{18,... | collective-permute-start | bytes 4718600 | tf_op jit(solution)/shard_map/ppermute | solution.py:224
  55.3 76.4 %collective-permute-start.4 = (bf16[256,6656]{1,0:T(8,128)(2,1)}, bf16[256,6656]{1,0:T(8,128)(2,1)}, u32[]{:S(2)}, u32[]{:S(2)}) collective-permute-start(bf16[256,6656]{1,0:T(8,128)(2,1)} %pad_maximum_fusion), channel_id=1, source_target_pairs={{0,1},{1,0},{2,3},{3,2},{4,5},{5,4},{6,7},{7,6},{8,9},{9,8},{10,11... | collective-permute-start | bytes 10223624 | tf_op jit(solution)/shard_map/ppermute | solution.py:227
  66.9 38.5 %all-to-all-start = ((bf16[16,128,384]{1,2,0:T(8,128)(2,1)}), bf16[16,128,384]{1,2,0:T(8,128)(2,1)}, u32[]{:S(2)}, u32[]{:S(2)}) async-start(bf16[16,128,384]{1,2,0:T(8,128)(2,1)} %bitcast.221), calls=%async_computation | async-start | bytes 3145728 | tf_op jit(solution)/shard_map/all_to_all | solution.py:481
  131.7 30.5 %collective-permute-start.5 = (bf16[256,6656]{1,0:T(8,128)(2,1)}, bf16[256,6656]{1,0:T(8,128)(2,1)}, u32[]{:S(2)}, u32[]{:S(2)}) collective-permute-start(bf16[256,6656]{1,0:T(8,128)(2,1)} %collective-permute-done.4), channel_id=1, source_target_pairs={{0,2},{2,0},{4,6},{6,4},{8,10},{10,8},{12,14},{14,12},{16,18},{18,... | collective-permute-start | bytes 10223624 | tf_op jit(solution)/shard_map/ppermute | solution.py:224
  141.4 20.3 %all-to-all-start.1 = ((bf16[16,128,128]{2,1,0:T(8,128)(2,1)}), bf16[16,128,128]{2,1,0:T(8,128)(2,1)S(1)}, u32[]{:S(2)}, u32[]{:S(2)}) async-start(bf16[16,128,128]{2,1,0:T(8,128)(2,1)} %bitcast.257), calls=%async_computation.1 | async-start | bytes 1048576 | tf_op jit(solution)/shard_map/all_to_all | solution.py:484
  147.5 34.2 %collective-permute-start.6 = (bf16[704,1024]{1,0:T(8,128)(2,1)}, bf16[704,1024]{1,0:T(8,128)(2,1)}, u32[]{:S(2)}, u32[]{:S(2)}) collective-permute-start(bf16[704,1024]{1,0:T(8,128)(2,1)} %constant_dynamic-slice_fusion.3), channel_id=1, source_target_pairs={{0,1},{1,0},{2,3},{3,2},{4,5},{5,4},{6,7},{7,6},{8,9},{9,8},{10,11... | collective-permute-start | bytes 4325384 | tf_op jit(solution)/shard_map/ppermute | solution.py:227
  181.7 5.9 %collective-permute-start.7 = (bf16[704,1024]{1,0:T(8,128)(2,1)}, bf16[704,1024]{1,0:T(8,128)(2,1)}, u32[]{:S(2)}, u32[]{:S(2)}) collective-permute-start(bf16[704,1024]{1,0:T(8,128)(2,1)} %collective-permute-done.6), channel_id=1, source_target_pairs={{0,2},{2,0},{4,6},{6,4},{8,10},{10,8},{12,14},{14,12},{16,18},{18,... | collective-permute-start | bytes 4325384 | tf_op jit(solution)/shard_map/ppermute | solution.py:224
  184.3 13.8 %collective-permute-start.8 = (bf16[2816,512]{1,0:T(8,128)(2,1)}, bf16[2816,512]{1,0:T(8,128)(2,1)}, u32[]{:S(2)}, u32[]{:S(2)}) collective-permute-start(bf16[2816,512]{1,0:T(8,128)(2,1)} %convolution_convert_fusion.1), channel_id=1, source_target_pairs={{0,2},{2,0},{4,6},{6,4},{8,10},{10,8},{12,14},{14,12},{16,18},{18,... | collective-permute-start | bytes 8650760 | tf_op jit(solution)/shard_map/ppermute | solution.py:224
  198.1 8.6 %collective-permute-start.9 = (bf16[512,2816]{1,0:T(8,128)(2,1)}, bf16[512,2816]{1,0:T(8,128)(2,1)}, u32[]{:S(2)}, u32[]{:S(2)}) collective-permute-start(bf16[512,2816]{1,0:T(8,128)(2,1)} %convolution_convert_fusion.2), channel_id=1, source_target_pairs={{0,2},{2,0},{4,6},{6,4},{8,10},{10,8},{12,14},{14,12},{16,18},{18,... | collective-permute-start | bytes 8650760 | tf_op jit(solution)/shard_map/ppermute | solution.py:224
  204.8 8.2 %collective-permute-start.10 = (bf16[512,2816]{1,0:T(8,128)(2,1)}, bf16[512,2816]{1,0:T(8,128)(2,1)}, u32[]{:S(2)}, u32[]{:S(2)}) collective-permute-start(bf16[512,2816]{1,0:T(8,128)(2,1)} %convolution_convert_fusion), channel_id=1, source_target_pairs={{0,2},{2,0},{4,6},{6,4},{8,10},{10,8},{12,14},{14,12},{16,18},{18,... | collective-permute-start | bytes 8650760 | tf_op jit(solution)/shard_map/ppermute | solution.py:224
  206.1 34.7 %collective-permute-start.12 = (bf16[1408,512]{1,0:T(8,128)(2,1)}, bf16[1408,512]{1,0:T(8,128)(2,1)}, u32[]{:S(2)}, u32[]{:S(2)}) collective-permute-start(bf16[1408,512]{1,0:T(8,128)(2,1)} %dynamic-slice_bitcast_fusion.1), channel_id=1, source_target_pairs={{0,1},{1,0},{2,3},{3,2},{4,5},{5,4},{6,7},{7,6},{8,9},{9,8},{10,11... | collective-permute-start | bytes 4325384 | tf_op jit(solution)/shard_map/ppermute | solution.py:227
  230.7 8.4 %collective-permute-start.11 = (bf16[512,1024]{1,0:T(8,128)(2,1)}, bf16[512,1024]{1,0:T(8,128)(2,1)}, u32[]{:S(2)}, u32[]{:S(2)}) collective-permute-start(bf16[512,1024]{1,0:T(8,128)(2,1)} %convolution_convert_fusion.3), channel_id=1, source_target_pairs={{0,2},{2,0},{4,6},{6,4},{8,10},{10,8},{12,14},{14,12},{16,18},{18,... | collective-permute-start | bytes 3145736 | tf_op jit(solution)/shard_map/ppermute | solution.py:224
  231.7 21.1 %all-to-all-start.2 = ((bf16[16,128,128]{2,1,0:T(8,128)(2,1)}), bf16[16,128,128]{2,1,0:T(8,128)(2,1)S(1)}, u32[]{:S(2)}, u32[]{:S(2)}) async-start(bf16[16,128,128]{2,1,0:T(8,128)(2,1)} %bitcast.26), calls=%async_computation.2 | async-start | bytes 1048576 | tf_op jit(solution)/shard_map/all_to_all | solution.py:481
  237.5 40.9 %collective-permute-start.13 = (bf16[256,2816]{1,0:T(8,128)(2,1)}, bf16[256,2816]{1,0:T(8,128)(2,1)}, u32[]{:S(2)}, u32[]{:S(2)}) collective-permute-start(bf16[256,2816]{1,0:T(8,128)(2,1)} %dynamic-slice_bitcast_fusion), channel_id=1, source_target_pairs={{0,1},{1,0},{2,3},{3,2},{4,5},{5,4},{6,7},{7,6},{8,9},{9,8},{10,11... | collective-permute-start | bytes 4325384 | tf_op jit(solution)/shard_map/ppermute | solution.py:227
  241.7 41.3 %collective-permute-start.14 = (bf16[256,1024]{1,0:T(8,128)(2,1)}, bf16[256,1024]{1,0:T(8,128)(2,1)}, u32[]{:S(2)}, u32[]{:S(2)}) collective-permute-start(bf16[256,1024]{1,0:T(8,128)(2,1)} %dynamic-slice_bitcast_fusion.6), channel_id=1, source_target_pairs={{0,1},{1,0},{2,3},{3,2},{4,5},{5,4},{6,7},{7,6},{8,9},{9,8},{10,11... | collective-permute-start | bytes 1572872 | tf_op jit(solution)/shard_map/ppermute | solution.py:227
  245.3 37.7 %collective-permute-start.15 = (bf16[704,512]{1,0:T(8,128)(2,1)}, bf16[704,512]{1,0:T(8,128)(2,1)}, u32[]{:S(2)}, u32[]{:S(2)}) collective-permute-start(bf16[704,512]{1,0:T(8,128)(2,1)} %dynamic-slice_bitcast_fusion.5), channel_id=1, source_target_pairs={{0,4},{2,6},{4,0},{6,2},{8,12},{10,14},{12,8},{14,10},{16,20},{18,... | collective-permute-start | bytes 2162696 | tf_op jit(solution)/shard_map/ppermute | solution.py:230
  254.2 46.5 %collective-permute-start.18 = (bf16[256,2816]{1,0:T(8,128)(2,1)S(1)}, bf16[256,2816]{1,0:T(8,128)(2,1)}, u32[]{:S(2)}, u32[]{:S(2)}) collective-permute-start(bf16[256,2816]{1,0:T(8,128)(2,1)S(1)} %bitcast.247), channel_id=1, source_target_pairs={{0,4},{2,6},{4,0},{6,2},{8,12},{10,14},{12,8},{14,10},{16,20},{18,... | collective-permute-start | bytes 4325384 | tf_op jit(solution)/shard_map/ppermute | solution.py:230
  288.1 12.5 %collective-permute-start.16 = (bf16[512,384]{1,0:T(8,128)(2,1)S(1)}, bf16[512,384]{1,0:T(8,128)(2,1)S(1)}, u32[]{:S(2)}, u32[]{:S(2)}) collective-permute-start(bf16[512,384]{1,0:T(8,128)(2,1)S(1)} %dynamic-slice_bitcast_fusion.8), channel_id=1, source_target_pairs={{0,1},{1,0},{2,3},{3,2},{4,5},{5,4},{6,7},{7,6},{8,9},{9,8},{10,11... | collective-permute-start | bytes 1179656 | tf_op jit(solution)/shard_map/ppermute | solution.py:227
  291.0 9.7 %collective-permute-start.17 = (bf16[352,512]{1,0:T(8,128)(2,1)S(1)}, bf16[352,512]{1,0:T(8,128)(2,1)S(1)}, u32[]{:S(2)}, u32[]{:S(2)}) collective-permute-start(bf16[352,512]{1,0:T(8,128)(2,1)S(1)} %dynamic-slice_bitcast_fusion.9), channel_id=1, source_target_pairs={{0,8},{2,10},{4,12},{6,14},{8,0},{10,2},{12,4},{14,6},{16,24},{18,... | collective-permute-start | bytes 1081352 | tf_op jit(solution)/shard_map/ppermute | solution.py:233
  295.5 25.7 %collective-permute-start.20 = (bf16[128,2816]{1,0:T(8,128)(2,1)}, bf16[128,2816]{1,0:T(8,128)(2,1)}, u32[]{:S(2)}, u32[]{:S(2)}) collective-permute-start(bf16[128,2816]{1,0:T(8,128)(2,1)} %dynamic-slice_bitcast_fusion.3), channel_id=1, source_target_pairs={{0,4},{2,6},{4,0},{6,2},{8,12},{10,14},{12,8},{14,10},{16,20},{18,... | collective-permute-start | bytes 2162696 | tf_op jit(solution)/shard_map/ppermute | solution.py:230
  299.1 22.2 %collective-permute-start.21 = (bf16[128,1024]{1,0:T(8,128)(2,1)}, bf16[128,1024]{1,0:T(8,128)(2,1)}, u32[]{:S(2)}, u32[]{:S(2)}) collective-permute-start(bf16[128,1024]{1,0:T(8,128)(2,1)} %dynamic-slice_bitcast_fusion.10), channel_id=1, source_target_pairs={{0,4},{2,6},{4,0},{6,2},{8,12},{10,14},{12,8},{14,10},{16,20},{18,... | collective-permute-start | bytes 786440 | tf_op jit(solution)/shard_map/ppermute | solution.py:230
  304.4 28.2 %collective-permute-start.19 = (bf16[128,2816]{1,0:T(8,128)(2,1)}, bf16[128,2816]{1,0:T(8,128)(2,1)}, u32[]{:S(2)}, u32[]{:S(2)}) collective-permute-start(bf16[128,2816]{1,0:T(8,128)(2,1)} %dynamic-slice_bitcast_fusion.4), channel_id=1, source_target_pairs={{0,1},{1,0},{2,3},{3,2},{4,5},{5,4},{6,7},{7,6},{8,9},{9,8},{10,11... | collective-permute-start | bytes 2162696 | tf_op jit(solution)/shard_map/ppermute | solution.py:227
  305.3 14.8 %collective-permute-start.23 = (bf16[256,384]{1,0:T(8,128)(2,1)S(1)}, bf16[256,384]{1,0:T(8,128)(2,1)}, u32[]{:S(2)}, u32[]{:S(2)}) collective-permute-start(bf16[256,384]{1,0:T(8,128)(2,1)S(1)} %constant_dynamic-slice_fusion), channel_id=1, source_target_pairs={{0,16},{2,18},{4,20},{6,22},{8,24},{10,26},{12,28},{14,30},{16,0},... | collective-permute-start | bytes 589832 | tf_op jit(solution)/shard_map/ppermute | solution.py:520
  309.2 23.4 %collective-permute-start.22 = (bf16[176,512]{1,0:T(8,128)(2,1)}, bf16[176,512]{1,0:T(8,128)(2,1)}, u32[]{:S(2)}, u32[]{:S(2)}) collective-permute-start(bf16[176,512]{1,0:T(8,128)(2,1)} %dynamic-slice_bitcast_fusion.12), channel_id=1, source_target_pairs={{0,16},{2,18},{4,20},{6,22},{8,24},{10,26},{12,28},{14,30},{16,0},... | collective-permute-start | bytes 540680 | tf_op jit(solution)/shard_map/ppermute | solution.py:236
  311.5 65.7 %all-to-all-start.3 = ((bf16[16,128,384]{1,2,0:T(8,128)(2,1)}), bf16[16,128,384]{1,2,0:T(8,128)(2,1)S(1)}, u32[]{:S(2)}, u32[]{:S(2)}) async-start(bf16[16,128,384]{1,2,0:T(8,128)(2,1)} %copy.45), calls=%async_computation.3 | async-start | bytes 3145728 | tf_op jit(solution)/shard_map/all_to_all | solution.py:484
  339.0 35.9 %collective-permute-start.24 = (bf16[64,6656]{1,0:T(8,128)(2,1)}, bf16[64,6656]{1,0:T(8,128)(2,1)}, u32[]{:S(2)}, u32[]{:S(2)}) collective-permute-start(bf16[64,6656]{1,0:T(8,128)(2,1)} %dynamic-slice_bitcast_fusion.2), channel_id=1, source_target_pairs={{0,8},{2,10},{4,12},{6,14},{8,0},{10,2},{12,4},{14,6},{16,24},{18,... | collective-permute-start | bytes 2555912 | tf_op jit(solution)/shard_map/ppermute | solution.py:233
  339.0 27.0 %collective-permute-start.25 = (bf16[176,512]{1,0:T(8,128)(2,1)}, bf16[176,512]{1,0:T(8,128)(2,1)}, u32[]{:S(2)}, u32[]{:S(2)}) collective-permute-start(bf16[176,512]{1,0:T(8,128)(2,1)} %fusion.31), channel_id=1, source_target_pairs={{0,16},{2,18},{4,20},{6,22},{8,24},{10,26},{12,28},{14,30},{16,0},... | collective-permute-start | bytes 540680 | tf_op jit(solution)/shard_map/ppermute | solution.py:236
  339.0 30.9 %collective-permute-start.26 = (bf16[256,384]{1,0:T(8,128)(2,1)S(1)}, bf16[256,384]{1,0:T(8,128)(2,1)}, u32[]{:S(2)}, u32[]{:S(2)}) collective-permute-start(bf16[256,384]{1,0:T(8,128)(2,1)S(1)} %add_convert_fusion.4), channel_id=1, source_target_pairs={{0,16},{2,18},{4,20},{6,22},{8,24},{10,26},{12,28},{14,30},{16,0},... | collective-permute-start | bytes 589832 | tf_op jit(solution)/shard_map/ppermute | solution.py:236
  381.6 21.9 %collective-permute-start.27 = (bf16[32,6656]{1,0:T(8,128)(2,1)S(1)}, bf16[32,6656]{1,0:T(8,128)(2,1)S(1)}, u32[]{:S(2)}, u32[]{:S(2)}) collective-permute-start(bf16[32,6656]{1,0:T(8,128)(2,1)S(1)} %dynamic-slice_bitcast_fusion.7), channel_id=1, source_target_pairs={{0,16},{2,18},{4,20},{6,22},{8,24},{10,26},{12,28},{14,30},{16,0},... | collective-permute-start | bytes 1277960 | tf_op jit(solution)/shard_map/ppermute | solution.py:236
  382.7 16.4 %collective-permute-start.28 = (bf16[352,512]{1,0:T(8,128)(2,1)}, bf16[352,512]{1,0:T(8,128)(2,1)S(1)}, u32[]{:S(2)}, u32[]{:S(2)}) collective-permute-start(bf16[352,512]{1,0:T(8,128)(2,1)} %maximum_select_fusion.10), channel_id=1, source_target_pairs={{0,8},{2,10},{4,12},{6,14},{8,0},{10,2},{12,4},{14,6},{16,24},{18,... | collective-permute-start | bytes 1081352 | tf_op jit(solution)/shard_map/ppermute | solution.py:233
  385.5 14.0 %collective-permute-start.29 = (bf16[512,384]{1,0:T(8,128)(2,1)S(1)}, bf16[512,384]{1,0:T(8,128)(2,1)S(1)}, u32[]{:S(2)}, u32[]{:S(2)}) collective-permute-start(bf16[512,384]{1,0:T(8,128)(2,1)S(1)} %copy-done.52), channel_id=1, source_target_pairs={{0,4},{2,6},{4,0},{6,2},{8,12},{10,14},{12,8},{14,10},{16,20},{18,... | collective-permute-start | bytes 1179656 | tf_op jit(solution)/shard_map/ppermute | solution.py:230
  403.6 20.5 %collective-permute-start.30 = (bf16[32,6656]{1,0:T(8,128)(2,1)S(1)}, bf16[32,6656]{1,0:T(8,128)(2,1)S(1)}, u32[]{:S(2)}, u32[]{:S(2)}) collective-permute-start(bf16[32,6656]{1,0:T(8,128)(2,1)S(1)} %fusion.26), channel_id=1, source_target_pairs={{0,16},{2,18},{4,20},{6,22},{8,24},{10,26},{12,28},{14,30},{16,0},... | collective-permute-start | bytes 1277960 | tf_op jit(solution)/shard_map/ppermute | solution.py:236
  403.7 20.5 %collective-permute-start.31 = (bf16[704,512]{1,0:T(8,128)(2,1)S(1)}, bf16[704,512]{1,0:T(8,128)(2,1)S(1)}, u32[]{:S(2)}, u32[]{:S(2)}) collective-permute-start(bf16[704,512]{1,0:T(8,128)(2,1)S(1)} %maximum_select_fusion.7), channel_id=1, source_target_pairs={{0,4},{2,6},{4,0},{6,2},{8,12},{10,14},{12,8},{14,10},{16,20},{18,... | collective-permute-start | bytes 2162696 | tf_op jit(solution)/shard_map/ppermute | solution.py:230
  407.3 28.5 %collective-permute-start.32 = (bf16[1024,384]{1,0:T(8,128)(2,1)S(1)}, bf16[1024,384]{1,0:T(8,128)(2,1)S(1)}, u32[]{:S(2)}, u32[]{:S(2)}) collective-permute-start(bf16[1024,384]{1,0:T(8,128)(2,1)S(1)} %maximum_select_fusion.6), channel_id=1, source_target_pairs={{0,8},{2,10},{4,12},{6,14},{8,0},{10,2},{12,4},{14,6},{16,24},{18,... | collective-permute-start | bytes 2359304 | tf_op jit(solution)/shard_map/ppermute | solution.py:233
  436.3 3.3 collective-permute-start.35
  436.4 6.2 %collective-permute-start.36 = (bf16[2048,384]{1,0:T(8,128)(2,1)S(1)}, bf16[2048,384]{1,0:T(8,128)(2,1)S(1)}, u32[]{:S(2)}, u32[]{:S(2)}) collective-permute-start(bf16[2048,384]{1,0:T(8,128)(2,1)S(1)} %maximum_select_fusion.1), channel_id=1, source_target_pairs={{0,2},{2,0},{4,6},{6,4},{8,10},{10,8},{12,14},{14,12},{16,18},{18,... | collective-permute-start | bytes 4718600 | tf_op jit(solution)/shard_map/ppermute | solution.py:224
  436.9 20.9 %collective-permute-start.33 = (bf16[64,6656]{1,0:T(8,128)(2,1)S(1)}, bf16[64,6656]{1,0:T(8,128)(2,1)S(1)}, u32[]{:S(2)}, u32[]{:S(2)}) collective-permute-start(bf16[64,6656]{1,0:T(8,128)(2,1)S(1)} %maximum_select_fusion.5.refs_0_), channel_id=1, source_target_pairs={{0,8},{2,10},{4,12},{6,14},{8,0},{10,2},{12,4},{14,6},{16,24},{18,... | collective-permute-start | bytes 2555912 | tf_op jit(solution)/shard_map/ppermute | solution.py:233
  436.9 21.0 %collective-permute-start.34 = (bf16[64,6656]{1,0:T(8,128)(2,1)S(1)}, bf16[64,6656]{1,0:T(8,128)(2,1)}, u32[]{:S(2)}, u32[]{:S(2)}) collective-permute-start(bf16[64,6656]{1,0:T(8,128)(2,1)S(1)} %maximum_select_fusion.5.refs_0_), channel_id=1, source_target_pairs={{0,4},{2,6},{4,0},{6,2},{8,12},{10,14},{12,8},{14,10},{16,20},{18,... | collective-permute-start | bytes 2555912 | tf_op jit(solution)/shard_map/ppermute | solution.py:230
  436.9 26.1 %collective-permute-start.39 = (bf16[64,6656]{1,0:T(8,128)(2,1)S(1)}, bf16[64,6656]{1,0:T(8,128)(2,1)}, u32[]{:S(2)}, u32[]{:S(2)}) collective-permute-start(bf16[64,6656]{1,0:T(8,128)(2,1)S(1)} %maximum_select_fusion.5.refs_0_), channel_id=1, source_target_pairs={{0,2},{2,0},{4,6},{6,4},{8,10},{10,8},{12,14},{14,12},{16,18},{18,... | collective-permute-start | bytes 2555912 | tf_op jit(solution)/shard_map/ppermute | solution.py:224
  457.9 5.1 %collective-permute-start.40 = (bf16[64,6656]{1,0:T(8,128)(2,1)S(1)}, bf16[64,6656]{1,0:T(8,128)(2,1)S(1)}, u32[]{:S(2)}, u32[]{:S(2)}) collective-permute-start(bf16[64,6656]{1,0:T(8,128)(2,1)S(1)} %collective-permute-done.33.refs_2_), channel_id=1, source_target_pairs={{0,2},{2,0},{4,6},{6,4},{8,10},{10,8},{12,14},{14,12},{16,18},{18,... | collective-permute-start | bytes 2555912 | tf_op jit(solution)/shard_map/ppermute | solution.py:224
  457.9 5.1 %collective-permute-start.41 = (bf16[64,6656]{1,0:T(8,128)(2,1)}, bf16[64,6656]{1,0:T(8,128)(2,1)}, u32[]{:S(2)}, u32[]{:S(2)}) collective-permute-start(bf16[64,6656]{1,0:T(8,128)(2,1)} %collective-permute-done.34.refs_3_), channel_id=1, source_target_pairs={{0,2},{2,0},{4,6},{6,4},{8,10},{10,8},{12,14},{14,12},{16,18},{18,... | collective-permute-start | bytes 2555912 | tf_op jit(solution)/shard_map/ppermute | solution.py:224
  460.3 14.1 %collective-permute-start.37 = (bf16[32,6656]{1,0:T(8,128)(2,1)}, bf16[32,6656]{1,0:T(8,128)(2,1)}, u32[]{:S(2)}, u32[]{:S(2)}) collective-permute-start(bf16[32,6656]{1,0:T(8,128)(2,1)} %slice.138), channel_id=1, source_target_pairs={{0,4},{2,6},{4,0},{6,2},{8,12},{10,14},{12,8},{14,10},{16,20},{18,... | collective-permute-start | bytes 1277960 | tf_op jit(solution)/shard_map/ppermute | solution.py:230
  460.7 13.7 %collective-permute-start.38 = (bf16[32,6656]{1,0:T(8,128)(2,1)S(1)}, bf16[32,6656]{1,0:T(8,128)(2,1)}, u32[]{:S(2)}, u32[]{:S(2)}) collective-permute-start(bf16[32,6656]{1,0:T(8,128)(2,1)S(1)} %slice.139), channel_id=1, source_target_pairs={{0,8},{2,10},{4,12},{6,14},{8,0},{10,2},{12,4},{14,6},{16,24},{18,... | collective-permute-start | bytes 1277960 | tf_op jit(solution)/shard_map/ppermute | solution.py:233
  474.5 2.6 collective-permute-start.43
  (78 other events, 494.8 us)
Sparse Core Ops, SparseCore 0:
  32.2 30.2 all-gather.1

commit v7 on v6

--- a/solution.py
+++ b/solution.py
@@ -848,7 +848,7 @@
     down_y = links.over_y(down_piece)
     down_piece = join(down_piece, down_y, links.y)
     part = join(joined_piece, joined_far, links.far)
-    part, down_piece, summed = fence(part, down_piece, summed)
+    part, down_piece = fence(part, down_piece)
 
     def slots(*bits):
         place = [
@@ -875,16 +875,22 @@
         layer.seqs,
         layer.groups,
     )
-    part_pair, part_y, grad_down, grad_wquery, grad_wkey, grad_wvalue = fence(
-        part_pair, part_y, grad_down, grad_wquery, grad_wkey, grad_wvalue
+    part_pair, part_y, grad_down, grad_wquery, grad_wkey, grad_wvalue, *filled = fence(
+        part_pair,
+        part_y,
+        grad_down,
+        grad_wquery,
+        grad_wkey,
+        grad_wvalue,
+        *finish(slots((0, 0, 0), (1, 0, 0)), (part, part_core), w_gate, w_up, ()),
     )
     middle = part.shape[0] // 2
     last = (links.over_y(part_pair[:middle]), links.over_pair(part_y[middle:]))
     pair_core, y_core = links.over_core(part_pair), links.over_core(part_y)
 
-    early = slots((0, 0, 0), (1, 0, 0), (0, 0, 1), (0, 1, 0), (1, 0, 1), (1, 1, 0))
-    early_parts = (part, part_core, part_pair, part_y, pair_core, y_core)
-    low, high, *filled = fence(*last, *finish(early, early_parts, w_gate, w_up, ()))
+    early = slots((0, 0, 1), (0, 1, 0), (1, 0, 1), (1, 1, 0))
+    early_parts = (part_pair, part_y, pair_core, y_core)
+    low, high, *filled = fence(*last, *finish(early, early_parts, w_gate, w_up, filled))
     late = slots((0, 1, 1), (1, 1, 1))
     late = jnp.concatenate([2 * late, 2 * late + 1])
     late_parts = (low, links.over_core(low), high, links.over_core(high))

time: 502 us -> 502 us (level)
  waiting for transfers between devices: 151 us -> 145 us
    ppermute x6, waiting for transfers between devices: 23.2 us -> 16 us  [over_pair(): return lax.ppermute(value, 'rep', self.to_pair)]
    pallas_call x2 -> x3, Pallas kernels: 16.8 us -> 18.9 us  [finish(): pl.pallas_call(functools.partial(finish_kernel, count, ff), out_shape=tup...]
    unnamed x157 -> x155, local copies, waits for them, and re-layouts: 16.6 us -> 16.9 us
  transfers between devices with their start and end apart: 49 -> 49, of which waited for: 22 -> 20; matrix products, arithmetic and copies ran while one was open for 35% -> 36% of each run, Pallas kernels for 12% -> 13%
where the time goes in v7:
time: 502 us; the launch traced here: 493 us
  waiting for transfers between devices  145 us (29%)
  local copies, waits for them, and re-layouts  85.8 us (17%)
  Pallas kernels  68.7 us (14%)
  starting transfers between devices  65.6 us (13%)
  matrix products  57.6 us (11%)
  other arithmetic  55 us (11%)
  between operations  15.7 us (3%)
    ppermute x6, waiting for transfers between devices, over_far(): return lax.ppermute(value, 'rep', self.to_far)  61.3 us
    dot_general x17, matrix products, dot(): lax.dot_general(left, right, ((contract[:1], contract[1:]), ((), ())), pr...  57.6 us
    all_to_all x2, waiting for transfers between devices, to_heads(): return lax.all_to_all(chunks, 'rep', 0, 0, tiled=True)  28.7 us
    pallas_call x1, Pallas kernels, attend_back(): pl.pallas_call(functools.partial(attend_back_kernel, head_dim, bq, bk), o...  24 us
    ppermute x9, waiting for transfers between devices, over_x(): return lax.ppermute(value, 'shard', [(0, 1), (1, 0)])  23.5 us
    pallas_call x3, Pallas kernels, finish(): pl.pallas_call(functools.partial(finish_kernel, count, ff), out_shape=tup...  18.9 us
    pallas_call x1, Pallas kernels, attend(): pl.pallas_call(functools.partial(attend_kernel, head_dim, bq, bk), out_sh...  17.9 us
    unnamed x155, local copies, waits for them, and re-layouts  16.9 us
  transfers between devices with their start and end apart: 49, of which 20 were waited for; matrix products, arithmetic and copies ran while one was open for 36% of the time, Pallas kernels for 13%

profile of v7, /device:TPU:0, one launch (start us, length us, event | category | flops | bytes accessed | tf_op | source)
XLA Modules:
  0.0 493.2 jit_solution(7816835329424509804)
XLA Ops:
  8.6 3.0 collective-permute-start
  16.7 3.1 collective-permute-start.1
  19.8 5.6 %fusion.17 = (f32[2048,128]{1,0:T(8,128)}, f32[2048,128]{1,0:T(8,128)}) fusion(f32[128]{0:T(128)S(1)} %get-tuple-element.257, f32[128]{0:T(128)S(1)} %get-tuple-element.258, f32[2048]{0:T(1024)S(1)} %iota_convert_fusion), kind=kLoop, calls=%fused_computation.57 | loop fusion | flops 524288 | bytes 2106368 | tf_op jit(solution)/shard_map/mul | solution.py:40
  25.4 5.8 %collective-permute-done.1 = bf16[128,1024]{1,0:T(8,128)(2,1)S(1)} collective-permute-done((bf16[128,1024]{1,0:T(8,128)(2,1)S(1)}, bf16[128,1024]{1,0:T(8,128)(2,1)S(1)}, u32[]{:S(2)}, u32[]{:S(2)}) %collective-permute-start.1) | collective-permute-done | bytes 262176 | tf_op jit(solution)/shard_map/ppermute | solution.py:236
  40.8 10.7 %collective-permute-done.2 = bf16[256,3072]{1,0:T(8,128)(2,1)} collective-permute-done((bf16[256,3072]{1,0:T(8,128)(2,1)}, bf16[256,3072]{1,0:T(8,128)(2,1)}, u32[]{:S(2)}, u32[]{:S(2)}) %collective-permute-start.2) | collective-permute-done | bytes 1572896 | tf_op jit(solution)/shard_map/ppermute | solution.py:227
  64.1 2.8 copy.44
  66.9 6.6 %all-to-all-start = ((bf16[16,128,384]{1,2,0:T(8,128)(2,1)}), bf16[16,128,384]{1,2,0:T(8,128)(2,1)}, u32[]{:S(2)}, u32[]{:S(2)}) async-start(bf16[16,128,384]{1,2,0:T(8,128)(2,1)} %bitcast.221), calls=%async_computation | async-start | bytes 3145728 | tf_op jit(solution)/shard_map/all_to_all | solution.py:481
  76.7 28.7 %all-to-all-done = bf16[16,128,384]{1,2,0:T(8,128)(2,1)} async-done(((bf16[16,128,384]{1,2,0:T(8,128)(2,1)}), bf16[16,128,384]{1,2,0:T(8,128)(2,1)}, u32[]{:S(2)}, u32[]{:S(2)}) %all-to-all-start) | async-done | bytes 1572896 | tf_op jit(solution)/shard_map/all_to_all | solution.py:481
  108.0 17.9 %shard_map.221 = (bf16[2048,128]{1,0:T(8,128)(2,1)}, f32[128,2048]{1,0:T(8,128)}, f32[2,2048]{1,0:T(2,128)}) custom-call(s32[1]{0:T(128)} %dynamic_slice.126.prefix_ref, bf16[2048,384]{1,0:T(8,128)(2,1)} %bitcast.200, bf16[2048,384]{1,0:T(8,128)(2,1)} %bitcast.201, bf16[2048,384]{1,0:T(8,128)(2,1)} %bitcast.202), custom_call_target="tpu_custom_call" | custom-call | flops 1 | bytes 1 | tf_op jit(solution)/shard_map/pallas_call | solution.py:298
  125.9 5.8 %collective-permute-done.4 = bf16[256,6656]{1,0:T(8,128)(2,1)} collective-permute-done((bf16[256,6656]{1,0:T(8,128)(2,1)}, bf16[256,6656]{1,0:T(8,128)(2,1)}, u32[]{:S(2)}, u32[]{:S(2)}) %collective-permute-start.4) | collective-permute-done | bytes 3407904 | tf_op jit(solution)/shard_map/ppermute | solution.py:227
  134.0 3.8 constant_dynamic-update-slice_fusion.4
  141.4 6.0 %all-to-all-start.1 = ((bf16[16,128,128]{2,1,0:T(8,128)(2,1)}), bf16[16,128,128]{2,1,0:T(8,128)(2,1)S(1)}, u32[]{:S(2)}, u32[]{:S(2)}) async-start(bf16[16,128,128]{2,1,0:T(8,128)(2,1)} %bitcast.256), calls=%async_computation.1 | async-start | bytes 1048576 | tf_op jit(solution)/shard_map/all_to_all | solution.py:484
  150.0 3.8 slice_dynamic-update-slice_fusion.1
  153.8 7.9 %all-to-all-done.1 = bf16[16,128,128]{2,1,0:T(8,128)(2,1)S(1)} async-done(((bf16[16,128,128]{2,1,0:T(8,128)(2,1)}), bf16[16,128,128]{2,1,0:T(8,128)(2,1)S(1)}, u32[]{:S(2)}, u32[]{:S(2)}) %all-to-all-start.1) | async-done | bytes 524320 | tf_op jit(solution)/shard_map/all_to_all | solution.py:484
  166.6 3.9 slice_dynamic-update-slice_fusion
  170.5 6.2 %fusion.74 = f32[256,5632]{1,0:T(8,128)S(1)} fusion(bf16[256,1024]{1,0:T(8,128)(2,1)S(1)} %multiply_convert_fusion.3, bf16[1024,5632]{1,0:T(8,128)(2,1)} %slice_dynamic-update-slice_fusion), kind=kOutput, calls=%fused_computation.208 | convolution fusion | flops 2952790016 | bytes 17825792 | tf_op jit(solution)/shard_map/dot_general | solution.py:20
  184.8 2.7 constant_dynamic-update-slice_fusion.1
  187.6 2.7 constant_dynamic-update-slice_fusion
  190.3 5.2 %multiply_convert_fusion = (bf16[256,2816]{1,0:T(8,128)(2,1)S(1)}, bf16[256,2816]{1,0:T(8,128)(2,1)S(1)}) fusion(f32[256,5632]{1,0:T(8,128)S(1)} %copy-done.6, bf16[2816,1024]{1,0:T(8,128)(2,1)} %constant_dynamic-update-slice_fusion, bf16[256,1024]{1,0:T(8,128)(2,1)S(1)} %bitcast.231), kind=kOutput, calls=%fused_computation.21 | convolution fusion | flops 1485766656 | bytes 14942208 | tf_op jit(solution)/shard_map/dot_general | solution.py:20
  198.1 2.8 add_convert_fusion.2
  206.8 3.5 add_convert_fusion.1
  213.6 3.1 add_convert_fusion
  219.5 6.5 %multiply_reduce_fusion.1 = (f32[256]{0:T(256)S(1)}, f32[256,1024]{1,0:T(8,128)}) fusion(f32[256,1024]{1,0:T(8,128)} %get-tuple-element.250, f32[256]{0:T(256)S(1)} %add_rsqrt_fusion, f32[1024]{0:T(1024)S(1)} %bitcast.261, bf16[1024,5632]{1,0:T(8,128)(2,1)S(1)} %bitcast.207, bf16[256,2816]{1,0:T(8,128)(2,1)} %copy-done.25, bf16[256,2816]{1,0:T(8,128)(2,1)} %copy-done.27), kind=kOutput, calls=%fused_computation.74 | convolution fusion | flops 2959605504 | bytes 16521216 | tf_op jit(solution)/shard_map/dot_general | solution.py:20
  231.7 5.8 %all-to-all-start.2 = ((bf16[16,128,128]{2,1,0:T(8,128)(2,1)}), bf16[16,128,128]{2,1,0:T(8,128)(2,1)S(1)}, u32[]{:S(2)}, u32[]{:S(2)}) async-start(bf16[16,128,128]{2,1,0:T(8,128)(2,1)} %bitcast.26), calls=%async_computation.2 | async-start | bytes 1048576 | tf_op jit(solution)/shard_map/all_to_all | solution.py:481
  247.3 5.4 %fusion.16 = bf16[256,1024]{1,0:T(8,128)(2,1)} fusion(f32[256,1024]{1,0:T(8,128)} %get-tuple-element.250, bf16[256,2816]{1,0:T(8,128)(2,1)S(1)} %multiply_convert_fusion.2, bf16[2816,1024]{1,0:T(8,128)(2,1)} %constant_dynamic-update-slice_fusion), kind=kOutput, calls=%fused_computation.55 | convolution fusion | flops 1476919296 | bytes 8781824 | tf_op jit(solution)/shard_map/dot_general | solution.py:20
  254.4 24.0 %shard_map.225 = bf16[2048,384]{1,0:T(8,128)(2,1)} custom-call(s32[1]{0:T(128)} %dynamic_slice.126.prefix_ref, bf16[2048,384]{1,0:T(8,128)(2,1)} %bitcast.203, bf16[2048,384]{1,0:T(8,128)(2,1)} %bitcast.204, bf16[2048,384]{1,0:T(8,128)(2,1)} %bitcast.205, bf16[2048,128]{1,0:T(8,128)(2,1)} %bitcast.240, f32[128,2048]{1,0:T(8,128)} %get-tuple-element.150.att_t_ref, ...), custom_call_target="tpu_custom_call" | custom-call | flops 1 | bytes 1 | tf_op jit(solution)/shard_map/pallas_call | solution.py:323
  278.5 4.6 collective-permute-done.14
  283.0 5.0 %convolution_convert_fusion.4 = bf16[1024,384]{1,0:T(8,128)(2,1)S(1)} fusion(bf16[2048,1024]{1,0:T(8,128)(2,1)} %bitcast.262, bf16[2048,384]{1,0:T(8,128)(2,1)} %shard_map.225), kind=kOutput, calls=%fused_computation.50 | convolution fusion | flops 1611005952 | bytes 6553600 | tf_op jit(solution)/shard_map/dot_general | solution.py:20
  311.5 5.6 %all-to-all-start.3 = ((bf16[16,128,384]{1,2,0:T(8,128)(2,1)}), bf16[16,128,384]{1,2,0:T(8,128)(2,1)S(1)}, u32[]{:S(2)}, u32[]{:S(2)}) async-start(bf16[16,128,384]{1,2,0:T(8,128)(2,1)} %copy.49), calls=%async_computation.3 | async-start | bytes 3145728 | tf_op jit(solution)/shard_map/all_to_all | solution.py:484
  317.1 3.1 collective-permute-done.23
  321.3 11.3 %collective-permute-done.22 = bf16[176,512]{1,0:T(8,128)(2,1)} collective-permute-done((bf16[176,512]{1,0:T(8,128)(2,1)}, bf16[176,512]{1,0:T(8,128)(2,1)}, u32[]{:S(2)}, u32[]{:S(2)}) %collective-permute-start.22) | collective-permute-done | bytes 180256 | tf_op jit(solution)/shard_map/ppermute | solution.py:236
  339.0 2.9 collective-permute-start.26
  342.0 24.1 %collective-permute-done.25 = bf16[176,512]{1,0:T(8,128)(2,1)} collective-permute-done((bf16[176,512]{1,0:T(8,128)(2,1)}, bf16[176,512]{1,0:T(8,128)(2,1)}, u32[]{:S(2)}, u32[]{:S(2)}) %collective-permute-start.25) | collective-permute-done | bytes 180256 | tf_op jit(solution)/shard_map/ppermute | solution.py:236
  371.8 3.1 collective-permute-done.24
  382.7 2.7 collective-permute-start.28
  385.5 3.3 collective-permute-start.29
  388.7 4.7 multiply_reduce_fusion
  393.5 2.8 multiply_add_fusion
  399.8 3.7 collective-permute-done.27
  403.7 3.6 collective-permute-start.31
  409.7 14.4 %collective-permute-done.30 = bf16[32,6656]{1,0:T(8,128)(2,1)S(1)} collective-permute-done((bf16[32,6656]{1,0:T(8,128)(2,1)S(1)}, bf16[32,6656]{1,0:T(8,128)(2,1)S(1)}, u32[]{:S(2)}, u32[]{:S(2)}) %collective-permute-start.30) | collective-permute-done | bytes 426016 | tf_op jit(solution)/shard_map/ppermute | solution.py:236
  425.9 9.9 %collective-permute-done.35 = bf16[1024,384]{1,0:T(8,128)(2,1)S(1)} collective-permute-done((bf16[1024,384]{1,0:T(8,128)(2,1)S(1)}, bf16[1024,384]{1,0:T(8,128)(2,1)S(1)}, u32[]{:S(2)}, u32[]{:S(2)}) %collective-permute-start.35) | collective-permute-done | bytes 786464 | tf_op jit(solution)/shard_map/ppermute | solution.py:233
  437.5 3.7 collective-permute-done.37.refs_1_
  441.1 4.9 shard_map.227
  446.1 4.8 fusion.4
  450.8 8.0 %shard_map.226 = (f32[512,1024]{1,0:T(8,128)}, f32[512,1024]{1,0:T(8,128)}, f32[512,1024]{1,0:T(8,128)}, f32[512,128]{1,0:T(8,128)}) custom-call(s32[1]{0:T(128)} %bitcast.71.core_ref, bf16[2,2,2,256,384]{4,3,2,1,0:T(8,128)(2,1)} %bitcast.223, bf16[2,2,2,256,384]{4,3,2,1,0:T(8,128)(2,1)} %bitcast.73.other_ref, bf16[512,1024]{1,0:T(8,128)(2,1)} %wq_ref.1, ...), custom_call_target="tpu_custom_call" | custom-call | flops 1 | bytes 1 | tf_op jit(solution)/shard_map/pallas_call | solution.py:370
  465.3 7.6 %shard_map.228 = (f32[512,2816]{1,0:T(8,128)}, f32[512,2816]{1,0:T(8,128)}, f32[512,1024]{1,0:T(8,128)}, f32[512,128]{1,0:T(8,128)}) custom-call(s32[4]{0:T(128)} %pad_add_fusion.2.slots_ref, bf16[64,6656]{1,0:T(8,128)(2,1)} %collective-permute-done.32.refs_0_, ...), custom_call_target="tpu_custom_call", output_to_operand_aliasing={{0}: (7, {}), {1}: (8, {}), {2}: (9, {}), {3}: (10, {})} | custom-call | flops 1 | bytes 1 | tf_op jit(solution)/shard_map/pallas_call | solution.py:437
  477.8 6.4 %shard_map.229 = (f32[512,2816]{1,0:T(8,128)}, f32[512,2816]{1,0:T(8,128)}, f32[512,1024]{1,0:T(8,128)}, f32[512,128]{1,0:T(8,128)}) custom-call(s32[4]{0:T(128)} %pad_add_fusion.1.slots_ref, bf16[32,6656]{1,0:T(8,128)(2,1)} %copy-done.60, bf16[32,6656]{1,0:T(8,128)(2,1)} %copy-done.62, ...), custom_call_target="tpu_custom_call", output_to_operand_aliasing={{0}: (7, {}), {1}: (8, {}), {2}: (9, {}), {3}: (10, {})} | custom-call | flops 1 | bytes 1 | tf_op jit(solution)/shard_map/pallas_call | solution.py:437
  (345 shorter events, 153.9 us)
Async XLA Ops:
  7.2 100.9 %all-gather.2.cloned.1.call-start = ((), (), s32[]{:S(2)}) async-start(), calls=%async_computation.4 | async-start | bytes 4718592 | tf_op jit(solution)/shard_map/all_gather | solution.py:706
  8.6 7.0 %collective-permute-start = (bf16[2,512]{1,0:T(2,128)(2,1)S(1)}, bf16[2,512]{1,0:T(2,128)(2,1)S(1)}, u32[]{:S(2)}, u32[]{:S(2)}) collective-permute-start(bf16[2,512]{1,0:T(2,128)(2,1)S(1)} %pad_maximum_fusion.11), channel_id=1, source_target_pairs={{0,1},{1,0},{2,3},{3,2},{4,5},{5,4},{6,7},{7,6},{8,9},{9,8},{10,11... | collective-permute-start | bytes 6152 | tf_op jit(solution)/shard_map/ppermute | solution.py:227
  15.3 36.2 %collective-permute-start.2 = (bf16[256,3072]{1,0:T(8,128)(2,1)}, bf16[256,3072]{1,0:T(8,128)(2,1)}, u32[]{:S(2)}, u32[]{:S(2)}) collective-permute-start(bf16[256,3072]{1,0:T(8,128)(2,1)} %pad_maximum_fusion.2), channel_id=1, source_target_pairs={{0,1},{1,0},{2,3},{3,2},{4,5},{5,4},{6,7},{7,6},{8,9},{9,8},{10,11... | collective-permute-start | bytes 4718600 | tf_op jit(solution)/shard_map/ppermute | solution.py:227
  16.7 14.5 %collective-permute-start.1 = (bf16[128,1024]{1,0:T(8,128)(2,1)S(1)}, bf16[128,1024]{1,0:T(8,128)(2,1)S(1)}, u32[]{:S(2)}, u32[]{:S(2)}) collective-permute-start(bf16[128,1024]{1,0:T(8,128)(2,1)S(1)} %get-tuple-element.242), channel_id=1, source_target_pairs={{0,16},{2,18},{4,20},{6,22},{8,24},{10,26},{12,28},{14,30},{16,0},... | collective-permute-start | bytes 786440 | tf_op jit(solution)/shard_map/ppermute | solution.py:236
  51.5 5.8 %collective-permute-start.3 = (bf16[256,3072]{1,0:T(8,128)(2,1)}, bf16[256,3072]{1,0:T(8,128)(2,1)S(1)}, u32[]{:S(2)}, u32[]{:S(2)}) collective-permute-start(bf16[256,3072]{1,0:T(8,128)(2,1)} %collective-permute-done.2), channel_id=1, source_target_pairs={{0,2},{2,0},{4,6},{6,4},{8,10},{10,8},{12,14},{14,12},{16,18},{18,... | collective-permute-start | bytes 4718600 | tf_op jit(solution)/shard_map/ppermute | solution.py:224
  55.3 76.4 %collective-permute-start.4 = (bf16[256,6656]{1,0:T(8,128)(2,1)}, bf16[256,6656]{1,0:T(8,128)(2,1)}, u32[]{:S(2)}, u32[]{:S(2)}) collective-permute-start(bf16[256,6656]{1,0:T(8,128)(2,1)} %pad_maximum_fusion), channel_id=1, source_target_pairs={{0,1},{1,0},{2,3},{3,2},{4,5},{5,4},{6,7},{7,6},{8,9},{9,8},{10,11... | collective-permute-start | bytes 10223624 | tf_op jit(solution)/shard_map/ppermute | solution.py:227
  66.9 38.5 %all-to-all-start = ((bf16[16,128,384]{1,2,0:T(8,128)(2,1)}), bf16[16,128,384]{1,2,0:T(8,128)(2,1)}, u32[]{:S(2)}, u32[]{:S(2)}) async-start(bf16[16,128,384]{1,2,0:T(8,128)(2,1)} %bitcast.221), calls=%async_computation | async-start | bytes 3145728 | tf_op jit(solution)/shard_map/all_to_all | solution.py:481
  131.7 30.5 %collective-permute-start.5 = (bf16[256,6656]{1,0:T(8,128)(2,1)}, bf16[256,6656]{1,0:T(8,128)(2,1)}, u32[]{:S(2)}, u32[]{:S(2)}) collective-permute-start(bf16[256,6656]{1,0:T(8,128)(2,1)} %collective-permute-done.4), channel_id=1, source_target_pairs={{0,2},{2,0},{4,6},{6,4},{8,10},{10,8},{12,14},{14,12},{16,18},{18,... | collective-permute-start | bytes 10223624 | tf_op jit(solution)/shard_map/ppermute | solution.py:224
  141.4 20.3 %all-to-all-start.1 = ((bf16[16,128,128]{2,1,0:T(8,128)(2,1)}), bf16[16,128,128]{2,1,0:T(8,128)(2,1)S(1)}, u32[]{:S(2)}, u32[]{:S(2)}) async-start(bf16[16,128,128]{2,1,0:T(8,128)(2,1)} %bitcast.256), calls=%async_computation.1 | async-start | bytes 1048576 | tf_op jit(solution)/shard_map/all_to_all | solution.py:484
  147.5 34.2 %collective-permute-start.6 = (bf16[704,1024]{1,0:T(8,128)(2,1)}, bf16[704,1024]{1,0:T(8,128)(2,1)}, u32[]{:S(2)}, u32[]{:S(2)}) collective-permute-start(bf16[704,1024]{1,0:T(8,128)(2,1)} %constant_dynamic-slice_fusion.3), channel_id=1, source_target_pairs={{0,1},{1,0},{2,3},{3,2},{4,5},{5,4},{6,7},{7,6},{8,9},{9,8},{10,11... | collective-permute-start | bytes 4325384 | tf_op jit(solution)/shard_map/ppermute | solution.py:227
  181.7 5.9 %collective-permute-start.7 = (bf16[704,1024]{1,0:T(8,128)(2,1)}, bf16[704,1024]{1,0:T(8,128)(2,1)}, u32[]{:S(2)}, u32[]{:S(2)}) collective-permute-start(bf16[704,1024]{1,0:T(8,128)(2,1)} %collective-permute-done.6), channel_id=1, source_target_pairs={{0,2},{2,0},{4,6},{6,4},{8,10},{10,8},{12,14},{14,12},{16,18},{18,... | collective-permute-start | bytes 4325384 | tf_op jit(solution)/shard_map/ppermute | solution.py:224
  184.3 13.8 %collective-permute-start.8 = (bf16[2816,512]{1,0:T(8,128)(2,1)}, bf16[2816,512]{1,0:T(8,128)(2,1)}, u32[]{:S(2)}, u32[]{:S(2)}) collective-permute-start(bf16[2816,512]{1,0:T(8,128)(2,1)} %convolution_convert_fusion.1), channel_id=1, source_target_pairs={{0,2},{2,0},{4,6},{6,4},{8,10},{10,8},{12,14},{14,12},{16,18},{18,... | collective-permute-start | bytes 8650760 | tf_op jit(solution)/shard_map/ppermute | solution.py:224
  198.1 8.6 %collective-permute-start.9 = (bf16[512,2816]{1,0:T(8,128)(2,1)}, bf16[512,2816]{1,0:T(8,128)(2,1)}, u32[]{:S(2)}, u32[]{:S(2)}) collective-permute-start(bf16[512,2816]{1,0:T(8,128)(2,1)} %convolution_convert_fusion.2), channel_id=1, source_target_pairs={{0,2},{2,0},{4,6},{6,4},{8,10},{10,8},{12,14},{14,12},{16,18},{18,... | collective-permute-start | bytes 8650760 | tf_op jit(solution)/shard_map/ppermute | solution.py:224
  204.8 8.2 %collective-permute-start.10 = (bf16[512,2816]{1,0:T(8,128)(2,1)}, bf16[512,2816]{1,0:T(8,128)(2,1)}, u32[]{:S(2)}, u32[]{:S(2)}) collective-permute-start(bf16[512,2816]{1,0:T(8,128)(2,1)} %convolution_convert_fusion), channel_id=1, source_target_pairs={{0,2},{2,0},{4,6},{6,4},{8,10},{10,8},{12,14},{14,12},{16,18},{18,... | collective-permute-start | bytes 8650760 | tf_op jit(solution)/shard_map/ppermute | solution.py:224
  206.1 34.7 %collective-permute-start.12 = (bf16[1408,512]{1,0:T(8,128)(2,1)}, bf16[1408,512]{1,0:T(8,128)(2,1)}, u32[]{:S(2)}, u32[]{:S(2)}) collective-permute-start(bf16[1408,512]{1,0:T(8,128)(2,1)} %dynamic-slice_bitcast_fusion.1), channel_id=1, source_target_pairs={{0,1},{1,0},{2,3},{3,2},{4,5},{5,4},{6,7},{7,6},{8,9},{9,8},{10,11... | collective-permute-start | bytes 4325384 | tf_op jit(solution)/shard_map/ppermute | solution.py:227
  230.7 8.4 %collective-permute-start.11 = (bf16[512,1024]{1,0:T(8,128)(2,1)}, bf16[512,1024]{1,0:T(8,128)(2,1)}, u32[]{:S(2)}, u32[]{:S(2)}) collective-permute-start(bf16[512,1024]{1,0:T(8,128)(2,1)} %convolution_convert_fusion.3), channel_id=1, source_target_pairs={{0,2},{2,0},{4,6},{6,4},{8,10},{10,8},{12,14},{14,12},{16,18},{18,... | collective-permute-start | bytes 3145736 | tf_op jit(solution)/shard_map/ppermute | solution.py:224
  231.7 21.1 %all-to-all-start.2 = ((bf16[16,128,128]{2,1,0:T(8,128)(2,1)}), bf16[16,128,128]{2,1,0:T(8,128)(2,1)S(1)}, u32[]{:S(2)}, u32[]{:S(2)}) async-start(bf16[16,128,128]{2,1,0:T(8,128)(2,1)} %bitcast.26), calls=%async_computation.2 | async-start | bytes 1048576 | tf_op jit(solution)/shard_map/all_to_all | solution.py:481
  237.5 40.9 %collective-permute-start.13 = (bf16[256,2816]{1,0:T(8,128)(2,1)}, bf16[256,2816]{1,0:T(8,128)(2,1)}, u32[]{:S(2)}, u32[]{:S(2)}) collective-permute-start(bf16[256,2816]{1,0:T(8,128)(2,1)} %dynamic-slice_bitcast_fusion), channel_id=1, source_target_pairs={{0,1},{1,0},{2,3},{3,2},{4,5},{5,4},{6,7},{7,6},{8,9},{9,8},{10,11... | collective-permute-start | bytes 4325384 | tf_op jit(solution)/shard_map/ppermute | solution.py:227
  241.7 41.3 %collective-permute-start.14 = (bf16[256,1024]{1,0:T(8,128)(2,1)}, bf16[256,1024]{1,0:T(8,128)(2,1)}, u32[]{:S(2)}, u32[]{:S(2)}) collective-permute-start(bf16[256,1024]{1,0:T(8,128)(2,1)} %dynamic-slice_bitcast_fusion.6), channel_id=1, source_target_pairs={{0,1},{1,0},{2,3},{3,2},{4,5},{5,4},{6,7},{7,6},{8,9},{9,8},{10,11... | collective-permute-start | bytes 1572872 | tf_op jit(solution)/shard_map/ppermute | solution.py:227
  245.3 37.7 %collective-permute-start.15 = (bf16[704,512]{1,0:T(8,128)(2,1)}, bf16[704,512]{1,0:T(8,128)(2,1)}, u32[]{:S(2)}, u32[]{:S(2)}) collective-permute-start(bf16[704,512]{1,0:T(8,128)(2,1)} %dynamic-slice_bitcast_fusion.5), channel_id=1, source_target_pairs={{0,4},{2,6},{4,0},{6,2},{8,12},{10,14},{12,8},{14,10},{16,20},{18,... | collective-permute-start | bytes 2162696 | tf_op jit(solution)/shard_map/ppermute | solution.py:230
  254.2 46.5 %collective-permute-start.18 = (bf16[256,2816]{1,0:T(8,128)(2,1)S(1)}, bf16[256,2816]{1,0:T(8,128)(2,1)}, u32[]{:S(2)}, u32[]{:S(2)}) collective-permute-start(bf16[256,2816]{1,0:T(8,128)(2,1)S(1)} %bitcast.246), channel_id=1, source_target_pairs={{0,4},{2,6},{4,0},{6,2},{8,12},{10,14},{12,8},{14,10},{16,20},{18,... | collective-permute-start | bytes 4325384 | tf_op jit(solution)/shard_map/ppermute | solution.py:230
  288.1 12.5 %collective-permute-start.16 = (bf16[512,384]{1,0:T(8,128)(2,1)S(1)}, bf16[512,384]{1,0:T(8,128)(2,1)S(1)}, u32[]{:S(2)}, u32[]{:S(2)}) collective-permute-start(bf16[512,384]{1,0:T(8,128)(2,1)S(1)} %dynamic-slice_bitcast_fusion.8), channel_id=1, source_target_pairs={{0,1},{1,0},{2,3},{3,2},{4,5},{5,4},{6,7},{7,6},{8,9},{9,8},{10,11... | collective-permute-start | bytes 1179656 | tf_op jit(solution)/shard_map/ppermute | solution.py:227
  291.0 9.7 %collective-permute-start.17 = (bf16[352,512]{1,0:T(8,128)(2,1)S(1)}, bf16[352,512]{1,0:T(8,128)(2,1)S(1)}, u32[]{:S(2)}, u32[]{:S(2)}) collective-permute-start(bf16[352,512]{1,0:T(8,128)(2,1)S(1)} %dynamic-slice_bitcast_fusion.9), channel_id=1, source_target_pairs={{0,8},{2,10},{4,12},{6,14},{8,0},{10,2},{12,4},{14,6},{16,24},{18,... | collective-permute-start | bytes 1081352 | tf_op jit(solution)/shard_map/ppermute | solution.py:233
  295.5 25.7 %collective-permute-start.20 = (bf16[128,2816]{1,0:T(8,128)(2,1)}, bf16[128,2816]{1,0:T(8,128)(2,1)}, u32[]{:S(2)}, u32[]{:S(2)}) collective-permute-start(bf16[128,2816]{1,0:T(8,128)(2,1)} %dynamic-slice_bitcast_fusion.3), channel_id=1, source_target_pairs={{0,4},{2,6},{4,0},{6,2},{8,12},{10,14},{12,8},{14,10},{16,20},{18,... | collective-permute-start | bytes 2162696 | tf_op jit(solution)/shard_map/ppermute | solution.py:230
  299.1 22.2 %collective-permute-start.21 = (bf16[128,1024]{1,0:T(8,128)(2,1)}, bf16[128,1024]{1,0:T(8,128)(2,1)}, u32[]{:S(2)}, u32[]{:S(2)}) collective-permute-start(bf16[128,1024]{1,0:T(8,128)(2,1)} %dynamic-slice_bitcast_fusion.10), channel_id=1, source_target_pairs={{0,4},{2,6},{4,0},{6,2},{8,12},{10,14},{12,8},{14,10},{16,20},{18,... | collective-permute-start | bytes 786440 | tf_op jit(solution)/shard_map/ppermute | solution.py:230
  304.4 28.2 %collective-permute-start.19 = (bf16[128,2816]{1,0:T(8,128)(2,1)}, bf16[128,2816]{1,0:T(8,128)(2,1)}, u32[]{:S(2)}, u32[]{:S(2)}) collective-permute-start(bf16[128,2816]{1,0:T(8,128)(2,1)} %dynamic-slice_bitcast_fusion.4), channel_id=1, source_target_pairs={{0,1},{1,0},{2,3},{3,2},{4,5},{5,4},{6,7},{7,6},{8,9},{9,8},{10,11... | collective-permute-start | bytes 2162696 | tf_op jit(solution)/shard_map/ppermute | solution.py:227
  305.3 14.8 %collective-permute-start.23 = (bf16[256,384]{1,0:T(8,128)(2,1)S(1)}, bf16[256,384]{1,0:T(8,128)(2,1)}, u32[]{:S(2)}, u32[]{:S(2)}) collective-permute-start(bf16[256,384]{1,0:T(8,128)(2,1)S(1)} %constant_dynamic-slice_fusion), channel_id=1, source_target_pairs={{0,16},{2,18},{4,20},{6,22},{8,24},{10,26},{12,28},{14,30},{16,0},... | collective-permute-start | bytes 589832 | tf_op jit(solution)/shard_map/ppermute | solution.py:520
  309.2 23.4 %collective-permute-start.22 = (bf16[176,512]{1,0:T(8,128)(2,1)}, bf16[176,512]{1,0:T(8,128)(2,1)}, u32[]{:S(2)}, u32[]{:S(2)}) collective-permute-start(bf16[176,512]{1,0:T(8,128)(2,1)} %dynamic-slice_bitcast_fusion.12), channel_id=1, source_target_pairs={{0,16},{2,18},{4,20},{6,22},{8,24},{10,26},{12,28},{14,30},{16,0},... | collective-permute-start | bytes 540680 | tf_op jit(solution)/shard_map/ppermute | solution.py:236
  311.5 65.7 %all-to-all-start.3 = ((bf16[16,128,384]{1,2,0:T(8,128)(2,1)}), bf16[16,128,384]{1,2,0:T(8,128)(2,1)S(1)}, u32[]{:S(2)}, u32[]{:S(2)}) async-start(bf16[16,128,384]{1,2,0:T(8,128)(2,1)} %copy.49), calls=%async_computation.3 | async-start | bytes 3145728 | tf_op jit(solution)/shard_map/all_to_all | solution.py:484
  339.0 35.9 %collective-permute-start.24 = (bf16[64,6656]{1,0:T(8,128)(2,1)}, bf16[64,6656]{1,0:T(8,128)(2,1)}, u32[]{:S(2)}, u32[]{:S(2)}) collective-permute-start(bf16[64,6656]{1,0:T(8,128)(2,1)} %dynamic-slice_bitcast_fusion.2), channel_id=1, source_target_pairs={{0,8},{2,10},{4,12},{6,14},{8,0},{10,2},{12,4},{14,6},{16,24},{18,... | collective-permute-start | bytes 2555912 | tf_op jit(solution)/shard_map/ppermute | solution.py:233
  339.0 27.0 %collective-permute-start.25 = (bf16[176,512]{1,0:T(8,128)(2,1)}, bf16[176,512]{1,0:T(8,128)(2,1)}, u32[]{:S(2)}, u32[]{:S(2)}) collective-permute-start(bf16[176,512]{1,0:T(8,128)(2,1)} %fusion.31), channel_id=1, source_target_pairs={{0,16},{2,18},{4,20},{6,22},{8,24},{10,26},{12,28},{14,30},{16,0},... | collective-permute-start | bytes 540680 | tf_op jit(solution)/shard_map/ppermute | solution.py:236
  339.0 30.9 %collective-permute-start.26 = (bf16[256,384]{1,0:T(8,128)(2,1)S(1)}, bf16[256,384]{1,0:T(8,128)(2,1)}, u32[]{:S(2)}, u32[]{:S(2)}) collective-permute-start(bf16[256,384]{1,0:T(8,128)(2,1)S(1)} %add_convert_fusion.4), channel_id=1, source_target_pairs={{0,16},{2,18},{4,20},{6,22},{8,24},{10,26},{12,28},{14,30},{16,0},... | collective-permute-start | bytes 589832 | tf_op jit(solution)/shard_map/ppermute | solution.py:236
  381.6 21.9 %collective-permute-start.27 = (bf16[32,6656]{1,0:T(8,128)(2,1)S(1)}, bf16[32,6656]{1,0:T(8,128)(2,1)S(1)}, u32[]{:S(2)}, u32[]{:S(2)}) collective-permute-start(bf16[32,6656]{1,0:T(8,128)(2,1)S(1)} %dynamic-slice_bitcast_fusion.7), channel_id=1, source_target_pairs={{0,16},{2,18},{4,20},{6,22},{8,24},{10,26},{12,28},{14,30},{16,0},... | collective-permute-start | bytes 1277960 | tf_op jit(solution)/shard_map/ppermute | solution.py:236
  382.7 16.4 %collective-permute-start.28 = (bf16[352,512]{1,0:T(8,128)(2,1)}, bf16[352,512]{1,0:T(8,128)(2,1)S(1)}, u32[]{:S(2)}, u32[]{:S(2)}) collective-permute-start(bf16[352,512]{1,0:T(8,128)(2,1)} %maximum_select_fusion.10), channel_id=1, source_target_pairs={{0,8},{2,10},{4,12},{6,14},{8,0},{10,2},{12,4},{14,6},{16,24},{18,... | collective-permute-start | bytes 1081352 | tf_op jit(solution)/shard_map/ppermute | solution.py:233
  385.5 14.0 %collective-permute-start.29 = (bf16[512,384]{1,0:T(8,128)(2,1)S(1)}, bf16[512,384]{1,0:T(8,128)(2,1)S(1)}, u32[]{:S(2)}, u32[]{:S(2)}) collective-permute-start(bf16[512,384]{1,0:T(8,128)(2,1)S(1)} %copy-done.49), channel_id=1, source_target_pairs={{0,4},{2,6},{4,0},{6,2},{8,12},{10,14},{12,8},{14,10},{16,20},{18,... | collective-permute-start | bytes 1179656 | tf_op jit(solution)/shard_map/ppermute | solution.py:230
  403.6 20.5 %collective-permute-start.30 = (bf16[32,6656]{1,0:T(8,128)(2,1)S(1)}, bf16[32,6656]{1,0:T(8,128)(2,1)S(1)}, u32[]{:S(2)}, u32[]{:S(2)}) collective-permute-start(bf16[32,6656]{1,0:T(8,128)(2,1)S(1)} %fusion.26), channel_id=1, source_target_pairs={{0,16},{2,18},{4,20},{6,22},{8,24},{10,26},{12,28},{14,30},{16,0},... | collective-permute-start | bytes 1277960 | tf_op jit(solution)/shard_map/ppermute | solution.py:236
  403.7 21.5 %collective-permute-start.31 = (bf16[704,512]{1,0:T(8,128)(2,1)S(1)}, bf16[704,512]{1,0:T(8,128)(2,1)S(1)}, u32[]{:S(2)}, u32[]{:S(2)}) collective-permute-start(bf16[704,512]{1,0:T(8,128)(2,1)S(1)} %maximum_select_fusion.7), channel_id=1, source_target_pairs={{0,4},{2,6},{4,0},{6,2},{8,12},{10,14},{12,8},{14,10},{16,20},{18,... | collective-permute-start | bytes 2162696 | tf_op jit(solution)/shard_map/ppermute | solution.py:230
  407.3 28.6 %collective-permute-start.35 = (bf16[1024,384]{1,0:T(8,128)(2,1)S(1)}, bf16[1024,384]{1,0:T(8,128)(2,1)S(1)}, u32[]{:S(2)}, u32[]{:S(2)}) collective-permute-start(bf16[1024,384]{1,0:T(8,128)(2,1)S(1)} %maximum_select_fusion.6), channel_id=1, source_target_pairs={{0,8},{2,10},{4,12},{6,14},{8,0},{10,2},{12,4},{14,6},{16,24},{18,... | collective-permute-start | bytes 2359304 | tf_op jit(solution)/shard_map/ppermute | solution.py:233
  425.9 20.2 %collective-permute-start.34 = (bf16[1408,512]{1,0:T(8,128)(2,1)S(1)}, bf16[1408,512]{1,0:T(8,128)(2,1)}, u32[]{:S(2)}, u32[]{:S(2)}) collective-permute-start(bf16[1408,512]{1,0:T(8,128)(2,1)S(1)} %maximum_select_fusion.2), channel_id=1, source_target_pairs={{0,2},{2,0},{4,6},{6,4},{8,10},{10,8},{12,14},{14,12},{16,18},{18,... | collective-permute-start | bytes 4325384 | tf_op jit(solution)/shard_map/ppermute | solution.py:224
  436.3 14.5 %collective-permute-start.36 = (bf16[2048,384]{1,0:T(8,128)(2,1)S(1)}, bf16[2048,384]{1,0:T(8,128)(2,1)}, u32[]{:S(2)}, u32[]{:S(2)}) collective-permute-start(bf16[2048,384]{1,0:T(8,128)(2,1)S(1)} %maximum_select_fusion.1), channel_id=1, source_target_pairs={{0,2},{2,0},{4,6},{6,4},{8,10},{10,8},{12,14},{14,12},{16,18},{18,... | collective-permute-start | bytes 4718600 | tf_op jit(solution)/shard_map/ppermute | solution.py:224
  436.4 4.7 collective-permute-start.37
  436.9 21.9 %collective-permute-start.32 = (bf16[64,6656]{1,0:T(8,128)(2,1)}, bf16[64,6656]{1,0:T(8,128)(2,1)}, u32[]{:S(2)}, u32[]{:S(2)}) collective-permute-start(bf16[64,6656]{1,0:T(8,128)(2,1)} %maximum_select_fusion.5.refs_0_), channel_id=1, source_target_pairs={{0,8},{2,10},{4,12},{6,14},{8,0},{10,2},{12,4},{14,6},{16,24},{18,... | collective-permute-start | bytes 2555912 | tf_op jit(solution)/shard_map/ppermute | solution.py:233
  436.9 21.9 %collective-permute-start.33 = (bf16[64,6656]{1,0:T(8,128)(2,1)}, bf16[64,6656]{1,0:T(8,128)(2,1)}, u32[]{:S(2)}, u32[]{:S(2)}) collective-permute-start(bf16[64,6656]{1,0:T(8,128)(2,1)} %maximum_select_fusion.5.refs_0_), channel_id=1, source_target_pairs={{0,4},{2,6},{4,0},{6,2},{8,12},{10,14},{12,8},{14,10},{16,20},{18,... | collective-permute-start | bytes 2555912 | tf_op jit(solution)/shard_map/ppermute | solution.py:230
  458.8 4.7 collective-permute-start.40
  459.0 4.5 collective-permute-start.41
  461.4 11.9 %collective-permute-start.38 = (bf16[32,6656]{1,0:T(8,128)(2,1)S(1)}, bf16[32,6656]{1,0:T(8,128)(2,1)S(1)}, u32[]{:S(2)}, u32[]{:S(2)}) collective-permute-start(bf16[32,6656]{1,0:T(8,128)(2,1)S(1)} %slice.138), channel_id=1, source_target_pairs={{0,4},{2,6},{4,0},{6,2},{8,12},{10,14},{12,8},{14,10},{16,20},{18,... | collective-permute-start | bytes 1277960 | tf_op jit(solution)/shard_map/ppermute | solution.py:230
  461.5 11.9 %collective-permute-start.39 = (bf16[32,6656]{1,0:T(8,128)(2,1)S(1)}, bf16[32,6656]{1,0:T(8,128)(2,1)S(1)}, u32[]{:S(2)}, u32[]{:S(2)}) collective-permute-start(bf16[32,6656]{1,0:T(8,128)(2,1)S(1)} %slice.139), channel_id=1, source_target_pairs={{0,8},{2,10},{4,12},{6,14},{8,0},{10,2},{12,4},{14,6},{16,24},{18,... | collective-permute-start | bytes 1277960 | tf_op jit(solution)/shard_map/ppermute | solution.py:233
  473.5 2.9 collective-permute-start.43
  (77 other events, 473.6 us)
Sparse Core Ops, SparseCore 0:
  32.2 30.2 all-gather.1
